TPU v7x, 32 devices: a whole 2x2x4 slice. The times are simulated.
32 devices in a mesh: dom: 32 (over z, y, x, core).
Axes of the slice: x: 2, y: 2, z: 4, core: 2. Of those that a mesh axis runs over, the one named last changes fastest.
Arguments:
- rhs: float32 [8, 212992], P(None, 'dom'), may hold values from -25 to 25, as said below
- potential: float32 [212992], P('dom'), may hold values from 0.5 to 2
- precond: float32 [212992], P('dom'), may hold values from 0.05 to 0.5
- shift: float32 [8], replicated, may hold values from 0.3 to 3
- stiffness: float32 [343, 343], replicated, may hold values from -0.4 to 2, as said below
- cell_scale: float32 [1024], P('dom'), may hold values from 0.5 to 2
- conn: int32 [1024, 343], P('dom'), may hold values from 0 to 7487, as said below
- cell_count: int32 [32], replicated, may hold values from 1 to 32, as said below
- projector: float32 [256, 8, 343], P('dom'), may hold values from -0.6 to 0.6
- support_cell: int32 [256], P('dom'), may hold values from 0 to 31, as said below
- support_atom: int32 [256], P('dom'), may hold values from 0 to 63, as said below
- support_count: int32 [32], replicated, may hold values from 4 to 8, as said below
- atom_matrix: float32 [64, 8, 8], P('dom'), may hold values from -2 to 15, as said below
Outputs:
- solution: float32 [8, 212992], P(None, 'dom')
- residual: float32 [8, 212992], P(None, 'dom')
Inputs may be any that keep to these rules, and one draw needn't show every extreme that they name: `rhs`: row v rises in scale along the nodes. `stiffness`: symmetric positive definite. `atom_matrix`: each atom's matrix is symmetric positive definite. Block b's live cells are its slots 0 to cell_count[b] - 1; blocks 2k and 2k + 1 together hold at most 40 live cells, and some block holds 32. `conn`: a local index i of block b is column b * 6656 + i of the field padded by 416 zero columns at each end: indices below 416 are the previous block's last nodes, indices from 7072 on the next block's first nodes. `support_cell`: every entry names a live cell of its block. `support_atom`: atom a is owned by block a // 2; an entry of block b names an atom owned by block b - 1, b or b + 1. Block b's live entries are its first support_count[b]; some block has 8.
All inputs are finite; a program needn't handle non-finite values.
Results may differ from a plain program's by a relative error of at most 0.0003.
Values sent between devices are 32-bit elements; how exact they have to be, the bound alone decides.
No kernel may reach another device: no remote copies, remote signals or barrier semaphores. Data moves between devices by JAX's collectives and lax.ppermute only.
A program may use at most 64 MiB of HBM per device.

v0:
```python
import jax
import jax.numpy as jnp
from jax import lax
from jax.sharding import PartitionSpec as P

ITERS = 2


HIGH = lax.Precision.HIGHEST


def with_halo(cells, sides, width):
    for axis, dim in sides:
        count = lax.axis_size(axis)
        ends = count - 1
        head = lax.slice_in_dim(cells, 0, width, axis=dim)
        tail = lax.slice_in_dim(cells, cells.shape[dim] - width, cells.shape[dim], axis=dim)
        cells = jnp.concatenate(
            [
                lax.ppermute(tail, axis, [(i, (i + 1) % count) for i in range(ends)]),
                cells,
                lax.ppermute(head, axis, [((i + 1) % count, i) for i in range(ends)]),
            ],
            axis=dim,
        )
    return cells


def on_device(
    rhs,
    potential,
    precond,
    shift,
    stiffness,
    cell_scale,
    conn,
    cell_count,
    projector,
    support_cell,
    support_atom,
    support_count,
    atom_matrix,
):
    position = lax.axis_index("dom")
    vectors = rhs.shape[0]
    node_dev = rhs.shape[1]
    slots = conn.shape[0]
    entries = projector.shape[0]
    channels = projector.shape[1]
    owned = atom_matrix.shape[0]
    ghost = node_dev // 16
    live_cells = cell_count[position]
    slot_number = jnp.arange(slots)
    cell_weight = cell_scale * (slot_number < live_cells).astype(jnp.float32)
    entry_live = jnp.arange(entries) < support_count[position]
    support_nodes = conn[support_cell]
    targets = jnp.arange(3 * owned)
    relative = support_atom - (position - 1) * owned
    selector = ((relative[:, None] == targets[None, :]) & entry_live[:, None]).astype(jnp.float32)
    solution = jnp.zeros_like(rhs)
    residual = rhs
    search = precond[None, :] * residual
    smoothed = search
    gamma = jnp.sum(residual * smoothed, axis=1)
    for step in range(ITERS):
        apply_window = with_halo(search, (("dom", 1),), ghost)
        scaled = apply_window[:, conn] * cell_weight[None, :, None]
        element_out = jnp.einsum("vcn,mn->vcm", scaled, stiffness, precision=HIGH)
        values = apply_window[:, support_nodes]
        partial_value = jnp.einsum("sjn,vsn->jvs", projector, values, precision=HIGH)
        flat = partial_value.reshape(channels * vectors, entries)
        summed = jnp.dot(flat, selector, precision=HIGH).reshape(channels, vectors, -1)
        sides = jnp.concatenate([summed[:, :, :owned], summed[:, :, 2 * owned :]], axis=2)
        arrived = with_halo(sides, (("dom", 2),), owned)
        mine = summed[:, :, owned : 2 * owned] + arrived[:, :, :owned] + arrived[:, :, 3 * owned :]
        applied = jnp.einsum("aij,jva->iva", atom_matrix, mine, precision=HIGH)
        spread = with_halo(applied, (("dom", 2),), owned)
        back = jnp.dot(spread.reshape(channels * vectors, -1), selector.T, precision=HIGH)
        back = back.reshape(channels, vectors, entries)
        support_out = jnp.einsum("sjn,jvs->vsn", projector, back, precision=HIGH)
        assembled = jnp.zeros_like(apply_window)
        assembled = assembled.at[:, conn].add(element_out)
        assembled = assembled.at[:, support_nodes].add(support_out)
        rims = jnp.concatenate([assembled[:, :ghost], assembled[:, ghost + node_dev :]], axis=1)
        apply_arrived = with_halo(rims, (("dom", 1),), ghost)
        inner = assembled[:, ghost : ghost + node_dev]
        inner = inner.at[:, :ghost].add(apply_arrived[:, :ghost])
        inner = inner.at[:, node_dev - ghost :].add(apply_arrived[:, 3 * ghost :])
        image = inner + (potential[None, :] + shift[:, None]) * search
        terms = [jnp.sum(search * image, axis=1)]
        if step == 0:
            terms.append(gamma)
        if step + 1 < ITERS:
            terms.append(jnp.sum(image * smoothed, axis=1))
            terms.append(jnp.sum(image * precond[None, :] * image, axis=1))
        totals = lax.psum(jnp.stack(terms), "dom")
        following = 1
        if step == 0:
            gamma = totals[1]
            following = 2
        step_size = gamma / totals[0]
        solution = solution + step_size[:, None] * search
        residual = residual - step_size[:, None] * image
        if step + 1 < ITERS:
            fresh = (
                gamma
                - 2.0 * step_size * totals[following]
                + step_size * step_size * totals[following + 1]
            )
            smoothed = precond[None, :] * residual
            search = smoothed + (fresh / gamma)[:, None] * search
            gamma = fresh
    return (solution, residual)


def solution(mesh):
    placed = (
        P(None, "dom"),
        P("dom"),
        P("dom"),
        P(),
        P(),
        P("dom"),
        P("dom", None),
        P(),
        P("dom", None, None),
        P("dom"),
        P("dom"),
        P(),
        P("dom", None, None),
    )
    return jax.shard_map(
        on_device,
        mesh=mesh,
        in_specs=placed,
        out_specs=(P(None, "dom"), P(None, "dom")),
        check_vma=False,
    )
```

profile of v0, /device:TPU:1, one launch (start us, length us, event | category | flops | bytes accessed | tf_op | source)
XLA Modules:
  0.0 417.5 jit_solution(7246007911148108436)
XLA Ops:
  3.8 4.5 %collective-permute-start = (f32[8,416]{1,0:T(8,128)S(1)}, f32[8,416]{1,0:T(8,128)S(1)}, u32[]{:S(2)}, u32[]{:S(2)}) collective-permute-start(f32[8,416]{1,0:T(8,128)S(1)} %get-tuple-element.75), channel_id=1, source_target_pairs={{0,1},{1,2},{2,3},{3,4},{4,5},{5,6},{6,7},{7,8},{8,9},{9,10},{10,1... | collective-permute-start | bytes 39944 | tf_op jit(solution)/shard_map/ppermute | solution.py:20
  18.3 6.9 %gather_fusion.2 = f32[2744,8]{1,0:T(8,128)S(1)} fusion(f32[8,7488]{0,1:T(8,128)} %copy.107, s32[3072]{0:T(1024)S(1)} %pad_clamp_fusion.1), kind=kCustom, calls=%fused_computation.2 | custom fusion | bytes 186592 | tf_op jit(solution)/shard_map/gather | solution.py:69
  31.6 23.2 %gather_fusion = f32[10976,8]{1,0:T(8,128)} fusion(f32[8,7488]{0,1:T(8,128)} %copy.107, s32[11264]{0:T(1024)S(1)} %pad_clamp_fusion), kind=kCustom, calls=%fused_computation | custom fusion | bytes 746368 | tf_op jit(solution)/shard_map/gather | solution.py:67
  54.8 3.4 copy.108
  60.8 3.9 collective-permute-start.4
  65.9 3.3 copy.109
  69.2 62.9 %scatter_custom_fusion = f32[8,7488]{0,1:T(8,128)} fusion(s32[10976]{0:T(1024)S(1)} %reshape.235, f32[10976,8]{1,0:T(8,128)} %copy.109, f32[]{:T(128)} %constant.111.clone.1), kind=kCustom, calls=%fused_computation.11 | custom fusion | flops 87808 | bytes 240128 | tf_op jit(solution)/shard_map/scatter-add | solution.py:82
  133.4 19.4 %scatter_fusion = f32[8,7488]{0,1:T(8,128)} fusion(f32[8,7488]{0,1:T(8,128)} %scatter_custom_fusion, s32[2744]{0:T(1024)S(1)} %reshape.243, f32[2744,8]{1,0:T(8,128)S(1)} %copy.119), kind=kCustom, calls=%fused_computation.6 | custom fusion | flops 21952 | bytes 274400 | tf_op jit(solution)/shard_map/scatter-add | solution.py:83
  157.1 4.0 slice.177
  170.5 41.3 %psum.14 = f32[4,8]{1,0:T(4,128)S(1)} all-reduce(f32[4,8]{1,0:T(4,128)S(1)} %pad_maximum_fusion.2), channel_id=1, replica_groups=mesh['dom'=32] {'dom'}, use_global_device_ids=true, to_apply=%region_6.0 | all-reduce | flops 32 | bytes 256 | tf_op jit(solution)/shard_map/psum | solution.py:96
  212.0 3.3 collective-permute-start.9
  215.3 3.8 collective-permute-start.8
  223.0 6.9 %gather_fusion.4 = f32[2744,8]{1,0:T(8,128)S(1)} fusion(f32[8,7488]{0,1:T(8,128)} %copy.124, s32[3072]{0:T(1024)S(1)} %pad_clamp_fusion.1), kind=kCustom, calls=%fused_computation.4 | custom fusion | bytes 186592 | tf_op jit(solution)/shard_map/gather | solution.py:69
  231.3 4.2 %collective-permute-start.10 = (f32[8,8,2]{1,2,0:T(2,128)S(1)}, f32[8,8,2]{1,2,0:T(2,128)S(1)}, u32[]{:S(2)}, u32[]{:S(2)}) collective-permute-start(f32[8,8,2]{1,2,0:T(2,128)S(1)} %get-tuple-element.76), channel_id=1, source_target_pairs={{0,1},{1,2},{2,3},{3,4},{4,5},{5,6},{6,7},{7,8},{8,9},{9,10},{10,1... | collective-permute-start | bytes 1544 | tf_op jit(solution)/shard_map/ppermute | solution.py:20
  237.5 23.2 %gather_fusion.3 = f32[10976,8]{1,0:T(8,128)} fusion(f32[8,7488]{0,1:T(8,128)} %copy.124, s32[11264]{0:T(1024)S(1)} %pad_clamp_fusion), kind=kCustom, calls=%fused_computation.3 | custom fusion | bytes 746368 | tf_op jit(solution)/shard_map/gather | solution.py:67
  260.6 3.4 copy.125
  266.6 3.6 collective-permute-start.12
  271.5 3.3 copy.126
  274.8 62.9 %scatter_custom_fusion.2 = f32[8,7488]{0,1:T(8,128)} fusion(s32[10976]{0:T(1024)S(1)} %reshape.235, f32[10976,8]{1,0:T(8,128)} %copy.126, f32[]{:T(128)} %constant.111.clone.1), kind=kCustom, calls=%fused_computation.9 | custom fusion | flops 87808 | bytes 240128 | tf_op jit(solution)/shard_map/scatter-add | solution.py:82
  339.0 19.4 %scatter_fusion.1 = f32[8,7488]{0,1:T(8,128)} fusion(f32[8,7488]{0,1:T(8,128)} %scatter_custom_fusion.2, s32[2744]{0:T(1024)S(1)} %reshape.243, f32[2744,8]{1,0:T(8,128)S(1)} %copy.136), kind=kCustom, calls=%fused_computation.8 | custom fusion | flops 21952 | bytes 274400 | tf_op jit(solution)/shard_map/scatter-add | solution.py:83
  359.7 3.3 collective-permute-start.14
  362.9 3.9 slice.187
  372.4 3.0 collective-permute-done.15
  376.1 40.4 %psum.15 = f32[8]{0:T(128)S(1)} all-reduce(f32[8]{0:T(128)S(1)} %multiply_reduce_fusion), channel_id=1, replica_groups=mesh['dom'=32] {'dom'}, use_global_device_ids=true, to_apply=%region_10.0 | all-reduce | flops 8 | bytes 64 | tf_op jit(solution)/shard_map/psum | solution.py:96
  (125 shorter events, 58.9 us)
Async XLA Ops:
  0.6 64.1 %copy-start = (f32[343,343]{1,0:T(8,128)S(1)}, f32[343,343]{1,0:T(8,128)}, u32[]{:S(2)}) copy-start(f32[343,343]{1,0:T(8,128)} %param.25) | copy-start | bytes 1411792
  1.7 24.0 %copy-start.2 = (f32[8,8,343]{2,1,0:T(8,128)S(1)}, f32[8,8,343]{2,1,0:T(8,128)}, u32[]{:S(2)}) copy-start(f32[8,8,343]{2,1,0:T(8,128)} %param.29) | copy-start | bytes 263428
  1.7 13.5 %collective-permute-start.1 = (f32[8,416]{1,0:T(8,128)S(1)}, f32[8,416]{1,0:T(8,128)S(1)}, u32[]{:S(2)}, u32[]{:S(2)}) collective-permute-start(f32[8,416]{1,0:T(8,128)S(1)} %get-tuple-element.74), channel_id=1, source_target_pairs={{1,0},{2,1},{3,2},{4,3},{5,4},{6,5},{7,6},{8,7},{9,8},{10,9},{11,1... | collective-permute-start | bytes 39944 | tf_op jit(solution)/shard_map/ppermute | solution.py:22
  3.8 11.4 %collective-permute-start = (f32[8,416]{1,0:T(8,128)S(1)}, f32[8,416]{1,0:T(8,128)S(1)}, u32[]{:S(2)}, u32[]{:S(2)}) collective-permute-start(f32[8,416]{1,0:T(8,128)S(1)} %get-tuple-element.75), channel_id=1, source_target_pairs={{0,1},{1,2},{2,3},{3,4},{4,5},{5,6},{6,7},{7,8},{8,9},{9,10},{10,1... | collective-permute-start | bytes 39944 | tf_op jit(solution)/shard_map/ppermute | solution.py:20
  11.4 19.6 %copy-start.7 = (f32[32]{0:T(128)S(1)}, f32[32]{0:T(128)}, u32[]{:S(2)}) copy-start(f32[32]{0:T(128)} %param.26) | copy-start | bytes 388
  26.6 32.0 %collective-permute-start.2 = (f32[8,8,2]{1,2,0:T(2,128)S(1)}, f32[8,8,2]{1,2,0:T(2,128)S(1)}, u32[]{:S(2)}, u32[]{:S(2)}) collective-permute-start(f32[8,8,2]{1,2,0:T(2,128)S(1)} %get-tuple-element.78), channel_id=1, source_target_pairs={{0,1},{1,2},{2,3},{3,4},{4,5},{5,6},{6,7},{7,8},{8,9},{9,10},{10,1... | collective-permute-start | bytes 1544 | tf_op jit(solution)/shard_map/ppermute | solution.py:20
  29.0 29.6 %collective-permute-start.3 = (f32[8,8,2]{1,2,0:T(2,128)S(1)}, f32[8,8,2]{1,2,0:T(2,128)S(1)}, u32[]{:S(2)}, u32[]{:S(2)}) collective-permute-start(f32[8,8,2]{1,2,0:T(2,128)S(1)} %get-tuple-element.79), channel_id=1, source_target_pairs={{1,0},{2,1},{3,2},{4,3},{5,4},{6,5},{7,6},{8,7},{9,8},{10,9},{11,1... | collective-permute-start | bytes 1544 | tf_op jit(solution)/shard_map/ppermute | solution.py:22
  54.8 3.9 copy-start.5
  58.9 73.2 %collective-permute-start.5 = (f32[8,8,2]{0,1,2:T(8,128)S(1)}, f32[8,8,2]{0,1,2:T(8,128)S(1)}, u32[]{:S(2)}, u32[]{:S(2)}) collective-permute-start(f32[8,8,2]{0,1,2:T(8,128)S(1)} %convolution_bitcast_fusion.7), channel_id=1, source_target_pairs={{1,0},{2,1},{3,2},{4,3},{5,4},{6,5},{7,6},{8,7},{9,8},{10,9},{11,1... | collective-permute-start | bytes 1544 | tf_op jit(solution)/shard_map/ppermute | solution.py:22
  60.8 71.3 %collective-permute-start.4 = (f32[8,8,2]{0,1,2:T(8,128)S(1)}, f32[8,8,2]{0,1,2:T(8,128)S(1)}, u32[]{:S(2)}, u32[]{:S(2)}) collective-permute-start(f32[8,8,2]{0,1,2:T(8,128)S(1)} %convolution_bitcast_fusion.7), channel_id=1, source_target_pairs={{0,1},{1,2},{2,3},{3,4},{4,5},{5,6},{6,7},{7,8},{8,9},{9,10},{10,1... | collective-permute-start | bytes 1544 | tf_op jit(solution)/shard_map/ppermute | solution.py:20
  154.1 11.8 %collective-permute-start.6 = (f32[8,416]{1,0:T(8,128)S(1)}, f32[8,416]{1,0:T(8,128)S(1)}, u32[]{:S(2)}, u32[]{:S(2)}) collective-permute-start(f32[8,416]{1,0:T(8,128)S(1)} %copy.147), channel_id=1, source_target_pairs={{0,1},{1,2},{2,3},{3,4},{4,5},{5,6},{6,7},{7,8},{8,9},{9,10},{10,1... | collective-permute-start | bytes 39944 | tf_op jit(solution)/shard_map/ppermute | solution.py:20
  157.1 13.0 %copy-start.1 = (f32[8,6656]{1,0:T(8,128)S(1)}, f32[8,6656]{1,0:T(8,128)}, u32[]{:S(2)}) copy-start(f32[8,6656]{1,0:T(8,128)} %param.21) | copy-start | bytes 638980
  157.1 13.0 %copy-start.3 = (f32[6656]{0:T(1024)S(1)}, f32[6656]{0:T(1024)}, u32[]{:S(2)}) copy-start(f32[6656]{0:T(1024)} %param.23) | copy-start | bytes 79876
  157.1 13.0 %copy-start.4 = (f32[6656]{0:T(1024)S(1)}, f32[6656]{0:T(1024)}, u32[]{:S(2)}) copy-start(f32[6656]{0:T(1024)} %param.22) | copy-start | bytes 79876
  157.1 13.0 %copy-start.6 = (f32[8]{0:T(128)S(1)}, f32[8]{0:T(128)}, u32[]{:S(2)}) copy-start(f32[8]{0:T(128)} %param.24) | copy-start | bytes 100
  163.7 6.0 %collective-permute-start.7 = (f32[8,416]{1,0:T(8,128)S(1)}, f32[8,416]{1,0:T(8,128)S(1)}, u32[]{:S(2)}, u32[]{:S(2)}) collective-permute-start(f32[8,416]{1,0:T(8,128)S(1)} %copy.148), channel_id=1, source_target_pairs={{1,0},{2,1},{3,2},{4,3},{5,4},{6,5},{7,6},{8,7},{9,8},{10,9},{11,1... | collective-permute-start | bytes 39944 | tf_op jit(solution)/shard_map/ppermute | solution.py:22
  212.0 7.1 %collective-permute-start.9 = (f32[8,416]{1,0:T(8,128)S(1)}, f32[8,416]{1,0:T(8,128)S(1)}, u32[]{:S(2)}, u32[]{:S(2)}) collective-permute-start(f32[8,416]{1,0:T(8,128)S(1)} %get-tuple-element.72), channel_id=1, source_target_pairs={{1,0},{2,1},{3,2},{4,3},{5,4},{6,5},{7,6},{8,7},{9,8},{10,9},{11,1... | collective-permute-start | bytes 39944 | tf_op jit(solution)/shard_map/ppermute | solution.py:22
  215.3 4.7 %collective-permute-start.8 = (f32[8,416]{1,0:T(8,128)S(1)}, f32[8,416]{1,0:T(8,128)S(1)}, u32[]{:S(2)}, u32[]{:S(2)}) collective-permute-start(f32[8,416]{1,0:T(8,128)S(1)} %get-tuple-element.73), channel_id=1, source_target_pairs={{0,1},{1,2},{2,3},{3,4},{4,5},{5,6},{6,7},{7,8},{8,9},{9,10},{10,1... | collective-permute-start | bytes 39944 | tf_op jit(solution)/shard_map/ppermute | solution.py:20
  231.3 33.1 %collective-permute-start.10 = (f32[8,8,2]{1,2,0:T(2,128)S(1)}, f32[8,8,2]{1,2,0:T(2,128)S(1)}, u32[]{:S(2)}, u32[]{:S(2)}) collective-permute-start(f32[8,8,2]{1,2,0:T(2,128)S(1)} %get-tuple-element.76), channel_id=1, source_target_pairs={{0,1},{1,2},{2,3},{3,4},{4,5},{5,6},{6,7},{7,8},{8,9},{9,10},{10,1... | collective-permute-start | bytes 1544 | tf_op jit(solution)/shard_map/ppermute | solution.py:20
  235.5 28.9 %collective-permute-start.11 = (f32[8,8,2]{1,2,0:T(2,128)S(1)}, f32[8,8,2]{1,2,0:T(2,128)S(1)}, u32[]{:S(2)}, u32[]{:S(2)}) collective-permute-start(f32[8,8,2]{1,2,0:T(2,128)S(1)} %get-tuple-element.77), channel_id=1, source_target_pairs={{1,0},{2,1},{3,2},{4,3},{5,4},{6,5},{7,6},{8,7},{9,8},{10,9},{11,1... | collective-permute-start | bytes 1544 | tf_op jit(solution)/shard_map/ppermute | solution.py:22
  264.7 73.0 %collective-permute-start.13 = (f32[8,8,2]{0,1,2:T(8,128)S(1)}, f32[8,8,2]{0,1,2:T(8,128)S(1)}, u32[]{:S(2)}, u32[]{:S(2)}) collective-permute-start(f32[8,8,2]{0,1,2:T(8,128)S(1)} %convolution_bitcast_fusion.6), channel_id=1, source_target_pairs={{1,0},{2,1},{3,2},{4,3},{5,4},{6,5},{7,6},{8,7},{9,8},{10,9},{11,1... | collective-permute-start | bytes 1544 | tf_op jit(solution)/shard_map/ppermute | solution.py:22
  266.6 71.1 %collective-permute-start.12 = (f32[8,8,2]{0,1,2:T(8,128)S(1)}, f32[8,8,2]{0,1,2:T(8,128)S(1)}, u32[]{:S(2)}, u32[]{:S(2)}) collective-permute-start(f32[8,8,2]{0,1,2:T(8,128)S(1)} %convolution_bitcast_fusion.6), channel_id=1, source_target_pairs={{0,1},{1,2},{2,3},{3,4},{4,5},{5,6},{6,7},{7,8},{8,9},{9,10},{10,1... | collective-permute-start | bytes 1544 | tf_op jit(solution)/shard_map/ppermute | solution.py:20
  359.7 11.8 %collective-permute-start.14 = (f32[8,416]{1,0:T(8,128)S(1)}, f32[8,416]{1,0:T(8,128)S(1)}, u32[]{:S(2)}, u32[]{:S(2)}) collective-permute-start(f32[8,416]{1,0:T(8,128)S(1)} %copy.151), channel_id=1, source_target_pairs={{0,1},{1,2},{2,3},{3,4},{4,5},{5,6},{6,7},{7,8},{8,9},{9,10},{10,1... | collective-permute-start | bytes 39944 | tf_op jit(solution)/shard_map/ppermute | solution.py:20
  369.5 6.0 %collective-permute-start.15 = (f32[8,416]{1,0:T(8,128)S(1)}, f32[8,416]{1,0:T(8,128)S(1)}, u32[]{:S(2)}, u32[]{:S(2)}) collective-permute-start(f32[8,416]{1,0:T(8,128)S(1)} %copy.152), channel_id=1, source_target_pairs={{1,0},{2,1},{3,2},{4,3},{5,4},{6,5},{7,6},{8,7},{9,8},{10,9},{11,1... | collective-permute-start | bytes 39944 | tf_op jit(solution)/shard_map/ppermute | solution.py:22
where the time goes:
time: 420 us; the launch traced here: 417 us
  other arithmetic  173 us (41%)
  local copies, waits for them, and re-layouts  105 us (25%)
  blocking collectives  81.7 us (19%)
  starting transfers between devices  45.1 us (11%)
  waiting for transfers between devices  6.72 us (2%)
  matrix products  4.8 us (1%)
    scatter-add x2, other arithmetic, on_device(): assembled = assembled.at[:, conn].add(element_out)  126 us
    psum x2, blocking collectives, on_device(): totals = lax.psum(jnp.stack(terms), 'dom')  81.7 us
    gather x6, local copies, waits for them, and re-layouts, on_device(): scaled = apply_window[:, conn] * cell_weight[None, :, None]  53.9 us
    scatter-add x2, other arithmetic, on_device(): assembled = assembled.at[:, support_nodes].add(support_out)  38.8 us
    ppermute x8, starting transfers between devices, with_halo(): lax.ppermute(tail, axis, [(i, (i + 1) % count) for i in range(ends)])  28.1 us
    ppermute x8, starting transfers between devices, with_halo(): lax.ppermute(head, axis, [((i + 1) % count, i) for i in range(ends)])  17 us
    gather x6, local copies, waits for them, and re-layouts, on_device(): values = apply_window[:, support_nodes]  14.8 us
  transfers between devices with their start and end apart: 16, of which 3 were waited for; matrix products, arithmetic and copies ran while one was open for 51% of the time, Pallas kernels for 0%

commit v1 on v0

v1 whole, which is shorter than its diff:
```python
import functools

import jax
import jax.numpy as jnp
from jax import lax
from jax.experimental import pallas as pl
from jax.experimental.pallas import tpu as pltpu
from jax.sharding import PartitionSpec as P

LANES = 128
ROWS = 8
WIDE = 256
F32 = jnp.float32
BF16 = jnp.bfloat16
HIGHEST = lax.Precision.HIGHEST
NT = (((1,), (1,)), ((), ()))
VMEM = pl.BlockSpec(memory_space=pltpu.VMEM)
SMEM = pl.BlockSpec(memory_space=pltpu.SMEM)


def round_up(value, step):
    return -(-value // step) * step


class Sizes:
    def __init__(self, count, rhs, conn, projector, atom_matrix):
        self.devices = count
        self.vectors, self.nodes = rhs.shape
        self.slots, self.elem = conn.shape
        self.entries, self.channels = projector.shape[:2]
        self.owned = atom_matrix.shape[0]
        self.ghost = self.nodes // 16
        self.rim = round_up(self.ghost, WIDE)
        self.shift = self.rim - self.ghost
        self.window = self.nodes + 2 * self.rim
        self.width = round_up(self.elem, LANES)
        self.tiles = self.width // LANES
        self.pairs = self.channels * self.vectors
        assert self.vectors == ROWS and self.channels == ROWS
        assert self.nodes % WIDE == 0 and self.owned * self.pairs == LANES


def lane_gather(values, index):
    return jnp.take_along_axis(values, index, axis=1, mode="promise_in_bounds")


def iota(shape, dim):
    return lax.broadcasted_iota(jnp.int32, shape, dim)


def split(values):
    high = values.astype(BF16)
    return high, (values - high.astype(F32)).astype(BF16)


def lanes_by_vector(z, values):
    total = jnp.sum(values, axis=1, keepdims=True)
    spread = jnp.broadcast_to(total, (ROWS, LANES))
    return jnp.sum(jnp.where(iota((ROWS, LANES), 1) == iota((ROWS, LANES), 0), spread, 0.0), axis=0, keepdims=True)


def load_index(z, conn_ref, index_ref):
    index_ref[...] = jnp.zeros_like(index_ref)
    for c in range(z.slots):
        index_ref[c, :, : z.elem] = conn_ref[c : c + 1, :] + z.shift


def gather_cells(z, index_ref, window_ref, scale_ref, live, u_ref, uw_ref):
    def cell(c, _):
        weight = jnp.where(c < live, scale_ref[c], 0.0)
        rows = pl.ds(pl.multiple_of(c * ROWS, ROWS), ROWS)
        for t in range(z.tiles):
            lanes = slice(t * LANES, (t + 1) * LANES)
            index = jnp.broadcast_to(index_ref[c, :, lanes], (ROWS, LANES))
            low, high = index & (LANES - 1), index >> 7
            value = jnp.zeros((ROWS, LANES), F32)
            for h in range(z.window // LANES):
                got = lane_gather(window_ref[:, h * LANES : (h + 1) * LANES], low)
                value = jnp.where(high == h, got, value)
            u_ref[rows, lanes] = value
            uw_ref[rows, lanes] = value * weight
        return 0

    lax.fori_loop(0, z.slots, cell, 0)


def stiffness_product(z, stiffness_ref, k_ref, uw_ref, e_ref):
    k_ref[...] = jnp.zeros_like(k_ref)
    k_ref[: z.elem, : z.elem] = stiffness_ref[...]
    k_high, k_low = split(k_ref[...])
    u_high, u_low = split(uw_ref[...])
    dot = functools.partial(lax.dot_general, dimension_numbers=NT, preferred_element_type=F32)
    e_ref[...] = dot(u_high, k_high) + (dot(u_high, k_low) + dot(u_low, k_high))


def entry_facts(z, position, atom_ref, count_ref, s):
    atom = atom_ref[s]
    owner = atom // z.owned
    return owner, atom - owner * z.owned, s < count_ref[position]


def contributions(z, position, projector_ref, pj_ref, cell_ref, atom_ref, count_ref, u_ref):
    pj_ref[...] = jnp.zeros_like(pj_ref)
    pj_ref[:, : z.elem] = projector_ref[...]
    values = [u_ref[pl.ds(pl.multiple_of(cell_ref[s] * ROWS, ROWS), ROWS), :] for s in range(z.entries)]
    sums = lax.dot_general(
        pj_ref[...], jnp.concatenate(values, axis=0), NT, precision=HIGHEST, preferred_element_type=F32
    )
    sums = jnp.concatenate([sums, jnp.zeros((sums.shape[0], LANES - sums.shape[1]), F32)], axis=1)
    lane, row = iota((ROWS, LANES), 1), iota((ROWS, LANES), 0)
    parts = [jnp.zeros((ROWS, LANES), F32)] * 3
    for s in range(z.entries):
        owner, local, alive = entry_facts(z, position, atom_ref, count_ref, s)
        got = lane_gather(sums[s * ROWS : (s + 1) * ROWS], s * ROWS + lane % ROWS)
        here = (lane // ROWS % ROWS == row) & (lane // z.pairs == local) & alive
        for k in range(3):
            parts[k] = parts[k] + jnp.where(here & (owner == position - 1 + k), got, 0.0)
    return [jnp.sum(part, axis=0, keepdims=True) for part in parts]


def first_kernel(
    z, pos_ref, count_ref, scale_ref, cell_ref, atom_ref, scount_ref, rhs_ref, precond_ref, potential_ref, shift_ref,
    halo_a_ref, halo_b_ref, conn_ref, stiffness_ref, projector_ref, coupling_ref,
    p_ref, diag_ref, out_ref, e_ref, pj_ref, k_ref, index_ref, gamma_ref, u_ref, uw_ref,
):
    position = pos_ref[0]
    even = position % 2 == 0
    a, b = halo_a_ref[...], halo_b_ref[...]
    left, right = jnp.where(even, b, a), jnp.where(even, a, b)
    own = slice(z.rim, z.rim + z.nodes)
    first, last = slice(0, z.rim), slice(z.rim + z.nodes, z.window)
    for where, side in ((first, left), (last, right)):
        p_ref[:, where] = side[:ROWS] * side[ROWS : ROWS + 1]
        diag_ref[0:1, where] = side[ROWS : ROWS + 1]
        diag_ref[1:2, where] = side[ROWS + 1 : ROWS + 2]
    diag_ref[0:1, own] = precond_ref[...]
    diag_ref[1:2, own] = potential_ref[...]
    product = rhs_ref[...] * precond_ref[...]
    p_ref[:, own] = product
    gamma_ref[...] = lanes_by_vector(z, product * rhs_ref[...])
    load_index(z, conn_ref, index_ref)
    gather_cells(z, index_ref, p_ref, scale_ref, count_ref[position], u_ref, uw_ref)
    parts = contributions(z, position, projector_ref, pj_ref, cell_ref, atom_ref, scount_ref, u_ref)
    message = jnp.concatenate(parts + [coupling_ref[...]], axis=0)
    for d in range(z.devices):
        out_ref[d] = message
    stiffness_product(z, stiffness_ref, k_ref, uw_ref, e_ref)


def second_kernel(
    z, pos_ref, count_ref, scale_ref, cell_ref, atom_ref, scount_ref, p_ref, diag_ref, shift_ref, gamma_ref,
    image_ref, halo_a_ref, halo_b_ref, index_ref, stiffness_ref, projector_ref,
    y_ref, q_ref, out_ref, e_ref, pj_ref, k_ref, u_ref, uw_ref,
):
    position = pos_ref[0]
    even = position % 2 == 0
    a, b = halo_a_ref[...], halo_b_ref[...]
    left, right = jnp.where(even, b, a), jnp.where(even, a, b)
    diagonal = diag_ref[1:2, :] + shift_ref[...]
    y_ref[...] = image_ref[...] + diagonal * p_ref[...]
    y_ref[:, : 2 * z.rim] += left
    y_ref[:, z.window - 2 * z.rim :] += right
    q_ref[...] = y_ref[...] * diag_ref[0:1, :]
    own = slice(z.rim, z.rim + z.nodes)
    y, q = y_ref[:, own], q_ref[:, own]
    dots = [
        gamma_ref[...],
        lanes_by_vector(z, y * p_ref[:, own]),
        lanes_by_vector(z, y * q),
    ]
    energy = jnp.sum(q * q * (diag_ref[1:2, own] + shift_ref[...]), axis=1, keepdims=True)
    gather_cells(z, index_ref, q_ref, scale_ref, count_ref[position], u_ref, uw_ref)
    parts = contributions(z, position, projector_ref, pj_ref, cell_ref, atom_ref, scount_ref, u_ref)
    stiffness_product(z, stiffness_ref, k_ref, uw_ref, e_ref)
    elements = jnp.zeros((ROWS, z.width), F32)
    for c in range(z.slots):
        rows = slice(c * ROWS, (c + 1) * ROWS)
        elements = elements + u_ref[rows, :] * e_ref[rows, :]
    energy = energy + jnp.sum(elements, axis=1, keepdims=True)
    dots.append(lanes_by_vector(z, energy))
    line = dots[0]
    for k in range(1, len(dots)):
        line = line + pltpu.roll(dots[k], k * ROWS, 1)
    message = jnp.concatenate(parts + [line], axis=0)
    for d in range(z.devices):
        out_ref[d] = message


def scatter_kernel(
    z, last, pos_ref, cell_ref, atom_ref, scount_ref, sums_ref, coupling_ref, e_in_ref, index_ref, pj_ref, *refs,
):
    if last:
        image_ref, send_a_ref, send_b_ref, dots_ref, e_ref, lhs_ref, hot_ref, acc_ref = refs
    else:
        image_ref, send_a_ref, send_b_ref, e_ref, lhs_ref, hot_ref, acc_ref = refs
    position = pos_ref[0]
    wanted = (
        pltpu.roll(sums_ref[:, 0, :], z.devices - 1, 0) + sums_ref[:, 1, :] + pltpu.roll(sums_ref[:, 2, :], 1, 0)
    )
    coupling = coupling_ref[:, 3, :]
    shape = (z.devices, LANES)
    lane = iota(shape, 1)
    term = jnp.zeros(shape, F32)
    for j in range(z.channels):
        matrix = lane_gather(coupling, lane // ROWS * ROWS + j)
        vector = lane_gather(wanted, lane // z.pairs * z.pairs + j * ROWS + lane % ROWS)
        term = term + matrix * vector
    if last:
        energy = jnp.sum(term * wanted, axis=0, keepdims=True)
        energy = jnp.broadcast_to(energy, (ROWS, LANES))
        step = ROWS
        while step < LANES:
            energy = energy + pltpu.roll(energy, step, 1)
            step *= 2
        line = iota((1, LANES), 1)
        dots_ref[...] = jnp.sum(sums_ref[:, 3, :], axis=0, keepdims=True) + jnp.where(
            line // ROWS == 3, energy[0:1], 0.0
        )
    block = iota(shape, 0)
    small_lane, small_row = iota((ROWS, LANES), 1), iota((ROWS, LANES), 0)
    spread = []
    for s in range(z.entries):
        owner, local, alive = entry_facts(z, position, atom_ref, scount_ref, s)
        mine = jnp.sum(jnp.where(block == owner, term, 0.0), axis=0, keepdims=True)
        got = lane_gather(
            jnp.broadcast_to(mine, (ROWS, LANES)), local * z.pairs + small_lane % ROWS * ROWS + small_row
        )
        spread.append(jnp.where((small_lane // ROWS == s) & alive, got, 0.0)[:, : z.entries * ROWS])
    support = jnp.dot(
        jnp.concatenate(spread, axis=0), pj_ref[...], precision=HIGHEST, preferred_element_type=F32
    )
    e_ref[...] = e_in_ref[...]
    for s in range(z.entries):
        rows = pl.ds(pl.multiple_of(cell_ref[s] * ROWS, ROWS), ROWS)
        e_ref[rows, :] += support[s * ROWS : (s + 1) * ROWS]

    groups = z.window // WIDE
    chunk = lhs_ref.shape[1] // z.width
    acc_ref[...] = jnp.zeros_like(acc_ref)
    sub = iota((2 * ROWS, LANES), 0)
    lows = [(sub + k * 2 * ROWS).astype(jnp.int16) for k in range(WIDE // (2 * ROWS))]
    one, none = jnp.ones((2 * ROWS, LANES), BF16), jnp.zeros((2 * ROWS, LANES), BF16)

    def some_cells(g, _):
        for cc in range(chunk):
            c = g * chunk + cc
            rows = pl.ds(pl.multiple_of(c * ROWS, ROWS), ROWS)
            for t in range(z.tiles):
                lanes = slice(t * LANES, (t + 1) * LANES)
                to = slice(cc * z.width + t * LANES, cc * z.width + (t + 1) * LANES)
                index = jnp.broadcast_to(index_ref[c, :, lanes], (2 * ROWS, LANES))
                low, high = (index & (WIDE - 1)).astype(jnp.int16), (index >> 8).astype(jnp.int16)
                value = e_ref[rows, lanes]
                rounded = value.astype(BF16).astype(F32)
                both = jnp.concatenate([rounded, value - rounded], axis=0).astype(BF16)
                for h in range(groups):
                    lhs_ref[h * 2 * ROWS : (h + 1) * 2 * ROWS, to] = jnp.where(high == jnp.int16(h), both, none)
                for k, ref_low in enumerate(lows):
                    hot_ref[k * 2 * ROWS : (k + 1) * 2 * ROWS, to] = jnp.where(low == ref_low, one, none)
        acc_ref[...] += lax.dot_general(lhs_ref[...], hot_ref[...], NT, preferred_element_type=F32)
        return 0

    lax.fori_loop(0, z.slots // chunk, some_cells, 0)
    for h in range(groups):
        at = h * 2 * ROWS
        image_ref[:, h * WIDE : (h + 1) * WIDE] = acc_ref[at : at + ROWS] + acc_ref[at + ROWS : at + 2 * ROWS]
    low_rim, high_rim = image_ref[:, : 2 * z.rim], image_ref[:, z.window - 2 * z.rim :]
    even = position % 2 == 0
    send_a_ref[...] = jnp.where(even, high_rim, low_rim)
    send_b_ref[...] = jnp.where(even, low_rim, high_rim)


def last_kernel(
    z, pos_ref, rhs_ref, p_ref, diag_ref, shift_ref, y_ref, q_ref, image_ref, halo_a_ref, halo_b_ref, dots_ref,
    solution_ref, residual_ref, z_ref,
):
    even = pos_ref[0] % 2 == 0
    a, b = halo_a_ref[...], halo_b_ref[...]
    left, right = jnp.where(even, b, a), jnp.where(even, a, b)
    own = slice(z.rim, z.rim + z.nodes)
    z_ref[...] = image_ref[...]
    z_ref[:, : 2 * z.rim] += left
    z_ref[:, z.window - 2 * z.rim :] += right
    lane, row = iota((ROWS, LANES), 1), iota((ROWS, LANES), 0)
    line = jnp.broadcast_to(dots_ref[...], (ROWS, LANES))

    def column(k):
        return jnp.sum(jnp.where(lane == k * ROWS + row, line, 0.0), axis=1, keepdims=True)

    gamma, py, qy, qq = (column(k) for k in range(4))
    alpha = gamma / py
    fresh = gamma - 2.0 * alpha * py + alpha * alpha * qy
    beta = fresh / gamma
    more = 1.0 + beta
    step = fresh / (more * more * py - 2.0 * more * alpha * qy + alpha * alpha * qq)
    p, q, y = p_ref[:, own], q_ref[:, own], y_ref[:, own]
    second = z_ref[:, own] + (diag_ref[1:2, own] + shift_ref[...]) * q
    search = (p - alpha * q) + beta * p
    solution_ref[...] = alpha * p + step * search
    residual_ref[...] = (rhs_ref[...] - alpha * y) - step * (more * y - alpha * second)


def on_device(
    rhs, potential, precond, shift, stiffness, cell_scale, conn, cell_count, projector, support_cell, support_atom,
    support_count, atom_matrix,
):
    count = lax.axis_size("dom")
    z = Sizes(count, rhs, conn, projector, atom_matrix)
    position = lax.axis_index("dom")
    even = position % 2 == 0
    pos = position.astype(jnp.int32).reshape(1)
    near = [(i, i ^ 1) for i in range(count)]
    far = [(i, j) for i in range(1, count - 1) for j in [i + 1 if i % 2 else i - 1]]

    def exchange(a, b):
        return lax.ppermute(a, "dom", near), lax.ppermute(b, "dom", far)

    def call(kernel, outs, scratch, specs, *args):
        return pl.pallas_call(
            functools.partial(kernel),
            out_shape=[jax.ShapeDtypeStruct(s, d) for s, d in outs],
            in_specs=specs,
            out_specs=[VMEM] * len(outs),
            scratch_shapes=[pltpu.VMEM(s, d) for s, d in scratch],
        )(*args)

    precond_row, potential_row = precond[None, :], potential[None, :]
    shift_column = shift[:, None]
    packed = jnp.concatenate([rhs, precond_row, potential_row], axis=0)
    head, tail = packed[:, : z.rim], packed[:, z.nodes - z.rim :]
    halo = exchange(jnp.where(even, tail, head), jnp.where(even, head, tail))
    flat_projector = projector.reshape(z.entries * z.channels, z.elem)
    coupling = atom_matrix.reshape(1, LANES)

    cells = (z.slots * ROWS, z.width)
    window = (z.vectors, z.window)
    message = (z.devices, 4, LANES)
    cell_scratch = [(cells, F32), (cells, F32)]
    p, diag, sums, e, pj, k_pad, index, gamma = call(
        functools.partial(first_kernel, z),
        [(window, F32), ((2, z.window), F32), (message, F32), (cells, F32), ((z.entries * ROWS, z.width), F32),
         ((z.width, z.width), F32), ((z.slots, 1, z.width), jnp.int32), ((1, LANES), F32)],
        cell_scratch,
        [SMEM] * 6 + [VMEM] * 10,
        pos, cell_count, cell_scale, support_cell, support_atom, support_count, rhs, precond_row, potential_row,
        shift_column, *halo, conn, stiffness, flat_projector, coupling,
    )
    chunk = 4 if z.slots % 4 == 0 else 1
    groups = z.window // WIDE
    scatter_scratch = [
        (cells, F32), ((groups * 2 * ROWS, chunk * z.width), BF16), ((WIDE, chunk * z.width), BF16),
        ((groups * 2 * ROWS, WIDE), F32),
    ]
    rim = (z.vectors, 2 * z.rim)
    coupled = lax.all_to_all(sums, "dom", 0, 0)
    image, send_a, send_b = call(
        functools.partial(scatter_kernel, z, False),
        [(window, F32), (rim, F32), (rim, F32)],
        scatter_scratch,
        [SMEM] * 4 + [VMEM] * 5,
        pos, support_cell, support_atom, support_count, coupled, coupled, e, index, pj,
    )
    halo = exchange(send_a, send_b)
    y, q, sums, e = call(
        functools.partial(second_kernel, z),
        [(window, F32), (window, F32), (message, F32), (cells, F32)],
        [((z.entries * ROWS, z.width), F32), ((z.width, z.width), F32)] + cell_scratch,
        [SMEM] * 6 + [VMEM] * 10 + [],
        pos, cell_count, cell_scale, support_cell, support_atom, support_count, p, diag, shift_column, gamma,
        image, *halo, index, stiffness, flat_projector,
    )
    totals = lax.all_to_all(sums, "dom", 0, 0)
    image, send_a, send_b, dots = call(
        functools.partial(scatter_kernel, z, True),
        [(window, F32), (rim, F32), (rim, F32), ((1, LANES), F32)],
        scatter_scratch,
        [SMEM] * 4 + [VMEM] * 5,
        pos, support_cell, support_atom, support_count, totals, coupled, e, index, pj,
    )
    halo = exchange(send_a, send_b)
    own = (z.vectors, z.nodes)
    return tuple(
        call(
            functools.partial(last_kernel, z),
            [(own, F32), (own, F32)],
            [(window, F32)],
            [SMEM] + [VMEM] * 10,
            pos, rhs, p, diag, shift_column, y, q, image, *halo, dots,
        )
    )


def solution(mesh):
    placed = (
        P(None, "dom"),
        P("dom"),
        P("dom"),
        P(),
        P(),
        P("dom"),
        P("dom", None),
        P(),
        P("dom", None, None),
        P("dom"),
        P("dom"),
        P(),
        P("dom", None, None),
    )
    return jax.shard_map(
        on_device,
        mesh=mesh,
        in_specs=placed,
        out_specs=(P(None, "dom"), P(None, "dom")),
        check_vma=False,
    )
```

time: 420 us -> 89 us (0.21)
  other arithmetic: 173 us -> 0.77 us
  local copies, waits for them, and re-layouts: 105 us -> 5.13 us
  blocking collectives: 81.7 us -> 24.3 us
  Pallas kernels: 0 us -> 41.3 us
  starting transfers between devices: 45.1 us -> 9.47 us
  matrix products: 4.8 us -> 0 us
    scatter-add x4 -> x0, other arithmetic: 165 us -> none  [the longest x2 126 us: on_device(): assembled = assembled.at[:, conn].add(element_out)]
    psum x2 -> x0, blocking collectives: 81.7 us -> none  [on_device(): totals = lax.psum(jnp.stack(terms), 'dom')]
    gather x13 -> x0, local copies, waits for them, and re-layouts: 70.1 us -> none  [the longest x6 53.9 us: on_device(): scaled = apply_window[:, conn] * cell_weight[None, :, None]]
    pallas_call x0 -> x5, Pallas kernels: none -> 41.3 us  [call(): pl.pallas_call(functools.partial(kernel), out_shape=[jax.ShapeDtypeStruct...]
    ppermute x16 -> x6, starting transfers between devices: 45.1 us -> 9.47 us  [exchange(): return (lax.ppermute(a, 'dom', near), lax.ppermute(b, 'dom', far))]
    all_to_all x0 -> x2, blocking collectives: none -> 24.3 us  [the longest x1 14.1 us: on_device(): coupled = lax.all_to_all(sums, 'dom', 0, 0)]
    slice x8 -> x0, local copies, waits for them, and re-layouts: 10.4 us -> none  [the longest x2 7.88 us: on_device(): inner = assembled[:, ghost:ghost + node_dev]]
    dot_general x6 -> x0, local copies, waits for them, and re-layouts: 7.29 us -> none  [the longest x4 7.11 us: on_device(): element_out = jnp.einsum('vcn,mn->vcm', scaled, stiffness, precision=HIGH)]
  transfers between devices with their start and end apart: 16 -> 6, of which waited for: 3 -> 2; matrix products, arithmetic and copies ran while one was open for 51% -> 2% of each run, Pallas kernels for 0% -> 0%
where the time goes in v1:
time: 89 us; the launch traced here: 88.5 us
  Pallas kernels  41.3 us (46%)
  blocking collectives  24.3 us (27%)
  starting transfers between devices  9.47 us (11%)
  waiting for transfers between devices  6.72 us (8%)
  local copies, waits for them, and re-layouts  5.13 us (6%)
    pallas_call x5, Pallas kernels, call(): pl.pallas_call(functools.partial(kernel), out_shape=[jax.ShapeDtypeStruct...  41.3 us
    all_to_all x1, blocking collectives, on_device(): coupled = lax.all_to_all(sums, 'dom', 0, 0)  14.1 us
    all_to_all x1, blocking collectives, on_device(): totals = lax.all_to_all(sums, 'dom', 0, 0)  10.2 us
    ppermute x6, starting transfers between devices, exchange(): return (lax.ppermute(a, 'dom', near), lax.ppermute(b, 'dom', far))  9.47 us
    ppermute x6, waiting for transfers between devices, exchange(): return (lax.ppermute(a, 'dom', near), lax.ppermute(b, 'dom', far))  6.72 us
    unnamed x24, local copies, waits for them, and re-layouts  3.76 us
  transfers between devices with their start and end apart: 6, of which 2 were waited for; matrix products, arithmetic and copies ran while one was open for 2% of the time, Pallas kernels for 0%

profile of v1, /device:TPU:1, one launch (start us, length us, event | category | flops | bytes accessed | tf_op | source)
XLA Modules:
  0.0 88.5 jit_solution(558324247005372548)
XLA Ops:
  0.7 0.7 copy-done.8
  1.4 0.6 copy-done
  2.0 0.8 broadcast_select_fusion
  2.8 0.1 collective-permute-start
  2.9 4.5 %collective-permute-start.1 = (f32[10,512]{1,0:T(8,128)S(1)}, f32[10,512]{1,0:T(8,128)S(1)}, u32[]{:S(2)}, u32[]{:S(2)}) collective-permute-start(f32[10,512]{1,0:T(8,128)S(1)} %get-tuple-element.38), channel_id=1, source_target_pairs={{1,2},{2,1},{3,4},{4,3},{5,6},{6,5},{7,8},{8,7},{9,10},{10,9},{11,... | collective-permute-start | bytes 61448 | tf_op jit(solution)/shard_map/ppermute | solution.py:316
  7.4 0.7 reshape.15.coupling_ref
  8.1 0.7 copy-done.11
  8.7 0.7 copy.15.shift_ref
  9.4 0.6 copy-done.2
  10.0 11.5 %shard_map.140 = (f32[8,7680]{1,0:T(8,128)}, f32[2,7680]{1,0:T(2,128)}, f32[32,4,128]{2,1,0:T(4,128)}, f32[256,384]{1,0:T(8,128)}, f32[64,384]{1,0:T(8,128)}, /*...) custom-call(s32[1]{0:T(128)} %bitcast.pos_ref, s32[32]{0:T(128)} %count_ref.3, f32[32]{0:T(128)} %scale_ref.3, ...), custom_call_target="tpu_custom_call" | custom-call | tf_op jit(solution)/shard_map/pallas_call | solution.py:319
  21.5 14.1 %all_to_all.10.sums_ref.coupling_ref = f32[32,4,128]{2,1,0:T(4,128)} all-to-all(f32[32,4,128]{2,1,0:T(4,128)} %get-tuple-element.23), channel_id=1, replica_groups=mesh['dom'=32] {'dom'}, dimensions={0} | all-to-all | bytes 131072 | tf_op jit(solution)/shard_map/all_to_all | solution.py:355
  35.6 7.7 %shard_map.141 = (f32[8,7680]{1,0:T(8,128)}, f32[8,1024]{1,0:T(8,128)}, f32[8,1024]{1,0:T(8,128)}) custom-call(s32[1]{0:T(128)} %bitcast.pos_ref, s32[8]{0:T(128)} %cell_ref.7, s32[8]{0:T(128)} %atom_ref.7, s32[32]{0:T(128)} %scount_ref.7, f32[32,4,128]{2,1,0:T(4,128)} %all_to_all.10.sums_ref.coupling_ref, f32[32,4,128]{2,1,0:T(4,128)} %all_to_all.10.sums_ref.coupling_ref, ...), custom_call_target="tpu_custom_call" | custom-call | tf_op jit(solution)/shard_map/pallas_call | solution.py:319
  43.3 0.4 collective-permute-start.2
  43.7 2.1 %collective-permute-start.3 = (f32[8,1024]{1,0:T(8,128)}, f32[8,1024]{1,0:T(8,128)S(1)}, u32[]{:S(2)}, u32[]{:S(2)}) collective-permute-start(f32[8,1024]{1,0:T(8,128)} %get-tuple-element.29), channel_id=1, source_target_pairs={{1,2},{2,1},{3,4},{4,3},{5,6},{6,5},{7,8},{8,7},{9,10},{10,9},{11,... | collective-permute-start | bytes 98312 | tf_op jit(solution)/shard_map/ppermute | solution.py:316
  45.8 3.4 %collective-permute-done.3.halo_b_ref = f32[8,1024]{1,0:T(8,128)S(1)} collective-permute-done((f32[8,1024]{1,0:T(8,128)}, f32[8,1024]{1,0:T(8,128)S(1)}, u32[]{:S(2)}, u32[]{:S(2)}) %collective-permute-start.3) | collective-permute-done | bytes 32800 | tf_op jit(solution)/shard_map/ppermute | solution.py:316
  49.1 0.6 copy-done.7
  49.7 12.0 %shard_map.142 = (f32[8,7680]{1,0:T(8,128)}, f32[8,7680]{1,0:T(8,128)}, f32[32,4,128]{2,1,0:T(4,128)}, f32[256,384]{1,0:T(8,128)}) custom-call(s32[1]{0:T(128)} %bitcast.pos_ref, s32[32]{0:T(128)} %count_ref.3, f32[32]{0:T(128)} %scale_ref.3, s32[8]{0:T(128)} %cell_ref.7, s32[8]{0:T(128)} %atom_ref.7, s32[32]{0:T(128)} %scount_ref.7, ...), custom_call_target="tpu_custom_call" | custom-call | tf_op jit(solution)/shard_map/pallas_call | solution.py:319
  61.7 10.2 %all_to_all.11.sums_ref = f32[32,4,128]{2,1,0:T(4,128)} all-to-all(f32[32,4,128]{2,1,0:T(4,128)} %get-tuple-element.32), channel_id=1, replica_groups=mesh['dom'=32] {'dom'}, dimensions={0} | all-to-all | bytes 131072 | tf_op jit(solution)/shard_map/all_to_all | solution.py:372
  71.9 7.7 %shard_map.143 = (f32[8,7680]{1,0:T(8,128)}, f32[8,1024]{1,0:T(8,128)}, f32[8,1024]{1,0:T(8,128)}, f32[1,128]{1,0:T(1,128)}) custom-call(s32[1]{0:T(128)} %bitcast.pos_ref, s32[8]{0:T(128)} %cell_ref.7, s32[8]{0:T(128)} %atom_ref.7, s32[32]{0:T(128)} %scount_ref.7, f32[32,4,128]{2,1,0:T(4,128)} %all_to_all.11.sums_ref, ...), custom_call_target="tpu_custom_call" | custom-call | tf_op jit(solution)/shard_map/pallas_call | solution.py:319
  79.7 0.4 collective-permute-start.4
  80.1 2.0 %collective-permute-start.5 = (f32[8,1024]{1,0:T(8,128)}, f32[8,1024]{1,0:T(8,128)S(1)}, u32[]{:S(2)}, u32[]{:S(2)}) collective-permute-start(f32[8,1024]{1,0:T(8,128)} %get-tuple-element.36), channel_id=1, source_target_pairs={{1,2},{2,1},{3,4},{4,3},{5,6},{6,5},{7,8},{8,7},{9,10},{10,9},{11,... | collective-permute-start | bytes 98312 | tf_op jit(solution)/shard_map/ppermute | solution.py:316
  82.1 3.4 %collective-permute-done.5.halo_b_ref = f32[8,1024]{1,0:T(8,128)S(1)} collective-permute-done((f32[8,1024]{1,0:T(8,128)}, f32[8,1024]{1,0:T(8,128)S(1)}, u32[]{:S(2)}, u32[]{:S(2)}) %collective-permute-start.5) | collective-permute-done | bytes 32800 | tf_op jit(solution)/shard_map/ppermute | solution.py:316
  85.5 0.6 copy-done.5
  86.1 2.4 %shard_map.144 = (f32[8,6656]{1,0:T(8,128)}, f32[8,6656]{1,0:T(8,128)}) custom-call(s32[1]{0:T(128)} %bitcast.pos_ref, f32[8,6656]{1,0:T(8,128)} %rhs_ref.3, f32[8,7680]{1,0:T(8,128)} %get-tuple-element.20.p_ref, f32[2,7680]{1,0:T(2,128)} %get-tuple-element.21.diag_ref, f32[8,1]{1,0:T(8,128)} %copy.15.shift_ref, f32[8,7680]{1,0:T(8,128)} %get-tuple-element.30.y_ref, ...), custom_call_target="tpu_custom_call" | custom-call | tf_op jit(solution)/shard_map/pallas_call | solution.py:319
  (25 shorter events, 0.1 us)
Async XLA Ops:
  0.6 0.7 copy-start.8
  0.7 0.8 copy-start.9
  1.4 0.6 copy-start
  2.0 0.8 copy-start.1
  2.8 4.6 %copy-start.10 = (f32[2,8,8]{2,1,0:T(8,128)S(1)}, f32[2,8,8]{2,1,0:T(8,128)}, u32[]{:S(2)}) copy-start(f32[2,8,8]{2,1,0:T(8,128)} %param.25) | copy-start | bytes 1540
  2.8 6.6 %collective-permute-start = (f32[10,512]{1,0:T(8,128)S(1)}, f32[10,512]{1,0:T(8,128)S(1)}, u32[]{:S(2)}, u32[]{:S(2)}) collective-permute-start(f32[10,512]{1,0:T(8,128)S(1)} %broadcast_select_fusion.1), channel_id=1, source_target_pairs={{0,1},{1,0},{2,3},{3,2},{4,5},{5,4},{6,7},{7,6},{8,9},{9,8},{10,11... | collective-permute-start | bytes 61448 | tf_op jit(solution)/shard_map/ppermute | solution.py:316
  2.9 6.5 %collective-permute-start.1 = (f32[10,512]{1,0:T(8,128)S(1)}, f32[10,512]{1,0:T(8,128)S(1)}, u32[]{:S(2)}, u32[]{:S(2)}) collective-permute-start(f32[10,512]{1,0:T(8,128)S(1)} %get-tuple-element.38), channel_id=1, source_target_pairs={{1,2},{2,1},{3,4},{4,3},{5,6},{6,5},{7,8},{8,7},{9,10},{10,9},{11,... | collective-permute-start | bytes 61448 | tf_op jit(solution)/shard_map/ppermute | solution.py:316
  8.1 0.7 copy-start.11
  9.4 0.6 copy-start.2
  9.4 0.6 copy-start.4
  43.3 2.5 %collective-permute-start.2 = (f32[8,1024]{1,0:T(8,128)}, f32[8,1024]{1,0:T(8,128)S(1)}, u32[]{:S(2)}, u32[]{:S(2)}) collective-permute-start(f32[8,1024]{1,0:T(8,128)} %get-tuple-element.28), channel_id=1, source_target_pairs={{0,1},{1,0},{2,3},{3,2},{4,5},{5,4},{6,7},{7,6},{8,9},{9,8},{10,11... | collective-permute-start | bytes 98312 | tf_op jit(solution)/shard_map/ppermute | solution.py:316
  43.7 5.4 %collective-permute-start.3 = (f32[8,1024]{1,0:T(8,128)}, f32[8,1024]{1,0:T(8,128)S(1)}, u32[]{:S(2)}, u32[]{:S(2)}) collective-permute-start(f32[8,1024]{1,0:T(8,128)} %get-tuple-element.29), channel_id=1, source_target_pairs={{1,2},{2,1},{3,4},{4,3},{5,6},{6,5},{7,8},{8,7},{9,10},{10,9},{11,... | collective-permute-start | bytes 98312 | tf_op jit(solution)/shard_map/ppermute | solution.py:316
  45.8 3.4 %copy-start.6 = (f32[8,1024]{1,0:T(8,128)}, f32[8,1024]{1,0:T(8,128)S(1)}, u32[]{:S(2)}) copy-start(f32[8,1024]{1,0:T(8,128)S(1)} %collective-permute-done.2.halo_a_ref) | copy-start | bytes 98308
  49.1 0.6 copy-start.7
  79.7 2.5 %collective-permute-start.4 = (f32[8,1024]{1,0:T(8,128)}, f32[8,1024]{1,0:T(8,128)S(1)}, u32[]{:S(2)}, u32[]{:S(2)}) collective-permute-start(f32[8,1024]{1,0:T(8,128)} %get-tuple-element.35), channel_id=1, source_target_pairs={{0,1},{1,0},{2,3},{3,2},{4,5},{5,4},{6,7},{7,6},{8,9},{9,8},{10,11... | collective-permute-start | bytes 98312 | tf_op jit(solution)/shard_map/ppermute | solution.py:316
  80.1 5.4 %collective-permute-start.5 = (f32[8,1024]{1,0:T(8,128)}, f32[8,1024]{1,0:T(8,128)S(1)}, u32[]{:S(2)}, u32[]{:S(2)}) collective-permute-start(f32[8,1024]{1,0:T(8,128)} %get-tuple-element.36), channel_id=1, source_target_pairs={{1,2},{2,1},{3,4},{4,3},{5,6},{6,5},{7,8},{8,7},{9,10},{10,9},{11,... | collective-permute-start | bytes 98312 | tf_op jit(solution)/shard_map/ppermute | solution.py:316
  82.1 3.4 %copy-start.3 = (f32[8,1024]{1,0:T(8,128)}, f32[8,1024]{1,0:T(8,128)S(1)}, u32[]{:S(2)}) copy-start(f32[8,1024]{1,0:T(8,128)S(1)} %collective-permute-done.4.halo_a_ref) | copy-start | bytes 98308
  85.5 0.6 copy-start.5

commit v2 on v1

--- a/solution.py
+++ b/solution.py
@@ -10,6 +10,7 @@
 LANES = 128
 ROWS = 8
 WIDE = 256
+CHAINS = 4
 F32 = jnp.float32
 BF16 = jnp.bfloat16
 HIGHEST = lax.Precision.HIGHEST
@@ -73,10 +74,11 @@
             lanes = slice(t * LANES, (t + 1) * LANES)
             index = jnp.broadcast_to(index_ref[c, :, lanes], (ROWS, LANES))
             low, high = index & (LANES - 1), index >> 7
-            value = jnp.zeros((ROWS, LANES), F32)
+            chains = [jnp.zeros((ROWS, LANES), F32)] * CHAINS
             for h in range(z.window // LANES):
                 got = lane_gather(window_ref[:, h * LANES : (h + 1) * LANES], low)
-                value = jnp.where(high == h, got, value)
+                chains[h % CHAINS] = jnp.where(high == h, got, chains[h % CHAINS])
+            value = functools.reduce(jnp.add, chains)
             u_ref[rows, lanes] = value
             uw_ref[rows, lanes] = value * weight
         return 0

time: 89 us -> 89.1 us (level)
  no operation moved by 1% of the time
where the time goes in v2:
time: 89.1 us; the launch traced here: 88.5 us
  Pallas kernels  41.4 us (46%)
  blocking collectives  24.2 us (27%)
  starting transfers between devices  9.48 us (11%)
  waiting for transfers between devices  6.71 us (8%)
  local copies, waits for them, and re-layouts  5.13 us (6%)
    pallas_call x5, Pallas kernels, call(): pl.pallas_call(functools.partial(kernel), out_shape=[jax.ShapeDtypeStruct...  41.4 us
    all_to_all x1, blocking collectives, on_device(): coupled = lax.all_to_all(sums, 'dom', 0, 0)  14.1 us
    all_to_all x1, blocking collectives, on_device(): totals = lax.all_to_all(sums, 'dom', 0, 0)  10.2 us
    ppermute x6, starting transfers between devices, exchange(): return (lax.ppermute(a, 'dom', near), lax.ppermute(b, 'dom', far))  9.48 us
    ppermute x6, waiting for transfers between devices, exchange(): return (lax.ppermute(a, 'dom', near), lax.ppermute(b, 'dom', far))  6.71 us
    unnamed x24, local copies, waits for them, and re-layouts  3.76 us
  transfers between devices with their start and end apart: 6, of which 2 were waited for; matrix products, arithmetic and copies ran while one was open for 2% of the time, Pallas kernels for 0%

profile of v2, /device:TPU:1, one launch (start us, length us, event | category | flops | bytes accessed | tf_op | source)
XLA Modules:
  0.0 88.5 jit_solution(12103001484093549159)
XLA Ops:
  0.7 0.7 copy-done.8
  1.4 0.6 copy-done
  2.0 0.8 broadcast_select_fusion
  2.8 0.1 collective-permute-start
  2.9 4.5 %collective-permute-start.1 = (f32[10,512]{1,0:T(8,128)S(1)}, f32[10,512]{1,0:T(8,128)S(1)}, u32[]{:S(2)}, u32[]{:S(2)}) collective-permute-start(f32[10,512]{1,0:T(8,128)S(1)} %get-tuple-element.38), channel_id=1, source_target_pairs={{1,2},{2,1},{3,4},{4,3},{5,6},{6,5},{7,8},{8,7},{9,10},{10,9},{11,... | collective-permute-start | bytes 61448 | tf_op jit(solution)/shard_map/ppermute | solution.py:318
  7.4 0.7 reshape.15.coupling_ref
  8.1 0.7 copy-done.11
  8.7 0.7 copy.15.shift_ref
  9.4 0.6 copy-done.2
  10.0 11.5 %shard_map.140 = (f32[8,7680]{1,0:T(8,128)}, f32[2,7680]{1,0:T(2,128)}, f32[32,4,128]{2,1,0:T(4,128)}, f32[256,384]{1,0:T(8,128)}, f32[64,384]{1,0:T(8,128)}, /*...) custom-call(s32[1]{0:T(128)} %bitcast.pos_ref, s32[32]{0:T(128)} %count_ref.3, f32[32]{0:T(128)} %scale_ref.3, ...), custom_call_target="tpu_custom_call" | custom-call | tf_op jit(solution)/shard_map/pallas_call | solution.py:321
  21.6 14.1 %all_to_all.10.sums_ref.coupling_ref = f32[32,4,128]{2,1,0:T(4,128)} all-to-all(f32[32,4,128]{2,1,0:T(4,128)} %get-tuple-element.23), channel_id=1, replica_groups=mesh['dom'=32] {'dom'}, dimensions={0} | all-to-all | bytes 131072 | tf_op jit(solution)/shard_map/all_to_all | solution.py:357
  35.6 7.7 %shard_map.141 = (f32[8,7680]{1,0:T(8,128)}, f32[8,1024]{1,0:T(8,128)}, f32[8,1024]{1,0:T(8,128)}) custom-call(s32[1]{0:T(128)} %bitcast.pos_ref, s32[8]{0:T(128)} %cell_ref.7, s32[8]{0:T(128)} %atom_ref.7, s32[32]{0:T(128)} %scount_ref.7, f32[32,4,128]{2,1,0:T(4,128)} %all_to_all.10.sums_ref.coupling_ref, f32[32,4,128]{2,1,0:T(4,128)} %all_to_all.10.sums_ref.coupling_ref, ...), custom_call_target="tpu_custom_call" | custom-call | tf_op jit(solution)/shard_map/pallas_call | solution.py:321
  43.3 0.4 collective-permute-start.2
  43.7 2.1 %collective-permute-start.3 = (f32[8,1024]{1,0:T(8,128)}, f32[8,1024]{1,0:T(8,128)S(1)}, u32[]{:S(2)}, u32[]{:S(2)}) collective-permute-start(f32[8,1024]{1,0:T(8,128)} %get-tuple-element.29), channel_id=1, source_target_pairs={{1,2},{2,1},{3,4},{4,3},{5,6},{6,5},{7,8},{8,7},{9,10},{10,9},{11,... | collective-permute-start | bytes 98312 | tf_op jit(solution)/shard_map/ppermute | solution.py:318
  45.8 3.4 %collective-permute-done.3.halo_b_ref = f32[8,1024]{1,0:T(8,128)S(1)} collective-permute-done((f32[8,1024]{1,0:T(8,128)}, f32[8,1024]{1,0:T(8,128)S(1)}, u32[]{:S(2)}, u32[]{:S(2)}) %collective-permute-start.3) | collective-permute-done | bytes 32800 | tf_op jit(solution)/shard_map/ppermute | solution.py:318
  49.2 0.6 copy-done.7
  49.8 12.0 %shard_map.142 = (f32[8,7680]{1,0:T(8,128)}, f32[8,7680]{1,0:T(8,128)}, f32[32,4,128]{2,1,0:T(4,128)}, f32[256,384]{1,0:T(8,128)}) custom-call(s32[1]{0:T(128)} %bitcast.pos_ref, s32[32]{0:T(128)} %count_ref.3, f32[32]{0:T(128)} %scale_ref.3, s32[8]{0:T(128)} %cell_ref.7, s32[8]{0:T(128)} %atom_ref.7, s32[32]{0:T(128)} %scount_ref.7, ...), custom_call_target="tpu_custom_call" | custom-call | tf_op jit(solution)/shard_map/pallas_call | solution.py:321
  61.8 10.2 %all_to_all.11.sums_ref = f32[32,4,128]{2,1,0:T(4,128)} all-to-all(f32[32,4,128]{2,1,0:T(4,128)} %get-tuple-element.32), channel_id=1, replica_groups=mesh['dom'=32] {'dom'}, dimensions={0} | all-to-all | bytes 131072 | tf_op jit(solution)/shard_map/all_to_all | solution.py:374
  72.0 7.7 %shard_map.143 = (f32[8,7680]{1,0:T(8,128)}, f32[8,1024]{1,0:T(8,128)}, f32[8,1024]{1,0:T(8,128)}, f32[1,128]{1,0:T(1,128)}) custom-call(s32[1]{0:T(128)} %bitcast.pos_ref, s32[8]{0:T(128)} %cell_ref.7, s32[8]{0:T(128)} %atom_ref.7, s32[32]{0:T(128)} %scount_ref.7, f32[32,4,128]{2,1,0:T(4,128)} %all_to_all.11.sums_ref, ...), custom_call_target="tpu_custom_call" | custom-call | tf_op jit(solution)/shard_map/pallas_call | solution.py:321
  79.7 0.4 collective-permute-start.4
  80.1 2.1 %collective-permute-start.5 = (f32[8,1024]{1,0:T(8,128)}, f32[8,1024]{1,0:T(8,128)S(1)}, u32[]{:S(2)}, u32[]{:S(2)}) collective-permute-start(f32[8,1024]{1,0:T(8,128)} %get-tuple-element.36), channel_id=1, source_target_pairs={{1,2},{2,1},{3,4},{4,3},{5,6},{6,5},{7,8},{8,7},{9,10},{10,9},{11,... | collective-permute-start | bytes 98312 | tf_op jit(solution)/shard_map/ppermute | solution.py:318
  82.2 3.4 %collective-permute-done.5.halo_b_ref = f32[8,1024]{1,0:T(8,128)S(1)} collective-permute-done((f32[8,1024]{1,0:T(8,128)}, f32[8,1024]{1,0:T(8,128)S(1)}, u32[]{:S(2)}, u32[]{:S(2)}) %collective-permute-start.5) | collective-permute-done | bytes 32800 | tf_op jit(solution)/shard_map/ppermute | solution.py:318
  85.5 0.6 copy-done.5
  86.1 2.4 %shard_map.144 = (f32[8,6656]{1,0:T(8,128)}, f32[8,6656]{1,0:T(8,128)}) custom-call(s32[1]{0:T(128)} %bitcast.pos_ref, f32[8,6656]{1,0:T(8,128)} %rhs_ref.3, f32[8,7680]{1,0:T(8,128)} %get-tuple-element.20.p_ref, f32[2,7680]{1,0:T(2,128)} %get-tuple-element.21.diag_ref, f32[8,1]{1,0:T(8,128)} %copy.15.shift_ref, f32[8,7680]{1,0:T(8,128)} %get-tuple-element.30.y_ref, ...), custom_call_target="tpu_custom_call" | custom-call | tf_op jit(solution)/shard_map/pallas_call | solution.py:321
  (25 shorter events, 0.1 us)
Async XLA Ops:
  0.6 0.7 copy-start.8
  0.7 0.8 copy-start.9
  1.4 0.6 copy-start
  2.0 0.8 copy-start.1
  2.8 4.6 %copy-start.10 = (f32[2,8,8]{2,1,0:T(8,128)S(1)}, f32[2,8,8]{2,1,0:T(8,128)}, u32[]{:S(2)}) copy-start(f32[2,8,8]{2,1,0:T(8,128)} %param.25) | copy-start | bytes 1540
  2.8 6.6 %collective-permute-start = (f32[10,512]{1,0:T(8,128)S(1)}, f32[10,512]{1,0:T(8,128)S(1)}, u32[]{:S(2)}, u32[]{:S(2)}) collective-permute-start(f32[10,512]{1,0:T(8,128)S(1)} %broadcast_select_fusion.1), channel_id=1, source_target_pairs={{0,1},{1,0},{2,3},{3,2},{4,5},{5,4},{6,7},{7,6},{8,9},{9,8},{10,11... | collective-permute-start | bytes 61448 | tf_op jit(solution)/shard_map/ppermute | solution.py:318
  2.9 6.5 %collective-permute-start.1 = (f32[10,512]{1,0:T(8,128)S(1)}, f32[10,512]{1,0:T(8,128)S(1)}, u32[]{:S(2)}, u32[]{:S(2)}) collective-permute-start(f32[10,512]{1,0:T(8,128)S(1)} %get-tuple-element.38), channel_id=1, source_target_pairs={{1,2},{2,1},{3,4},{4,3},{5,6},{6,5},{7,8},{8,7},{9,10},{10,9},{11,... | collective-permute-start | bytes 61448 | tf_op jit(solution)/shard_map/ppermute | solution.py:318
  8.1 0.7 copy-start.11
  9.4 0.6 copy-start.2
  9.4 0.6 copy-start.4
  43.3 2.5 %collective-permute-start.2 = (f32[8,1024]{1,0:T(8,128)}, f32[8,1024]{1,0:T(8,128)S(1)}, u32[]{:S(2)}, u32[]{:S(2)}) collective-permute-start(f32[8,1024]{1,0:T(8,128)} %get-tuple-element.28), channel_id=1, source_target_pairs={{0,1},{1,0},{2,3},{3,2},{4,5},{5,4},{6,7},{7,6},{8,9},{9,8},{10,11... | collective-permute-start | bytes 98312 | tf_op jit(solution)/shard_map/ppermute | solution.py:318
  43.7 5.4 %collective-permute-start.3 = (f32[8,1024]{1,0:T(8,128)}, f32[8,1024]{1,0:T(8,128)S(1)}, u32[]{:S(2)}, u32[]{:S(2)}) collective-permute-start(f32[8,1024]{1,0:T(8,128)} %get-tuple-element.29), channel_id=1, source_target_pairs={{1,2},{2,1},{3,4},{4,3},{5,6},{6,5},{7,8},{8,7},{9,10},{10,9},{11,... | collective-permute-start | bytes 98312 | tf_op jit(solution)/shard_map/ppermute | solution.py:318
  45.8 3.4 %copy-start.6 = (f32[8,1024]{1,0:T(8,128)}, f32[8,1024]{1,0:T(8,128)S(1)}, u32[]{:S(2)}) copy-start(f32[8,1024]{1,0:T(8,128)S(1)} %collective-permute-done.2.halo_a_ref) | copy-start | bytes 98308
  49.2 0.6 copy-start.7
  79.7 2.5 %collective-permute-start.4 = (f32[8,1024]{1,0:T(8,128)}, f32[8,1024]{1,0:T(8,128)S(1)}, u32[]{:S(2)}, u32[]{:S(2)}) collective-permute-start(f32[8,1024]{1,0:T(8,128)} %get-tuple-element.35), channel_id=1, source_target_pairs={{0,1},{1,0},{2,3},{3,2},{4,5},{5,4},{6,7},{7,6},{8,9},{9,8},{10,11... | collective-permute-start | bytes 98312 | tf_op jit(solution)/shard_map/ppermute | solution.py:318
  80.1 5.4 %collective-permute-start.5 = (f32[8,1024]{1,0:T(8,128)}, f32[8,1024]{1,0:T(8,128)S(1)}, u32[]{:S(2)}, u32[]{:S(2)}) collective-permute-start(f32[8,1024]{1,0:T(8,128)} %get-tuple-element.36), channel_id=1, source_target_pairs={{1,2},{2,1},{3,4},{4,3},{5,6},{6,5},{7,8},{8,7},{9,10},{10,9},{11,... | collective-permute-start | bytes 98312 | tf_op jit(solution)/shard_map/ppermute | solution.py:318
  82.2 3.4 %copy-start.3 = (f32[8,1024]{1,0:T(8,128)}, f32[8,1024]{1,0:T(8,128)S(1)}, u32[]{:S(2)}) copy-start(f32[8,1024]{1,0:T(8,128)S(1)} %collective-permute-done.4.halo_a_ref) | copy-start | bytes 98308
  85.5 0.6 copy-start.5

commit v3 on v2

v3 whole, which is shorter than its diff:
```python
import functools

import jax
import jax.numpy as jnp
from jax import lax
from jax.experimental import pallas as pl
from jax.experimental.pallas import tpu as pltpu
from jax.sharding import PartitionSpec as P

LANES = 128
ROWS = 8
WIDE = 256
CHAINS = 4
SPAN = 14
BAND = 8
TOGETHER = 4
F32 = jnp.float32
BF16 = jnp.bfloat16
HIGHEST = lax.Precision.HIGHEST
NT = (((1,), (1,)), ((), ()))
VMEM = pl.BlockSpec(memory_space=pltpu.VMEM)
SMEM = pl.BlockSpec(memory_space=pltpu.SMEM)


def round_up(value, step):
    return -(-value // step) * step


class Sizes:
    def __init__(self, count, rhs, conn, projector, atom_matrix):
        self.devices = count
        self.vectors, self.nodes = rhs.shape
        self.slots, self.elem = conn.shape
        self.entries, self.channels = projector.shape[:2]
        self.owned = atom_matrix.shape[0]
        self.ghost = self.nodes // 16
        self.rim = round_up(self.ghost, WIDE)
        self.shift = self.rim - self.ghost
        self.window = self.nodes + 2 * self.rim
        self.width = round_up(self.elem, LANES)
        self.tiles = self.width // LANES
        self.pairs = self.channels * self.vectors
        self.reach = self.window + SPAN * LANES
        self.together = TOGETHER if self.slots % TOGETHER == 0 else 1
        assert self.vectors == ROWS and self.channels == ROWS and 2 * self.slots <= LANES
        assert self.nodes % WIDE == 0 and self.owned * self.pairs == LANES


def lane_gather(values, index):
    return jnp.take_along_axis(values, index, axis=1, mode="promise_in_bounds")


def iota(shape, dim):
    return lax.broadcasted_iota(jnp.int32, shape, dim)


def split(values):
    high = values.astype(BF16)
    return high, (values - high.astype(F32)).astype(BF16)


def lanes_by_vector(z, values):
    total = jnp.sum(values, axis=1, keepdims=True)
    spread = jnp.broadcast_to(total, (ROWS, LANES))
    return jnp.sum(jnp.where(iota((ROWS, LANES), 1) == iota((ROWS, LANES), 0), spread, 0.0), axis=0, keepdims=True)


def prepare_kernel(z, conn_ref, stiffness_ref, projector_ref, index_ref, k_high_ref, k_low_ref, pj_ref, k_ref):
    index_ref[...] = jnp.zeros_like(index_ref)
    for c in range(z.slots):
        index_ref[c, :, : z.elem] = conn_ref[c : c + 1, :] + z.shift
    k_ref[...] = jnp.zeros_like(k_ref)
    k_ref[: z.elem, : z.elem] = stiffness_ref[...]
    k_high_ref[...], k_low_ref[...] = split(k_ref[...])
    pj_ref[...] = jnp.zeros_like(pj_ref)
    pj_ref[:, : z.elem] = projector_ref[...]


def gather_cells(z, index_ref, corner_ref, range_ref, window_ref, scale_ref, live, u_ref, uw_ref):
    total = z.window // LANES
    tile = (ROWS, LANES)
    corner = jnp.broadcast_to(corner_ref[...], tile)
    low, high = corner & (LANES - 1), corner >> 7
    chains = [jnp.zeros(tile, F32)] * CHAINS
    for h in range(total):
        got = lane_gather(window_ref[:, h * LANES : (h + 1) * LANES], low)
        chains[h % CHAINS] = jnp.where(high == h, got, chains[h % CHAINS])
    corners = functools.reduce(jnp.add, chains)
    lane = iota(tile, 1)
    last = (z.elem - 1) % LANES

    def some_cells(g, _):
        cells = [g * z.together + i for i in range(z.together)]
        starts = [range_ref[0, c] >> 7 for c in cells]
        ends = [range_ref[1, c] >> 7 for c in cells]
        passes = functools.reduce(jnp.maximum, [(e - s) // SPAN + 1 for s, e in zip(starts, ends)])

        def one_pass(k, values):
            values = list(values)
            for i, c in enumerate(cells):
                start = jnp.minimum(starts[i] + k * SPAN, total)
                for t in range(z.tiles):
                    index = jnp.broadcast_to(index_ref[c, :, t * LANES : (t + 1) * LANES], tile)
                    low, high = index & (LANES - 1), (index >> 7) - start
                    value = values[i * z.tiles + t]
                    for h in range(SPAN):
                        at = pl.ds(pl.multiple_of((start + h) * LANES, LANES), LANES)
                        value = jnp.where(high == h, lane_gather(window_ref[:, at], low), value)
                    values[i * z.tiles + t] = value
            return tuple(values)

        values = lax.fori_loop(0, passes, one_pass, (jnp.zeros(tile, F32),) * (z.together * z.tiles))
        for i, c in enumerate(cells):
            weight = jnp.where(c < live, scale_ref[c], 0.0)
            rows = pl.ds(pl.multiple_of(c * ROWS, ROWS), ROWS)
            for t in range(z.tiles):
                value = values[i * z.tiles + t]
                if t == 0:
                    value = jnp.where(lane == 0, lane_gather(corners, jnp.full(tile, 0, jnp.int32) + c), value)
                if t == z.tiles - 1:
                    got = lane_gather(corners, jnp.full(tile, z.slots, jnp.int32) + c)
                    value = jnp.where(lane == last, got, value)
                u_ref[rows, t * LANES : (t + 1) * LANES] = value
                uw_ref[rows, t * LANES : (t + 1) * LANES] = value * weight
        return 0

    lax.fori_loop(0, z.slots // z.together, some_cells, 0)


def stiffness_product(k_high_ref, k_low_ref, uw_ref, e_ref):
    k_high, k_low = k_high_ref[...], k_low_ref[...]
    u_high, u_low = split(uw_ref[...])
    dot = functools.partial(lax.dot_general, dimension_numbers=NT, preferred_element_type=F32)
    e_ref[...] = dot(u_high, k_high) + (dot(u_high, k_low) + dot(u_low, k_high))


def entry_facts(z, position, atom_ref, count_ref, s):
    atom = atom_ref[s]
    owner = atom // z.owned
    return owner, atom - owner * z.owned, s < count_ref[position]


def contributions(z, position, pj_ref, cell_ref, atom_ref, count_ref, u_ref):
    values = [u_ref[pl.ds(pl.multiple_of(cell_ref[s] * ROWS, ROWS), ROWS), :] for s in range(z.entries)]
    sums = lax.dot_general(
        pj_ref[...], jnp.concatenate(values, axis=0), NT, precision=HIGHEST, preferred_element_type=F32
    )
    sums = jnp.concatenate([sums, jnp.zeros((sums.shape[0], LANES - sums.shape[1]), F32)], axis=1)
    lane, row = iota((ROWS, LANES), 1), iota((ROWS, LANES), 0)
    parts = [jnp.zeros((ROWS, LANES), F32)] * 3
    for s in range(z.entries):
        owner, local, alive = entry_facts(z, position, atom_ref, count_ref, s)
        got = lane_gather(sums[s * ROWS : (s + 1) * ROWS], s * ROWS + lane % ROWS)
        here = (lane // ROWS % ROWS == row) & (lane // z.pairs == local) & alive
        for k in range(3):
            parts[k] = parts[k] + jnp.where(here & (owner == position - 1 + k), got, 0.0)
    return [jnp.sum(part, axis=0, keepdims=True) for part in parts]


def first_kernel(
    z, pos_ref, count_ref, scale_ref, cell_ref, atom_ref, scount_ref, range_ref, rhs_ref, precond_ref, potential_ref,
    halo_a_ref, halo_b_ref, index_ref, corner_ref, k_high_ref, k_low_ref, pj_ref, coupling_ref,
    p_ref, diag_ref, out_ref, e_ref, gamma_ref, u_ref, uw_ref,
):
    position = pos_ref[0]
    even = position % 2 == 0
    a, b = halo_a_ref[...], halo_b_ref[...]
    left, right = jnp.where(even, b, a), jnp.where(even, a, b)
    own = slice(z.rim, z.rim + z.nodes)
    first, last = slice(0, z.rim), slice(z.rim + z.nodes, z.window)
    for where, side in ((first, left), (last, right)):
        p_ref[:, where] = side[:ROWS] * side[ROWS : ROWS + 1]
        diag_ref[0:1, where] = side[ROWS : ROWS + 1]
        diag_ref[1:2, where] = side[ROWS + 1 : ROWS + 2]
    diag_ref[0:1, own] = precond_ref[...]
    diag_ref[1:2, own] = potential_ref[...]
    product = rhs_ref[...] * precond_ref[...]
    p_ref[:, own] = product
    gamma_ref[...] = lanes_by_vector(z, product * rhs_ref[...])
    p_ref[:, z.window :] = jnp.zeros((ROWS, z.reach - z.window), F32)
    gather_cells(z, index_ref, corner_ref, range_ref, p_ref, scale_ref, count_ref[position], u_ref, uw_ref)
    parts = contributions(z, position, pj_ref, cell_ref, atom_ref, scount_ref, u_ref)
    message = jnp.concatenate(parts + [coupling_ref[...]], axis=0)
    for d in range(z.devices):
        out_ref[d] = message
    stiffness_product(k_high_ref, k_low_ref, uw_ref, e_ref)


def second_kernel(
    z, pos_ref, count_ref, scale_ref, cell_ref, atom_ref, scount_ref, range_ref, p_ref, diag_ref, shift_ref, gamma_ref,
    image_ref, halo_a_ref, halo_b_ref, index_ref, corner_ref, k_high_ref, k_low_ref, pj_ref,
    y_ref, q_ref, out_ref, e_ref, u_ref, uw_ref,
):
    position = pos_ref[0]
    even = position % 2 == 0
    a, b = halo_a_ref[...], halo_b_ref[...]
    left, right = jnp.where(even, b, a), jnp.where(even, a, b)
    diagonal = diag_ref[1:2, :] + shift_ref[...]
    y_ref[...] = image_ref[...] + diagonal * p_ref[:, : z.window]
    y_ref[:, : 2 * z.rim] += left
    y_ref[:, z.window - 2 * z.rim :] += right
    q_ref[:, : z.window] = y_ref[...] * diag_ref[0:1, :]
    q_ref[:, z.window :] = jnp.zeros((ROWS, z.reach - z.window), F32)
    own = slice(z.rim, z.rim + z.nodes)
    y, q = y_ref[:, own], q_ref[:, own]
    dots = [
        gamma_ref[...],
        lanes_by_vector(z, y * p_ref[:, own]),
        lanes_by_vector(z, y * q),
    ]
    energy = jnp.sum(q * q * (diag_ref[1:2, own] + shift_ref[...]), axis=1, keepdims=True)
    gather_cells(z, index_ref, corner_ref, range_ref, q_ref, scale_ref, count_ref[position], u_ref, uw_ref)
    parts = contributions(z, position, pj_ref, cell_ref, atom_ref, scount_ref, u_ref)
    stiffness_product(k_high_ref, k_low_ref, uw_ref, e_ref)
    elements = jnp.zeros((ROWS, z.width), F32)
    for c in range(z.slots):
        rows = slice(c * ROWS, (c + 1) * ROWS)
        elements = elements + u_ref[rows, :] * e_ref[rows, :]
    energy = energy + jnp.sum(elements, axis=1, keepdims=True)
    dots.append(lanes_by_vector(z, energy))
    line = dots[0]
    for k in range(1, len(dots)):
        line = line + pltpu.roll(dots[k], k * ROWS, 1)
    message = jnp.concatenate(parts + [line], axis=0)
    for d in range(z.devices):
        out_ref[d] = message


def scatter_kernel(
    z, last, pos_ref, cell_ref, atom_ref, scount_ref, range_ref, sums_ref, coupling_ref, e_in_ref, index_ref,
    corner_ref, pj_ref, *refs,
):
    if last:
        image_ref, send_a_ref, send_b_ref, dots_ref, e_ref, acc_ref = refs
    else:
        image_ref, send_a_ref, send_b_ref, e_ref, acc_ref = refs
    position = pos_ref[0]
    wanted = (
        pltpu.roll(sums_ref[:, 0, :], z.devices - 1, 0) + sums_ref[:, 1, :] + pltpu.roll(sums_ref[:, 2, :], 1, 0)
    )
    coupling = coupling_ref[:, 3, :]
    shape = (z.devices, LANES)
    lane = iota(shape, 1)
    term = jnp.zeros(shape, F32)
    for j in range(z.channels):
        matrix = lane_gather(coupling, lane // ROWS * ROWS + j)
        vector = lane_gather(wanted, lane // z.pairs * z.pairs + j * ROWS + lane % ROWS)
        term = term + matrix * vector
    if last:
        energy = jnp.sum(term * wanted, axis=0, keepdims=True)
        energy = jnp.broadcast_to(energy, (ROWS, LANES))
        step = ROWS
        while step < LANES:
            energy = energy + pltpu.roll(energy, step, 1)
            step *= 2
        line = iota((1, LANES), 1)
        dots_ref[...] = jnp.sum(sums_ref[:, 3, :], axis=0, keepdims=True) + jnp.where(
            line // ROWS == 3, energy[0:1], 0.0
        )
    block = iota(shape, 0)
    small_lane, small_row = iota((ROWS, LANES), 1), iota((ROWS, LANES), 0)
    spread = []
    for s in range(z.entries):
        owner, local, alive = entry_facts(z, position, atom_ref, scount_ref, s)
        mine = jnp.sum(jnp.where(block == owner, term, 0.0), axis=0, keepdims=True)
        got = lane_gather(
            jnp.broadcast_to(mine, (ROWS, LANES)), local * z.pairs + small_lane % ROWS * ROWS + small_row
        )
        spread.append(jnp.where((small_lane // ROWS == s) & alive, got, 0.0)[:, : z.entries * ROWS])
    support = jnp.dot(
        jnp.concatenate(spread, axis=0), pj_ref[...], precision=HIGHEST, preferred_element_type=F32
    )
    e_ref[...] = e_in_ref[...]
    for s in range(z.entries):
        rows = pl.ds(pl.multiple_of(cell_ref[s] * ROWS, ROWS), ROWS)
        e_ref[rows, :] += support[s * ROWS : (s + 1) * ROWS]

    groups = z.window // WIDE
    pair = (2 * ROWS, LANES)
    sub, lane = iota(pair, 0), iota(pair, 1)
    lows = [(sub + k * 2 * ROWS).astype(jnp.int16) for k in range(WIDE // (2 * ROWS))]
    one, none = jnp.ones(pair, BF16), jnp.zeros(pair, BF16)

    def two_parts(value):
        rounded = value.astype(BF16).astype(F32)
        return jnp.concatenate([rounded, value - rounded], axis=0).astype(BF16)

    def hot_rows(index):
        low = (index & (WIDE - 1)).astype(jnp.int16)
        return jnp.concatenate([jnp.where(low == k, one, none) for k in lows], axis=0)

    def masked(high, both, rows):
        high = high.astype(jnp.int16)
        return jnp.concatenate([jnp.where(high == jnp.int16(h), both, none) for h in range(rows)], axis=0)

    def product(lhs, hot):
        return lax.dot_general(lhs, hot, NT, preferred_element_type=F32)

    corners = jnp.zeros((ROWS, LANES), F32)
    end = (z.elem - 1) % LANES
    for c in range(z.slots):
        tiles = e_ref[c * ROWS : (c + 1) * ROWS, :]
        at = (z.tiles - 1) * LANES + end
        corners = jnp.where(small_lane == c, tiles[:, 0:1], corners)
        corners = jnp.where(small_lane == z.slots + c, tiles[:, at : at + 1], corners)
    index = jnp.broadcast_to(corner_ref[...], pair)
    acc_ref[: groups * 2 * ROWS, :] = product(masked(index >> 8, two_parts(corners), groups), hot_rows(index))
    acc_ref[groups * 2 * ROWS :, :] = jnp.zeros((BAND * 2 * ROWS, WIDE), F32)

    def some_cells(g, _):
        cells = [g * z.together + i for i in range(z.together)]
        starts = [range_ref[0, c] >> 8 for c in cells]
        ends = [range_ref[1, c] >> 8 for c in cells]
        passes = functools.reduce(jnp.maximum, [(e - s) // BAND + 1 for s, e in zip(starts, ends)])

        def one_pass(k, _):
            for i, c in enumerate(cells):
                start = jnp.minimum(starts[i] + k * BAND, groups)
                rows = pl.ds(pl.multiple_of(c * ROWS, ROWS), ROWS)
                lhs, hot = [], []
                for t in range(z.tiles):
                    lanes = slice(t * LANES, (t + 1) * LANES)
                    index = jnp.broadcast_to(index_ref[c, :, lanes], pair)
                    value = e_ref[rows, lanes]
                    if t == 0:
                        value = jnp.where(small_lane == 0, 0.0, value)
                    if t == z.tiles - 1:
                        value = jnp.where(small_lane == end, 0.0, value)
                    lhs.append(masked((index >> 8) - start, two_parts(value), BAND))
                    hot.append(hot_rows(index))
                to = pl.ds(pl.multiple_of(start * 2 * ROWS, 2 * ROWS), BAND * 2 * ROWS)
                acc_ref[to, :] += product(jnp.concatenate(lhs, axis=1), jnp.concatenate(hot, axis=1))
            return 0

        lax.fori_loop(0, passes, one_pass, 0)
        return 0

    lax.fori_loop(0, z.slots // z.together, some_cells, 0)
    for h in range(groups):
        at = h * 2 * ROWS
        image_ref[:, h * WIDE : (h + 1) * WIDE] = acc_ref[at : at + ROWS] + acc_ref[at + ROWS : at + 2 * ROWS]
    low_rim, high_rim = image_ref[:, : 2 * z.rim], image_ref[:, z.window - 2 * z.rim :]
    even = position % 2 == 0
    send_a_ref[...] = jnp.where(even, high_rim, low_rim)
    send_b_ref[...] = jnp.where(even, low_rim, high_rim)


def last_kernel(
    z, rhs_ref, p_ref, diag_ref, shift_ref, y_ref, q_ref, image_ref, dots_ref, solution_ref, residual_ref, factor_ref,
):
    own = slice(z.rim, z.rim + z.nodes)
    lane, row = iota((ROWS, LANES), 1), iota((ROWS, LANES), 0)
    line = jnp.broadcast_to(dots_ref[...], (ROWS, LANES))

    def column(k):
        return jnp.sum(jnp.where(lane == k * ROWS + row, line, 0.0), axis=1, keepdims=True)

    gamma, py, qy, qq = (column(k) for k in range(4))
    alpha = gamma / py
    fresh = gamma - 2.0 * alpha * py + alpha * alpha * qy
    beta = fresh / gamma
    more = 1.0 + beta
    step = fresh / (more * more * py - 2.0 * more * alpha * qy + alpha * alpha * qq)
    p, q, y = p_ref[:, own], q_ref[:, own], y_ref[:, own]
    second = image_ref[:, own] + (diag_ref[1:2, own] + shift_ref[...]) * q
    search = (p - alpha * q) + beta * p
    solution_ref[...] = alpha * p + step * search
    residual_ref[...] = (rhs_ref[...] - alpha * y) - step * (more * y - alpha * second)
    factor_ref[...] = jnp.broadcast_to(step * alpha, (ROWS, LANES))


def rim_kernel(z, pos_ref, residual_in_ref, halo_a_ref, halo_b_ref, factor_ref, residual_ref):
    even = pos_ref[0] % 2 == 0
    a, b = halo_a_ref[...], halo_b_ref[...]
    left, right = jnp.where(even, b, a), jnp.where(even, a, b)
    side = jnp.where(pl.program_id(0) == 0, left[:, z.rim :], right[:, : z.rim])
    residual_ref[...] = residual_in_ref[...] + factor_ref[:, 0:1] * side


def on_device(
    rhs, potential, precond, shift, stiffness, cell_scale, conn, cell_count, projector, support_cell, support_atom,
    support_count, atom_matrix,
):
    count = lax.axis_size("dom")
    z = Sizes(count, rhs, conn, projector, atom_matrix)
    position = lax.axis_index("dom")
    even = position % 2 == 0
    pos = position.astype(jnp.int32).reshape(1)
    near = [(i, i ^ 1) for i in range(count)]
    far = [(i, j) for i in range(1, count - 1) for j in [i + 1 if i % 2 else i - 1]]

    def exchange(a, b):
        return lax.ppermute(a, "dom", near), lax.ppermute(b, "dom", far)

    def call(kernel, outs, scratch, specs, *args):
        return pl.pallas_call(
            functools.partial(kernel),
            out_shape=[jax.ShapeDtypeStruct(s, d) for s, d in outs],
            in_specs=specs,
            out_specs=[VMEM] * len(outs),
            scratch_shapes=[pltpu.VMEM(s, d) for s, d in scratch],
        )(*args)

    precond_row, potential_row = precond[None, :], potential[None, :]
    shift_column = shift[:, None]
    packed = jnp.concatenate([rhs, precond_row, potential_row], axis=0)
    head, tail = packed[:, : z.rim], packed[:, z.nodes - z.rim :]
    halo = exchange(jnp.where(even, tail, head), jnp.where(even, head, tail))
    flat_projector = projector.reshape(z.entries * z.channels, z.elem)
    coupling = atom_matrix.reshape(1, LANES)
    middle = conn[:, 1:-1] + z.shift
    ranges = jnp.stack([jnp.min(middle, axis=1), jnp.max(middle, axis=1)])
    corner = jnp.concatenate([conn[:, 0], conn[:, -1]]) + z.shift
    corner = jnp.pad(corner, (0, LANES - 2 * z.slots))[None, :]

    cells = (z.slots * ROWS, z.width)
    window, reach = (z.vectors, z.window), (z.vectors, z.reach)
    message = (z.devices, 4, LANES)
    cell_scratch = [(cells, F32), (cells, F32)]
    square = (z.width, z.width)
    index, k_high, k_low, pj = call(
        functools.partial(prepare_kernel, z),
        [((z.slots, 1, z.width), jnp.int32), (square, BF16), (square, BF16), ((z.entries * ROWS, z.width), F32)],
        [(square, F32)],
        [VMEM] * 3,
        conn, stiffness, flat_projector,
    )
    p, diag, sums, e, gamma = call(
        functools.partial(first_kernel, z),
        [(reach, F32), ((2, z.window), F32), (message, F32), (cells, F32), ((1, LANES), F32)],
        cell_scratch,
        [SMEM] * 7 + [VMEM] * 11,
        pos, cell_count, cell_scale, support_cell, support_atom, support_count, ranges, rhs, precond_row,
        potential_row, *halo, index, corner, k_high, k_low, pj, coupling,
    )
    groups = z.window // WIDE
    scatter_scratch = [(cells, F32), (((groups + BAND) * 2 * ROWS, WIDE), F32)]
    rim = (z.vectors, 2 * z.rim)
    coupled = lax.all_to_all(sums, "dom", 0, 0)
    image, send_a, send_b = call(
        functools.partial(scatter_kernel, z, False),
        [(window, F32), (rim, F32), (rim, F32)],
        scatter_scratch,
        [SMEM] * 5 + [VMEM] * 6,
        pos, support_cell, support_atom, support_count, ranges, coupled, coupled, e, index, corner, pj,
    )
    halo = exchange(send_a, send_b)
    y, q, sums, e = call(
        functools.partial(second_kernel, z),
        [(window, F32), (reach, F32), (message, F32), (cells, F32)],
        cell_scratch,
        [SMEM] * 7 + [VMEM] * 12,
        pos, cell_count, cell_scale, support_cell, support_atom, support_count, ranges, p, diag, shift_column, gamma,
        image, *halo, index, corner, k_high, k_low, pj,
    )
    totals = lax.all_to_all(sums, "dom", 0, 0)
    image, send_a, send_b, dots = call(
        functools.partial(scatter_kernel, z, True),
        [(window, F32), (rim, F32), (rim, F32), ((1, LANES), F32)],
        scatter_scratch,
        [SMEM] * 5 + [VMEM] * 6,
        pos, support_cell, support_atom, support_count, ranges, totals, coupled, e, index, corner, pj,
    )
    halo = exchange(send_a, send_b)
    own = (z.vectors, z.nodes)
    answer, residual, factor = call(
        functools.partial(last_kernel, z),
        [(own, F32), (own, F32), ((ROWS, LANES), F32)],
        [],
        [VMEM] * 8,
        rhs, p, diag, shift_column, y, q, image, dots,
    )
    ends = pl.BlockSpec((ROWS, z.rim), lambda i: (0, i * (z.nodes // z.rim - 1)))
    residual = pl.pallas_call(
        functools.partial(rim_kernel, z),
        grid=(2,),
        out_shape=jax.ShapeDtypeStruct(own, F32),
        in_specs=[SMEM, ends, VMEM, VMEM, VMEM],
        out_specs=ends,
        input_output_aliases={1: 0},
    )(pos, residual, *halo, factor)
    return answer, residual


def solution(mesh):
    placed = (
        P(None, "dom"),
        P("dom"),
        P("dom"),
        P(),
        P(),
        P("dom"),
        P("dom", None),
        P(),
        P("dom", None, None),
        P("dom"),
        P("dom"),
        P(),
        P("dom", None, None),
    )
    return jax.shard_map(
        on_device,
        mesh=mesh,
        in_specs=placed,
        out_specs=(P(None, "dom"), P(None, "dom")),
        check_vma=False,
    )
```

time: 89.1 us -> 75.5 us (0.85)
  Pallas kernels: 41.4 us -> 31.2 us
  waiting for transfers between devices: 6.71 us -> 3.74 us
  blocking collectives: 24.2 us -> 22.7 us
    pallas_call x5 -> x6, Pallas kernels: 41.4 us -> 29.7 us  [call(): pl.pallas_call(functools.partial(kernel), out_shape=[jax.ShapeDtypeStruct...]
    ppermute x6, waiting for transfers between devices: 6.71 us -> 3.74 us  [exchange(): return (lax.ppermute(a, 'dom', near), lax.ppermute(b, 'dom', far))]
    all_to_all x1, blocking collectives: 14.1 us -> 12.5 us  [on_device(): coupled = lax.all_to_all(sums, 'dom', 0, 0)]
    pallas_call x0 -> x1, Pallas kernels: none -> 1.55 us  [on_device(): pl.pallas_call(functools.partial(rim_kernel, z), grid=(2,), out_shape=jax...]
    unnamed x24 -> x26, local copies, waits for them, and re-layouts: 3.76 us -> 3.15 us
  transfers between devices with their start and end apart: 6 -> 6, of which waited for: 2 -> 2; matrix products, arithmetic and copies ran while one was open for 2% -> 4% of each run, Pallas kernels for 0% -> 6%
where the time goes in v3:
time: 75.5 us; the launch traced here: 74.9 us
  Pallas kernels  31.2 us (41%)
  blocking collectives  22.7 us (30%)
  starting transfers between devices  9.58 us (13%)
  local copies, waits for them, and re-layouts  5.24 us (7%)
  waiting for transfers between devices  3.74 us (5%)
  other arithmetic  1.62 us (2%)
  between operations  0.81 us (1%)
    pallas_call x6, Pallas kernels, call(): pl.pallas_call(functools.partial(kernel), out_shape=[jax.ShapeDtypeStruct...  29.7 us
    all_to_all x1, blocking collectives, on_device(): coupled = lax.all_to_all(sums, 'dom', 0, 0)  12.5 us
    all_to_all x1, blocking collectives, on_device(): totals = lax.all_to_all(sums, 'dom', 0, 0)  10.2 us
    ppermute x6, starting transfers between devices, exchange(): return (lax.ppermute(a, 'dom', near), lax.ppermute(b, 'dom', far))  9.58 us
    ppermute x6, waiting for transfers between devices, exchange(): return (lax.ppermute(a, 'dom', near), lax.ppermute(b, 'dom', far))  3.74 us
    unnamed x26, local copies, waits for them, and re-layouts  3.15 us
    pallas_call x1, Pallas kernels, on_device(): pl.pallas_call(functools.partial(rim_kernel, z), grid=(2,), out_shape=jax...  1.55 us
  transfers between devices with their start and end apart: 6, of which 2 were waited for; matrix products, arithmetic and copies ran while one was open for 4% of the time, Pallas kernels for 6%

profile of v3, /device:TPU:1, one launch (start us, length us, event | category | flops | bytes accessed | tf_op | source)
XLA Modules:
  0.0 74.9 jit_solution(11938638059807066328)
XLA Ops:
  0.7 0.7 copy-done.9
  1.4 0.6 copy-done.1
  2.0 0.8 %broadcast_select_fusion = (f32[10,512]{1,0:T(8,128)S(1)}, f32[10,512]{1,0:T(8,128)S(1)}, f32[10,512]{1,0:T(8,128)S(1)}) fusion(pred[]{:T(512)S(6)} %eq.5, f32[1,6656]{1,0:T(1,128)S(1)} %broadcast_in_dim.13.potential_ref, f32[1,6656]{1,0:T(1,128)S(1)} %broadcast_in_dim.12.precond_ref, f32[8,6656]{1,0:T(8,128)} %rhs_ref.3), kind=kLoop, calls=%fused_computation.8 | loop fusion | flops 25600 | bytes 327681 | tf_op jit(solution)/shard_map/jit(_where)/select_n | solution.py:408
  2.9 4.5 %collective-permute-start.1 = (f32[10,512]{1,0:T(8,128)S(1)}, f32[10,512]{1,0:T(8,128)S(1)}, u32[]{:S(2)}, u32[]{:S(2)}) collective-permute-start(f32[10,512]{1,0:T(8,128)S(1)} %get-tuple-element.52), channel_id=1, source_target_pairs={{1,2},{2,1},{3,4},{4,3},{5,6},{6,5},{7,8},{8,7},{9,10},{10,9},{11,... | collective-permute-start | bytes 61448 | tf_op jit(solution)/shard_map/ppermute | solution.py:393
  7.8 0.6 pad_add_fusion.range_ref
  8.5 0.6 pad_bitcast_fusion.corner_ref
  9.0 0.6 reshape.15.coupling_ref
  9.7 2.0 %shard_map.140 = (s32[32,1,384]{2,1,0:T(1,128)}, bf16[384,384]{1,0:T(8,128)(2,1)}, bf16[384,384]{1,0:T(8,128)(2,1)}, f32[64,384]{1,0:T(8,128)}) custom-call(s32[32,343]{1,0:T(8,128)} %conn_ref.1, f32[343,343]{1,0:T(8,128)} %stiffness_ref.1, f32[64,343]{1,0:T(8,128)} %bitcast.7), custom_call_target="tpu_custom_call" | custom-call | tf_op jit(solution)/shard_map/pallas_call | solution.py:396
  11.7 0.6 copy-done.3
  12.3 6.2 %shard_map.141 = (f32[8,9472]{1,0:T(8,128)}, f32[2,7680]{1,0:T(2,128)}, f32[32,4,128]{2,1,0:T(4,128)}, f32[256,384]{1,0:T(8,128)}, f32[1,128]{1,0:T(1,128)}) custom-call(s32[1]{0:T(128)} %bitcast.pos_ref, s32[32]{0:T(128)} %count_ref.3, f32[32]{0:T(128)} %scale_ref.3, s32[8]{0:T(128)} %cell_ref.7, s32[8]{0:T(128)} %atom_ref.7, s32[32]{0:T(128)} %scount_ref.7, ...), custom_call_target="tpu_custom_call" | custom-call | tf_op jit(solution)/shard_map/pallas_call | solution.py:396
  18.5 12.5 %all_to_all.10.sums_ref.coupling_ref = f32[32,4,128]{2,1,0:T(4,128)} all-to-all(f32[32,4,128]{2,1,0:T(4,128)} %get-tuple-element.32), channel_id=1, replica_groups=mesh['dom'=32] {'dom'}, dimensions={0} | all-to-all | bytes 131072 | tf_op jit(solution)/shard_map/all_to_all | solution.py:439
  31.0 6.4 %shard_map.142 = (f32[8,7680]{1,0:T(8,128)}, f32[8,1024]{1,0:T(8,128)}, f32[8,1024]{1,0:T(8,128)}) custom-call(s32[1]{0:T(128)} %bitcast.pos_ref, s32[8]{0:T(128)} %cell_ref.7, s32[8]{0:T(128)} %atom_ref.7, s32[32]{0:T(128)} %scount_ref.7, s32[2,32]{1,0:T(2,128)} %pad_add_fusion.range_ref, f32[32,4,128]{2,1,0:T(4,128)} %all_to_all.10.sums_ref.coupling_ref, ...), custom_call_target="tpu_custom_call" | custom-call | tf_op jit(solution)/shard_map/pallas_call | solution.py:396
  37.8 2.2 %collective-permute-start.3 = (f32[8,1024]{1,0:T(8,128)}, f32[8,1024]{1,0:T(8,128)S(1)}, u32[]{:S(2)}, u32[]{:S(2)}) collective-permute-start(f32[8,1024]{1,0:T(8,128)} %get-tuple-element.36), channel_id=1, source_target_pairs={{1,2},{2,1},{3,4},{4,3},{5,6},{6,5},{7,8},{8,7},{9,10},{10,9},{11,... | collective-permute-start | bytes 98312 | tf_op jit(solution)/shard_map/ppermute | solution.py:393
  40.0 0.7 copy.19.shift_ref
  40.7 2.7 %collective-permute-done.3.halo_b_ref = f32[8,1024]{1,0:T(8,128)S(1)} collective-permute-done((f32[8,1024]{1,0:T(8,128)}, f32[8,1024]{1,0:T(8,128)S(1)}, u32[]{:S(2)}, u32[]{:S(2)}) %collective-permute-start.3) | collective-permute-done | bytes 32800 | tf_op jit(solution)/shard_map/ppermute | solution.py:393
  43.4 0.6 copy-done.8
  44.0 6.4 %shard_map.143 = (f32[8,7680]{1,0:T(8,128)}, f32[8,9472]{1,0:T(8,128)}, f32[32,4,128]{2,1,0:T(4,128)}, f32[256,384]{1,0:T(8,128)}) custom-call(s32[1]{0:T(128)} %bitcast.pos_ref, s32[32]{0:T(128)} %count_ref.3, f32[32]{0:T(128)} %scale_ref.3, s32[8]{0:T(128)} %cell_ref.7, s32[8]{0:T(128)} %atom_ref.7, s32[32]{0:T(128)} %scount_ref.7, ...), custom_call_target="tpu_custom_call" | custom-call | tf_op jit(solution)/shard_map/pallas_call | solution.py:396
  50.4 10.2 %all_to_all.11.sums_ref = f32[32,4,128]{2,1,0:T(4,128)} all-to-all(f32[32,4,128]{2,1,0:T(4,128)} %get-tuple-element.39), channel_id=1, replica_groups=mesh['dom'=32] {'dom'}, dimensions={0} | all-to-all | bytes 131072 | tf_op jit(solution)/shard_map/all_to_all | solution.py:456
  60.6 6.3 %shard_map.144 = (f32[8,7680]{1,0:T(8,128)}, f32[8,1024]{1,0:T(8,128)}, f32[8,1024]{1,0:T(8,128)}, f32[1,128]{1,0:T(1,128)}) custom-call(s32[1]{0:T(128)} %bitcast.pos_ref, s32[8]{0:T(128)} %cell_ref.7, s32[8]{0:T(128)} %atom_ref.7, s32[32]{0:T(128)} %scount_ref.7, s32[2,32]{1,0:T(2,128)} %pad_add_fusion.range_ref, f32[32,4,128]{2,1,0:T(4,128)} %all_to_all.11.sums_ref, ...), custom_call_target="tpu_custom_call" | custom-call | tf_op jit(solution)/shard_map/pallas_call | solution.py:396
  67.3 2.1 %collective-permute-start.5 = (f32[8,1024]{1,0:T(8,128)}, f32[8,1024]{1,0:T(8,128)S(1)}, u32[]{:S(2)}, u32[]{:S(2)}) collective-permute-start(f32[8,1024]{1,0:T(8,128)} %get-tuple-element.46), channel_id=1, source_target_pairs={{1,2},{2,1},{3,4},{4,3},{5,6},{6,5},{7,8},{8,7},{9,10},{10,9},{11,... | collective-permute-start | bytes 98312 | tf_op jit(solution)/shard_map/ppermute | solution.py:393
  69.4 2.3 %shard_map.145 = (f32[8,6656]{1,0:T(8,128)}, f32[8,6656]{1,0:T(8,128)}, f32[8,128]{1,0:T(8,128)}) custom-call(f32[8,6656]{1,0:T(8,128)} %rhs_ref.3, f32[8,9472]{1,0:T(8,128)} %get-tuple-element.29.p_ref, f32[2,7680]{1,0:T(2,128)} %get-tuple-element.30.diag_ref, f32[8,1]{1,0:T(8,128)} %copy.19.shift_ref, f32[8,7680]{1,0:T(8,128)} %get-tuple-element.37.y_ref, ...), custom_call_target="tpu_custom_call" | custom-call | tf_op jit(solution)/shard_map/pallas_call | solution.py:396
  71.7 1.0 %collective-permute-done.5.halo_b_ref = f32[8,1024]{1,0:T(8,128)S(1)} collective-permute-done((f32[8,1024]{1,0:T(8,128)}, f32[8,1024]{1,0:T(8,128)S(1)}, u32[]{:S(2)}, u32[]{:S(2)}) %collective-permute-start.5) | collective-permute-done | bytes 32800 | tf_op jit(solution)/shard_map/ppermute | solution.py:393
  72.7 0.6 copy-done.7
  73.4 1.5 %shard_map.146 = f32[8,6656]{1,0:T(8,128)} custom-call(s32[1]{0:T(128)} %bitcast.pos_ref, f32[8,6656]{1,0:T(8,128)} %get-tuple-element.44.residual_in_ref, f32[8,1024]{1,0:T(8,128)} %copy-done.5, f32[8,1024]{1,0:T(8,128)} %copy-done.7, f32[8,128]{1,0:T(8,128)} %get-tuple-element.47.factor_ref), custom_call_target="tpu_custom_call", output_to_operand_aliasing={{}: (1, {})} | custom-call | tf_op jit(solution)/shard_map/pallas_call | solution.py:474
  (34 shorter events, 1.4 us)
Async XLA Ops:
  0.6 0.7 copy-start.9
  0.7 0.8 %copy-start.10 = (f32[6656]{0:T(1024)S(1)}, f32[6656]{0:T(1024)}, u32[]{:S(2)}) copy-start(f32[6656]{0:T(1024)} %param.15) | copy-start | bytes 79876
  1.4 0.6 copy-start.1
  2.0 0.8 %copy-start.2 = (f32[1,6656]{1,0:T(1,128)}, f32[1,6656]{1,0:T(1,128)S(1)}, u32[]{:S(2)}) copy-start(f32[1,6656]{1,0:T(1,128)S(1)} %broadcast_in_dim.12.precond_ref) | copy-start | bytes 79876
  2.8 4.6 %copy-start = (s32[32,343]{1,0:T(8,128)S(1)}, s32[32,343]{1,0:T(8,128)}, u32[]{:S(2)}) copy-start(s32[32,343]{1,0:T(8,128)} %conn_ref.1) | copy-start | bytes 131716
  2.8 8.9 %collective-permute-start = (f32[10,512]{1,0:T(8,128)S(1)}, f32[10,512]{1,0:T(8,128)S(1)}, u32[]{:S(2)}, u32[]{:S(2)}) collective-permute-start(f32[10,512]{1,0:T(8,128)S(1)} %broadcast_select_fusion.1), channel_id=1, source_target_pairs={{0,1},{1,0},{2,3},{3,2},{4,5},{5,4},{6,7},{7,6},{8,9},{9,8},{10,11... | collective-permute-start | bytes 61448 | tf_op jit(solution)/shard_map/ppermute | solution.py:393
  2.9 8.8 %collective-permute-start.1 = (f32[10,512]{1,0:T(8,128)S(1)}, f32[10,512]{1,0:T(8,128)S(1)}, u32[]{:S(2)}, u32[]{:S(2)}) collective-permute-start(f32[10,512]{1,0:T(8,128)S(1)} %get-tuple-element.52), channel_id=1, source_target_pairs={{1,2},{2,1},{3,4},{4,3},{5,6},{6,5},{7,8},{8,7},{9,10},{10,9},{11,... | collective-permute-start | bytes 61448 | tf_op jit(solution)/shard_map/ppermute | solution.py:393
  7.8 1.3 %copy-start.11 = (f32[2,8,8]{2,1,0:T(8,128)S(1)}, f32[2,8,8]{2,1,0:T(8,128)}, u32[]{:S(2)}) copy-start(f32[2,8,8]{2,1,0:T(8,128)} %param.25) | copy-start | bytes 1540
  11.7 0.6 copy-start.3
  11.7 0.6 copy-start.4
  37.4 3.3 %collective-permute-start.2 = (f32[8,1024]{1,0:T(8,128)}, f32[8,1024]{1,0:T(8,128)S(1)}, u32[]{:S(2)}, u32[]{:S(2)}) collective-permute-start(f32[8,1024]{1,0:T(8,128)} %get-tuple-element.35), channel_id=1, source_target_pairs={{0,1},{1,0},{2,3},{3,2},{4,5},{5,4},{6,7},{7,6},{8,9},{9,8},{10,11... | collective-permute-start | bytes 98312 | tf_op jit(solution)/shard_map/ppermute | solution.py:393
  37.8 2.2 %copy-start.12 = (f32[8]{0:T(128)S(1)}, f32[8]{0:T(128)}, u32[]{:S(2)}) copy-start(f32[8]{0:T(128)} %param.16) | copy-start | bytes 100
  37.8 5.6 %collective-permute-start.3 = (f32[8,1024]{1,0:T(8,128)}, f32[8,1024]{1,0:T(8,128)S(1)}, u32[]{:S(2)}, u32[]{:S(2)}) collective-permute-start(f32[8,1024]{1,0:T(8,128)} %get-tuple-element.36), channel_id=1, source_target_pairs={{1,2},{2,1},{3,4},{4,3},{5,6},{6,5},{7,8},{8,7},{9,10},{10,9},{11,... | collective-permute-start | bytes 98312 | tf_op jit(solution)/shard_map/ppermute | solution.py:393
  40.7 2.7 %copy-start.6 = (f32[8,1024]{1,0:T(8,128)}, f32[8,1024]{1,0:T(8,128)S(1)}, u32[]{:S(2)}) copy-start(f32[8,1024]{1,0:T(8,128)S(1)} %collective-permute-done.2.halo_a_ref) | copy-start | bytes 98308
  43.4 0.6 copy-start.8
  66.9 4.8 %collective-permute-start.4 = (f32[8,1024]{1,0:T(8,128)}, f32[8,1024]{1,0:T(8,128)S(1)}, u32[]{:S(2)}, u32[]{:S(2)}) collective-permute-start(f32[8,1024]{1,0:T(8,128)} %get-tuple-element.45), channel_id=1, source_target_pairs={{0,1},{1,0},{2,3},{3,2},{4,5},{5,4},{6,7},{7,6},{8,9},{9,8},{10,11... | collective-permute-start | bytes 98312 | tf_op jit(solution)/shard_map/ppermute | solution.py:393
  67.3 5.4 %collective-permute-start.5 = (f32[8,1024]{1,0:T(8,128)}, f32[8,1024]{1,0:T(8,128)S(1)}, u32[]{:S(2)}, u32[]{:S(2)}) collective-permute-start(f32[8,1024]{1,0:T(8,128)} %get-tuple-element.46), channel_id=1, source_target_pairs={{1,2},{2,1},{3,4},{4,3},{5,6},{6,5},{7,8},{8,7},{9,10},{10,9},{11,... | collective-permute-start | bytes 98312 | tf_op jit(solution)/shard_map/ppermute | solution.py:393
  71.7 1.1 %copy-start.5 = (f32[8,1024]{1,0:T(8,128)}, f32[8,1024]{1,0:T(8,128)S(1)}, u32[]{:S(2)}) copy-start(f32[8,1024]{1,0:T(8,128)S(1)} %collective-permute-done.4.halo_a_ref) | copy-start | bytes 98308
  72.7 0.6 copy-start.7

commit v4 on v3

--- a/solution.py
+++ b/solution.py
@@ -65,10 +65,18 @@
     return jnp.sum(jnp.where(iota((ROWS, LANES), 1) == iota((ROWS, LANES), 0), spread, 0.0), axis=0, keepdims=True)
 
 
-def prepare_kernel(z, conn_ref, stiffness_ref, projector_ref, index_ref, k_high_ref, k_low_ref, pj_ref, k_ref):
+def prepare_kernel(
+    z, conn_ref, stiffness_ref, projector_ref, index_ref, corner_ref, k_high_ref, k_low_ref, pj_ref, k_ref
+):
+    line = iota((1, LANES), 1)
+    corner = jnp.zeros((1, LANES), jnp.int32)
     index_ref[...] = jnp.zeros_like(index_ref)
     for c in range(z.slots):
-        index_ref[c, :, : z.elem] = conn_ref[c : c + 1, :] + z.shift
+        row = conn_ref[c : c + 1, :] + z.shift
+        index_ref[c, :, : z.elem] = row
+        corner = jnp.where(line == c, row[:, :1], corner)
+        corner = jnp.where(line == z.slots + c, row[:, z.elem - 1 :], corner)
+    corner_ref[...] = corner
     k_ref[...] = jnp.zeros_like(k_ref)
     k_ref[: z.elem, : z.elem] = stiffness_ref[...]
     k_high_ref[...], k_low_ref[...] = split(k_ref[...])
@@ -76,7 +84,9 @@
     pj_ref[:, : z.elem] = projector_ref[...]
 
 
-def gather_cells(z, index_ref, corner_ref, range_ref, window_ref, scale_ref, live, u_ref, uw_ref):
+def gather_cells(
+    z, index_ref, corner_ref, low_ref, high_ref, window_ref, scale_ref, live, u_ref, uw_ref
+):
     total = z.window // LANES
     tile = (ROWS, LANES)
     corner = jnp.broadcast_to(corner_ref[...], tile)
@@ -91,8 +101,8 @@
 
     def some_cells(g, _):
         cells = [g * z.together + i for i in range(z.together)]
-        starts = [range_ref[0, c] >> 7 for c in cells]
-        ends = [range_ref[1, c] >> 7 for c in cells]
+        starts = [(low_ref[c] + z.shift) >> 7 for c in cells]
+        ends = [(high_ref[c] + z.shift) >> 7 for c in cells]
         passes = functools.reduce(jnp.maximum, [(e - s) // SPAN + 1 for s, e in zip(starts, ends)])
 
         def one_pass(k, values):
@@ -157,51 +167,56 @@
     return [jnp.sum(part, axis=0, keepdims=True) for part in parts]
 
 
+def sides(position, near, far):
+    even = position % 2 == 0
+    return jnp.where(even, far, near), jnp.where(even, near, far)
+
+
 def first_kernel(
-    z, pos_ref, count_ref, scale_ref, cell_ref, atom_ref, scount_ref, range_ref, rhs_ref, precond_ref, potential_ref,
-    halo_a_ref, halo_b_ref, index_ref, corner_ref, k_high_ref, k_low_ref, pj_ref, coupling_ref,
+    z, pos_ref, count_ref, scale_ref, cell_ref, atom_ref, scount_ref, low_ref, high_ref, rhs_ref, precond_ref,
+    potential_ref, halo_a_ref, halo_b_ref, index_ref, corner_ref, k_high_ref, k_low_ref, pj_ref, coupling_ref,
     p_ref, diag_ref, out_ref, e_ref, gamma_ref, u_ref, uw_ref,
 ):
     position = pos_ref[0]
-    even = position % 2 == 0
-    a, b = halo_a_ref[...], halo_b_ref[...]
-    left, right = jnp.where(even, b, a), jnp.where(even, a, b)
     own = slice(z.rim, z.rim + z.nodes)
-    first, last = slice(0, z.rim), slice(z.rim + z.nodes, z.window)
-    for where, side in ((first, left), (last, right)):
-        p_ref[:, where] = side[:ROWS] * side[ROWS : ROWS + 1]
-        diag_ref[0:1, where] = side[ROWS : ROWS + 1]
-        diag_ref[1:2, where] = side[ROWS + 1 : ROWS + 2]
+    p_ref[:, : z.rim], p_ref[:, z.rim + z.nodes : z.window] = sides(position, halo_a_ref[...], halo_b_ref[...])
+    diag_ref[...] = jnp.zeros_like(diag_ref)
     diag_ref[0:1, own] = precond_ref[...]
     diag_ref[1:2, own] = potential_ref[...]
     product = rhs_ref[...] * precond_ref[...]
     p_ref[:, own] = product
     gamma_ref[...] = lanes_by_vector(z, product * rhs_ref[...])
     p_ref[:, z.window :] = jnp.zeros((ROWS, z.reach - z.window), F32)
-    gather_cells(z, index_ref, corner_ref, range_ref, p_ref, scale_ref, count_ref[position], u_ref, uw_ref)
+    gather_cells(z, index_ref, corner_ref, low_ref, high_ref, p_ref, scale_ref, count_ref[position], u_ref, uw_ref)
     parts = contributions(z, position, pj_ref, cell_ref, atom_ref, scount_ref, u_ref)
-    message = jnp.concatenate(parts + [coupling_ref[...]], axis=0)
+    small_lane, small_row = iota((ROWS, LANES), 1), iota((ROWS, LANES), 0)
+    matrices = jnp.zeros((ROWS, LANES), F32)
+    for atom in range(z.owned):
+        block = jnp.concatenate([coupling_ref[atom], jnp.zeros((ROWS, LANES - z.channels), F32)], axis=1)
+        got = lane_gather(block, small_lane % ROWS)
+        matrices = jnp.where(small_lane // ROWS == atom * ROWS + small_row, got, matrices)
+    message = jnp.concatenate(parts + [jnp.sum(matrices, axis=0, keepdims=True)], axis=0)
     for d in range(z.devices):
         out_ref[d] = message
     stiffness_product(k_high_ref, k_low_ref, uw_ref, e_ref)
 
 
 def second_kernel(
-    z, pos_ref, count_ref, scale_ref, cell_ref, atom_ref, scount_ref, range_ref, p_ref, diag_ref, shift_ref, gamma_ref,
-    image_ref, halo_a_ref, halo_b_ref, index_ref, corner_ref, k_high_ref, k_low_ref, pj_ref,
-    y_ref, q_ref, out_ref, e_ref, u_ref, uw_ref,
+    z, pos_ref, count_ref, scale_ref, cell_ref, atom_ref, scount_ref, low_ref, high_ref, p_ref, diag_in_ref, shift_ref,
+    gamma_ref, image_ref, halo_a_ref, halo_b_ref, index_ref, corner_ref, k_high_ref, k_low_ref, pj_ref,
+    y_ref, q_ref, out_ref, e_ref, diag_ref, u_ref, uw_ref,
 ):
     position = pos_ref[0]
-    even = position % 2 == 0
-    a, b = halo_a_ref[...], halo_b_ref[...]
-    left, right = jnp.where(even, b, a), jnp.where(even, a, b)
-    diagonal = diag_ref[1:2, :] + shift_ref[...]
-    y_ref[...] = image_ref[...] + diagonal * p_ref[:, : z.window]
-    y_ref[:, : 2 * z.rim] += left
-    y_ref[:, z.window - 2 * z.rim :] += right
+    left, right = sides(position, halo_a_ref[...], halo_b_ref[...])
+    own = slice(z.rim, z.rim + z.nodes)
+    diag_ref[:, own] = diag_in_ref[:, own]
+    diag_ref[:, : z.rim] = left[ROWS : ROWS + 2, : z.rim]
+    diag_ref[:, z.rim + z.nodes :] = right[ROWS : ROWS + 2, z.rim :]
+    y_ref[...] = image_ref[...] + (diag_ref[1:2, :] + shift_ref[...]) * p_ref[:, : z.window]
+    y_ref[:, : 2 * z.rim] += left[:ROWS]
+    y_ref[:, z.window - 2 * z.rim :] += right[:ROWS]
     q_ref[:, : z.window] = y_ref[...] * diag_ref[0:1, :]
     q_ref[:, z.window :] = jnp.zeros((ROWS, z.reach - z.window), F32)
-    own = slice(z.rim, z.rim + z.nodes)
     y, q = y_ref[:, own], q_ref[:, own]
     dots = [
         gamma_ref[...],
@@ -209,7 +224,7 @@
         lanes_by_vector(z, y * q),
     ]
     energy = jnp.sum(q * q * (diag_ref[1:2, own] + shift_ref[...]), axis=1, keepdims=True)
-    gather_cells(z, index_ref, corner_ref, range_ref, q_ref, scale_ref, count_ref[position], u_ref, uw_ref)
+    gather_cells(z, index_ref, corner_ref, low_ref, high_ref, q_ref, scale_ref, count_ref[position], u_ref, uw_ref)
     parts = contributions(z, position, pj_ref, cell_ref, atom_ref, scount_ref, u_ref)
     stiffness_product(k_high_ref, k_low_ref, uw_ref, e_ref)
     elements = jnp.zeros((ROWS, z.width), F32)
@@ -227,8 +242,8 @@
 
 
 def scatter_kernel(
-    z, last, pos_ref, cell_ref, atom_ref, scount_ref, range_ref, sums_ref, coupling_ref, e_in_ref, index_ref,
-    corner_ref, pj_ref, *refs,
+    z, last, pos_ref, cell_ref, atom_ref, scount_ref, low_ref, high_ref, sums_ref, coupling_ref, e_in_ref, index_ref,
+    corner_ref, pj_ref, diag_ref, *refs,
 ):
     if last:
         image_ref, send_a_ref, send_b_ref, dots_ref, e_ref, acc_ref = refs
@@ -309,8 +324,8 @@
 
     def some_cells(g, _):
         cells = [g * z.together + i for i in range(z.together)]
-        starts = [range_ref[0, c] >> 8 for c in cells]
-        ends = [range_ref[1, c] >> 8 for c in cells]
+        starts = [(low_ref[c] + z.shift) >> 8 for c in cells]
+        ends = [(high_ref[c] + z.shift) >> 8 for c in cells]
         passes = functools.reduce(jnp.maximum, [(e - s) // BAND + 1 for s, e in zip(starts, ends)])
 
         def one_pass(k, _):
@@ -339,10 +354,12 @@
     for h in range(groups):
         at = h * 2 * ROWS
         image_ref[:, h * WIDE : (h + 1) * WIDE] = acc_ref[at : at + ROWS] + acc_ref[at + ROWS : at + 2 * ROWS]
-    low_rim, high_rim = image_ref[:, : 2 * z.rim], image_ref[:, z.window - 2 * z.rim :]
     even = position % 2 == 0
-    send_a_ref[...] = jnp.where(even, high_rim, low_rim)
-    send_b_ref[...] = jnp.where(even, low_rim, high_rim)
+    ends = [slice(0, 2 * z.rim), slice(z.window - 2 * z.rim, z.window)]
+    for source_ref, rows in ((image_ref, slice(0, ROWS)),) + (() if last else ((diag_ref, slice(ROWS, ROWS + 2)),)):
+        low_rim, high_rim = (source_ref[:, end] for end in ends)
+        send_a_ref[rows, :] = jnp.where(even, high_rim, low_rim)
+        send_b_ref[rows, :] = jnp.where(even, low_rim, high_rim)
 
 
 def last_kernel(
@@ -369,14 +386,6 @@
     factor_ref[...] = jnp.broadcast_to(step * alpha, (ROWS, LANES))
 
 
-def rim_kernel(z, pos_ref, residual_in_ref, halo_a_ref, halo_b_ref, factor_ref, residual_ref):
-    even = pos_ref[0] % 2 == 0
-    a, b = halo_a_ref[...], halo_b_ref[...]
-    left, right = jnp.where(even, b, a), jnp.where(even, a, b)
-    side = jnp.where(pl.program_id(0) == 0, left[:, z.rim :], right[:, : z.rim])
-    residual_ref[...] = residual_in_ref[...] + factor_ref[:, 0:1] * side
-
-
 def on_device(
     rhs, potential, precond, shift, stiffness, cell_scale, conn, cell_count, projector, support_cell, support_atom,
     support_count, atom_matrix,
@@ -392,35 +401,38 @@
     def exchange(a, b):
         return lax.ppermute(a, "dom", near), lax.ppermute(b, "dom", far)
 
-    def call(kernel, outs, scratch, specs, *args):
+    def call(kernel, outs, scratch, specs, *args, final=False):
+        args = [
+            x if spec is SMEM else pltpu.with_memory_space_constraint(x, pltpu.VMEM) for x, spec in zip(args, specs)
+        ]
+        shapes = [jax.ShapeDtypeStruct(s, d) if final else pltpu.VMEM(s, d) for s, d in outs]
         return pl.pallas_call(
-            functools.partial(kernel),
-            out_shape=[jax.ShapeDtypeStruct(s, d) for s, d in outs],
+            kernel,
+            out_shape=shapes,
             in_specs=specs,
             out_specs=[VMEM] * len(outs),
             scratch_shapes=[pltpu.VMEM(s, d) for s, d in scratch],
+            compiler_params=pltpu.CompilerParams(vmem_limit_bytes=16 * 1024 * 1024),
         )(*args)
 
     precond_row, potential_row = precond[None, :], potential[None, :]
     shift_column = shift[:, None]
-    packed = jnp.concatenate([rhs, precond_row, potential_row], axis=0)
-    head, tail = packed[:, : z.rim], packed[:, z.nodes - z.rim :]
+    head = rhs[:, : z.rim] * precond[: z.rim]
+    tail = rhs[:, z.nodes - z.rim :] * precond[z.nodes - z.rim :]
     halo = exchange(jnp.where(even, tail, head), jnp.where(even, head, tail))
     flat_projector = projector.reshape(z.entries * z.channels, z.elem)
-    coupling = atom_matrix.reshape(1, LANES)
-    middle = conn[:, 1:-1] + z.shift
-    ranges = jnp.stack([jnp.min(middle, axis=1), jnp.max(middle, axis=1)])
-    corner = jnp.concatenate([conn[:, 0], conn[:, -1]]) + z.shift
-    corner = jnp.pad(corner, (0, LANES - 2 * z.slots))[None, :]
+    middle = conn[:, 1:-1]
+    ranges = jnp.min(middle, axis=1), jnp.max(middle, axis=1)
 
     cells = (z.slots * ROWS, z.width)
     window, reach = (z.vectors, z.window), (z.vectors, z.reach)
     message = (z.devices, 4, LANES)
     cell_scratch = [(cells, F32), (cells, F32)]
     square = (z.width, z.width)
-    index, k_high, k_low, pj = call(
+    index, corner, k_high, k_low, pj = call(
         functools.partial(prepare_kernel, z),
-        [((z.slots, 1, z.width), jnp.int32), (square, BF16), (square, BF16), ((z.entries * ROWS, z.width), F32)],
+        [((z.slots, 1, z.width), jnp.int32), ((1, LANES), jnp.int32), (square, BF16), (square, BF16),
+         ((z.entries * ROWS, z.width), F32)],
         [(square, F32)],
         [VMEM] * 3,
         conn, stiffness, flat_projector,
@@ -429,28 +441,28 @@
         functools.partial(first_kernel, z),
         [(reach, F32), ((2, z.window), F32), (message, F32), (cells, F32), ((1, LANES), F32)],
         cell_scratch,
-        [SMEM] * 7 + [VMEM] * 11,
-        pos, cell_count, cell_scale, support_cell, support_atom, support_count, ranges, rhs, precond_row,
-        potential_row, *halo, index, corner, k_high, k_low, pj, coupling,
+        [SMEM] * 8 + [VMEM] * 11,
+        pos, cell_count, cell_scale, support_cell, support_atom, support_count, *ranges, rhs, precond_row,
+        potential_row, *halo, index, corner, k_high, k_low, pj, atom_matrix,
     )
     groups = z.window // WIDE
     scatter_scratch = [(cells, F32), (((groups + BAND) * 2 * ROWS, WIDE), F32)]
-    rim = (z.vectors, 2 * z.rim)
+    rim, more_rim = (z.vectors, 2 * z.rim), (z.vectors + 2, 2 * z.rim)
     coupled = lax.all_to_all(sums, "dom", 0, 0)
     image, send_a, send_b = call(
         functools.partial(scatter_kernel, z, False),
-        [(window, F32), (rim, F32), (rim, F32)],
+        [(window, F32), (more_rim, F32), (more_rim, F32)],
         scatter_scratch,
-        [SMEM] * 5 + [VMEM] * 6,
-        pos, support_cell, support_atom, support_count, ranges, coupled, coupled, e, index, corner, pj,
+        [SMEM] * 6 + [VMEM] * 7,
+        pos, support_cell, support_atom, support_count, *ranges, coupled, coupled, e, index, corner, pj, diag,
     )
     halo = exchange(send_a, send_b)
     y, q, sums, e = call(
         functools.partial(second_kernel, z),
         [(window, F32), (reach, F32), (message, F32), (cells, F32)],
-        cell_scratch,
-        [SMEM] * 7 + [VMEM] * 12,
-        pos, cell_count, cell_scale, support_cell, support_atom, support_count, ranges, p, diag, shift_column, gamma,
+        [((2, z.window), F32)] + cell_scratch,
+        [SMEM] * 8 + [VMEM] * 12,
+        pos, cell_count, cell_scale, support_cell, support_atom, support_count, *ranges, p, diag, shift_column, gamma,
         image, *halo, index, corner, k_high, k_low, pj,
     )
     totals = lax.all_to_all(sums, "dom", 0, 0)
@@ -458,8 +470,8 @@
         functools.partial(scatter_kernel, z, True),
         [(window, F32), (rim, F32), (rim, F32), ((1, LANES), F32)],
         scatter_scratch,
-        [SMEM] * 5 + [VMEM] * 6,
-        pos, support_cell, support_atom, support_count, ranges, totals, coupled, e, index, corner, pj,
+        [SMEM] * 6 + [VMEM] * 7,
+        pos, support_cell, support_atom, support_count, *ranges, totals, coupled, e, index, corner, pj, diag,
     )
     halo = exchange(send_a, send_b)
     own = (z.vectors, z.nodes)
@@ -468,17 +480,11 @@
         [(own, F32), (own, F32), ((ROWS, LANES), F32)],
         [],
         [VMEM] * 8,
-        rhs, p, diag, shift_column, y, q, image, dots,
-    )
-    ends = pl.BlockSpec((ROWS, z.rim), lambda i: (0, i * (z.nodes // z.rim - 1)))
-    residual = pl.pallas_call(
-        functools.partial(rim_kernel, z),
-        grid=(2,),
-        out_shape=jax.ShapeDtypeStruct(own, F32),
-        in_specs=[SMEM, ends, VMEM, VMEM, VMEM],
-        out_specs=ends,
-        input_output_aliases={1: 0},
-    )(pos, residual, *halo, factor)
+        rhs, p, diag, shift_column, y, q, image, dots, final=True,
+    )
+    left, right = sides(position, *halo)
+    residual = residual.at[:, : z.rim].add(factor[:, :1] * left[:, z.rim :])
+    residual = residual.at[:, z.nodes - z.rim :].add(factor[:, :1] * right[:, : z.rim])
     return answer, residual
 
 

time: 75.5 us -> 69 us (0.914)
  Pallas kernels: 31.2 us -> 21.6 us
  blocking collectives: 22.7 us -> 14 us
  waiting for transfers between devices: 3.74 us -> 11.8 us
  other arithmetic: 1.62 us -> 5.13 us
  starting transfers between devices: 9.58 us -> 12.3 us
  local copies, waits for them, and re-layouts: 5.24 us -> 2.72 us
    all_to_all x1 -> x0, blocking collectives: 10.2 us -> none  [on_device(): totals = lax.all_to_all(sums, 'dom', 0, 0)]
    pallas_call x7 -> x6, Pallas kernels: 31.2 us -> 21.6 us  [call(): pl.pallas_call(kernel, out_shape=shapes, in_specs=specs, out_specs=[VMEM]...]
    all_to_all x0 -> x1, waiting for transfers between devices: none -> 6.56 us  [on_device(): totals = lax.all_to_all(sums, 'dom', 0, 0)]
    scatter-add x0 -> x2, other arithmetic: none -> 3.47 us  [the longest x1 2.08 us: on_device(): residual = residual.at[:, :z.rim].add(factor[:, :1] * left[:, z.rim:])]
    all_to_all x0 -> x1, starting transfers between devices: none -> 2.7 us  [on_device(): totals = lax.all_to_all(sums, 'dom', 0, 0)]
    ppermute x6, waiting for transfers between devices: 3.74 us -> 5.26 us  [exchange(): return (lax.ppermute(a, 'dom', near), lax.ppermute(b, 'dom', far))]
    all_to_all x1, blocking collectives: 12.5 us -> 14 us  [on_device(): coupled = lax.all_to_all(sums, 'dom', 0, 0)]
  transfers between devices with their start and end apart: 6 -> 7, of which waited for: 2 -> 3; matrix products, arithmetic and copies ran while one was open for 4% -> 2% of each run, Pallas kernels for 6% -> 2%
where the time goes in v4:
time: 69 us; the launch traced here: 68.5 us
  Pallas kernels  21.6 us (31%)
  blocking collectives  14 us (20%)
  starting transfers between devices  12.3 us (18%)
  waiting for transfers between devices  11.8 us (17%)
  other arithmetic  5.13 us (7%)
  local copies, waits for them, and re-layouts  2.72 us (4%)
  between operations  0.86 us (1%)
    pallas_call x6, Pallas kernels, call(): pl.pallas_call(kernel, out_shape=shapes, in_specs=specs, out_specs=[VMEM]...  21.6 us
    all_to_all x1, blocking collectives, on_device(): coupled = lax.all_to_all(sums, 'dom', 0, 0)  14 us
    ppermute x6, starting transfers between devices, exchange(): return (lax.ppermute(a, 'dom', near), lax.ppermute(b, 'dom', far))  9.63 us
    all_to_all x1, waiting for transfers between devices, on_device(): totals = lax.all_to_all(sums, 'dom', 0, 0)  6.56 us
    ppermute x6, waiting for transfers between devices, exchange(): return (lax.ppermute(a, 'dom', near), lax.ppermute(b, 'dom', far))  5.26 us
    all_to_all x1, starting transfers between devices, on_device(): totals = lax.all_to_all(sums, 'dom', 0, 0)  2.7 us
    unnamed x26, local copies, waits for them, and re-layouts  2.48 us
    scatter-add x1, other arithmetic, on_device(): residual = residual.at[:, :z.rim].add(factor[:, :1] * left[:, z.rim:])  2.08 us
  transfers between devices with their start and end apart: 7, of which 3 were waited for; matrix products, arithmetic and copies ran while one was open for 2% of the time, Pallas kernels for 2%

profile of v4, /device:TPU:1, one launch (start us, length us, event | category | flops | bytes accessed | tf_op | source)
XLA Modules:
  0.0 68.5 jit_solution(5133953963609542829)
XLA Ops:
  0.7 0.7 %copy-done.10 = f32[6656]{0:T(1024)S(1)} copy-done((f32[6656]{0:T(1024)S(1)}, f32[6656]{0:T(1024)}, u32[]{:S(2)}) %copy-start.10) | copy-done | bytes 26648
  1.4 0.8 %fusion.5 = (f32[8,512]{1,0:T(8,128)S(1)}, f32[8,512]{1,0:T(8,128)S(1)}) fusion(f32[8,6656]{1,0:T(8,128)} %rhs_ref.3, f32[512]{0:T(512)S(1)} %get-tuple-element.79, f32[512]{0:T(512)S(1)} %get-tuple-element.78, pred[]{:T(512)S(6)} %eq.7), kind=kLoop, calls=%fused_computation.12 | loop fusion | flops 16384 | bytes 69633 | tf_op jit(solution)/shard_map/jit(_where)/select_n | solution.py:422
  2.2 4.5 %collective-permute-start.1 = (f32[8,512]{1,0:T(8,128)S(1)}, f32[8,512]{1,0:T(8,128)S(1)}, u32[]{:S(2)}, u32[]{:S(2)}) collective-permute-start(f32[8,512]{1,0:T(8,128)S(1)} %get-tuple-element.76), channel_id=1, source_target_pairs={{1,2},{2,1},{3,4},{4,3},{5,6},{6,5},{7,8},{8,7},{9,10},{10,9},{11,... | collective-permute-start | bytes 49160 | tf_op jit(solution)/shard_map/ppermute | solution.py:402
  6.7 0.2 slice_reduce_fusion
  7.0 1.0 %copy-done.1 = f32[343,343]{1,0:T(8,128)S(1)} copy-done((f32[343,343]{1,0:T(8,128)S(1)}, f32[343,343]{1,0:T(8,128)}, u32[]{:S(2)}) %copy-start.1) | copy-done | bytes 470620
  8.0 0.2 shard_map.140
  8.4 0.6 copy-done
  9.1 4.7 %shard_map.141 = (f32[8,9472]{1,0:T(8,128)S(1)}, f32[2,7680]{1,0:T(2,128)S(1)}, f32[32,4,128]{2,1,0:T(4,128)S(1)}, f32[256,384]{1,0:T(8,128)S(1)}, f32[1,128]{1,0:T(1,128)S(1)}) custom-call(s32[1]{0:T(128)} %bitcast.pos_ref, s32[32]{0:T(128)S(1)} %copy-done.8, f32[32]{0:T(128)S(1)} %copy-done.9, s32[8]{0:T(128)S(1)} %copy-done.4, s32[8]{0:T(128)S(1)} %copy-done.5, ...), custom_call_target="tpu_custom_call" | custom-call | tf_op jit(solution)/shard_map/pallas_call | solution.py:409
  13.7 14.0 %all_to_all.10.sums_ref.coupling_ref = f32[32,4,128]{2,1,0:T(4,128)S(1)} all-to-all(f32[32,4,128]{2,1,0:T(4,128)S(1)} %get-tuple-element.58), channel_id=1, replica_groups=mesh['dom'=32] {'dom'}, dimensions={0} | all-to-all | bytes 131072 | tf_op jit(solution)/shard_map/all_to_all | solution.py:451
  27.7 5.1 %shard_map.142 = (f32[8,7680]{1,0:T(8,128)S(1)}, f32[10,1024]{1,0:T(8,128)S(1)}, f32[10,1024]{1,0:T(8,128)S(1)}) custom-call(s32[1]{0:T(128)} %bitcast.pos_ref, s32[8]{0:T(128)S(1)} %copy-done.4, s32[8]{0:T(128)S(1)} %copy-done.5, s32[32]{0:T(128)S(1)} %copy-done.6, s32[32]{0:T(128)S(1)} %get-tuple-element.75.low_ref, s32[32]{0:T(128)S(1)} %get-tuple-element.74.high_ref, ...), custom_call_target="tpu_custom_call" | custom-call | tf_op jit(solution)/shard_map/pallas_call | solution.py:409
  32.8 0.5 collective-permute-start.2
  33.2 2.2 %collective-permute-start.3 = (f32[10,1024]{1,0:T(8,128)S(1)}, f32[10,1024]{1,0:T(8,128)S(1)}, u32[]{:S(2)}, u32[]{:S(2)}) collective-permute-start(f32[10,1024]{1,0:T(8,128)S(1)} %get-tuple-element.62), channel_id=1, source_target_pairs={{1,2},{2,1},{3,4},{4,3},{5,6},{6,5},{7,8},{8,7},{9,10},{10,9},{11,... | collective-permute-start | bytes 122888 | tf_op jit(solution)/shard_map/ppermute | solution.py:402
  35.5 3.5 %collective-permute-done.3.halo_b_ref = f32[10,1024]{1,0:T(8,128)S(1)} collective-permute-done((f32[10,1024]{1,0:T(8,128)S(1)}, f32[10,1024]{1,0:T(8,128)S(1)}, u32[]{:S(2)}, u32[]{:S(2)}) %collective-permute-start.3) | collective-permute-done | bytes 40992 | tf_op jit(solution)/shard_map/ppermute | solution.py:402
  39.0 5.6 %shard_map.143 = (f32[8,7680]{1,0:T(8,128)S(1)}, f32[8,9472]{1,0:T(8,128)S(1)}, f32[32,4,128]{2,1,0:T(4,128)}, f32[256,384]{1,0:T(8,128)S(1)}) custom-call(s32[1]{0:T(128)} %bitcast.pos_ref, s32[32]{0:T(128)S(1)} %copy-done.8, f32[32]{0:T(128)S(1)} %copy-done.9, s32[8]{0:T(128)S(1)} %copy-done.4, s32[8]{0:T(128)S(1)} %copy-done.5, s32[32]{0:T(128)S(1)} %copy-done.6, ...), custom_call_target="tpu_custom_call" | custom-call | tf_op jit(solution)/shard_map/pallas_call | solution.py:409
  44.6 2.7 %all-to-all-start.1 = ((f32[32,4,128]{2,1,0:T(4,128)}), f32[32,4,128]{2,1,0:T(4,128)S(1)}, u32[]{:S(2)}, u32[]{:S(2)}) async-start(f32[32,4,128]{2,1,0:T(4,128)} %get-tuple-element.65), calls=%async_computation.1 | async-start | bytes 131072 | tf_op jit(solution)/shard_map/all_to_all | solution.py:468
  47.3 0.7 %compare_reduce_fusion = pred[]{:T(512)} fusion(), kind=kLoop, calls=%fused_computation.15 | loop fusion | flops 5 | bytes 1 | tf_op jit(solution)/shard_map/reduce.2
  48.1 6.6 %all-to-all-done.1.sums_ref = f32[32,4,128]{2,1,0:T(4,128)S(1)} async-done(((f32[32,4,128]{2,1,0:T(4,128)}), f32[32,4,128]{2,1,0:T(4,128)S(1)}, u32[]{:S(2)}, u32[]{:S(2)}) %all-to-all-start.1) | async-done | bytes 65568 | tf_op jit(solution)/shard_map/all_to_all | solution.py:468
  54.6 5.0 %shard_map.144 = (f32[8,7680]{1,0:T(8,128)S(1)}, f32[8,1024]{1,0:T(8,128)S(1)}, f32[8,1024]{1,0:T(8,128)S(1)}, f32[1,128]{1,0:T(1,128)S(1)}) custom-call(s32[1]{0:T(128)} %bitcast.pos_ref, s32[8]{0:T(128)S(1)} %copy-done.4, s32[8]{0:T(128)S(1)} %copy-done.5, s32[32]{0:T(128)S(1)} %copy-done.6, s32[32]{0:T(128)S(1)} %get-tuple-element.75.low_ref, ...), custom_call_target="tpu_custom_call" | custom-call | tf_op jit(solution)/shard_map/pallas_call | solution.py:409
  59.7 2.3 %collective-permute-start.4 = (f32[8,1024]{1,0:T(8,128)S(1)}, f32[8,1024]{1,0:T(8,128)S(1)}, u32[]{:S(2)}, u32[]{:S(2)}) collective-permute-start(f32[8,1024]{1,0:T(8,128)S(1)} %get-tuple-element.72), channel_id=1, source_target_pairs={{1,2},{2,1},{3,4},{4,3},{5,6},{6,5},{7,8},{8,7},{9,10},{10,9},{11,... | collective-permute-start | bytes 98312 | tf_op jit(solution)/shard_map/ppermute | solution.py:402
  62.1 1.0 %shard_map.145 = (f32[8,6656]{1,0:T(8,128)}, f32[8,6656]{1,0:T(8,128)}, f32[8,128]{1,0:T(8,128)S(1)}) custom-call(f32[8,6656]{1,0:T(8,128)S(1)} %copy-done, f32[8,9472]{1,0:T(8,128)S(1)} %get-tuple-element.55.p_ref, f32[2,7680]{1,0:T(2,128)S(1)} %get-tuple-element.56.diag_ref.diag_in_ref, f32[8,1]{1,0:T(8,128)S(1)} %copy.18.shift_ref, ...), custom_call_target="tpu_custom_call" | custom-call | tf_op jit(solution)/shard_map/pallas_call | solution.py:409
  63.1 0.1 slice_reduce_fusion.2
  63.3 1.7 %collective-permute-done.4 = f32[8,1024]{1,0:T(8,128)S(1)} collective-permute-done((f32[8,1024]{1,0:T(8,128)S(1)}, f32[8,1024]{1,0:T(8,128)S(1)}, u32[]{:S(2)}, u32[]{:S(2)}) %collective-permute-start.4) | collective-permute-done | bytes 32800 | tf_op jit(solution)/shard_map/ppermute | solution.py:402
  65.0 2.1 %fusion = f32[8,6656]{1,0:T(8,128)} fusion(f32[8,6656]{1,0:T(8,128)} %get-tuple-element.70, f32[8,1024]{1,0:T(8,128)S(1)} %collective-permute-done.5, f32[8,1024]{1,0:T(8,128)S(1)} %collective-permute-done.4, f32[8]{0:T(128)S(1)} %slice_reduce_fusion.2, pred[]{:T(512)} %compare_reduce_fusion, pred[]{:T(512)S(6)} %eq.7), kind=kLoop, calls=%fused_computation.3 | loop fusion | flops 16384 | bytes 66081 | tf_op jit(solution)/shard_map/scatter-add | solution.py:486
  67.1 1.4 %fusion.3 = f32[8,6656]{1,0:T(8,128)} fusion(f32[8,6656]{1,0:T(8,128)} %fusion, f32[8,1024]{1,0:T(8,128)S(1)} %collective-permute-done.4, f32[8,1024]{1,0:T(8,128)S(1)} %collective-permute-done.5, f32[8]{0:T(128)S(1)} %slice_reduce_fusion.2, pred[]{:T(512)S(6)} %eq.7), kind=kLoop, calls=%fused_computation.7 | loop fusion | flops 12288 | bytes 65569 | tf_op jit(solution)/shard_map/scatter-add | solution.py:487
  (33 shorter events, 0.4 us)
Async XLA Ops:
  0.6 0.7 %copy-start.10 = (f32[6656]{0:T(1024)S(1)}, f32[6656]{0:T(1024)}, u32[]{:S(2)}) copy-start(f32[6656]{0:T(1024)} %param.19) | copy-start | bytes 79876
  0.6 6.1 %copy-start.2 = (s32[32,343]{1,0:T(8,128)S(1)}, s32[32,343]{1,0:T(8,128)}, u32[]{:S(2)}) copy-start(s32[32,343]{1,0:T(8,128)} %conn_ref.1) | copy-start | bytes 131716
  1.4 5.6 %copy-start.11 = (f32[6656]{0:T(1024)S(1)}, f32[6656]{0:T(1024)}, u32[]{:S(2)}) copy-start(f32[6656]{0:T(1024)} %param.18) | copy-start | bytes 79876
  2.1 4.8 %copy-start.3 = (f32[8,8,343]{2,1,0:T(8,128)S(1)}, f32[8,8,343]{2,1,0:T(8,128)}, u32[]{:S(2)}) copy-start(f32[8,8,343]{2,1,0:T(8,128)} %param.25) | copy-start | bytes 263428
  2.1 6.2 %collective-permute-start = (f32[8,512]{1,0:T(8,128)S(1)}, f32[8,512]{1,0:T(8,128)S(1)}, u32[]{:S(2)}, u32[]{:S(2)}) collective-permute-start(f32[8,512]{1,0:T(8,128)S(1)} %get-tuple-element.77), channel_id=1, source_target_pairs={{0,1},{1,0},{2,3},{3,2},{4,5},{5,4},{6,7},{7,6},{8,9},{9,8},{10,11... | collective-permute-start | bytes 49160 | tf_op jit(solution)/shard_map/ppermute | solution.py:402
  2.2 6.1 %collective-permute-start.1 = (f32[8,512]{1,0:T(8,128)S(1)}, f32[8,512]{1,0:T(8,128)S(1)}, u32[]{:S(2)}, u32[]{:S(2)}) collective-permute-start(f32[8,512]{1,0:T(8,128)S(1)} %get-tuple-element.76), channel_id=1, source_target_pairs={{1,2},{2,1},{3,4},{4,3},{5,6},{6,5},{7,8},{8,7},{9,10},{10,9},{11,... | collective-permute-start | bytes 49160 | tf_op jit(solution)/shard_map/ppermute | solution.py:402
  7.0 1.0 %copy-start.1 = (f32[343,343]{1,0:T(8,128)S(1)}, f32[343,343]{1,0:T(8,128)}, u32[]{:S(2)}) copy-start(f32[343,343]{1,0:T(8,128)} %stiffness_ref.1) | copy-start | bytes 1411792
  8.0 0.9 %copy-start = (f32[8,6656]{1,0:T(8,128)S(1)}, f32[8,6656]{1,0:T(8,128)}, u32[]{:S(2)}) copy-start(f32[8,6656]{1,0:T(8,128)} %rhs_ref.3) | copy-start | bytes 638980
  8.3 0.7 %copy-start.7 = (f32[2,8,8]{2,1,0:T(8,128)S(1)}, f32[2,8,8]{2,1,0:T(8,128)}, u32[]{:S(2)}) copy-start(f32[2,8,8]{2,1,0:T(8,128)} %coupling_ref.1) | copy-start | bytes 1540
  8.3 0.7 %copy-start.8 = (s32[32]{0:T(128)S(1)}, s32[32]{0:T(128)}, u32[]{:S(2)}) copy-start(s32[32]{0:T(128)} %count_ref.3) | copy-start | bytes 388
  8.3 0.7 %copy-start.9 = (f32[32]{0:T(128)S(1)}, f32[32]{0:T(128)}, u32[]{:S(2)}) copy-start(f32[32]{0:T(128)} %scale_ref.3) | copy-start | bytes 388
  8.3 0.7 %copy-start.4 = (s32[8]{0:T(128)S(1)}, s32[8]{0:T(128)}, u32[]{:S(2)}) copy-start(s32[8]{0:T(128)} %cell_ref.7) | copy-start | bytes 100
  8.3 0.7 %copy-start.5 = (s32[8]{0:T(128)S(1)}, s32[8]{0:T(128)}, u32[]{:S(2)}) copy-start(s32[8]{0:T(128)} %atom_ref.7) | copy-start | bytes 100
  8.4 0.7 %copy-start.6 = (s32[32]{0:T(128)S(1)}, s32[32]{0:T(128)}, u32[]{:S(2)}) copy-start(s32[32]{0:T(128)} %scount_ref.7) | copy-start | bytes 388
  32.8 2.8 %collective-permute-start.2 = (f32[10,1024]{1,0:T(8,128)S(1)}, f32[10,1024]{1,0:T(8,128)S(1)}, u32[]{:S(2)}, u32[]{:S(2)}) collective-permute-start(f32[10,1024]{1,0:T(8,128)S(1)} %get-tuple-element.61), channel_id=1, source_target_pairs={{0,1},{1,0},{2,3},{3,2},{4,5},{5,4},{6,7},{7,6},{8,9},{9,8},{10,11... | collective-permute-start | bytes 122888 | tf_op jit(solution)/shard_map/ppermute | solution.py:402
  33.2 2.2 %copy-start.12 = (f32[8]{0:T(128)S(1)}, f32[8]{0:T(128)}, u32[]{:S(2)}) copy-start(f32[8]{0:T(128)} %param.20) | copy-start | bytes 100
  33.2 5.8 %collective-permute-start.3 = (f32[10,1024]{1,0:T(8,128)S(1)}, f32[10,1024]{1,0:T(8,128)S(1)}, u32[]{:S(2)}, u32[]{:S(2)}) collective-permute-start(f32[10,1024]{1,0:T(8,128)S(1)} %get-tuple-element.62), channel_id=1, source_target_pairs={{1,2},{2,1},{3,4},{4,3},{5,6},{6,5},{7,8},{8,7},{9,10},{10,9},{11,... | collective-permute-start | bytes 122888 | tf_op jit(solution)/shard_map/ppermute | solution.py:402
  44.6 10.0 %all-to-all-start.1 = ((f32[32,4,128]{2,1,0:T(4,128)}), f32[32,4,128]{2,1,0:T(4,128)S(1)}, u32[]{:S(2)}, u32[]{:S(2)}) async-start(f32[32,4,128]{2,1,0:T(4,128)} %get-tuple-element.65), calls=%async_computation.1 | async-start | bytes 131072 | tf_op jit(solution)/shard_map/all_to_all | solution.py:468
  59.7 5.3 %collective-permute-start.4 = (f32[8,1024]{1,0:T(8,128)S(1)}, f32[8,1024]{1,0:T(8,128)S(1)}, u32[]{:S(2)}, u32[]{:S(2)}) collective-permute-start(f32[8,1024]{1,0:T(8,128)S(1)} %get-tuple-element.72), channel_id=1, source_target_pairs={{1,2},{2,1},{3,4},{4,3},{5,6},{6,5},{7,8},{8,7},{9,10},{10,9},{11,... | collective-permute-start | bytes 98312 | tf_op jit(solution)/shard_map/ppermute | solution.py:402
  62.0 3.0 %collective-permute-start.5 = (f32[8,1024]{1,0:T(8,128)S(1)}, f32[8,1024]{1,0:T(8,128)S(1)}, u32[]{:S(2)}, u32[]{:S(2)}) collective-permute-start(f32[8,1024]{1,0:T(8,128)S(1)} %get-tuple-element.73), channel_id=1, source_target_pairs={{0,1},{1,0},{2,3},{3,2},{4,5},{5,4},{6,7},{7,6},{8,9},{9,8},{10,11... | collective-permute-start | bytes 98312 | tf_op jit(solution)/shard_map/ppermute | solution.py:402

commit v5 on v4

--- a/solution.py
+++ b/solution.py
@@ -174,8 +174,8 @@
 
 def first_kernel(
     z, pos_ref, count_ref, scale_ref, cell_ref, atom_ref, scount_ref, low_ref, high_ref, rhs_ref, precond_ref,
-    potential_ref, halo_a_ref, halo_b_ref, index_ref, corner_ref, k_high_ref, k_low_ref, pj_ref, coupling_ref,
-    p_ref, diag_ref, out_ref, e_ref, gamma_ref, u_ref, uw_ref,
+    potential_ref, halo_a_ref, halo_b_ref, index_ref, corner_ref, pj_ref, coupling_ref,
+    p_ref, diag_ref, out_ref, uw_ref, gamma_ref, u_ref,
 ):
     position = pos_ref[0]
     own = slice(z.rim, z.rim + z.nodes)
@@ -198,7 +198,6 @@
     message = jnp.concatenate(parts + [jnp.sum(matrices, axis=0, keepdims=True)], axis=0)
     for d in range(z.devices):
         out_ref[d] = message
-    stiffness_product(k_high_ref, k_low_ref, uw_ref, e_ref)
 
 
 def second_kernel(
@@ -241,14 +240,109 @@
         out_ref[d] = message
 
 
-def scatter_kernel(
-    z, last, pos_ref, cell_ref, atom_ref, scount_ref, low_ref, high_ref, sums_ref, coupling_ref, e_in_ref, index_ref,
-    corner_ref, pj_ref, diag_ref, *refs,
+class Scatter:
+    def __init__(self, z, index_ref, corner_ref, low_ref, high_ref, acc_ref):
+        self.z, self.index_ref, self.corner_ref, self.acc_ref = z, index_ref, corner_ref, acc_ref
+        self.low_ref, self.high_ref = low_ref, high_ref
+        self.groups = z.window // WIDE
+        self.pair = (2 * ROWS, LANES)
+        sub = iota(self.pair, 0)
+        self.lows = [(sub + k * 2 * ROWS).astype(jnp.int16) for k in range(WIDE // (2 * ROWS))]
+        self.one, self.none = jnp.ones(self.pair, BF16), jnp.zeros(self.pair, BF16)
+        self.lane = iota((ROWS, LANES), 1)
+        self.end = (z.elem - 1) % LANES
+
+    def two_parts(self, value):
+        rounded = value.astype(BF16).astype(F32)
+        return jnp.concatenate([rounded, value - rounded], axis=0).astype(BF16)
+
+    def hot_rows(self, index):
+        low = (index & (WIDE - 1)).astype(jnp.int16)
+        return jnp.concatenate([jnp.where(low == k, self.one, self.none) for k in self.lows], axis=0)
+
+    def masked(self, high, both, rows):
+        high = high.astype(jnp.int16)
+        return jnp.concatenate([jnp.where(high == jnp.int16(h), both, self.none) for h in range(rows)], axis=0)
+
+    def product(self, lhs, hot):
+        return lax.dot_general(lhs, hot, NT, preferred_element_type=F32)
+
+    def start(self, sources):
+        z = self.z
+        corners = jnp.zeros((ROWS, LANES), F32)
+        at = (z.tiles - 1) * LANES + self.end
+        for cell, values in sources:
+            corners = corners + jnp.where(self.lane == cell, values[:, 0:1], 0.0)
+            corners = corners + jnp.where(self.lane == z.slots + cell, values[:, at : at + 1], 0.0)
+        index = jnp.broadcast_to(self.corner_ref[...], self.pair)
+        rows = self.groups * 2 * ROWS
+        self.acc_ref[:rows, :] = self.product(
+            self.masked(index >> 8, self.two_parts(corners), self.groups), self.hot_rows(index)
+        )
+        self.acc_ref[rows:, :] = jnp.zeros((BAND * 2 * ROWS, WIDE), F32)
+
+    def add(self, cells, value_of):
+        z = self.z
+        starts = [(self.low_ref[c] + z.shift) >> 8 for c in cells]
+        ends = [(self.high_ref[c] + z.shift) >> 8 for c in cells]
+        passes = functools.reduce(jnp.maximum, [(e - s) // BAND + 1 for s, e in zip(starts, ends)])
+
+        def one_pass(k, _):
+            for i, c in enumerate(cells):
+                start = jnp.minimum(starts[i] + k * BAND, self.groups)
+                lhs, hot = [], []
+                for t in range(z.tiles):
+                    index = jnp.broadcast_to(self.index_ref[c, :, t * LANES : (t + 1) * LANES], self.pair)
+                    value = value_of(i, t)
+                    if t == 0:
+                        value = jnp.where(self.lane == 0, 0.0, value)
+                    if t == z.tiles - 1:
+                        value = jnp.where(self.lane == self.end, 0.0, value)
+                    lhs.append(self.masked((index >> 8) - start, self.two_parts(value), BAND))
+                    hot.append(self.hot_rows(index))
+                to = pl.ds(pl.multiple_of(start * 2 * ROWS, 2 * ROWS), BAND * 2 * ROWS)
+                self.acc_ref[to, :] += self.product(jnp.concatenate(lhs, axis=1), jnp.concatenate(hot, axis=1))
+            return 0
+
+        lax.fori_loop(0, passes, one_pass, 0)
+
+    def result(self, h):
+        at = h * 2 * ROWS
+        return self.acc_ref[at : at + ROWS] + self.acc_ref[at + ROWS : at + 2 * ROWS]
+
+
+def cells_kernel(z, multiply, low_ref, high_ref, index_ref, corner_ref, *refs):
+    if multiply:
+        uw_ref, k_high_ref, k_low_ref, image_ref, e_ref, acc_ref = refs
+        stiffness_product(k_high_ref, k_low_ref, uw_ref, e_ref)
+    else:
+        e_ref, image_ref, acc_ref = refs
+    scatter = Scatter(z, index_ref, corner_ref, low_ref, high_ref, acc_ref)
+    scatter.start([(c, e_ref[c * ROWS : (c + 1) * ROWS, :]) for c in range(z.slots)])
+
+    def some_cells(g, _):
+        cells = [g * z.together + i for i in range(z.together)]
+
+        def value_of(i, t):
+            rows = pl.ds(pl.multiple_of(cells[i] * ROWS, ROWS), ROWS)
+            return e_ref[rows, t * LANES : (t + 1) * LANES]
+
+        scatter.add(cells, value_of)
+        return 0
+
+    lax.fori_loop(0, z.slots // z.together, some_cells, 0)
+    for h in range(scatter.groups):
+        image_ref[:, h * WIDE : (h + 1) * WIDE] = scatter.result(h)
+
+
+def support_kernel(
+    z, last, pos_ref, cell_ref, atom_ref, scount_ref, low_ref, high_ref, sums_ref, coupling_ref, index_ref, corner_ref,
+    pj_ref, diag_ref, cells_ref, *refs,
 ):
     if last:
-        image_ref, send_a_ref, send_b_ref, dots_ref, e_ref, acc_ref = refs
+        image_ref, send_a_ref, send_b_ref, dots_ref, support_ref, acc_ref = refs
     else:
-        image_ref, send_a_ref, send_b_ref, e_ref, acc_ref = refs
+        image_ref, send_a_ref, send_b_ref, support_ref, acc_ref = refs
     position = pos_ref[0]
     wanted = (
         pltpu.roll(sums_ref[:, 0, :], z.devices - 1, 0) + sums_ref[:, 1, :] + pltpu.roll(sums_ref[:, 2, :], 1, 0)
@@ -282,78 +376,23 @@
             jnp.broadcast_to(mine, (ROWS, LANES)), local * z.pairs + small_lane % ROWS * ROWS + small_row
         )
         spread.append(jnp.where((small_lane // ROWS == s) & alive, got, 0.0)[:, : z.entries * ROWS])
-    support = jnp.dot(
+    support_ref[...] = jnp.dot(
         jnp.concatenate(spread, axis=0), pj_ref[...], precision=HIGHEST, preferred_element_type=F32
     )
-    e_ref[...] = e_in_ref[...]
-    for s in range(z.entries):
-        rows = pl.ds(pl.multiple_of(cell_ref[s] * ROWS, ROWS), ROWS)
-        e_ref[rows, :] += support[s * ROWS : (s + 1) * ROWS]
-
-    groups = z.window // WIDE
-    pair = (2 * ROWS, LANES)
-    sub, lane = iota(pair, 0), iota(pair, 1)
-    lows = [(sub + k * 2 * ROWS).astype(jnp.int16) for k in range(WIDE // (2 * ROWS))]
-    one, none = jnp.ones(pair, BF16), jnp.zeros(pair, BF16)
-
-    def two_parts(value):
-        rounded = value.astype(BF16).astype(F32)
-        return jnp.concatenate([rounded, value - rounded], axis=0).astype(BF16)
-
-    def hot_rows(index):
-        low = (index & (WIDE - 1)).astype(jnp.int16)
-        return jnp.concatenate([jnp.where(low == k, one, none) for k in lows], axis=0)
-
-    def masked(high, both, rows):
-        high = high.astype(jnp.int16)
-        return jnp.concatenate([jnp.where(high == jnp.int16(h), both, none) for h in range(rows)], axis=0)
-
-    def product(lhs, hot):
-        return lax.dot_general(lhs, hot, NT, preferred_element_type=F32)
-
-    corners = jnp.zeros((ROWS, LANES), F32)
-    end = (z.elem - 1) % LANES
-    for c in range(z.slots):
-        tiles = e_ref[c * ROWS : (c + 1) * ROWS, :]
-        at = (z.tiles - 1) * LANES + end
-        corners = jnp.where(small_lane == c, tiles[:, 0:1], corners)
-        corners = jnp.where(small_lane == z.slots + c, tiles[:, at : at + 1], corners)
-    index = jnp.broadcast_to(corner_ref[...], pair)
-    acc_ref[: groups * 2 * ROWS, :] = product(masked(index >> 8, two_parts(corners), groups), hot_rows(index))
-    acc_ref[groups * 2 * ROWS :, :] = jnp.zeros((BAND * 2 * ROWS, WIDE), F32)
-
-    def some_cells(g, _):
-        cells = [g * z.together + i for i in range(z.together)]
-        starts = [(low_ref[c] + z.shift) >> 8 for c in cells]
-        ends = [(high_ref[c] + z.shift) >> 8 for c in cells]
-        passes = functools.reduce(jnp.maximum, [(e - s) // BAND + 1 for s, e in zip(starts, ends)])
-
-        def one_pass(k, _):
-            for i, c in enumerate(cells):
-                start = jnp.minimum(starts[i] + k * BAND, groups)
-                rows = pl.ds(pl.multiple_of(c * ROWS, ROWS), ROWS)
-                lhs, hot = [], []
-                for t in range(z.tiles):
-                    lanes = slice(t * LANES, (t + 1) * LANES)
-                    index = jnp.broadcast_to(index_ref[c, :, lanes], pair)
-                    value = e_ref[rows, lanes]
-                    if t == 0:
-                        value = jnp.where(small_lane == 0, 0.0, value)
-                    if t == z.tiles - 1:
-                        value = jnp.where(small_lane == end, 0.0, value)
-                    lhs.append(masked((index >> 8) - start, two_parts(value), BAND))
-                    hot.append(hot_rows(index))
-                to = pl.ds(pl.multiple_of(start * 2 * ROWS, 2 * ROWS), BAND * 2 * ROWS)
-                acc_ref[to, :] += product(jnp.concatenate(lhs, axis=1), jnp.concatenate(hot, axis=1))
-            return 0
-
-        lax.fori_loop(0, passes, one_pass, 0)
-        return 0
-
-    lax.fori_loop(0, z.slots // z.together, some_cells, 0)
-    for h in range(groups):
-        at = h * 2 * ROWS
-        image_ref[:, h * WIDE : (h + 1) * WIDE] = acc_ref[at : at + ROWS] + acc_ref[at + ROWS : at + 2 * ROWS]
+    scatter = Scatter(z, index_ref, corner_ref, low_ref, high_ref, acc_ref)
+    cells = [cell_ref[s] for s in range(z.entries)]
+    scatter.start([(cell, support_ref[s * ROWS : (s + 1) * ROWS, :]) for s, cell in enumerate(cells)])
+    for first in range(0, z.entries, z.together):
+        some = cells[first : first + z.together]
+
+        def value_of(i, t):
+            s = first + i
+            return support_ref[s * ROWS : (s + 1) * ROWS, t * LANES : (t + 1) * LANES]
+
+        scatter.add(some, value_of)
+    for h in range(scatter.groups):
+        at = slice(h * WIDE, (h + 1) * WIDE)
+        image_ref[:, at] = cells_ref[:, at] + scatter.result(h)
     even = position % 2 == 0
     ends = [slice(0, 2 * z.rim), slice(z.window - 2 * z.rim, z.window)]
     for source_ref, rows in ((image_ref, slice(0, ROWS)),) + (() if last else ((diag_ref, slice(ROWS, ROWS + 2)),)):
@@ -386,6 +425,15 @@
     factor_ref[...] = jnp.broadcast_to(step * alpha, (ROWS, LANES))
 
 
+def rim_kernel(z, pos_ref, residual_in_ref, halo_a_ref, halo_b_ref, factor_ref, residual_ref):
+    left, right = sides(pos_ref[0], halo_a_ref[...], halo_b_ref[...])
+    factor = factor_ref[:, :1]
+    first, last = slice(0, z.rim), slice(z.nodes - z.rim, z.nodes)
+    residual_ref[:, z.rim : z.nodes - z.rim] = residual_in_ref[:, z.rim : z.nodes - z.rim]
+    residual_ref[:, first] = residual_in_ref[:, first] + factor * left[:, z.rim :]
+    residual_ref[:, last] = residual_in_ref[:, last] + factor * right[:, : z.rim]
+
+
 def on_device(
     rhs, potential, precond, shift, stiffness, cell_scale, conn, cell_count, projector, support_cell, support_atom,
     support_count, atom_matrix,
@@ -401,19 +449,18 @@
     def exchange(a, b):
         return lax.ppermute(a, "dom", near), lax.ppermute(b, "dom", far)
 
-    def call(kernel, outs, scratch, specs, *args, final=False):
-        args = [
-            x if spec is SMEM else pltpu.with_memory_space_constraint(x, pltpu.VMEM) for x, spec in zip(args, specs)
-        ]
-        shapes = [jax.ShapeDtypeStruct(s, d) if final else pltpu.VMEM(s, d) for s, d in outs]
+    def call(kernel, outs, scratch, scalars, *args, in_hbm=()):
+        args = [pltpu.with_memory_space_constraint(x, pltpu.VMEM) for x in args]
         return pl.pallas_call(
             kernel,
-            out_shape=shapes,
-            in_specs=specs,
+            out_shape=[
+                jax.ShapeDtypeStruct(s, d) if i in in_hbm else pltpu.VMEM(s, d) for i, (s, d) in enumerate(outs)
+            ],
+            in_specs=[SMEM] * len(scalars) + [VMEM] * len(args),
             out_specs=[VMEM] * len(outs),
             scratch_shapes=[pltpu.VMEM(s, d) for s, d in scratch],
             compiler_params=pltpu.CompilerParams(vmem_limit_bytes=16 * 1024 * 1024),
-        )(*args)
+        )(*scalars, *args)
 
     precond_row, potential_row = precond[None, :], potential[None, :]
     shift_column = shift[:, None]
@@ -425,66 +472,68 @@
     ranges = jnp.min(middle, axis=1), jnp.max(middle, axis=1)
 
     cells = (z.slots * ROWS, z.width)
-    window, reach = (z.vectors, z.window), (z.vectors, z.reach)
+    window, reach, own = (z.vectors, z.window), (z.vectors, z.reach), (z.vectors, z.nodes)
     message = (z.devices, 4, LANES)
-    cell_scratch = [(cells, F32), (cells, F32)]
-    square = (z.width, z.width)
+    square, entries = (z.width, z.width), (z.entries * ROWS, z.width)
+    rim, more_rim = (z.vectors, 2 * z.rim), (z.vectors + 2, 2 * z.rim)
+    acc = ((z.window // WIDE + BAND) * 2 * ROWS, WIDE)
+    supports = support_cell, support_atom, support_count
+
     index, corner, k_high, k_low, pj = call(
         functools.partial(prepare_kernel, z),
-        [((z.slots, 1, z.width), jnp.int32), ((1, LANES), jnp.int32), (square, BF16), (square, BF16),
-         ((z.entries * ROWS, z.width), F32)],
+        [((z.slots, 1, z.width), jnp.int32), ((1, LANES), jnp.int32), (square, BF16), (square, BF16), (entries, F32)],
         [(square, F32)],
-        [VMEM] * 3,
+        (),
         conn, stiffness, flat_projector,
     )
-    p, diag, sums, e, gamma = call(
+    p, diag, sums, uw, gamma = call(
         functools.partial(first_kernel, z),
         [(reach, F32), ((2, z.window), F32), (message, F32), (cells, F32), ((1, LANES), F32)],
-        cell_scratch,
-        [SMEM] * 8 + [VMEM] * 11,
-        pos, cell_count, cell_scale, support_cell, support_atom, support_count, *ranges, rhs, precond_row,
-        potential_row, *halo, index, corner, k_high, k_low, pj, atom_matrix,
-    )
-    groups = z.window // WIDE
-    scatter_scratch = [(cells, F32), (((groups + BAND) * 2 * ROWS, WIDE), F32)]
-    rim, more_rim = (z.vectors, 2 * z.rim), (z.vectors + 2, 2 * z.rim)
+        [(cells, F32)],
+        (pos, cell_count, cell_scale, *supports, *ranges),
+        rhs, precond_row, potential_row, *halo, index, corner, pj, atom_matrix,
+    )
     coupled = lax.all_to_all(sums, "dom", 0, 0)
+    (image,) = call(
+        functools.partial(cells_kernel, z, True),
+        [(window, F32)],
+        [(cells, F32), (acc, F32)],
+        ranges,
+        index, corner, uw, k_high, k_low,
+    )
     image, send_a, send_b = call(
-        functools.partial(scatter_kernel, z, False),
+        functools.partial(support_kernel, z, False),
         [(window, F32), (more_rim, F32), (more_rim, F32)],
-        scatter_scratch,
-        [SMEM] * 6 + [VMEM] * 7,
-        pos, support_cell, support_atom, support_count, *ranges, coupled, coupled, e, index, corner, pj, diag,
+        [(entries, F32), (acc, F32)],
+        (pos, *supports, *ranges),
+        coupled, coupled, index, corner, pj, diag, image,
     )
     halo = exchange(send_a, send_b)
     y, q, sums, e = call(
         functools.partial(second_kernel, z),
         [(window, F32), (reach, F32), (message, F32), (cells, F32)],
-        [((2, z.window), F32)] + cell_scratch,
-        [SMEM] * 8 + [VMEM] * 12,
-        pos, cell_count, cell_scale, support_cell, support_atom, support_count, *ranges, p, diag, shift_column, gamma,
-        image, *halo, index, corner, k_high, k_low, pj,
+        [((2, z.window), F32), (cells, F32), (cells, F32)],
+        (pos, cell_count, cell_scale, *supports, *ranges),
+        p, diag, shift_column, gamma, image, *halo, index, corner, k_high, k_low, pj,
     )
     totals = lax.all_to_all(sums, "dom", 0, 0)
+    (image,) = call(functools.partial(cells_kernel, z, False), [(window, F32)], [(acc, F32)], ranges, index, corner, e)
     image, send_a, send_b, dots = call(
-        functools.partial(scatter_kernel, z, True),
+        functools.partial(support_kernel, z, True),
         [(window, F32), (rim, F32), (rim, F32), ((1, LANES), F32)],
-        scatter_scratch,
-        [SMEM] * 6 + [VMEM] * 7,
-        pos, support_cell, support_atom, support_count, *ranges, totals, coupled, e, index, corner, pj, diag,
+        [(entries, F32), (acc, F32)],
+        (pos, *supports, *ranges),
+        totals, coupled, index, corner, pj, diag, image,
     )
     halo = exchange(send_a, send_b)
-    own = (z.vectors, z.nodes)
     answer, residual, factor = call(
         functools.partial(last_kernel, z),
         [(own, F32), (own, F32), ((ROWS, LANES), F32)],
         [],
-        [VMEM] * 8,
-        rhs, p, diag, shift_column, y, q, image, dots, final=True,
-    )
-    left, right = sides(position, *halo)
-    residual = residual.at[:, : z.rim].add(factor[:, :1] * left[:, z.rim :])
-    residual = residual.at[:, z.nodes - z.rim :].add(factor[:, :1] * right[:, : z.rim])
+        (),
+        rhs, p, diag, shift_column, y, q, image, dots, in_hbm=(0,),
+    )
+    (residual,) = call(functools.partial(rim_kernel, z), [(own, F32)], [], (pos,), residual, *halo, factor, in_hbm=(0,))
     return answer, residual
 
 

time: 69 us -> 62.3 us (0.903)
  blocking collectives: 14 us -> 0 us
  starting transfers between devices: 12.3 us -> 20 us
  Pallas kernels: 21.6 us -> 26.5 us
  other arithmetic: 5.13 us -> 0.94 us
  waiting for transfers between devices: 11.8 us -> 10.9 us
    all_to_all x1 -> x0, blocking collectives: 14 us -> none  [on_device(): coupled = lax.all_to_all(sums, 'dom', 0, 0)]
    all_to_all x0 -> x1, starting transfers between devices: none -> 6.17 us  [on_device(): coupled = lax.all_to_all(sums, 'dom', 0, 0)]
    pallas_call x6 -> x9, Pallas kernels: 21.6 us -> 26.5 us  [call(): pl.pallas_call(kernel, out_shape=[jax.ShapeDtypeStruct(s, d) if i in in_h...]
    all_to_all x1, waiting for transfers between devices: 6.56 us -> 2.87 us  [on_device(): totals = lax.all_to_all(sums, 'dom', 0, 0)]
    scatter-add x2 -> x0, other arithmetic: 3.47 us -> none  [the longest x1 2.08 us: on_device(): residual = residual.at[:, :z.rim].add(factor[:, :1] * left[:, z.rim:])]
    all_to_all x0 -> x1, waiting for transfers between devices: none -> 2.29 us  [on_device(): coupled = lax.all_to_all(sums, 'dom', 0, 0)]
    all_to_all x1, starting transfers between devices: 2.7 us -> 4.03 us  [on_device(): totals = lax.all_to_all(sums, 'dom', 0, 0)]
    another operation x1 -> x0, other arithmetic: 0.72 us -> none
  transfers between devices with their start and end apart: 7 -> 8, of which waited for: 3 -> 4; matrix products, arithmetic and copies ran while one was open for 2% -> 0% of each run, Pallas kernels for 2% -> 17%
where the time goes in v5:
time: 62.3 us; the launch traced here: 61.8 us
  Pallas kernels  26.5 us (43%)
  starting transfers between devices  20 us (32%)
  waiting for transfers between devices  10.9 us (17%)
  local copies, waits for them, and re-layouts  2.61 us (4%)
  other arithmetic  0.94 us (2%)
  between operations  0.87 us (1%)
    pallas_call x9, Pallas kernels, call(): pl.pallas_call(kernel, out_shape=[jax.ShapeDtypeStruct(s, d) if i in in_h...  26.5 us
    ppermute x6, starting transfers between devices, exchange(): return (lax.ppermute(a, 'dom', near), lax.ppermute(b, 'dom', far))  9.84 us
    all_to_all x1, starting transfers between devices, on_device(): coupled = lax.all_to_all(sums, 'dom', 0, 0)  6.17 us
    ppermute x6, waiting for transfers between devices, exchange(): return (lax.ppermute(a, 'dom', near), lax.ppermute(b, 'dom', far))  5.73 us
    all_to_all x1, starting transfers between devices, on_device(): totals = lax.all_to_all(sums, 'dom', 0, 0)  4.03 us
    all_to_all x1, waiting for transfers between devices, on_device(): totals = lax.all_to_all(sums, 'dom', 0, 0)  2.87 us
    unnamed x26, local copies, waits for them, and re-layouts  2.48 us
    all_to_all x1, waiting for transfers between devices, on_device(): coupled = lax.all_to_all(sums, 'dom', 0, 0)  2.29 us
  transfers between devices with their start and end apart: 8, of which 4 were waited for; matrix products, arithmetic and copies ran while one was open for 0% of the time, Pallas kernels for 17%

profile of v5, /device:TPU:1, one launch (start us, length us, event | category | flops | bytes accessed | tf_op | source)
XLA Modules:
  0.0 61.8 jit_solution(14038316679481350554)
XLA Ops:
  0.7 0.7 %copy-done.10 = f32[6656]{0:T(1024)S(1)} copy-done((f32[6656]{0:T(1024)S(1)}, f32[6656]{0:T(1024)}, u32[]{:S(2)}) %copy-start.10) | copy-done | bytes 26648
  1.4 0.8 %fusion = (f32[8,512]{1,0:T(8,128)S(1)}, f32[8,512]{1,0:T(8,128)S(1)}) fusion(f32[8,6656]{1,0:T(8,128)} %rhs_ref.3, f32[512]{0:T(512)S(1)} %get-tuple-element.55, f32[512]{0:T(512)S(1)} %get-tuple-element.54, pred[]{:T(512)S(6)} %eq.5), kind=kLoop, calls=%fused_computation.4 | loop fusion | flops 16384 | bytes 69633 | tf_op jit(solution)/shard_map/jit(_where)/select_n | solution.py:469
  2.1 4.6 %collective-permute-start.1 = (f32[8,512]{1,0:T(8,128)S(1)}, f32[8,512]{1,0:T(8,128)S(1)}, u32[]{:S(2)}, u32[]{:S(2)}) collective-permute-start(f32[8,512]{1,0:T(8,128)S(1)} %get-tuple-element.52), channel_id=1, source_target_pairs={{1,2},{2,1},{3,4},{4,3},{5,6},{6,5},{7,8},{8,7},{9,10},{10,9},{11,... | collective-permute-start | bytes 49160 | tf_op jit(solution)/shard_map/ppermute | solution.py:450
  7.1 1.0 %copy-done.1 = f32[343,343]{1,0:T(8,128)S(1)} copy-done((f32[343,343]{1,0:T(8,128)S(1)}, f32[343,343]{1,0:T(8,128)}, u32[]{:S(2)}) %copy-start.1) | copy-done | bytes 470620
  8.2 0.2 shard_map.140
  8.5 0.6 copy-done
  9.2 5.0 %shard_map.141 = (f32[8,9472]{1,0:T(8,128)S(1)}, f32[2,7680]{1,0:T(2,128)S(1)}, f32[32,4,128]{2,1,0:T(4,128)}, f32[256,384]{1,0:T(8,128)S(1)}, f32[1,128]{1,0:T(1,128)S(1)}) custom-call(s32[1]{0:T(128)} %bitcast.pos_ref, s32[32]{0:T(128)S(1)} %copy-done.8, f32[32]{0:T(128)S(1)} %copy-done.9, s32[8]{0:T(128)S(1)} %copy-done.5, s32[8]{0:T(128)S(1)} %copy-done.6, ...), custom_call_target="tpu_custom_call" | custom-call | tf_op jit(solution)/shard_map/pallas_call | solution.py:454
  14.2 6.2 %all-to-all-start = ((f32[32,4,128]{2,1,0:T(4,128)}), f32[32,4,128]{2,1,0:T(4,128)S(1)}, u32[]{:S(2)}, u32[]{:S(2)}) async-start(f32[32,4,128]{2,1,0:T(4,128)} %get-tuple-element.32), calls=%async_computation | async-start | bytes 131072 | tf_op jit(solution)/shard_map/all_to_all | solution.py:496
  20.4 5.0 %shard_map.142.cells_ref = f32[8,7680]{1,0:T(8,128)S(1)} custom-call(s32[32]{0:T(128)S(1)} %get-tuple-element.51.low_ref, s32[32]{0:T(128)S(1)} %get-tuple-element.50.high_ref, s32[32,1,384]{2,1,0:T(1,128)S(1)} %get-tuple-element.26.index_ref, s32[1,128]{1,0:T(1,128)S(1)} %get-tuple-element.27.corner_ref, f32[256,384]{1,0:T(8,128)S(1)} %get-tuple-element.33.refs_0_, ...), custom_call_target="tpu_custom_call" | custom-call | tf_op jit(solution)/shard_map/pallas_call | solution.py:454
  25.4 2.3 %all-to-all-done.sums_ref.coupling_ref = f32[32,4,128]{2,1,0:T(4,128)S(1)} async-done(((f32[32,4,128]{2,1,0:T(4,128)}), f32[32,4,128]{2,1,0:T(4,128)S(1)}, u32[]{:S(2)}, u32[]{:S(2)}) %all-to-all-start) | async-done | bytes 65568 | tf_op jit(solution)/shard_map/all_to_all | solution.py:496
  27.6 2.3 %shard_map.143 = (f32[8,7680]{1,0:T(8,128)S(1)}, f32[10,1024]{1,0:T(8,128)S(1)}, f32[10,1024]{1,0:T(8,128)S(1)}) custom-call(s32[1]{0:T(128)} %bitcast.pos_ref, s32[8]{0:T(128)S(1)} %copy-done.5, s32[8]{0:T(128)S(1)} %copy-done.6, s32[32]{0:T(128)S(1)} %copy-done.7, s32[32]{0:T(128)S(1)} %get-tuple-element.51.low_ref, s32[32]{0:T(128)S(1)} %get-tuple-element.50.high_ref, ...), custom_call_target="tpu_custom_call" | custom-call | tf_op jit(solution)/shard_map/pallas_call | solution.py:454
  29.9 0.5 collective-permute-start.2
  30.4 2.2 %collective-permute-start.3 = (f32[10,1024]{1,0:T(8,128)S(1)}, f32[10,1024]{1,0:T(8,128)S(1)}, u32[]{:S(2)}, u32[]{:S(2)}) collective-permute-start(f32[10,1024]{1,0:T(8,128)S(1)} %get-tuple-element.38), channel_id=1, source_target_pairs={{1,2},{2,1},{3,4},{4,3},{5,6},{6,5},{7,8},{8,7},{9,10},{10,9},{11,... | collective-permute-start | bytes 122888 | tf_op jit(solution)/shard_map/ppermute | solution.py:450
  32.7 3.5 %collective-permute-done.3.halo_b_ref = f32[10,1024]{1,0:T(8,128)S(1)} collective-permute-done((f32[10,1024]{1,0:T(8,128)S(1)}, f32[10,1024]{1,0:T(8,128)S(1)}, u32[]{:S(2)}, u32[]{:S(2)}) %collective-permute-start.3) | collective-permute-done | bytes 40992 | tf_op jit(solution)/shard_map/ppermute | solution.py:450
  36.2 5.6 %shard_map.144 = (f32[8,7680]{1,0:T(8,128)S(1)}, f32[8,9472]{1,0:T(8,128)S(1)}, f32[32,4,128]{2,1,0:T(4,128)}, f32[256,384]{1,0:T(8,128)S(1)}) custom-call(s32[1]{0:T(128)} %bitcast.pos_ref, s32[32]{0:T(128)S(1)} %copy-done.8, f32[32]{0:T(128)S(1)} %copy-done.9, s32[8]{0:T(128)S(1)} %copy-done.5, s32[8]{0:T(128)S(1)} %copy-done.6, s32[32]{0:T(128)S(1)} %copy-done.7, ...), custom_call_target="tpu_custom_call" | custom-call | tf_op jit(solution)/shard_map/pallas_call | solution.py:454
  41.8 4.0 %all-to-all-start.1 = ((f32[32,4,128]{2,1,0:T(4,128)}), f32[32,4,128]{2,1,0:T(4,128)S(1)}, u32[]{:S(2)}, u32[]{:S(2)}) async-start(f32[32,4,128]{2,1,0:T(4,128)} %get-tuple-element.41), calls=%async_computation.1 | async-start | bytes 131072 | tf_op jit(solution)/shard_map/all_to_all | solution.py:519
  45.8 4.4 %shard_map.145.cells_ref = f32[8,7680]{1,0:T(8,128)S(1)} custom-call(s32[32]{0:T(128)S(1)} %get-tuple-element.51.low_ref, s32[32]{0:T(128)S(1)} %get-tuple-element.50.high_ref, s32[32,1,384]{2,1,0:T(1,128)S(1)} %get-tuple-element.26.index_ref, s32[1,128]{1,0:T(1,128)S(1)} %get-tuple-element.27.corner_ref, f32[256,384]{1,0:T(8,128)S(1)} %get-tuple-element.42.refs_0_), custom_call_target="tpu_custom_call" | custom-call | tf_op jit(solution)/shard_map/pallas_call | solution.py:454
  50.2 2.9 %all-to-all-done.1.sums_ref = f32[32,4,128]{2,1,0:T(4,128)S(1)} async-done(((f32[32,4,128]{2,1,0:T(4,128)}), f32[32,4,128]{2,1,0:T(4,128)S(1)}, u32[]{:S(2)}, u32[]{:S(2)}) %all-to-all-start.1) | async-done | bytes 65568 | tf_op jit(solution)/shard_map/all_to_all | solution.py:519
  53.1 2.3 %shard_map.146 = (f32[8,7680]{1,0:T(8,128)S(1)}, f32[8,1024]{1,0:T(8,128)S(1)}, f32[8,1024]{1,0:T(8,128)S(1)}, f32[1,128]{1,0:T(1,128)S(1)}) custom-call(s32[1]{0:T(128)} %bitcast.pos_ref, s32[8]{0:T(128)S(1)} %copy-done.5, s32[8]{0:T(128)S(1)} %copy-done.6, s32[32]{0:T(128)S(1)} %copy-done.7, s32[32]{0:T(128)S(1)} %get-tuple-element.51.low_ref, ...), custom_call_target="tpu_custom_call" | custom-call | tf_op jit(solution)/shard_map/pallas_call | solution.py:454
  55.4 0.5 collective-permute-start.4
  55.9 2.0 %collective-permute-start.5 = (f32[8,1024]{1,0:T(8,128)S(1)}, f32[8,1024]{1,0:T(8,128)S(1)}, u32[]{:S(2)}, u32[]{:S(2)}) collective-permute-start(f32[8,1024]{1,0:T(8,128)S(1)} %get-tuple-element.48), channel_id=1, source_target_pairs={{1,2},{2,1},{3,4},{4,3},{5,6},{6,5},{7,8},{8,7},{9,10},{10,9},{11,... | collective-permute-start | bytes 98312 | tf_op jit(solution)/shard_map/ppermute | solution.py:450
  57.9 0.9 %shard_map.147 = (f32[8,6656]{1,0:T(8,128)}, f32[8,6656]{1,0:T(8,128)S(1)}, f32[8,128]{1,0:T(8,128)S(1)}) custom-call(f32[8,6656]{1,0:T(8,128)S(1)} %copy-done, f32[8,9472]{1,0:T(8,128)S(1)} %get-tuple-element.29.p_ref, f32[2,7680]{1,0:T(2,128)S(1)} %get-tuple-element.30.diag_ref.diag_in_ref, f32[8,1]{1,0:T(8,128)S(1)} %copy.16.shift_ref, ...), custom_call_target="tpu_custom_call" | custom-call | tf_op jit(solution)/shard_map/pallas_call | solution.py:454
  58.9 2.2 %collective-permute-done.5.halo_b_ref = f32[8,1024]{1,0:T(8,128)S(1)} collective-permute-done((f32[8,1024]{1,0:T(8,128)S(1)}, f32[8,1024]{1,0:T(8,128)S(1)}, u32[]{:S(2)}, u32[]{:S(2)}) %collective-permute-start.5) | collective-permute-done | bytes 32800 | tf_op jit(solution)/shard_map/ppermute | solution.py:450
  61.1 0.8 %shard_map.148 = f32[8,6656]{1,0:T(8,128)} custom-call(s32[1]{0:T(128)} %bitcast.pos_ref, f32[8,6656]{1,0:T(8,128)S(1)} %get-tuple-element.46.residual_in_ref, f32[8,1024]{1,0:T(8,128)S(1)} %collective-permute-done.4.halo_a_ref, f32[8,1024]{1,0:T(8,128)S(1)} %collective-permute-done.5.halo_b_ref, f32[8,128]{1,0:T(8,128)S(1)} %get-tuple-element.49.factor_ref), custom_call_target="tpu_custom_call" | custom-call | tf_op jit(solution)/shard_map/pallas_call | solution.py:454
  (33 shorter events, 0.5 us)
Async XLA Ops:
  0.6 0.7 %copy-start.10 = (f32[6656]{0:T(1024)S(1)}, f32[6656]{0:T(1024)}, u32[]{:S(2)}) copy-start(f32[6656]{0:T(1024)} %param.15) | copy-start | bytes 79876
  0.6 6.2 %copy-start.2 = (s32[32,343]{1,0:T(8,128)S(1)}, s32[32,343]{1,0:T(8,128)}, u32[]{:S(2)}) copy-start(s32[32,343]{1,0:T(8,128)} %conn_ref.1) | copy-start | bytes 131716
  1.4 5.7 %copy-start.11 = (f32[6656]{0:T(1024)S(1)}, f32[6656]{0:T(1024)}, u32[]{:S(2)}) copy-start(f32[6656]{0:T(1024)} %param.14) | copy-start | bytes 79876
  2.1 5.0 %copy-start.3 = (f32[8,8,343]{2,1,0:T(8,128)S(1)}, f32[8,8,343]{2,1,0:T(8,128)}, u32[]{:S(2)}) copy-start(f32[8,8,343]{2,1,0:T(8,128)} %param.21) | copy-start | bytes 263428
  2.1 6.3 %collective-permute-start.1 = (f32[8,512]{1,0:T(8,128)S(1)}, f32[8,512]{1,0:T(8,128)S(1)}, u32[]{:S(2)}, u32[]{:S(2)}) collective-permute-start(f32[8,512]{1,0:T(8,128)S(1)} %get-tuple-element.52), channel_id=1, source_target_pairs={{1,2},{2,1},{3,4},{4,3},{5,6},{6,5},{7,8},{8,7},{9,10},{10,9},{11,... | collective-permute-start | bytes 49160 | tf_op jit(solution)/shard_map/ppermute | solution.py:450
  6.8 1.7 %collective-permute-start = (f32[8,512]{1,0:T(8,128)S(1)}, f32[8,512]{1,0:T(8,128)S(1)}, u32[]{:S(2)}, u32[]{:S(2)}) collective-permute-start(f32[8,512]{1,0:T(8,128)S(1)} %get-tuple-element.53), channel_id=1, source_target_pairs={{0,1},{1,0},{2,3},{3,2},{4,5},{5,4},{6,7},{7,6},{8,9},{9,8},{10,11... | collective-permute-start | bytes 49160 | tf_op jit(solution)/shard_map/ppermute | solution.py:450
  7.1 1.0 %copy-start.1 = (f32[343,343]{1,0:T(8,128)S(1)}, f32[343,343]{1,0:T(8,128)}, u32[]{:S(2)}) copy-start(f32[343,343]{1,0:T(8,128)} %stiffness_ref.1) | copy-start | bytes 1411792
  8.2 0.9 %copy-start = (f32[8,6656]{1,0:T(8,128)S(1)}, f32[8,6656]{1,0:T(8,128)}, u32[]{:S(2)}) copy-start(f32[8,6656]{1,0:T(8,128)} %rhs_ref.3) | copy-start | bytes 638980
  8.4 0.7 %copy-start.4 = (f32[2,8,8]{2,1,0:T(8,128)S(1)}, f32[2,8,8]{2,1,0:T(8,128)}, u32[]{:S(2)}) copy-start(f32[2,8,8]{2,1,0:T(8,128)} %coupling_ref.1) | copy-start | bytes 1540
  8.4 0.7 %copy-start.8 = (s32[32]{0:T(128)S(1)}, s32[32]{0:T(128)}, u32[]{:S(2)}) copy-start(s32[32]{0:T(128)} %count_ref.3) | copy-start | bytes 388
  8.5 0.7 %copy-start.9 = (f32[32]{0:T(128)S(1)}, f32[32]{0:T(128)}, u32[]{:S(2)}) copy-start(f32[32]{0:T(128)} %scale_ref.3) | copy-start | bytes 388
  8.5 0.7 %copy-start.5 = (s32[8]{0:T(128)S(1)}, s32[8]{0:T(128)}, u32[]{:S(2)}) copy-start(s32[8]{0:T(128)} %cell_ref.7) | copy-start | bytes 100
  8.5 0.7 %copy-start.6 = (s32[8]{0:T(128)S(1)}, s32[8]{0:T(128)}, u32[]{:S(2)}) copy-start(s32[8]{0:T(128)} %atom_ref.7) | copy-start | bytes 100
  8.5 0.7 %copy-start.7 = (s32[32]{0:T(128)S(1)}, s32[32]{0:T(128)}, u32[]{:S(2)}) copy-start(s32[32]{0:T(128)} %scount_ref.7) | copy-start | bytes 388
  14.2 13.4 %all-to-all-start = ((f32[32,4,128]{2,1,0:T(4,128)}), f32[32,4,128]{2,1,0:T(4,128)S(1)}, u32[]{:S(2)}, u32[]{:S(2)}) async-start(f32[32,4,128]{2,1,0:T(4,128)} %get-tuple-element.32), calls=%async_computation | async-start | bytes 131072 | tf_op jit(solution)/shard_map/all_to_all | solution.py:496
  29.9 2.8 %collective-permute-start.2 = (f32[10,1024]{1,0:T(8,128)S(1)}, f32[10,1024]{1,0:T(8,128)S(1)}, u32[]{:S(2)}, u32[]{:S(2)}) collective-permute-start(f32[10,1024]{1,0:T(8,128)S(1)} %get-tuple-element.37), channel_id=1, source_target_pairs={{0,1},{1,0},{2,3},{3,2},{4,5},{5,4},{6,7},{7,6},{8,9},{9,8},{10,11... | collective-permute-start | bytes 122888 | tf_op jit(solution)/shard_map/ppermute | solution.py:450
  30.4 2.2 %copy-start.12 = (f32[8]{0:T(128)S(1)}, f32[8]{0:T(128)}, u32[]{:S(2)}) copy-start(f32[8]{0:T(128)} %param.16) | copy-start | bytes 100
  30.4 5.8 %collective-permute-start.3 = (f32[10,1024]{1,0:T(8,128)S(1)}, f32[10,1024]{1,0:T(8,128)S(1)}, u32[]{:S(2)}, u32[]{:S(2)}) collective-permute-start(f32[10,1024]{1,0:T(8,128)S(1)} %get-tuple-element.38), channel_id=1, source_target_pairs={{1,2},{2,1},{3,4},{4,3},{5,6},{6,5},{7,8},{8,7},{9,10},{10,9},{11,... | collective-permute-start | bytes 122888 | tf_op jit(solution)/shard_map/ppermute | solution.py:450
  41.8 11.3 %all-to-all-start.1 = ((f32[32,4,128]{2,1,0:T(4,128)}), f32[32,4,128]{2,1,0:T(4,128)S(1)}, u32[]{:S(2)}, u32[]{:S(2)}) async-start(f32[32,4,128]{2,1,0:T(4,128)} %get-tuple-element.41), calls=%async_computation.1 | async-start | bytes 131072 | tf_op jit(solution)/shard_map/all_to_all | solution.py:519
  55.4 3.5 %collective-permute-start.4 = (f32[8,1024]{1,0:T(8,128)S(1)}, f32[8,1024]{1,0:T(8,128)S(1)}, u32[]{:S(2)}, u32[]{:S(2)}) collective-permute-start(f32[8,1024]{1,0:T(8,128)S(1)} %get-tuple-element.47), channel_id=1, source_target_pairs={{0,1},{1,0},{2,3},{3,2},{4,5},{5,4},{6,7},{7,6},{8,9},{9,8},{10,11... | collective-permute-start | bytes 98312 | tf_op jit(solution)/shard_map/ppermute | solution.py:450
  55.9 5.2 %collective-permute-start.5 = (f32[8,1024]{1,0:T(8,128)S(1)}, f32[8,1024]{1,0:T(8,128)S(1)}, u32[]{:S(2)}, u32[]{:S(2)}) collective-permute-start(f32[8,1024]{1,0:T(8,128)S(1)} %get-tuple-element.48), channel_id=1, source_target_pairs={{1,2},{2,1},{3,4},{4,3},{5,6},{6,5},{7,8},{8,7},{9,10},{10,9},{11,... | collective-permute-start | bytes 98312 | tf_op jit(solution)/shard_map/ppermute | solution.py:450

commit v6 on v5

--- a/solution.py
+++ b/solution.py
@@ -65,9 +65,19 @@
     return jnp.sum(jnp.where(iota((ROWS, LANES), 1) == iota((ROWS, LANES), 0), spread, 0.0), axis=0, keepdims=True)
 
 
-def prepare_kernel(
-    z, conn_ref, stiffness_ref, projector_ref, index_ref, corner_ref, k_high_ref, k_low_ref, pj_ref, k_ref
-):
+def list_cells(z, margin, low_ref, high_ref, list_ref):
+    def place(c, counts):
+        inside, outside = counts
+        good = (low_ref[c] + z.shift >= margin) & (high_ref[c] + z.shift < z.window - margin)
+        list_ref[jnp.where(good, inside, z.slots - 1 - outside)] = c
+        one = good.astype(jnp.int32)
+        return inside + one, outside + 1 - one
+
+    inside, _ = lax.fori_loop(0, z.slots, place, (jnp.int32(0), jnp.int32(0)))
+    list_ref[z.slots] = inside // z.together
+
+
+def prepare_kernel(z, low_ref, high_ref, conn_ref, index_ref, corner_ref, first_list_ref, second_list_ref):
     line = iota((1, LANES), 1)
     corner = jnp.zeros((1, LANES), jnp.int32)
     index_ref[...] = jnp.zeros_like(index_ref)
@@ -77,6 +87,11 @@
         corner = jnp.where(line == c, row[:, :1], corner)
         corner = jnp.where(line == z.slots + c, row[:, z.elem - 1 :], corner)
     corner_ref[...] = corner
+    list_cells(z, z.rim, low_ref, high_ref, first_list_ref)
+    list_cells(z, 2 * z.rim, low_ref, high_ref, second_list_ref)
+
+
+def pad_kernel(z, stiffness_ref, projector_ref, k_high_ref, k_low_ref, pj_ref, k_ref):
     k_ref[...] = jnp.zeros_like(k_ref)
     k_ref[: z.elem, : z.elem] = stiffness_ref[...]
     k_high_ref[...], k_low_ref[...] = split(k_ref[...])
@@ -84,23 +99,12 @@
     pj_ref[:, : z.elem] = projector_ref[...]
 
 
-def gather_cells(
-    z, index_ref, corner_ref, low_ref, high_ref, window_ref, scale_ref, live, u_ref, uw_ref
-):
+def gather_middle(z, groups, list_ref, index_ref, low_ref, high_ref, window_ref, u_ref):
     total = z.window // LANES
     tile = (ROWS, LANES)
-    corner = jnp.broadcast_to(corner_ref[...], tile)
-    low, high = corner & (LANES - 1), corner >> 7
-    chains = [jnp.zeros(tile, F32)] * CHAINS
-    for h in range(total):
-        got = lane_gather(window_ref[:, h * LANES : (h + 1) * LANES], low)
-        chains[h % CHAINS] = jnp.where(high == h, got, chains[h % CHAINS])
-    corners = functools.reduce(jnp.add, chains)
-    lane = iota(tile, 1)
-    last = (z.elem - 1) % LANES
 
     def some_cells(g, _):
-        cells = [g * z.together + i for i in range(z.together)]
+        cells = [list_ref[g * z.together + i] for i in range(z.together)]
         starts = [(low_ref[c] + z.shift) >> 7 for c in cells]
         ends = [(high_ref[c] + z.shift) >> 7 for c in cells]
         passes = functools.reduce(jnp.maximum, [(e - s) // SPAN + 1 for s, e in zip(starts, ends)])
@@ -121,20 +125,37 @@
 
         values = lax.fori_loop(0, passes, one_pass, (jnp.zeros(tile, F32),) * (z.together * z.tiles))
         for i, c in enumerate(cells):
-            weight = jnp.where(c < live, scale_ref[c], 0.0)
             rows = pl.ds(pl.multiple_of(c * ROWS, ROWS), ROWS)
             for t in range(z.tiles):
-                value = values[i * z.tiles + t]
-                if t == 0:
-                    value = jnp.where(lane == 0, lane_gather(corners, jnp.full(tile, 0, jnp.int32) + c), value)
-                if t == z.tiles - 1:
-                    got = lane_gather(corners, jnp.full(tile, z.slots, jnp.int32) + c)
-                    value = jnp.where(lane == last, got, value)
-                u_ref[rows, t * LANES : (t + 1) * LANES] = value
-                uw_ref[rows, t * LANES : (t + 1) * LANES] = value * weight
+                u_ref[rows, t * LANES : (t + 1) * LANES] = values[i * z.tiles + t]
         return 0
 
-    lax.fori_loop(0, z.slots // z.together, some_cells, 0)
+    lax.fori_loop(*groups, some_cells, 0)
+
+
+def gather_corners(z, corner_ref, window_ref, scale_ref, live, u_ref, uw_ref):
+    tile = (ROWS, LANES)
+    corner = jnp.broadcast_to(corner_ref[...], tile)
+    low, high = corner & (LANES - 1), corner >> 7
+    chains = [jnp.zeros(tile, F32)] * CHAINS
+    for h in range(z.window // LANES):
+        got = lane_gather(window_ref[:, h * LANES : (h + 1) * LANES], low)
+        chains[h % CHAINS] = jnp.where(high == h, got, chains[h % CHAINS])
+    corners = functools.reduce(jnp.add, chains)
+    lane = iota(tile, 1)
+    last = (z.elem - 1) % LANES
+    for c in range(z.slots):
+        weight = jnp.where(c < live, scale_ref[c], 0.0)
+        rows = slice(c * ROWS, (c + 1) * ROWS)
+        for t in range(z.tiles):
+            lanes = slice(t * LANES, (t + 1) * LANES)
+            value = u_ref[rows, lanes]
+            if t == 0:
+                value = jnp.where(lane == 0, corners[:, c : c + 1], value)
+            if t == z.tiles - 1:
+                value = jnp.where(lane == last, corners[:, z.slots + c : z.slots + c + 1], value)
+            u_ref[rows, lanes] = value
+            uw_ref[rows, lanes] = value * weight
 
 
 def stiffness_product(k_high_ref, k_low_ref, uw_ref, e_ref):
@@ -172,22 +193,33 @@
     return jnp.where(even, far, near), jnp.where(even, near, far)
 
 
+def first_window_kernel(
+    z, low_ref, high_ref, list_ref, rhs_ref, precond_ref, index_ref, p_ref, u_ref, gamma_ref,
+):
+    product = rhs_ref[...] * precond_ref[...]
+    p_ref[:, z.rim : z.rim + z.nodes] = product
+    gamma_ref[...] = lanes_by_vector(z, product * rhs_ref[...])
+    p_ref[:, z.window :] = jnp.zeros((ROWS, z.reach - z.window), F32)
+    gather_middle(z, (0, list_ref[z.slots]), list_ref, index_ref, low_ref, high_ref, p_ref, u_ref)
+
+
 def first_kernel(
-    z, pos_ref, count_ref, scale_ref, cell_ref, atom_ref, scount_ref, low_ref, high_ref, rhs_ref, precond_ref,
-    potential_ref, halo_a_ref, halo_b_ref, index_ref, corner_ref, pj_ref, coupling_ref,
-    p_ref, diag_ref, out_ref, uw_ref, gamma_ref, u_ref,
+    z, pos_ref, count_ref, scale_ref, cell_ref, atom_ref, scount_ref, low_ref, high_ref, list_ref, p_in_ref, u_in_ref,
+    precond_ref, potential_ref, halo_a_ref, halo_b_ref, index_ref, corner_ref, pj_ref, coupling_ref,
+    p_ref, diag_ref, out_ref, uw_ref, u_ref,
 ):
     position = pos_ref[0]
     own = slice(z.rim, z.rim + z.nodes)
     p_ref[:, : z.rim], p_ref[:, z.rim + z.nodes : z.window] = sides(position, halo_a_ref[...], halo_b_ref[...])
+    p_ref[:, own] = p_in_ref[:, own]
+    p_ref[:, z.window :] = p_in_ref[:, z.window :]
+    u_ref[...] = u_in_ref[...]
     diag_ref[...] = jnp.zeros_like(diag_ref)
     diag_ref[0:1, own] = precond_ref[...]
     diag_ref[1:2, own] = potential_ref[...]
-    product = rhs_ref[...] * precond_ref[...]
-    p_ref[:, own] = product
-    gamma_ref[...] = lanes_by_vector(z, product * rhs_ref[...])
-    p_ref[:, z.window :] = jnp.zeros((ROWS, z.reach - z.window), F32)
-    gather_cells(z, index_ref, corner_ref, low_ref, high_ref, p_ref, scale_ref, count_ref[position], u_ref, uw_ref)
+    groups = list_ref[z.slots], z.slots // z.together
+    gather_middle(z, groups, list_ref, index_ref, low_ref, high_ref, p_ref, u_ref)
+    gather_corners(z, corner_ref, p_ref, scale_ref, count_ref[position], u_ref, uw_ref)
     parts = contributions(z, position, pj_ref, cell_ref, atom_ref, scount_ref, u_ref)
     small_lane, small_row = iota((ROWS, LANES), 1), iota((ROWS, LANES), 0)
     matrices = jnp.zeros((ROWS, LANES), F32)
@@ -200,22 +232,36 @@
         out_ref[d] = message
 
 
+def second_window_kernel(
+    z, low_ref, high_ref, list_ref, p_ref, diag_ref, shift_ref, image_ref, index_ref, y_ref, q_ref, u_ref,
+):
+    y_ref[...] = image_ref[...] + (diag_ref[1:2, :] + shift_ref[...]) * p_ref[:, : z.window]
+    q_ref[:, : z.window] = y_ref[...] * diag_ref[0:1, :]
+    q_ref[:, z.window :] = jnp.zeros((ROWS, z.reach - z.window), F32)
+    gather_middle(z, (0, list_ref[z.slots]), list_ref, index_ref, low_ref, high_ref, q_ref, u_ref)
+
+
 def second_kernel(
-    z, pos_ref, count_ref, scale_ref, cell_ref, atom_ref, scount_ref, low_ref, high_ref, p_ref, diag_in_ref, shift_ref,
-    gamma_ref, image_ref, halo_a_ref, halo_b_ref, index_ref, corner_ref, k_high_ref, k_low_ref, pj_ref,
-    y_ref, q_ref, out_ref, e_ref, diag_ref, u_ref, uw_ref,
+    z, pos_ref, count_ref, scale_ref, cell_ref, atom_ref, scount_ref, low_ref, high_ref, list_ref, y_in_ref, q_in_ref,
+    u_in_ref, p_ref, diag_in_ref, shift_ref, gamma_ref, halo_a_ref, halo_b_ref, index_ref, corner_ref, k_high_ref,
+    k_low_ref, pj_ref, y_ref, q_ref, out_ref, e_ref, diag_ref, u_ref, uw_ref,
 ):
     position = pos_ref[0]
     left, right = sides(position, halo_a_ref[...], halo_b_ref[...])
     own = slice(z.rim, z.rim + z.nodes)
+    ghosts = slice(0, z.rim), slice(z.rim + z.nodes, z.window)
     diag_ref[:, own] = diag_in_ref[:, own]
-    diag_ref[:, : z.rim] = left[ROWS : ROWS + 2, : z.rim]
-    diag_ref[:, z.rim + z.nodes :] = right[ROWS : ROWS + 2, z.rim :]
-    y_ref[...] = image_ref[...] + (diag_ref[1:2, :] + shift_ref[...]) * p_ref[:, : z.window]
+    diag_ref[:, ghosts[0]] = left[ROWS : ROWS + 2, : z.rim]
+    diag_ref[:, ghosts[1]] = right[ROWS : ROWS + 2, z.rim :]
+    y_ref[...] = y_in_ref[...]
+    for ghost in ghosts:
+        y_ref[:, ghost] += (diag_ref[1:2, ghost] - diag_in_ref[1:2, ghost]) * p_ref[:, ghost]
     y_ref[:, : 2 * z.rim] += left[:ROWS]
     y_ref[:, z.window - 2 * z.rim :] += right[:ROWS]
-    q_ref[:, : z.window] = y_ref[...] * diag_ref[0:1, :]
-    q_ref[:, z.window :] = jnp.zeros((ROWS, z.reach - z.window), F32)
+    q_ref[...] = q_in_ref[...]
+    for rims in (slice(0, 2 * z.rim), slice(z.window - 2 * z.rim, z.window)):
+        q_ref[:, rims] = y_ref[:, rims] * diag_ref[0:1, rims]
+    u_ref[...] = u_in_ref[...]
     y, q = y_ref[:, own], q_ref[:, own]
     dots = [
         gamma_ref[...],
@@ -223,7 +269,9 @@
         lanes_by_vector(z, y * q),
     ]
     energy = jnp.sum(q * q * (diag_ref[1:2, own] + shift_ref[...]), axis=1, keepdims=True)
-    gather_cells(z, index_ref, corner_ref, low_ref, high_ref, q_ref, scale_ref, count_ref[position], u_ref, uw_ref)
+    groups = list_ref[z.slots], z.slots // z.together
+    gather_middle(z, groups, list_ref, index_ref, low_ref, high_ref, q_ref, u_ref)
+    gather_corners(z, corner_ref, q_ref, scale_ref, count_ref[position], u_ref, uw_ref)
     parts = contributions(z, position, pj_ref, cell_ref, atom_ref, scount_ref, u_ref)
     stiffness_product(k_high_ref, k_low_ref, uw_ref, e_ref)
     elements = jnp.zeros((ROWS, z.width), F32)
@@ -449,15 +497,16 @@
     def exchange(a, b):
         return lax.ppermute(a, "dom", near), lax.ppermute(b, "dom", far)
 
-    def call(kernel, outs, scratch, scalars, *args, in_hbm=()):
+    def call(kernel, outs, scratch, scalars, *args, in_hbm=(), in_smem=()):
         args = [pltpu.with_memory_space_constraint(x, pltpu.VMEM) for x in args]
         return pl.pallas_call(
             kernel,
             out_shape=[
-                jax.ShapeDtypeStruct(s, d) if i in in_hbm else pltpu.VMEM(s, d) for i, (s, d) in enumerate(outs)
+                jax.ShapeDtypeStruct(s, d) if i in in_hbm + in_smem else pltpu.VMEM(s, d)
+                for i, (s, d) in enumerate(outs)
             ],
             in_specs=[SMEM] * len(scalars) + [VMEM] * len(args),
-            out_specs=[VMEM] * len(outs),
+            out_specs=[SMEM if i in in_smem else VMEM for i in range(len(outs))],
             scratch_shapes=[pltpu.VMEM(s, d) for s, d in scratch],
             compiler_params=pltpu.CompilerParams(vmem_limit_bytes=16 * 1024 * 1024),
         )(*scalars, *args)
@@ -479,19 +528,33 @@
     acc = ((z.window // WIDE + BAND) * 2 * ROWS, WIDE)
     supports = support_cell, support_atom, support_count
 
-    index, corner, k_high, k_low, pj = call(
+    index, corner, first_list, second_list = call(
         functools.partial(prepare_kernel, z),
-        [((z.slots, 1, z.width), jnp.int32), ((1, LANES), jnp.int32), (square, BF16), (square, BF16), (entries, F32)],
+        [((z.slots, 1, z.width), jnp.int32), ((1, LANES), jnp.int32)] + [((z.slots + 1,), jnp.int32)] * 2,
+        [],
+        ranges,
+        conn, in_smem=(2, 3),
+    )
+    p, u, gamma = call(
+        functools.partial(first_window_kernel, z),
+        [(reach, F32), (cells, F32), ((1, LANES), F32)],
+        [],
+        (*ranges, first_list),
+        rhs, precond_row, index,
+    )
+    k_high, k_low, pj = call(
+        functools.partial(pad_kernel, z),
+        [(square, BF16), (square, BF16), (entries, F32)],
         [(square, F32)],
         (),
-        conn, stiffness, flat_projector,
-    )
-    p, diag, sums, uw, gamma = call(
+        stiffness, flat_projector,
+    )
+    p, diag, sums, uw = call(
         functools.partial(first_kernel, z),
-        [(reach, F32), ((2, z.window), F32), (message, F32), (cells, F32), ((1, LANES), F32)],
+        [(reach, F32), ((2, z.window), F32), (message, F32), (cells, F32)],
         [(cells, F32)],
-        (pos, cell_count, cell_scale, *supports, *ranges),
-        rhs, precond_row, potential_row, *halo, index, corner, pj, atom_matrix,
+        (pos, cell_count, cell_scale, *supports, *ranges, first_list),
+        p, u, precond_row, potential_row, *halo, index, corner, pj, atom_matrix,
     )
     coupled = lax.all_to_all(sums, "dom", 0, 0)
     (image,) = call(
@@ -509,12 +572,19 @@
         coupled, coupled, index, corner, pj, diag, image,
     )
     halo = exchange(send_a, send_b)
+    y, q, u = call(
+        functools.partial(second_window_kernel, z),
+        [(window, F32), (reach, F32), (cells, F32)],
+        [],
+        (*ranges, second_list),
+        p, diag, shift_column, image, index,
+    )
     y, q, sums, e = call(
         functools.partial(second_kernel, z),
         [(window, F32), (reach, F32), (message, F32), (cells, F32)],
         [((2, z.window), F32), (cells, F32), (cells, F32)],
-        (pos, cell_count, cell_scale, *supports, *ranges),
-        p, diag, shift_column, gamma, image, *halo, index, corner, k_high, k_low, pj,
+        (pos, cell_count, cell_scale, *supports, *ranges, second_list),
+        y, q, u, p, diag, shift_column, gamma, *halo, index, corner, k_high, k_low, pj,
     )
     totals = lax.all_to_all(sums, "dom", 0, 0)
     (image,) = call(functools.partial(cells_kernel, z, False), [(window, F32)], [(acc, F32)], ranges, index, corner, e)

time: 62.3 us -> 62.3 us (level)
  Pallas kernels: 26.5 us -> 29.2 us
  waiting for transfers between devices: 10.9 us -> 8.52 us
  starting transfers between devices: 20 us -> 18.9 us
  local copies, waits for them, and re-layouts: 2.61 us -> 3.29 us
    pallas_call x9 -> x12, Pallas kernels: 26.5 us -> 29.2 us  [call(): pl.pallas_call(kernel, out_shape=[jax.ShapeDtypeStruct(s, d) if i in in_h...]
    ppermute x6, waiting for transfers between devices: 5.73 us -> 3.34 us  [exchange(): return (lax.ppermute(a, 'dom', near), lax.ppermute(b, 'dom', far))]
    all_to_all x1, starting transfers between devices: 6.17 us -> 5.15 us  [on_device(): coupled = lax.all_to_all(sums, 'dom', 0, 0)]
    unnamed x26, local copies, waits for them, and re-layouts: 2.48 us -> 3.17 us
  transfers between devices with their start and end apart: 8 -> 8, of which waited for: 4 -> 4; matrix products, arithmetic and copies ran while one was open for 0% -> 1% of each run, Pallas kernels for 17% -> 29%
where the time goes in v6:
time: 62.3 us; the launch traced here: 61.7 us
  Pallas kernels  29.2 us (47%)
  starting transfers between devices  18.9 us (30%)
  waiting for transfers between devices  8.52 us (14%)
  local copies, waits for them, and re-layouts  3.29 us (5%)
  other arithmetic  0.93 us (1%)
  between operations  0.91 us (1%)
    pallas_call x12, Pallas kernels, call(): pl.pallas_call(kernel, out_shape=[jax.ShapeDtypeStruct(s, d) if i in in_h...  29.2 us
    ppermute x6, starting transfers between devices, exchange(): return (lax.ppermute(a, 'dom', near), lax.ppermute(b, 'dom', far))  9.85 us
    all_to_all x1, starting transfers between devices, on_device(): coupled = lax.all_to_all(sums, 'dom', 0, 0)  5.15 us
    all_to_all x1, starting transfers between devices, on_device(): totals = lax.all_to_all(sums, 'dom', 0, 0)  3.85 us
    ppermute x6, waiting for transfers between devices, exchange(): return (lax.ppermute(a, 'dom', near), lax.ppermute(b, 'dom', far))  3.34 us
    unnamed x26, local copies, waits for them, and re-layouts  3.17 us
    all_to_all x1, waiting for transfers between devices, on_device(): totals = lax.all_to_all(sums, 'dom', 0, 0)  2.88 us
    all_to_all x1, waiting for transfers between devices, on_device(): coupled = lax.all_to_all(sums, 'dom', 0, 0)  2.29 us
  transfers between devices with their start and end apart: 8, of which 4 were waited for; matrix products, arithmetic and copies ran while one was open for 1% of the time, Pallas kernels for 29%

profile of v6, /device:TPU:1, one launch (start us, length us, event | category | flops | bytes accessed | tf_op | source)
XLA Modules:
  0.0 61.7 jit_solution(2632507421456714103)
XLA Ops:
  0.7 0.7 %copy-done.10 = f32[6656]{0:T(1024)S(1)} copy-done((f32[6656]{0:T(1024)S(1)}, f32[6656]{0:T(1024)}, u32[]{:S(2)}) %copy-start.10) | copy-done | bytes 26648
  1.4 0.7 %fusion = (f32[8,512]{1,0:T(8,128)S(1)}, f32[8,512]{1,0:T(8,128)S(1)}) fusion(f32[8,6656]{1,0:T(8,128)} %rhs_ref.3, f32[512]{0:T(512)S(1)} %get-tuple-element.69, f32[512]{0:T(512)S(1)} %get-tuple-element.68, pred[]{:T(512)S(6)} %eq.5), kind=kLoop, calls=%fused_computation.4 | loop fusion | flops 16384 | bytes 69633 | tf_op jit(solution)/shard_map/jit(_where)/select_n | solution.py:518
  2.1 4.6 %collective-permute-start.1 = (f32[8,512]{1,0:T(8,128)S(1)}, f32[8,512]{1,0:T(8,128)S(1)}, u32[]{:S(2)}, u32[]{:S(2)}) collective-permute-start(f32[8,512]{1,0:T(8,128)S(1)} %get-tuple-element.66), channel_id=1, source_target_pairs={{1,2},{2,1},{3,4},{4,3},{5,6},{6,5},{7,8},{8,7},{9,10},{10,9},{11,... | collective-permute-start | bytes 49160 | tf_op jit(solution)/shard_map/ppermute | solution.py:498
  7.1 2.2 %shard_map.140 = (s32[32,1,384]{2,1,0:T(1,128)S(1)}, s32[1,128]{1,0:T(1,128)S(1)}, s32[33]{0:T(128)S(1)}, s32[33]{0:T(128)S(1)}) custom-call(s32[32]{0:T(128)S(1)} %get-tuple-element.65.low_ref, s32[32]{0:T(128)S(1)} %get-tuple-element.64.high_ref, s32[32,343]{1,0:T(8,128)S(1)} %copy-done.2), custom_call_target="tpu_custom_call" | custom-call | tf_op jit(solution)/shard_map/pallas_call | solution.py:502
  9.3 1.0 %copy-done.1 = f32[343,343]{1,0:T(8,128)S(1)} copy-done((f32[343,343]{1,0:T(8,128)S(1)}, f32[343,343]{1,0:T(8,128)}, u32[]{:S(2)}) %copy-start.1) | copy-done | bytes 470620
  10.5 0.8 %copy-done = f32[8,6656]{1,0:T(8,128)S(1)} copy-done((f32[8,6656]{1,0:T(8,128)S(1)}, f32[8,6656]{1,0:T(8,128)}, u32[]{:S(2)}) %copy-start) | copy-done | bytes 213016
  11.3 3.0 %shard_map.141 = (f32[8,9472]{1,0:T(8,128)S(1)}, f32[256,384]{1,0:T(8,128)S(1)}, f32[1,128]{1,0:T(1,128)S(1)}) custom-call(s32[32]{0:T(128)S(1)} %get-tuple-element.65.low_ref, s32[32]{0:T(128)S(1)} %get-tuple-element.64.high_ref, s32[33]{0:T(128)S(1)} %get-tuple-element.33.list_ref, f32[8,6656]{1,0:T(8,128)S(1)} %copy-done, ...), custom_call_target="tpu_custom_call" | custom-call | tf_op jit(solution)/shard_map/pallas_call | solution.py:502
  15.0 2.3 %shard_map.143 = (f32[8,9472]{1,0:T(8,128)S(1)}, f32[2,7680]{1,0:T(2,128)S(1)}, f32[32,4,128]{2,1,0:T(4,128)}, f32[256,384]{1,0:T(8,128)S(1)}) custom-call(s32[1]{0:T(128)} %bitcast.pos_ref, s32[32]{0:T(128)S(1)} %copy-done.8, f32[32]{0:T(128)S(1)} %copy-done.9, s32[8]{0:T(128)S(1)} %copy-done.5, s32[8]{0:T(128)S(1)} %copy-done.6, s32[32]{0:T(128)S(1)} %copy-done.7, ...), custom_call_target="tpu_custom_call" | custom-call | tf_op jit(solution)/shard_map/pallas_call | solution.py:502
  17.3 5.1 %all-to-all-start = ((f32[32,4,128]{2,1,0:T(4,128)}), f32[32,4,128]{2,1,0:T(4,128)S(1)}, u32[]{:S(2)}, u32[]{:S(2)}) async-start(f32[32,4,128]{2,1,0:T(4,128)} %get-tuple-element.42), calls=%async_computation | async-start | bytes 131072 | tf_op jit(solution)/shard_map/all_to_all | solution.py:559
  22.4 5.0 %shard_map.144.cells_ref = f32[8,7680]{1,0:T(8,128)S(1)} custom-call(s32[32]{0:T(128)S(1)} %get-tuple-element.65.low_ref, s32[32]{0:T(128)S(1)} %get-tuple-element.64.high_ref, s32[32,1,384]{2,1,0:T(1,128)S(1)} %get-tuple-element.34.index_ref, s32[1,128]{1,0:T(1,128)S(1)} %get-tuple-element.37.corner_ref, f32[256,384]{1,0:T(8,128)S(1)} %get-tuple-element.43.refs_0_, ...), custom_call_target="tpu_custom_call" | custom-call | tf_op jit(solution)/shard_map/pallas_call | solution.py:502
  27.4 2.3 %all-to-all-done.sums_ref.coupling_ref = f32[32,4,128]{2,1,0:T(4,128)S(1)} async-done(((f32[32,4,128]{2,1,0:T(4,128)}), f32[32,4,128]{2,1,0:T(4,128)S(1)}, u32[]{:S(2)}, u32[]{:S(2)}) %all-to-all-start) | async-done | bytes 65568 | tf_op jit(solution)/shard_map/all_to_all | solution.py:559
  29.7 2.3 %shard_map.145 = (f32[8,7680]{1,0:T(8,128)S(1)}, f32[10,1024]{1,0:T(8,128)S(1)}, f32[10,1024]{1,0:T(8,128)S(1)}) custom-call(s32[1]{0:T(128)} %bitcast.pos_ref, s32[8]{0:T(128)S(1)} %copy-done.5, s32[8]{0:T(128)S(1)} %copy-done.6, s32[32]{0:T(128)S(1)} %copy-done.7, s32[32]{0:T(128)S(1)} %get-tuple-element.65.low_ref, s32[32]{0:T(128)S(1)} %get-tuple-element.64.high_ref, ...), custom_call_target="tpu_custom_call" | custom-call | tf_op jit(solution)/shard_map/pallas_call | solution.py:502
  32.5 2.2 %collective-permute-start.3 = (f32[10,1024]{1,0:T(8,128)S(1)}, f32[10,1024]{1,0:T(8,128)S(1)}, u32[]{:S(2)}, u32[]{:S(2)}) collective-permute-start(f32[10,1024]{1,0:T(8,128)S(1)} %get-tuple-element.52), channel_id=1, source_target_pairs={{1,2},{2,1},{3,4},{4,3},{5,6},{6,5},{7,8},{8,7},{9,10},{10,9},{11,... | collective-permute-start | bytes 122888 | tf_op jit(solution)/shard_map/ppermute | solution.py:498
  34.8 2.4 %shard_map.146 = (f32[8,7680]{1,0:T(8,128)S(1)}, f32[8,9472]{1,0:T(8,128)S(1)}, f32[256,384]{1,0:T(8,128)S(1)}) custom-call(s32[32]{0:T(128)S(1)} %get-tuple-element.65.low_ref, s32[32]{0:T(128)S(1)} %get-tuple-element.64.high_ref, s32[33]{0:T(128)S(1)} %get-tuple-element.41.list_ref, f32[8,9472]{1,0:T(8,128)S(1)} %get-tuple-element.39.p_ref, ...), custom_call_target="tpu_custom_call" | custom-call | tf_op jit(solution)/shard_map/pallas_call | solution.py:502
  37.2 1.1 %collective-permute-done.3.halo_b_ref = f32[10,1024]{1,0:T(8,128)S(1)} collective-permute-done((f32[10,1024]{1,0:T(8,128)S(1)}, f32[10,1024]{1,0:T(8,128)S(1)}, u32[]{:S(2)}, u32[]{:S(2)}) %collective-permute-start.3) | collective-permute-done | bytes 40992 | tf_op jit(solution)/shard_map/ppermute | solution.py:498
  38.3 3.6 %shard_map.147 = (f32[8,7680]{1,0:T(8,128)S(1)}, f32[8,9472]{1,0:T(8,128)S(1)}, f32[32,4,128]{2,1,0:T(4,128)}, f32[256,384]{1,0:T(8,128)S(1)}) custom-call(s32[1]{0:T(128)} %bitcast.pos_ref, s32[32]{0:T(128)S(1)} %copy-done.8, f32[32]{0:T(128)S(1)} %copy-done.9, s32[8]{0:T(128)S(1)} %copy-done.5, s32[8]{0:T(128)S(1)} %copy-done.6, s32[32]{0:T(128)S(1)} %copy-done.7, ...), custom_call_target="tpu_custom_call" | custom-call | tf_op jit(solution)/shard_map/pallas_call | solution.py:502
  41.8 3.9 %all-to-all-start.1 = ((f32[32,4,128]{2,1,0:T(4,128)}), f32[32,4,128]{2,1,0:T(4,128)S(1)}, u32[]{:S(2)}, u32[]{:S(2)}) async-start(f32[32,4,128]{2,1,0:T(4,128)} %get-tuple-element.55), calls=%async_computation.1 | async-start | bytes 131072 | tf_op jit(solution)/shard_map/all_to_all | solution.py:589
  45.7 4.4 %shard_map.148.cells_ref = f32[8,7680]{1,0:T(8,128)S(1)} custom-call(s32[32]{0:T(128)S(1)} %get-tuple-element.65.low_ref, s32[32]{0:T(128)S(1)} %get-tuple-element.64.high_ref, s32[32,1,384]{2,1,0:T(1,128)S(1)} %get-tuple-element.34.index_ref, s32[1,128]{1,0:T(1,128)S(1)} %get-tuple-element.37.corner_ref, f32[256,384]{1,0:T(8,128)S(1)} %get-tuple-element.56.refs_0_), custom_call_target="tpu_custom_call" | custom-call | tf_op jit(solution)/shard_map/pallas_call | solution.py:502
  50.1 2.9 %all-to-all-done.1.sums_ref = f32[32,4,128]{2,1,0:T(4,128)S(1)} async-done(((f32[32,4,128]{2,1,0:T(4,128)}), f32[32,4,128]{2,1,0:T(4,128)S(1)}, u32[]{:S(2)}, u32[]{:S(2)}) %all-to-all-start.1) | async-done | bytes 65568 | tf_op jit(solution)/shard_map/all_to_all | solution.py:589
  53.0 2.3 %shard_map.149 = (f32[8,7680]{1,0:T(8,128)S(1)}, f32[8,1024]{1,0:T(8,128)S(1)}, f32[8,1024]{1,0:T(8,128)S(1)}, f32[1,128]{1,0:T(1,128)S(1)}) custom-call(s32[1]{0:T(128)} %bitcast.pos_ref, s32[8]{0:T(128)S(1)} %copy-done.5, s32[8]{0:T(128)S(1)} %copy-done.6, s32[32]{0:T(128)S(1)} %copy-done.7, s32[32]{0:T(128)S(1)} %get-tuple-element.65.low_ref, ...), custom_call_target="tpu_custom_call" | custom-call | tf_op jit(solution)/shard_map/pallas_call | solution.py:502
  55.7 2.1 %collective-permute-start.5 = (f32[8,1024]{1,0:T(8,128)S(1)}, f32[8,1024]{1,0:T(8,128)S(1)}, u32[]{:S(2)}, u32[]{:S(2)}) collective-permute-start(f32[8,1024]{1,0:T(8,128)S(1)} %get-tuple-element.62), channel_id=1, source_target_pairs={{1,2},{2,1},{3,4},{4,3},{5,6},{6,5},{7,8},{8,7},{9,10},{10,9},{11,... | collective-permute-start | bytes 98312 | tf_op jit(solution)/shard_map/ppermute | solution.py:498
  57.8 0.9 %shard_map.150 = (f32[8,6656]{1,0:T(8,128)}, f32[8,6656]{1,0:T(8,128)S(1)}, f32[8,128]{1,0:T(8,128)S(1)}) custom-call(f32[8,6656]{1,0:T(8,128)S(1)} %copy-done, f32[8,9472]{1,0:T(8,128)S(1)} %get-tuple-element.39.p_ref, f32[2,7680]{1,0:T(2,128)S(1)} %get-tuple-element.40.diag_ref.diag_in_ref, f32[8,1]{1,0:T(8,128)S(1)} %copy.17.shift_ref, ...), custom_call_target="tpu_custom_call" | custom-call | tf_op jit(solution)/shard_map/pallas_call | solution.py:502
  58.7 2.2 %collective-permute-done.5.halo_b_ref = f32[8,1024]{1,0:T(8,128)S(1)} collective-permute-done((f32[8,1024]{1,0:T(8,128)S(1)}, f32[8,1024]{1,0:T(8,128)S(1)}, u32[]{:S(2)}, u32[]{:S(2)}) %collective-permute-start.5) | collective-permute-done | bytes 32800 | tf_op jit(solution)/shard_map/ppermute | solution.py:498
  61.0 0.8 %shard_map.151 = f32[8,6656]{1,0:T(8,128)} custom-call(s32[1]{0:T(128)} %bitcast.pos_ref, f32[8,6656]{1,0:T(8,128)S(1)} %get-tuple-element.60.residual_in_ref, f32[8,1024]{1,0:T(8,128)S(1)} %collective-permute-done.4.halo_a_ref, f32[8,1024]{1,0:T(8,128)S(1)} %collective-permute-done.5.halo_b_ref, f32[8,128]{1,0:T(8,128)S(1)} %get-tuple-element.63.factor_ref), custom_call_target="tpu_custom_call" | custom-call | tf_op jit(solution)/shard_map/pallas_call | solution.py:502
  (36 shorter events, 2.2 us)
Async XLA Ops:
  0.6 0.7 %copy-start.10 = (f32[6656]{0:T(1024)S(1)}, f32[6656]{0:T(1024)}, u32[]{:S(2)}) copy-start(f32[6656]{0:T(1024)} %param.15) | copy-start | bytes 79876
  0.6 6.2 %copy-start.2 = (s32[32,343]{1,0:T(8,128)S(1)}, s32[32,343]{1,0:T(8,128)}, u32[]{:S(2)}) copy-start(s32[32,343]{1,0:T(8,128)} %conn_ref.1) | copy-start | bytes 131716
  2.1 5.0 %copy-start.11 = (f32[6656]{0:T(1024)S(1)}, f32[6656]{0:T(1024)}, u32[]{:S(2)}) copy-start(f32[6656]{0:T(1024)} %param.14) | copy-start | bytes 79876
  2.1 12.2 %collective-permute-start.1 = (f32[8,512]{1,0:T(8,128)S(1)}, f32[8,512]{1,0:T(8,128)S(1)}, u32[]{:S(2)}, u32[]{:S(2)}) collective-permute-start(f32[8,512]{1,0:T(8,128)S(1)} %get-tuple-element.66), channel_id=1, source_target_pairs={{1,2},{2,1},{3,4},{4,3},{5,6},{6,5},{7,8},{8,7},{9,10},{10,9},{11,... | collective-permute-start | bytes 49160 | tf_op jit(solution)/shard_map/ppermute | solution.py:498
  6.8 2.5 %copy-start.3 = (f32[8,8,343]{2,1,0:T(8,128)S(1)}, f32[8,8,343]{2,1,0:T(8,128)}, u32[]{:S(2)}) copy-start(f32[8,8,343]{2,1,0:T(8,128)} %param.21) | copy-start | bytes 263428
  6.8 7.6 %collective-permute-start = (f32[8,512]{1,0:T(8,128)S(1)}, f32[8,512]{1,0:T(8,128)S(1)}, u32[]{:S(2)}, u32[]{:S(2)}) collective-permute-start(f32[8,512]{1,0:T(8,128)S(1)} %get-tuple-element.67), channel_id=1, source_target_pairs={{0,1},{1,0},{2,3},{3,2},{4,5},{5,4},{6,7},{7,6},{8,9},{9,8},{10,11... | collective-permute-start | bytes 49160 | tf_op jit(solution)/shard_map/ppermute | solution.py:498
  9.3 1.0 %copy-start.1 = (f32[343,343]{1,0:T(8,128)S(1)}, f32[343,343]{1,0:T(8,128)}, u32[]{:S(2)}) copy-start(f32[343,343]{1,0:T(8,128)} %stiffness_ref.1) | copy-start | bytes 1411792
  10.3 0.9 %copy-start = (f32[8,6656]{1,0:T(8,128)S(1)}, f32[8,6656]{1,0:T(8,128)}, u32[]{:S(2)}) copy-start(f32[8,6656]{1,0:T(8,128)} %rhs_ref.3) | copy-start | bytes 638980
  11.3 3.1 %copy-start.7 = (s32[32]{0:T(128)S(1)}, s32[32]{0:T(128)}, u32[]{:S(2)}) copy-start(s32[32]{0:T(128)} %scount_ref.7) | copy-start | bytes 388
  11.3 3.1 %copy-start.8 = (s32[32]{0:T(128)S(1)}, s32[32]{0:T(128)}, u32[]{:S(2)}) copy-start(s32[32]{0:T(128)} %count_ref.3) | copy-start | bytes 388
  11.3 3.1 %copy-start.9 = (f32[32]{0:T(128)S(1)}, f32[32]{0:T(128)}, u32[]{:S(2)}) copy-start(f32[32]{0:T(128)} %scale_ref.3) | copy-start | bytes 388
  14.3 0.7 %copy-start.4 = (f32[2,8,8]{2,1,0:T(8,128)S(1)}, f32[2,8,8]{2,1,0:T(8,128)}, u32[]{:S(2)}) copy-start(f32[2,8,8]{2,1,0:T(8,128)} %coupling_ref.1) | copy-start | bytes 1540
  14.3 0.7 %copy-start.5 = (s32[8]{0:T(128)S(1)}, s32[8]{0:T(128)}, u32[]{:S(2)}) copy-start(s32[8]{0:T(128)} %cell_ref.7) | copy-start | bytes 100
  14.4 0.7 %copy-start.6 = (s32[8]{0:T(128)S(1)}, s32[8]{0:T(128)}, u32[]{:S(2)}) copy-start(s32[8]{0:T(128)} %atom_ref.7) | copy-start | bytes 100
  17.3 12.4 %all-to-all-start = ((f32[32,4,128]{2,1,0:T(4,128)}), f32[32,4,128]{2,1,0:T(4,128)S(1)}, u32[]{:S(2)}, u32[]{:S(2)}) async-start(f32[32,4,128]{2,1,0:T(4,128)} %get-tuple-element.42), calls=%async_computation | async-start | bytes 131072 | tf_op jit(solution)/shard_map/all_to_all | solution.py:559
  32.0 5.1 %collective-permute-start.2 = (f32[10,1024]{1,0:T(8,128)S(1)}, f32[10,1024]{1,0:T(8,128)S(1)}, u32[]{:S(2)}, u32[]{:S(2)}) collective-permute-start(f32[10,1024]{1,0:T(8,128)S(1)} %get-tuple-element.51), channel_id=1, source_target_pairs={{0,1},{1,0},{2,3},{3,2},{4,5},{5,4},{6,7},{7,6},{8,9},{9,8},{10,11... | collective-permute-start | bytes 122888 | tf_op jit(solution)/shard_map/ppermute | solution.py:498
  32.5 2.2 %copy-start.12 = (f32[8]{0:T(128)S(1)}, f32[8]{0:T(128)}, u32[]{:S(2)}) copy-start(f32[8]{0:T(128)} %param.16) | copy-start | bytes 100
  32.5 5.8 %collective-permute-start.3 = (f32[10,1024]{1,0:T(8,128)S(1)}, f32[10,1024]{1,0:T(8,128)S(1)}, u32[]{:S(2)}, u32[]{:S(2)}) collective-permute-start(f32[10,1024]{1,0:T(8,128)S(1)} %get-tuple-element.52), channel_id=1, source_target_pairs={{1,2},{2,1},{3,4},{4,3},{5,6},{6,5},{7,8},{8,7},{9,10},{10,9},{11,... | collective-permute-start | bytes 122888 | tf_op jit(solution)/shard_map/ppermute | solution.py:498
  41.8 11.1 %all-to-all-start.1 = ((f32[32,4,128]{2,1,0:T(4,128)}), f32[32,4,128]{2,1,0:T(4,128)S(1)}, u32[]{:S(2)}, u32[]{:S(2)}) async-start(f32[32,4,128]{2,1,0:T(4,128)} %get-tuple-element.55), calls=%async_computation.1 | async-start | bytes 131072 | tf_op jit(solution)/shard_map/all_to_all | solution.py:589
  55.3 3.5 %collective-permute-start.4 = (f32[8,1024]{1,0:T(8,128)S(1)}, f32[8,1024]{1,0:T(8,128)S(1)}, u32[]{:S(2)}, u32[]{:S(2)}) collective-permute-start(f32[8,1024]{1,0:T(8,128)S(1)} %get-tuple-element.61), channel_id=1, source_target_pairs={{0,1},{1,0},{2,3},{3,2},{4,5},{5,4},{6,7},{7,6},{8,9},{9,8},{10,11... | collective-permute-start | bytes 98312 | tf_op jit(solution)/shard_map/ppermute | solution.py:498
  55.7 5.2 %collective-permute-start.5 = (f32[8,1024]{1,0:T(8,128)S(1)}, f32[8,1024]{1,0:T(8,128)S(1)}, u32[]{:S(2)}, u32[]{:S(2)}) collective-permute-start(f32[8,1024]{1,0:T(8,128)S(1)} %get-tuple-element.62), channel_id=1, source_target_pairs={{1,2},{2,1},{3,4},{4,3},{5,6},{6,5},{7,8},{8,7},{9,10},{10,9},{11,... | collective-permute-start | bytes 98312 | tf_op jit(solution)/shard_map/ppermute | solution.py:498

commit v7 on v6

--- a/solution.py
+++ b/solution.py
@@ -13,7 +13,7 @@
 CHAINS = 4
 SPAN = 14
 BAND = 8
-TOGETHER = 4
+TOGETHER = 8
 F32 = jnp.float32
 BF16 = jnp.bfloat16
 HIGHEST = lax.Precision.HIGHEST
@@ -65,19 +65,7 @@
     return jnp.sum(jnp.where(iota((ROWS, LANES), 1) == iota((ROWS, LANES), 0), spread, 0.0), axis=0, keepdims=True)
 
 
-def list_cells(z, margin, low_ref, high_ref, list_ref):
-    def place(c, counts):
-        inside, outside = counts
-        good = (low_ref[c] + z.shift >= margin) & (high_ref[c] + z.shift < z.window - margin)
-        list_ref[jnp.where(good, inside, z.slots - 1 - outside)] = c
-        one = good.astype(jnp.int32)
-        return inside + one, outside + 1 - one
-
-    inside, _ = lax.fori_loop(0, z.slots, place, (jnp.int32(0), jnp.int32(0)))
-    list_ref[z.slots] = inside // z.together
-
-
-def prepare_kernel(z, low_ref, high_ref, conn_ref, index_ref, corner_ref, first_list_ref, second_list_ref):
+def prepare_kernel(z, conn_ref, index_ref, corner_ref):
     line = iota((1, LANES), 1)
     corner = jnp.zeros((1, LANES), jnp.int32)
     index_ref[...] = jnp.zeros_like(index_ref)
@@ -87,16 +75,18 @@
         corner = jnp.where(line == c, row[:, :1], corner)
         corner = jnp.where(line == z.slots + c, row[:, z.elem - 1 :], corner)
     corner_ref[...] = corner
-    list_cells(z, z.rim, low_ref, high_ref, first_list_ref)
-    list_cells(z, 2 * z.rim, low_ref, high_ref, second_list_ref)
-
-
-def pad_kernel(z, stiffness_ref, projector_ref, k_high_ref, k_low_ref, pj_ref, k_ref):
-    k_ref[...] = jnp.zeros_like(k_ref)
-    k_ref[: z.elem, : z.elem] = stiffness_ref[...]
-    k_high_ref[...], k_low_ref[...] = split(k_ref[...])
-    pj_ref[...] = jnp.zeros_like(pj_ref)
-    pj_ref[:, : z.elem] = projector_ref[...]
+
+
+def start_kernel(z, pos_ref, rhs_ref, precond_ref, p_ref, send_a_ref, send_b_ref, gamma_ref):
+    product = rhs_ref[...] * precond_ref[...]
+    own = slice(z.rim, z.rim + z.nodes)
+    p_ref[:, own] = product
+    p_ref[:, z.window :] = jnp.zeros((ROWS, z.reach - z.window), F32)
+    gamma_ref[...] = lanes_by_vector(z, product * rhs_ref[...])
+    head, tail = product[:, : z.rim], product[:, z.nodes - z.rim :]
+    even = pos_ref[0] % 2 == 0
+    send_a_ref[...] = jnp.where(even, tail, head)
+    send_b_ref[...] = jnp.where(even, head, tail)
 
 
 def gather_middle(z, groups, list_ref, index_ref, low_ref, high_ref, window_ref, u_ref):
@@ -193,20 +183,14 @@
     return jnp.where(even, far, near), jnp.where(even, near, far)
 
 
-def first_window_kernel(
-    z, low_ref, high_ref, list_ref, rhs_ref, precond_ref, index_ref, p_ref, u_ref, gamma_ref,
-):
-    product = rhs_ref[...] * precond_ref[...]
-    p_ref[:, z.rim : z.rim + z.nodes] = product
-    gamma_ref[...] = lanes_by_vector(z, product * rhs_ref[...])
-    p_ref[:, z.window :] = jnp.zeros((ROWS, z.reach - z.window), F32)
-    gather_middle(z, (0, list_ref[z.slots]), list_ref, index_ref, low_ref, high_ref, p_ref, u_ref)
+def first_window_kernel(z, low_ref, high_ref, list_ref, groups_ref, p_ref, index_ref, u_ref):
+    gather_middle(z, (0, groups_ref[0]), list_ref, index_ref, low_ref, high_ref, p_ref, u_ref)
 
 
 def first_kernel(
-    z, pos_ref, count_ref, scale_ref, cell_ref, atom_ref, scount_ref, low_ref, high_ref, list_ref, p_in_ref, u_in_ref,
-    precond_ref, potential_ref, halo_a_ref, halo_b_ref, index_ref, corner_ref, pj_ref, coupling_ref,
-    p_ref, diag_ref, out_ref, uw_ref, u_ref,
+    z, pos_ref, count_ref, scale_ref, cell_ref, atom_ref, scount_ref, low_ref, high_ref, list_ref, groups_ref,
+    p_in_ref, u_in_ref, precond_ref, potential_ref, halo_a_ref, halo_b_ref, index_ref, corner_ref, projector_ref,
+    coupling_ref, p_ref, diag_ref, out_ref, uw_ref, pj_ref, u_ref,
 ):
     position = pos_ref[0]
     own = slice(z.rim, z.rim + z.nodes)
@@ -217,7 +201,9 @@
     diag_ref[...] = jnp.zeros_like(diag_ref)
     diag_ref[0:1, own] = precond_ref[...]
     diag_ref[1:2, own] = potential_ref[...]
-    groups = list_ref[z.slots], z.slots // z.together
+    pj_ref[...] = jnp.zeros_like(pj_ref)
+    pj_ref[:, : z.elem] = projector_ref[...]
+    groups = groups_ref[0], z.slots // z.together
     gather_middle(z, groups, list_ref, index_ref, low_ref, high_ref, p_ref, u_ref)
     gather_corners(z, corner_ref, p_ref, scale_ref, count_ref[position], u_ref, uw_ref)
     parts = contributions(z, position, pj_ref, cell_ref, atom_ref, scount_ref, u_ref)
@@ -233,17 +219,17 @@
 
 
 def second_window_kernel(
-    z, low_ref, high_ref, list_ref, p_ref, diag_ref, shift_ref, image_ref, index_ref, y_ref, q_ref, u_ref,
+    z, low_ref, high_ref, list_ref, groups_ref, p_ref, diag_ref, shift_ref, image_ref, index_ref, y_ref, q_ref, u_ref,
 ):
     y_ref[...] = image_ref[...] + (diag_ref[1:2, :] + shift_ref[...]) * p_ref[:, : z.window]
     q_ref[:, : z.window] = y_ref[...] * diag_ref[0:1, :]
     q_ref[:, z.window :] = jnp.zeros((ROWS, z.reach - z.window), F32)
-    gather_middle(z, (0, list_ref[z.slots]), list_ref, index_ref, low_ref, high_ref, q_ref, u_ref)
+    gather_middle(z, (0, groups_ref[0]), list_ref, index_ref, low_ref, high_ref, q_ref, u_ref)
 
 
 def second_kernel(
-    z, pos_ref, count_ref, scale_ref, cell_ref, atom_ref, scount_ref, low_ref, high_ref, list_ref, y_in_ref, q_in_ref,
-    u_in_ref, p_ref, diag_in_ref, shift_ref, gamma_ref, halo_a_ref, halo_b_ref, index_ref, corner_ref, k_high_ref,
+    z, pos_ref, count_ref, scale_ref, cell_ref, atom_ref, scount_ref, low_ref, high_ref, list_ref, groups_ref,
+    y_in_ref, q_in_ref, u_in_ref, p_ref, diag_in_ref, shift_ref, gamma_ref, halo_a_ref, halo_b_ref, index_ref, corner_ref, k_high_ref,
     k_low_ref, pj_ref, y_ref, q_ref, out_ref, e_ref, diag_ref, u_ref, uw_ref,
 ):
     position = pos_ref[0]
@@ -269,7 +255,7 @@
         lanes_by_vector(z, y * q),
     ]
     energy = jnp.sum(q * q * (diag_ref[1:2, own] + shift_ref[...]), axis=1, keepdims=True)
-    groups = list_ref[z.slots], z.slots // z.together
+    groups = groups_ref[0], z.slots // z.together
     gather_middle(z, groups, list_ref, index_ref, low_ref, high_ref, q_ref, u_ref)
     gather_corners(z, corner_ref, q_ref, scale_ref, count_ref[position], u_ref, uw_ref)
     parts = contributions(z, position, pj_ref, cell_ref, atom_ref, scount_ref, u_ref)
@@ -361,7 +347,10 @@
 
 def cells_kernel(z, multiply, low_ref, high_ref, index_ref, corner_ref, *refs):
     if multiply:
-        uw_ref, k_high_ref, k_low_ref, image_ref, e_ref, acc_ref = refs
+        uw_ref, stiffness_ref, image_ref, k_high_ref, k_low_ref, e_ref, k_ref, acc_ref = refs
+        k_ref[...] = jnp.zeros_like(k_ref)
+        k_ref[: z.elem, : z.elem] = stiffness_ref[...]
+        k_high_ref[...], k_low_ref[...] = split(k_ref[...])
         stiffness_product(k_high_ref, k_low_ref, uw_ref, e_ref)
     else:
         e_ref, image_ref, acc_ref = refs
@@ -497,28 +486,34 @@
     def exchange(a, b):
         return lax.ppermute(a, "dom", near), lax.ppermute(b, "dom", far)
 
-    def call(kernel, outs, scratch, scalars, *args, in_hbm=(), in_smem=()):
+    def call(kernel, outs, scratch, scalars, *args, in_hbm=()):
         args = [pltpu.with_memory_space_constraint(x, pltpu.VMEM) for x in args]
         return pl.pallas_call(
             kernel,
             out_shape=[
-                jax.ShapeDtypeStruct(s, d) if i in in_hbm + in_smem else pltpu.VMEM(s, d)
-                for i, (s, d) in enumerate(outs)
+                jax.ShapeDtypeStruct(s, d) if i in in_hbm else pltpu.VMEM(s, d) for i, (s, d) in enumerate(outs)
             ],
             in_specs=[SMEM] * len(scalars) + [VMEM] * len(args),
-            out_specs=[SMEM if i in in_smem else VMEM for i in range(len(outs))],
+            out_specs=[VMEM] * len(outs),
             scratch_shapes=[pltpu.VMEM(s, d) for s, d in scratch],
             compiler_params=pltpu.CompilerParams(vmem_limit_bytes=16 * 1024 * 1024),
         )(*scalars, *args)
 
     precond_row, potential_row = precond[None, :], potential[None, :]
     shift_column = shift[:, None]
-    head = rhs[:, : z.rim] * precond[: z.rim]
-    tail = rhs[:, z.nodes - z.rim :] * precond[z.nodes - z.rim :]
-    halo = exchange(jnp.where(even, tail, head), jnp.where(even, head, tail))
     flat_projector = projector.reshape(z.entries * z.channels, z.elem)
     middle = conn[:, 1:-1]
     ranges = jnp.min(middle, axis=1), jnp.max(middle, axis=1)
+
+    def listed(margin):
+        good = (ranges[0] + z.shift >= margin) & (ranges[1] + z.shift < z.window - margin)
+        one = good.astype(jnp.int32)
+        number = jnp.arange(z.slots)
+        before = jnp.sum(jnp.where(number[None, :] < number[:, None], one[None, :], 0), axis=1)
+        total = jnp.sum(one)
+        place = jnp.where(good, before, total + number - before)
+        order = jnp.sum(jnp.where(place[None, :] == number[:, None], number[None, :], 0), axis=1)
+        return order.astype(jnp.int32), (total // z.together).astype(jnp.int32).reshape(1)
 
     cells = (z.slots * ROWS, z.width)
     window, reach, own = (z.vectors, z.window), (z.vectors, z.reach), (z.vectors, z.nodes)
@@ -528,41 +523,39 @@
     acc = ((z.window // WIDE + BAND) * 2 * ROWS, WIDE)
     supports = support_cell, support_atom, support_count
 
-    index, corner, first_list, second_list = call(
+    p, send_a, send_b, gamma = call(
+        functools.partial(start_kernel, z),
+        [(reach, F32), ((z.vectors, z.rim), F32), ((z.vectors, z.rim), F32), ((1, LANES), F32)],
+        [],
+        (pos,),
+        rhs, precond_row,
+    )
+    halo = exchange(send_a, send_b)
+    first_list, second_list = listed(z.rim), listed(2 * z.rim)
+    index, corner = call(
         functools.partial(prepare_kernel, z),
-        [((z.slots, 1, z.width), jnp.int32), ((1, LANES), jnp.int32)] + [((z.slots + 1,), jnp.int32)] * 2,
+        [((z.slots, 1, z.width), jnp.int32), ((1, LANES), jnp.int32)],
         [],
+        (),
+        conn,
+    )
+    (u,) = call(
+        functools.partial(first_window_kernel, z), [(cells, F32)], [], (*ranges, *first_list), p, index,
+    )
+    p, diag, sums, uw, pj = call(
+        functools.partial(first_kernel, z),
+        [(reach, F32), ((2, z.window), F32), (message, F32), (cells, F32), (entries, F32)],
+        [(cells, F32)],
+        (pos, cell_count, cell_scale, *supports, *ranges, *first_list),
+        p, u, precond_row, potential_row, *halo, index, corner, flat_projector, atom_matrix,
+    )
+    coupled = lax.all_to_all(sums, "dom", 0, 0)
+    image, k_high, k_low = call(
+        functools.partial(cells_kernel, z, True),
+        [(window, F32), (square, BF16), (square, BF16)],
+        [(cells, F32), (square, F32), (acc, F32)],
         ranges,
-        conn, in_smem=(2, 3),
-    )
-    p, u, gamma = call(
-        functools.partial(first_window_kernel, z),
-        [(reach, F32), (cells, F32), ((1, LANES), F32)],
-        [],
-        (*ranges, first_list),
-        rhs, precond_row, index,
-    )
-    k_high, k_low, pj = call(
-        functools.partial(pad_kernel, z),
-        [(square, BF16), (square, BF16), (entries, F32)],
-        [(square, F32)],
-        (),
-        stiffness, flat_projector,
-    )
-    p, diag, sums, uw = call(
-        functools.partial(first_kernel, z),
-        [(reach, F32), ((2, z.window), F32), (message, F32), (cells, F32)],
-        [(cells, F32)],
-        (pos, cell_count, cell_scale, *supports, *ranges, first_list),
-        p, u, precond_row, potential_row, *halo, index, corner, pj, atom_matrix,
-    )
-    coupled = lax.all_to_all(sums, "dom", 0, 0)
-    (image,) = call(
-        functools.partial(cells_kernel, z, True),
-        [(window, F32)],
-        [(cells, F32), (acc, F32)],
-        ranges,
-        index, corner, uw, k_high, k_low,
+        index, corner, uw, stiffness,
     )
     image, send_a, send_b = call(
         functools.partial(support_kernel, z, False),
@@ -576,14 +569,14 @@
         functools.partial(second_window_kernel, z),
         [(window, F32), (reach, F32), (cells, F32)],
         [],
-        (*ranges, second_list),
+        (*ranges, *second_list),
         p, diag, shift_column, image, index,
     )
     y, q, sums, e = call(
         functools.partial(second_kernel, z),
         [(window, F32), (reach, F32), (message, F32), (cells, F32)],
         [((2, z.window), F32), (cells, F32), (cells, F32)],
-        (pos, cell_count, cell_scale, *supports, *ranges, second_list),
+        (pos, cell_count, cell_scale, *supports, *ranges, *second_list),
         y, q, u, p, diag, shift_column, gamma, *halo, index, corner, k_high, k_low, pj,
     )
     totals = lax.all_to_all(sums, "dom", 0, 0)

time: 62.3 us -> 63.7 us (1.022)
  between operations: 0.91 us -> 6.19 us
  Pallas kernels: 29.2 us -> 24.9 us
  other arithmetic: 0.93 us -> 2.6 us
    pallas_call x12, Pallas kernels: 29.2 us -> 24.9 us  [call(): pl.pallas_call(kernel, out_shape=[jax.ShapeDtypeStruct(s, d) if i in in_h...]
    ppermute x6, waiting for transfers between devices: 3.34 us -> 2.22 us  [exchange(): return (lax.ppermute(a, 'dom', near), lax.ppermute(b, 'dom', far))]
    reduce_sum x0 -> x5, other arithmetic: none -> 1.09 us  [the longest x1 0.64 us: listed(): total = jnp.sum(one)]
    unnamed x26, local copies, waits for them, and re-layouts: 3.17 us -> 2.25 us
    broadcast_in_dim x2, local copies, waits for them, and re-layouts: 0.04 us -> 0.79 us  [on_device(): precond_row, potential_row = (precond[None, :], potential[None, :])]
    all_to_all x1, waiting for transfers between devices: 2.88 us -> 3.52 us  [on_device(): totals = lax.all_to_all(sums, 'dom', 0, 0)]
    select_n x1 -> x2, other arithmetic: 0.74 us -> 1.31 us  [listed(): place = jnp.where(good, before, total + number - before)]
  transfers between devices with their start and end apart: 8 -> 8, of which waited for: 4 -> 3; matrix products, arithmetic and copies ran while one was open for 1% -> 4% of each run, Pallas kernels for 29% -> 20%
where the time goes in v7:
time: 63.7 us; the launch traced here: 63.1 us
  Pallas kernels  24.9 us (39%)
  starting transfers between devices  18.4 us (29%)
  waiting for transfers between devices  7.92 us (12%)
  between operations  6.19 us (10%)
  local copies, waits for them, and re-layouts  3.12 us (5%)
  other arithmetic  2.6 us (4%)
    pallas_call x12, Pallas kernels, call(): pl.pallas_call(kernel, out_shape=[jax.ShapeDtypeStruct(s, d) if i in in_h...  24.9 us
    ppermute x6, starting transfers between devices, exchange(): return (lax.ppermute(a, 'dom', near), lax.ppermute(b, 'dom', far))  9.52 us
    all_to_all x1, starting transfers between devices, on_device(): coupled = lax.all_to_all(sums, 'dom', 0, 0)  5.13 us
    all_to_all x1, starting transfers between devices, on_device(): totals = lax.all_to_all(sums, 'dom', 0, 0)  3.8 us
    all_to_all x1, waiting for transfers between devices, on_device(): totals = lax.all_to_all(sums, 'dom', 0, 0)  3.52 us
    unnamed x26, local copies, waits for them, and re-layouts  2.25 us
    ppermute x6, waiting for transfers between devices, exchange(): return (lax.ppermute(a, 'dom', near), lax.ppermute(b, 'dom', far))  2.22 us
    all_to_all x1, waiting for transfers between devices, on_device(): coupled = lax.all_to_all(sums, 'dom', 0, 0)  2.17 us
  transfers between devices with their start and end apart: 8, of which 3 were waited for; matrix products, arithmetic and copies ran while one was open for 4% of the time, Pallas kernels for 20%

profile of v7, /device:TPU:1, one launch (start us, length us, event | category | flops | bytes accessed | tf_op | source)
XLA Modules:
  0.0 63.1 jit_solution(18273830990621978866)
XLA Ops:
  0.6 0.8 %broadcast_in_dim.49.precond_ref = f32[1,6656]{1,0:T(1,128)S(1)} reshape(f32[6656]{0:T(1024)} %param.15) | data formatting | bytes 53248 | tf_op jit(solution)/shard_map/broadcast_in_dim | solution.py:502
  1.4 0.9 %copy-done = f32[8,6656]{1,0:T(8,128)S(1)} copy-done((f32[8,6656]{1,0:T(8,128)S(1)}, f32[8,6656]{1,0:T(8,128)}, u32[]{:S(2)}) %copy-start) | copy-done | bytes 213016
  2.5 4.5 %collective-permute-start.1 = (f32[8,512]{1,0:T(8,128)S(1)}, f32[8,512]{1,0:T(8,128)S(1)}, u32[]{:S(2)}, u32[]{:S(2)}) collective-permute-start(f32[8,512]{1,0:T(8,128)S(1)} %get-tuple-element.36), channel_id=1, source_target_pairs={{1,2},{2,1},{3,4},{4,3},{5,6},{6,5},{7,8},{8,7},{9,10},{10,9},{11,... | collective-permute-start | bytes 49160 | tf_op jit(solution)/shard_map/ppermute | solution.py:487
  7.2 0.6 %convert_reduce_fusion = (s32[]{:T(128)}, pred[32]{0:T(512)(128)(4,1)S(1)}, s32[]{:T(128)}, pred[32]{0:T(512)(128)(4,1)S(1)}) fusion(s32[32]{0:T(128)S(1)} %get-tuple-element.64.high_ref, s32[32]{0:T(128)S(1)} %get-tuple-element.65.low_ref), kind=kLoop, calls=%fused_computation.13 | loop fusion | flops 382 | bytes 328 | tf_op jit(solution)/shard_map/reduce_sum | solution.py:513
  8.1 0.7 %subtract_select_fusion.1 = s32[32]{0:T(128)S(1)} fusion(pred[32]{0:T(512)(128)(4,1)S(1)} %get-tuple-element.71, s32[32]{0:T(128)S(1)} %select_reduce_fusion.3, s32[]{:T(128)} %get-tuple-element.70), kind=kLoop, calls=%fused_computation.12 | loop fusion | flops 96 | bytes 292 | tf_op jit(solution)/shard_map/jit(_where)/select_n | solution.py:514
  11.8 1.7 %shard_map.142.u_in_ref = f32[256,384]{1,0:T(8,128)S(1)} custom-call(s32[32]{0:T(128)S(1)} %get-tuple-element.65.low_ref, s32[32]{0:T(128)S(1)} %get-tuple-element.64.high_ref, s32[32]{0:T(128)S(1)} %select_reduce_fusion.2.list_ref, s32[1]{0:T(128)} %bitcast.1.groups_ref, f32[8,9472]{1,0:T(8,128)S(1)} %get-tuple-element.33.p_ref.p_in_ref, ...), custom_call_target="tpu_custom_call" | custom-call | tf_op jit(solution)/shard_map/pallas_call | solution.py:491
  14.2 3.1 %shard_map.143 = (f32[8,9472]{1,0:T(8,128)S(1)}, f32[2,7680]{1,0:T(2,128)S(1)}, f32[32,4,128]{2,1,0:T(4,128)}, f32[256,384]{1,0:T(8,128)S(1)}, f32[64,384]{1,0:T(8,128)S(1)}) custom-call(s32[1]{0:T(128)} %bitcast.pos_ref, s32[32]{0:T(128)S(1)} %copy-done.9, f32[32]{0:T(128)S(1)} %copy-done.10, s32[8]{0:T(128)S(1)} %copy-done.6, s32[8]{0:T(128)S(1)} %copy-done.7, ...), custom_call_target="tpu_custom_call" | custom-call | tf_op jit(solution)/shard_map/pallas_call | solution.py:491
  17.3 5.1 %all-to-all-start = ((f32[32,4,128]{2,1,0:T(4,128)}), f32[32,4,128]{2,1,0:T(4,128)S(1)}, u32[]{:S(2)}, u32[]{:S(2)}) async-start(f32[32,4,128]{2,1,0:T(4,128)} %get-tuple-element.40), calls=%async_computation | async-start | bytes 131072 | tf_op jit(solution)/shard_map/all_to_all | solution.py:552
  22.5 0.7 %subtract_select_fusion = s32[32]{0:T(128)S(1)} fusion(pred[32]{0:T(512)(128)(4,1)S(1)} %get-tuple-element.67, s32[32]{0:T(128)S(1)} %select_reduce_fusion.1, s32[]{:T(128)} %get-tuple-element.66), kind=kLoop, calls=%fused_computation.11 | loop fusion | flops 96 | bytes 292 | tf_op jit(solution)/shard_map/jit(_where)/select_n | solution.py:514
  23.1 4.4 %shard_map.144 = (f32[8,7680]{1,0:T(8,128)S(1)}, bf16[384,384]{1,0:T(8,128)(2,1)S(1)}, bf16[384,384]{1,0:T(8,128)(2,1)S(1)}) custom-call(s32[32]{0:T(128)S(1)} %get-tuple-element.65.low_ref, s32[32]{0:T(128)S(1)} %get-tuple-element.64.high_ref, s32[32,1,384]{2,1,0:T(1,128)S(1)} %get-tuple-element.34.index_ref, s32[1,128]{1,0:T(1,128)S(1)} %get-tuple-element.37.corner_ref, ...), custom_call_target="tpu_custom_call" | custom-call | tf_op jit(solution)/shard_map/pallas_call | solution.py:491
  27.6 2.2 %all-to-all-done.sums_ref.coupling_ref = f32[32,4,128]{2,1,0:T(4,128)S(1)} async-done(((f32[32,4,128]{2,1,0:T(4,128)}), f32[32,4,128]{2,1,0:T(4,128)S(1)}, u32[]{:S(2)}, u32[]{:S(2)}) %all-to-all-start) | async-done | bytes 65568 | tf_op jit(solution)/shard_map/all_to_all | solution.py:552
  29.7 2.1 %shard_map.145 = (f32[8,7680]{1,0:T(8,128)S(1)}, f32[10,1024]{1,0:T(8,128)S(1)}, f32[10,1024]{1,0:T(8,128)S(1)}) custom-call(s32[1]{0:T(128)} %bitcast.pos_ref, s32[8]{0:T(128)S(1)} %copy-done.6, s32[8]{0:T(128)S(1)} %copy-done.7, s32[32]{0:T(128)S(1)} %copy-done.8, s32[32]{0:T(128)S(1)} %get-tuple-element.65.low_ref, s32[32]{0:T(128)S(1)} %get-tuple-element.64.high_ref, ...), custom_call_target="tpu_custom_call" | custom-call | tf_op jit(solution)/shard_map/pallas_call | solution.py:491
  32.3 2.1 %collective-permute-start.3 = (f32[10,1024]{1,0:T(8,128)S(1)}, f32[10,1024]{1,0:T(8,128)S(1)}, u32[]{:S(2)}, u32[]{:S(2)}) collective-permute-start(f32[10,1024]{1,0:T(8,128)S(1)} %get-tuple-element.50), channel_id=1, source_target_pairs={{1,2},{2,1},{3,4},{4,3},{5,6},{6,5},{7,8},{8,7},{9,10},{10,9},{11,... | collective-permute-start | bytes 122888 | tf_op jit(solution)/shard_map/ppermute | solution.py:487
  37.1 0.6 %copy-done.12 = f32[8]{0:T(128)S(1)} copy-done((f32[8]{0:T(128)S(1)}, f32[8]{0:T(128)}, u32[]{:S(2)}) %copy-start.12) | copy-done | bytes 56
  37.8 1.9 %shard_map.146 = (f32[8,7680]{1,0:T(8,128)S(1)}, f32[8,9472]{1,0:T(8,128)S(1)}, f32[256,384]{1,0:T(8,128)S(1)}) custom-call(s32[32]{0:T(128)S(1)} %get-tuple-element.65.low_ref, s32[32]{0:T(128)S(1)} %get-tuple-element.64.high_ref, s32[32]{0:T(128)S(1)} %select_reduce_fusion.list_ref, s32[1]{0:T(128)} %bitcast.4.groups_ref, ...), custom_call_target="tpu_custom_call" | custom-call | tf_op jit(solution)/shard_map/pallas_call | solution.py:491
  39.7 3.8 %shard_map.147 = (f32[8,7680]{1,0:T(8,128)S(1)}, f32[8,9472]{1,0:T(8,128)S(1)}, f32[32,4,128]{2,1,0:T(4,128)}, f32[256,384]{1,0:T(8,128)S(1)}) custom-call(s32[1]{0:T(128)} %bitcast.pos_ref, s32[32]{0:T(128)S(1)} %copy-done.9, f32[32]{0:T(128)S(1)} %copy-done.10, s32[8]{0:T(128)S(1)} %copy-done.6, s32[8]{0:T(128)S(1)} %copy-done.7, s32[32]{0:T(128)S(1)} %copy-done.8, ...), custom_call_target="tpu_custom_call" | custom-call | tf_op jit(solution)/shard_map/pallas_call | solution.py:491
  43.5 3.8 %all-to-all-start.1 = ((f32[32,4,128]{2,1,0:T(4,128)}), f32[32,4,128]{2,1,0:T(4,128)S(1)}, u32[]{:S(2)}, u32[]{:S(2)}) async-start(f32[32,4,128]{2,1,0:T(4,128)} %get-tuple-element.55), calls=%async_computation.1 | async-start | bytes 131072 | tf_op jit(solution)/shard_map/all_to_all | solution.py:582
  47.3 3.7 %shard_map.148.cells_ref = f32[8,7680]{1,0:T(8,128)S(1)} custom-call(s32[32]{0:T(128)S(1)} %get-tuple-element.65.low_ref, s32[32]{0:T(128)S(1)} %get-tuple-element.64.high_ref, s32[32,1,384]{2,1,0:T(1,128)S(1)} %get-tuple-element.34.index_ref, s32[1,128]{1,0:T(1,128)S(1)} %get-tuple-element.37.corner_ref, f32[256,384]{1,0:T(8,128)S(1)} %get-tuple-element.56.refs_0_), custom_call_target="tpu_custom_call" | custom-call | tf_op jit(solution)/shard_map/pallas_call | solution.py:491
  51.1 3.5 %all-to-all-done.1.sums_ref = f32[32,4,128]{2,1,0:T(4,128)S(1)} async-done(((f32[32,4,128]{2,1,0:T(4,128)}), f32[32,4,128]{2,1,0:T(4,128)S(1)}, u32[]{:S(2)}, u32[]{:S(2)}) %all-to-all-start.1) | async-done | bytes 65568 | tf_op jit(solution)/shard_map/all_to_all | solution.py:582
  54.6 2.1 %shard_map.149 = (f32[8,7680]{1,0:T(8,128)S(1)}, f32[8,1024]{1,0:T(8,128)S(1)}, f32[8,1024]{1,0:T(8,128)S(1)}, f32[1,128]{1,0:T(1,128)S(1)}) custom-call(s32[1]{0:T(128)} %bitcast.pos_ref, s32[8]{0:T(128)S(1)} %copy-done.6, s32[8]{0:T(128)S(1)} %copy-done.7, s32[32]{0:T(128)S(1)} %copy-done.8, s32[32]{0:T(128)S(1)} %get-tuple-element.65.low_ref, ...), custom_call_target="tpu_custom_call" | custom-call | tf_op jit(solution)/shard_map/pallas_call | solution.py:491
  57.2 2.0 %collective-permute-start.5 = (f32[8,1024]{1,0:T(8,128)S(1)}, f32[8,1024]{1,0:T(8,128)S(1)}, u32[]{:S(2)}, u32[]{:S(2)}) collective-permute-start(f32[8,1024]{1,0:T(8,128)S(1)} %get-tuple-element.62), channel_id=1, source_target_pairs={{1,2},{2,1},{3,4},{4,3},{5,6},{6,5},{7,8},{8,7},{9,10},{10,9},{11,... | collective-permute-start | bytes 98312 | tf_op jit(solution)/shard_map/ppermute | solution.py:487
  59.2 0.9 %shard_map.150 = (f32[8,6656]{1,0:T(8,128)}, f32[8,6656]{1,0:T(8,128)S(1)}, f32[8,128]{1,0:T(8,128)S(1)}) custom-call(f32[8,6656]{1,0:T(8,128)S(1)} %copy-done.1, f32[8,9472]{1,0:T(8,128)S(1)} %get-tuple-element.38.p_ref, f32[2,7680]{1,0:T(2,128)S(1)} %get-tuple-element.39.diag_ref.diag_in_ref, f32[8,1]{1,0:T(8,128)S(1)} %copy.20.shift_ref, ...), custom_call_target="tpu_custom_call" | custom-call | tf_op jit(solution)/shard_map/pallas_call | solution.py:491
  60.2 2.2 %collective-permute-done.5.halo_b_ref = f32[8,1024]{1,0:T(8,128)S(1)} collective-permute-done((f32[8,1024]{1,0:T(8,128)S(1)}, f32[8,1024]{1,0:T(8,128)S(1)}, u32[]{:S(2)}, u32[]{:S(2)}) %collective-permute-start.5) | collective-permute-done | bytes 32800 | tf_op jit(solution)/shard_map/ppermute | solution.py:487
  62.4 0.8 %shard_map.151 = f32[8,6656]{1,0:T(8,128)} custom-call(s32[1]{0:T(128)} %bitcast.pos_ref, f32[8,6656]{1,0:T(8,128)S(1)} %get-tuple-element.60.residual_in_ref, f32[8,1024]{1,0:T(8,128)S(1)} %collective-permute-done.4.halo_a_ref, f32[8,1024]{1,0:T(8,128)S(1)} %collective-permute-done.5.halo_b_ref, f32[8,128]{1,0:T(8,128)S(1)} %get-tuple-element.63.factor_ref), custom_call_target="tpu_custom_call" | custom-call | tf_op jit(solution)/shard_map/pallas_call | solution.py:491
  (43 shorter events, 2.7 us)
Async XLA Ops:
  1.4 0.9 %copy-start = (f32[8,6656]{1,0:T(8,128)S(1)}, f32[8,6656]{1,0:T(8,128)}, u32[]{:S(2)}) copy-start(f32[8,6656]{1,0:T(8,128)} %rhs_ref.3) | copy-start | bytes 638980
  2.3 4.7 %copy-start.3 = (s32[32,343]{1,0:T(8,128)S(1)}, s32[32,343]{1,0:T(8,128)}, u32[]{:S(2)}) copy-start(s32[32,343]{1,0:T(8,128)} %conn_ref.1) | copy-start | bytes 131716
  2.5 11.0 %collective-permute-start = (f32[8,512]{1,0:T(8,128)S(1)}, f32[8,512]{1,0:T(8,128)S(1)}, u32[]{:S(2)}, u32[]{:S(2)}) collective-permute-start(f32[8,512]{1,0:T(8,128)S(1)} %get-tuple-element.35), channel_id=1, source_target_pairs={{0,1},{1,0},{2,3},{3,2},{4,5},{5,4},{6,7},{7,6},{8,9},{9,8},{10,11... | collective-permute-start | bytes 49160 | tf_op jit(solution)/shard_map/ppermute | solution.py:487
  2.5 11.0 %collective-permute-start.1 = (f32[8,512]{1,0:T(8,128)S(1)}, f32[8,512]{1,0:T(8,128)S(1)}, u32[]{:S(2)}, u32[]{:S(2)}) collective-permute-start(f32[8,512]{1,0:T(8,128)S(1)} %get-tuple-element.36), channel_id=1, source_target_pairs={{1,2},{2,1},{3,4},{4,3},{5,6},{6,5},{7,8},{8,7},{9,10},{10,9},{11,... | collective-permute-start | bytes 49160 | tf_op jit(solution)/shard_map/ppermute | solution.py:487
  10.2 1.5 %copy-start.11 = (f32[6656]{0:T(1024)S(1)}, f32[6656]{0:T(1024)}, u32[]{:S(2)}) copy-start(f32[6656]{0:T(1024)} %param.14) | copy-start | bytes 79876
  11.7 1.9 %copy-start.4 = (f32[8,8,343]{2,1,0:T(8,128)S(1)}, f32[8,8,343]{2,1,0:T(8,128)}, u32[]{:S(2)}) copy-start(f32[8,8,343]{2,1,0:T(8,128)} %param.21) | copy-start | bytes 263428
  11.7 1.9 %copy-start.5 = (f32[2,8,8]{2,1,0:T(8,128)S(1)}, f32[2,8,8]{2,1,0:T(8,128)}, u32[]{:S(2)}) copy-start(f32[2,8,8]{2,1,0:T(8,128)} %coupling_ref.1) | copy-start | bytes 1540
  11.7 1.8 %copy-start.9 = (s32[32]{0:T(128)S(1)}, s32[32]{0:T(128)}, u32[]{:S(2)}) copy-start(s32[32]{0:T(128)} %count_ref.3) | copy-start | bytes 388
  11.7 1.8 %copy-start.10 = (f32[32]{0:T(128)S(1)}, f32[32]{0:T(128)}, u32[]{:S(2)}) copy-start(f32[32]{0:T(128)} %scale_ref.3) | copy-start | bytes 388
  13.5 0.7 %copy-start.6 = (s32[8]{0:T(128)S(1)}, s32[8]{0:T(128)}, u32[]{:S(2)}) copy-start(s32[8]{0:T(128)} %cell_ref.7) | copy-start | bytes 100
  13.5 0.7 %copy-start.7 = (s32[8]{0:T(128)S(1)}, s32[8]{0:T(128)}, u32[]{:S(2)}) copy-start(s32[8]{0:T(128)} %atom_ref.7) | copy-start | bytes 100
  13.5 0.7 %copy-start.8 = (s32[32]{0:T(128)S(1)}, s32[32]{0:T(128)}, u32[]{:S(2)}) copy-start(s32[32]{0:T(128)} %scount_ref.7) | copy-start | bytes 388
  14.2 8.9 %copy-start.2 = (f32[343,343]{1,0:T(8,128)S(1)}, f32[343,343]{1,0:T(8,128)}, u32[]{:S(2)}) copy-start(f32[343,343]{1,0:T(8,128)} %refs_1_.1) | copy-start | bytes 1411792
  17.3 12.4 %all-to-all-start = ((f32[32,4,128]{2,1,0:T(4,128)}), f32[32,4,128]{2,1,0:T(4,128)S(1)}, u32[]{:S(2)}, u32[]{:S(2)}) async-start(f32[32,4,128]{2,1,0:T(4,128)} %get-tuple-element.40), calls=%async_computation | async-start | bytes 131072 | tf_op jit(solution)/shard_map/all_to_all | solution.py:552
  31.9 7.9 %collective-permute-start.2 = (f32[10,1024]{1,0:T(8,128)S(1)}, f32[10,1024]{1,0:T(8,128)S(1)}, u32[]{:S(2)}, u32[]{:S(2)}) collective-permute-start(f32[10,1024]{1,0:T(8,128)S(1)} %get-tuple-element.49), channel_id=1, source_target_pairs={{0,1},{1,0},{2,3},{3,2},{4,5},{5,4},{6,7},{7,6},{8,9},{9,8},{10,11... | collective-permute-start | bytes 122888 | tf_op jit(solution)/shard_map/ppermute | solution.py:487
  32.3 7.4 %collective-permute-start.3 = (f32[10,1024]{1,0:T(8,128)S(1)}, f32[10,1024]{1,0:T(8,128)S(1)}, u32[]{:S(2)}, u32[]{:S(2)}) collective-permute-start(f32[10,1024]{1,0:T(8,128)S(1)} %get-tuple-element.50), channel_id=1, source_target_pairs={{1,2},{2,1},{3,4},{4,3},{5,6},{6,5},{7,8},{8,7},{9,10},{10,9},{11,... | collective-permute-start | bytes 122888 | tf_op jit(solution)/shard_map/ppermute | solution.py:487
  37.1 0.7 %copy-start.12 = (f32[8]{0:T(128)S(1)}, f32[8]{0:T(128)}, u32[]{:S(2)}) copy-start(f32[8]{0:T(128)} %param.16) | copy-start | bytes 100
  43.5 11.1 %all-to-all-start.1 = ((f32[32,4,128]{2,1,0:T(4,128)}), f32[32,4,128]{2,1,0:T(4,128)S(1)}, u32[]{:S(2)}, u32[]{:S(2)}) async-start(f32[32,4,128]{2,1,0:T(4,128)} %get-tuple-element.55), calls=%async_computation.1 | async-start | bytes 131072 | tf_op jit(solution)/shard_map/all_to_all | solution.py:582
  51.0 8.2 %copy-start.1 = (f32[8,6656]{1,0:T(8,128)S(1)}, f32[8,6656]{1,0:T(8,128)}, u32[]{:S(2)}) copy-start(f32[8,6656]{1,0:T(8,128)} %rhs_ref.3) | copy-start | bytes 638980
  56.7 3.5 %collective-permute-start.4 = (f32[8,1024]{1,0:T(8,128)S(1)}, f32[8,1024]{1,0:T(8,128)S(1)}, u32[]{:S(2)}, u32[]{:S(2)}) collective-permute-start(f32[8,1024]{1,0:T(8,128)S(1)} %get-tuple-element.61), channel_id=1, source_target_pairs={{0,1},{1,0},{2,3},{3,2},{4,5},{5,4},{6,7},{7,6},{8,9},{9,8},{10,11... | collective-permute-start | bytes 98312 | tf_op jit(solution)/shard_map/ppermute | solution.py:487
  57.2 5.2 %collective-permute-start.5 = (f32[8,1024]{1,0:T(8,128)S(1)}, f32[8,1024]{1,0:T(8,128)S(1)}, u32[]{:S(2)}, u32[]{:S(2)}) collective-permute-start(f32[8,1024]{1,0:T(8,128)S(1)} %get-tuple-element.62), channel_id=1, source_target_pairs={{1,2},{2,1},{3,4},{4,3},{5,6},{6,5},{7,8},{8,7},{9,10},{10,9},{11,... | collective-permute-start | bytes 98312 | tf_op jit(solution)/shard_map/ppermute | solution.py:487

commit v8 on v7

--- a/solution.py
+++ b/solution.py
@@ -65,38 +65,94 @@
     return jnp.sum(jnp.where(iota((ROWS, LANES), 1) == iota((ROWS, LANES), 0), spread, 0.0), axis=0, keepdims=True)
 
 
-def prepare_kernel(z, conn_ref, index_ref, corner_ref):
+LOW, HIGH, FIRST_LIST, SECOND_LIST, CELL, OWNER, LOCAL, OTHER = range(8)
+
+
+def prepare_kernel(
+    z, pos_ref, count_ref, scale_ref, cell_ref, atom_ref, scount_ref, conn_ref,
+    index_ref, corner_ref, table_ref, weight_ref,
+):
+    position = pos_ref[0]
     line = iota((1, LANES), 1)
     corner = jnp.zeros((1, LANES), jnp.int32)
     index_ref[...] = jnp.zeros_like(index_ref)
+    live = count_ref[position]
     for c in range(z.slots):
         row = conn_ref[c : c + 1, :] + z.shift
         index_ref[c, :, : z.elem] = row
         corner = jnp.where(line == c, row[:, :1], corner)
         corner = jnp.where(line == z.slots + c, row[:, z.elem - 1 :], corner)
+        weight = jnp.where(c < live, scale_ref[c], 0.0)
+        weight_ref[c * ROWS : (c + 1) * ROWS, :] = jnp.zeros((ROWS, LANES), F32) + weight
     corner_ref[...] = corner
-
-
-def start_kernel(z, pos_ref, rhs_ref, precond_ref, p_ref, send_a_ref, send_b_ref, gamma_ref):
+    nodes = (conn_ref[...] + z.shift).astype(F32)
+    place = iota(nodes.shape, 1)
+    middle = (place > 0) & (place < z.elem - 1)
+    low = jnp.min(jnp.where(middle, nodes, 1.0 * z.window), axis=1, keepdims=True)
+    high = jnp.max(jnp.where(middle, nodes, 0.0), axis=1, keepdims=True)
+    lane, cell = iota((z.slots, LANES), 1), iota((z.slots, LANES), 0)
+
+    def as_row(column):
+        return jnp.sum(jnp.where(lane == cell, column, 0.0), axis=0, keepdims=True)
+
+    rows = [as_row(low), as_row(high)]
+    for margin in (z.rim, 2 * z.rim):
+        good = jnp.where((low >= margin) & (high < z.window - margin), 1.0, 0.0)
+        good = jnp.broadcast_to(good, (z.slots, LANES))
+        number = cell.astype(F32)
+        before = jnp.sum(jnp.where(lane < cell, as_row(good), 0.0), axis=1, keepdims=True)
+        at = jnp.where(good > 0.5, before, z.slots - 1.0 - (number - before))
+        rows.append(
+            jnp.sum(jnp.where(lane.astype(F32) == at, number + z.slots * good, 0.0), axis=0, keepdims=True)
+        )
+    table = [row.astype(jnp.int32) for row in rows]
+    facts = [jnp.zeros((1, LANES), jnp.int32)] * 3
+    for s in range(z.entries):
+        atom = atom_ref[s]
+        owner = atom // z.owned
+        for k, fact in enumerate((cell_ref[s], owner, atom - owner * z.owned)):
+            facts[k] = jnp.where(line == s, fact, facts[k])
+    other = jnp.where(line == 0, position, jnp.where(line == 1, scount_ref[position], 0))
+    table_ref[...] = jnp.concatenate(table + facts + [other], axis=0)
+
+
+def start_kernel(
+    z, pos_ref, shift_ref, rhs_ref, precond_ref, potential_ref,
+    p_ref, send_a_ref, send_b_ref, gamma_ref, diag_ref, shift_tile_ref,
+):
     product = rhs_ref[...] * precond_ref[...]
     own = slice(z.rim, z.rim + z.nodes)
-    p_ref[:, own] = product
-    p_ref[:, z.window :] = jnp.zeros((ROWS, z.reach - z.window), F32)
-    gamma_ref[...] = lanes_by_vector(z, product * rhs_ref[...])
     head, tail = product[:, : z.rim], product[:, z.nodes - z.rim :]
     even = pos_ref[0] % 2 == 0
     send_a_ref[...] = jnp.where(even, tail, head)
     send_b_ref[...] = jnp.where(even, head, tail)
-
-
-def gather_middle(z, groups, list_ref, index_ref, low_ref, high_ref, window_ref, u_ref):
+    p_ref[:, own] = product
+    p_ref[:, z.window :] = jnp.zeros((ROWS, z.reach - z.window), F32)
+    gamma_ref[...] = lanes_by_vector(z, product * rhs_ref[...])
+    diag_ref[...] = jnp.zeros_like(diag_ref)
+    diag_ref[0:1, own] = precond_ref[...]
+    diag_ref[1:2, own] = potential_ref[...]
+    row = iota((ROWS, LANES), 0)
+    tile = jnp.zeros((ROWS, LANES), F32)
+    for v in range(z.vectors):
+        tile = jnp.where(row == v, shift_ref[v], tile)
+    shift_tile_ref[...] = tile
+
+
+def full_groups(z, table_ref, which):
+    ends = [table_ref[which, g * z.together + z.together - 1] for g in range(z.slots // z.together)]
+    return functools.reduce(jnp.add, [(end >= z.slots).astype(jnp.int32) for end in ends])
+
+
+def gather_middle(z, groups, which, table_ref, index_ref, window_ref, u_ref):
     total = z.window // LANES
     tile = (ROWS, LANES)
 
     def some_cells(g, _):
-        cells = [list_ref[g * z.together + i] for i in range(z.together)]
-        starts = [(low_ref[c] + z.shift) >> 7 for c in cells]
-        ends = [(high_ref[c] + z.shift) >> 7 for c in cells]
+        cells = [table_ref[which, g * z.together + i] for i in range(z.together)]
+        cells = [jnp.where(c >= z.slots, c - z.slots, c) for c in cells]
+        starts = [table_ref[LOW, c] >> 7 for c in cells]
+        ends = [table_ref[HIGH, c] >> 7 for c in cells]
         passes = functools.reduce(jnp.maximum, [(e - s) // SPAN + 1 for s, e in zip(starts, ends)])
 
         def one_pass(k, values):
@@ -123,7 +179,7 @@
     lax.fori_loop(*groups, some_cells, 0)
 
 
-def gather_corners(z, corner_ref, window_ref, scale_ref, live, u_ref, uw_ref):
+def gather_corners(z, corner_ref, window_ref, weight_ref, u_ref, uw_ref):
     tile = (ROWS, LANES)
     corner = jnp.broadcast_to(corner_ref[...], tile)
     low, high = corner & (LANES - 1), corner >> 7
@@ -135,8 +191,8 @@
     lane = iota(tile, 1)
     last = (z.elem - 1) % LANES
     for c in range(z.slots):
-        weight = jnp.where(c < live, scale_ref[c], 0.0)
         rows = slice(c * ROWS, (c + 1) * ROWS)
+        weight = weight_ref[rows, :]
         for t in range(z.tiles):
             lanes = slice(t * LANES, (t + 1) * LANES)
             value = u_ref[rows, lanes]
@@ -155,22 +211,21 @@
     e_ref[...] = dot(u_high, k_high) + (dot(u_high, k_low) + dot(u_low, k_high))
 
 
-def entry_facts(z, position, atom_ref, count_ref, s):
-    atom = atom_ref[s]
-    owner = atom // z.owned
-    return owner, atom - owner * z.owned, s < count_ref[position]
-
-
-def contributions(z, position, pj_ref, cell_ref, atom_ref, count_ref, u_ref):
-    values = [u_ref[pl.ds(pl.multiple_of(cell_ref[s] * ROWS, ROWS), ROWS), :] for s in range(z.entries)]
+def entry_facts(table_ref, s):
+    return table_ref[OWNER, s], table_ref[LOCAL, s], s < table_ref[OTHER, 1]
+
+
+def contributions(z, table_ref, pj_ref, u_ref):
+    values = [u_ref[pl.ds(pl.multiple_of(table_ref[CELL, s] * ROWS, ROWS), ROWS), :] for s in range(z.entries)]
     sums = lax.dot_general(
         pj_ref[...], jnp.concatenate(values, axis=0), NT, precision=HIGHEST, preferred_element_type=F32
     )
     sums = jnp.concatenate([sums, jnp.zeros((sums.shape[0], LANES - sums.shape[1]), F32)], axis=1)
     lane, row = iota((ROWS, LANES), 1), iota((ROWS, LANES), 0)
+    position = table_ref[OTHER, 0]
     parts = [jnp.zeros((ROWS, LANES), F32)] * 3
     for s in range(z.entries):
-        owner, local, alive = entry_facts(z, position, atom_ref, count_ref, s)
+        owner, local, alive = entry_facts(table_ref, s)
         got = lane_gather(sums[s * ROWS : (s + 1) * ROWS], s * ROWS + lane % ROWS)
         here = (lane // ROWS % ROWS == row) & (lane // z.pairs == local) & alive
         for k in range(3):
@@ -183,30 +238,27 @@
     return jnp.where(even, far, near), jnp.where(even, near, far)
 
 
-def first_window_kernel(z, low_ref, high_ref, list_ref, groups_ref, p_ref, index_ref, u_ref):
-    gather_middle(z, (0, groups_ref[0]), list_ref, index_ref, low_ref, high_ref, p_ref, u_ref)
+def first_window_kernel(z, table_ref, p_ref, index_ref, u_ref):
+    groups = 0, full_groups(z, table_ref, FIRST_LIST)
+    gather_middle(z, groups, FIRST_LIST, table_ref, index_ref, p_ref, u_ref)
 
 
 def first_kernel(
-    z, pos_ref, count_ref, scale_ref, cell_ref, atom_ref, scount_ref, low_ref, high_ref, list_ref, groups_ref,
-    p_in_ref, u_in_ref, precond_ref, potential_ref, halo_a_ref, halo_b_ref, index_ref, corner_ref, projector_ref,
-    coupling_ref, p_ref, diag_ref, out_ref, uw_ref, pj_ref, u_ref,
-):
-    position = pos_ref[0]
+    z, table_ref, p_in_ref, u_in_ref, halo_a_ref, halo_b_ref, index_ref, corner_ref, weight_ref, projector_ref,
+    coupling_ref, p_ref, out_ref, uw_ref, pj_ref, u_ref,
+):
     own = slice(z.rim, z.rim + z.nodes)
-    p_ref[:, : z.rim], p_ref[:, z.rim + z.nodes : z.window] = sides(position, halo_a_ref[...], halo_b_ref[...])
+    halo = sides(table_ref[OTHER, 0], halo_a_ref[...], halo_b_ref[...])
+    p_ref[:, : z.rim], p_ref[:, z.rim + z.nodes : z.window] = halo
     p_ref[:, own] = p_in_ref[:, own]
     p_ref[:, z.window :] = p_in_ref[:, z.window :]
     u_ref[...] = u_in_ref[...]
-    diag_ref[...] = jnp.zeros_like(diag_ref)
-    diag_ref[0:1, own] = precond_ref[...]
-    diag_ref[1:2, own] = potential_ref[...]
     pj_ref[...] = jnp.zeros_like(pj_ref)
     pj_ref[:, : z.elem] = projector_ref[...]
-    groups = groups_ref[0], z.slots // z.together
-    gather_middle(z, groups, list_ref, index_ref, low_ref, high_ref, p_ref, u_ref)
-    gather_corners(z, corner_ref, p_ref, scale_ref, count_ref[position], u_ref, uw_ref)
-    parts = contributions(z, position, pj_ref, cell_ref, atom_ref, scount_ref, u_ref)
+    groups = full_groups(z, table_ref, FIRST_LIST), z.slots // z.together
+    gather_middle(z, groups, FIRST_LIST, table_ref, index_ref, p_ref, u_ref)
+    gather_corners(z, corner_ref, p_ref, weight_ref, u_ref, uw_ref)
+    parts = contributions(z, table_ref, pj_ref, u_ref)
     small_lane, small_row = iota((ROWS, LANES), 1), iota((ROWS, LANES), 0)
     matrices = jnp.zeros((ROWS, LANES), F32)
     for atom in range(z.owned):
@@ -219,21 +271,20 @@
 
 
 def second_window_kernel(
-    z, low_ref, high_ref, list_ref, groups_ref, p_ref, diag_ref, shift_ref, image_ref, index_ref, y_ref, q_ref, u_ref,
-):
-    y_ref[...] = image_ref[...] + (diag_ref[1:2, :] + shift_ref[...]) * p_ref[:, : z.window]
+    z, table_ref, p_ref, diag_ref, shift_ref, image_ref, index_ref, y_ref, q_ref, u_ref,
+):
+    y_ref[...] = image_ref[...] + (diag_ref[1:2, :] + shift_ref[:, :1]) * p_ref[:, : z.window]
     q_ref[:, : z.window] = y_ref[...] * diag_ref[0:1, :]
     q_ref[:, z.window :] = jnp.zeros((ROWS, z.reach - z.window), F32)
-    gather_middle(z, (0, groups_ref[0]), list_ref, index_ref, low_ref, high_ref, q_ref, u_ref)
+    groups = 0, full_groups(z, table_ref, SECOND_LIST)
+    gather_middle(z, groups, SECOND_LIST, table_ref, index_ref, q_ref, u_ref)
 
 
 def second_kernel(
-    z, pos_ref, count_ref, scale_ref, cell_ref, atom_ref, scount_ref, low_ref, high_ref, list_ref, groups_ref,
-    y_in_ref, q_in_ref, u_in_ref, p_ref, diag_in_ref, shift_ref, gamma_ref, halo_a_ref, halo_b_ref, index_ref, corner_ref, k_high_ref,
-    k_low_ref, pj_ref, y_ref, q_ref, out_ref, e_ref, diag_ref, u_ref, uw_ref,
-):
-    position = pos_ref[0]
-    left, right = sides(position, halo_a_ref[...], halo_b_ref[...])
+    z, table_ref, y_in_ref, q_in_ref, u_in_ref, p_ref, diag_in_ref, shift_ref, gamma_ref, halo_a_ref, halo_b_ref,
+    index_ref, corner_ref, weight_ref, k_high_ref, k_low_ref, pj_ref, y_ref, q_ref, out_ref, e_ref, diag_ref, u_ref, uw_ref,
+):
+    left, right = sides(table_ref[OTHER, 0], halo_a_ref[...], halo_b_ref[...])
     own = slice(z.rim, z.rim + z.nodes)
     ghosts = slice(0, z.rim), slice(z.rim + z.nodes, z.window)
     diag_ref[:, own] = diag_in_ref[:, own]
@@ -254,11 +305,11 @@
         lanes_by_vector(z, y * p_ref[:, own]),
         lanes_by_vector(z, y * q),
     ]
-    energy = jnp.sum(q * q * (diag_ref[1:2, own] + shift_ref[...]), axis=1, keepdims=True)
-    groups = groups_ref[0], z.slots // z.together
-    gather_middle(z, groups, list_ref, index_ref, low_ref, high_ref, q_ref, u_ref)
-    gather_corners(z, corner_ref, q_ref, scale_ref, count_ref[position], u_ref, uw_ref)
-    parts = contributions(z, position, pj_ref, cell_ref, atom_ref, scount_ref, u_ref)
+    energy = jnp.sum(q * q * (diag_ref[1:2, own] + shift_ref[:, :1]), axis=1, keepdims=True)
+    groups = full_groups(z, table_ref, SECOND_LIST), z.slots // z.together
+    gather_middle(z, groups, SECOND_LIST, table_ref, index_ref, q_ref, u_ref)
+    gather_corners(z, corner_ref, q_ref, weight_ref, u_ref, uw_ref)
+    parts = contributions(z, table_ref, pj_ref, u_ref)
     stiffness_product(k_high_ref, k_low_ref, uw_ref, e_ref)
     elements = jnp.zeros((ROWS, z.width), F32)
     for c in range(z.slots):
@@ -275,9 +326,9 @@
 
 
 class Scatter:
-    def __init__(self, z, index_ref, corner_ref, low_ref, high_ref, acc_ref):
+    def __init__(self, z, table_ref, index_ref, corner_ref, acc_ref):
         self.z, self.index_ref, self.corner_ref, self.acc_ref = z, index_ref, corner_ref, acc_ref
-        self.low_ref, self.high_ref = low_ref, high_ref
+        self.table_ref = table_ref
         self.groups = z.window // WIDE
         self.pair = (2 * ROWS, LANES)
         sub = iota(self.pair, 0)
@@ -317,8 +368,8 @@
 
     def add(self, cells, value_of):
         z = self.z
-        starts = [(self.low_ref[c] + z.shift) >> 8 for c in cells]
-        ends = [(self.high_ref[c] + z.shift) >> 8 for c in cells]
+        starts = [self.table_ref[LOW, c] >> 8 for c in cells]
+        ends = [self.table_ref[HIGH, c] >> 8 for c in cells]
         passes = functools.reduce(jnp.maximum, [(e - s) // BAND + 1 for s, e in zip(starts, ends)])
 
         def one_pass(k, _):
@@ -345,7 +396,7 @@
         return self.acc_ref[at : at + ROWS] + self.acc_ref[at + ROWS : at + 2 * ROWS]
 
 
-def cells_kernel(z, multiply, low_ref, high_ref, index_ref, corner_ref, *refs):
+def cells_kernel(z, multiply, table_ref, index_ref, corner_ref, *refs):
     if multiply:
         uw_ref, stiffness_ref, image_ref, k_high_ref, k_low_ref, e_ref, k_ref, acc_ref = refs
         k_ref[...] = jnp.zeros_like(k_ref)
@@ -354,7 +405,7 @@
         stiffness_product(k_high_ref, k_low_ref, uw_ref, e_ref)
     else:
         e_ref, image_ref, acc_ref = refs
-    scatter = Scatter(z, index_ref, corner_ref, low_ref, high_ref, acc_ref)
+    scatter = Scatter(z, table_ref, index_ref, corner_ref, acc_ref)
     scatter.start([(c, e_ref[c * ROWS : (c + 1) * ROWS, :]) for c in range(z.slots)])
 
     def some_cells(g, _):
@@ -373,14 +424,13 @@
 
 
 def support_kernel(
-    z, last, pos_ref, cell_ref, atom_ref, scount_ref, low_ref, high_ref, sums_ref, coupling_ref, index_ref, corner_ref,
-    pj_ref, diag_ref, cells_ref, *refs,
+    z, last, table_ref, sums_ref, coupling_ref, index_ref, corner_ref, pj_ref, diag_ref, cells_ref, *refs,
 ):
     if last:
         image_ref, send_a_ref, send_b_ref, dots_ref, support_ref, acc_ref = refs
     else:
         image_ref, send_a_ref, send_b_ref, support_ref, acc_ref = refs
-    position = pos_ref[0]
+    position = table_ref[OTHER, 0]
     wanted = (
         pltpu.roll(sums_ref[:, 0, :], z.devices - 1, 0) + sums_ref[:, 1, :] + pltpu.roll(sums_ref[:, 2, :], 1, 0)
     )
@@ -407,7 +457,7 @@
     small_lane, small_row = iota((ROWS, LANES), 1), iota((ROWS, LANES), 0)
     spread = []
     for s in range(z.entries):
-        owner, local, alive = entry_facts(z, position, atom_ref, scount_ref, s)
+        owner, local, alive = entry_facts(table_ref, s)
         mine = jnp.sum(jnp.where(block == owner, term, 0.0), axis=0, keepdims=True)
         got = lane_gather(
             jnp.broadcast_to(mine, (ROWS, LANES)), local * z.pairs + small_lane % ROWS * ROWS + small_row
@@ -416,8 +466,8 @@
     support_ref[...] = jnp.dot(
         jnp.concatenate(spread, axis=0), pj_ref[...], precision=HIGHEST, preferred_element_type=F32
     )
-    scatter = Scatter(z, index_ref, corner_ref, low_ref, high_ref, acc_ref)
-    cells = [cell_ref[s] for s in range(z.entries)]
+    scatter = Scatter(z, table_ref, index_ref, corner_ref, acc_ref)
+    cells = [table_ref[CELL, s] for s in range(z.entries)]
     scatter.start([(cell, support_ref[s * ROWS : (s + 1) * ROWS, :]) for s, cell in enumerate(cells)])
     for first in range(0, z.entries, z.together):
         some = cells[first : first + z.together]
@@ -455,15 +505,15 @@
     more = 1.0 + beta
     step = fresh / (more * more * py - 2.0 * more * alpha * qy + alpha * alpha * qq)
     p, q, y = p_ref[:, own], q_ref[:, own], y_ref[:, own]
-    second = image_ref[:, own] + (diag_ref[1:2, own] + shift_ref[...]) * q
+    second = image_ref[:, own] + (diag_ref[1:2, own] + shift_ref[:, :1]) * q
     search = (p - alpha * q) + beta * p
     solution_ref[...] = alpha * p + step * search
     residual_ref[...] = (rhs_ref[...] - alpha * y) - step * (more * y - alpha * second)
     factor_ref[...] = jnp.broadcast_to(step * alpha, (ROWS, LANES))
 
 
-def rim_kernel(z, pos_ref, residual_in_ref, halo_a_ref, halo_b_ref, factor_ref, residual_ref):
-    left, right = sides(pos_ref[0], halo_a_ref[...], halo_b_ref[...])
+def rim_kernel(z, table_ref, residual_in_ref, halo_a_ref, halo_b_ref, factor_ref, residual_ref):
+    left, right = sides(table_ref[OTHER, 0], halo_a_ref[...], halo_b_ref[...])
     factor = factor_ref[:, :1]
     first, last = slice(0, z.rim), slice(z.nodes - z.rim, z.nodes)
     residual_ref[:, z.rim : z.nodes - z.rim] = residual_in_ref[:, z.rim : z.nodes - z.rim]
@@ -478,7 +528,6 @@
     count = lax.axis_size("dom")
     z = Sizes(count, rhs, conn, projector, atom_matrix)
     position = lax.axis_index("dom")
-    even = position % 2 == 0
     pos = position.astype(jnp.int32).reshape(1)
     near = [(i, i ^ 1) for i in range(count)]
     far = [(i, j) for i in range(1, count - 1) for j in [i + 1 if i % 2 else i - 1]]
@@ -486,8 +535,9 @@
     def exchange(a, b):
         return lax.ppermute(a, "dom", near), lax.ppermute(b, "dom", far)
 
-    def call(kernel, outs, scratch, scalars, *args, in_hbm=()):
-        args = [pltpu.with_memory_space_constraint(x, pltpu.VMEM) for x in args]
+    def call(kernel, outs, scratch, scalars, *args, in_hbm=(), copied=False):
+        if not copied:
+            args = [pltpu.with_memory_space_constraint(x, pltpu.VMEM) for x in args]
         return pl.pallas_call(
             kernel,
             out_shape=[
@@ -499,69 +549,53 @@
             compiler_params=pltpu.CompilerParams(vmem_limit_bytes=16 * 1024 * 1024),
         )(*scalars, *args)
 
-    precond_row, potential_row = precond[None, :], potential[None, :]
-    shift_column = shift[:, None]
     flat_projector = projector.reshape(z.entries * z.channels, z.elem)
-    middle = conn[:, 1:-1]
-    ranges = jnp.min(middle, axis=1), jnp.max(middle, axis=1)
-
-    def listed(margin):
-        good = (ranges[0] + z.shift >= margin) & (ranges[1] + z.shift < z.window - margin)
-        one = good.astype(jnp.int32)
-        number = jnp.arange(z.slots)
-        before = jnp.sum(jnp.where(number[None, :] < number[:, None], one[None, :], 0), axis=1)
-        total = jnp.sum(one)
-        place = jnp.where(good, before, total + number - before)
-        order = jnp.sum(jnp.where(place[None, :] == number[:, None], number[None, :], 0), axis=1)
-        return order.astype(jnp.int32), (total // z.together).astype(jnp.int32).reshape(1)
-
     cells = (z.slots * ROWS, z.width)
     window, reach, own = (z.vectors, z.window), (z.vectors, z.reach), (z.vectors, z.nodes)
     message = (z.devices, 4, LANES)
     square, entries = (z.width, z.width), (z.entries * ROWS, z.width)
     rim, more_rim = (z.vectors, 2 * z.rim), (z.vectors + 2, 2 * z.rim)
     acc = ((z.window // WIDE + BAND) * 2 * ROWS, WIDE)
-    supports = support_cell, support_atom, support_count
-
-    p, send_a, send_b, gamma = call(
+
+    tile = (ROWS, LANES)
+    p, send_a, send_b, gamma, diag, shift_tile = call(
         functools.partial(start_kernel, z),
-        [(reach, F32), ((z.vectors, z.rim), F32), ((z.vectors, z.rim), F32), ((1, LANES), F32)],
+        [(reach, F32), ((z.vectors, z.rim), F32), ((z.vectors, z.rim), F32), ((1, LANES), F32), ((2, z.window), F32),
+         (tile, F32)],
         [],
-        (pos,),
-        rhs, precond_row,
+        (pos, shift),
+        rhs, precond[None, :], potential[None, :], copied=True,
     )
     halo = exchange(send_a, send_b)
-    first_list, second_list = listed(z.rim), listed(2 * z.rim)
-    index, corner = call(
+    index, corner, table, weight = call(
         functools.partial(prepare_kernel, z),
-        [((z.slots, 1, z.width), jnp.int32), ((1, LANES), jnp.int32)],
+        [((z.slots, 1, z.width), jnp.int32), ((1, LANES), jnp.int32), ((ROWS, LANES), jnp.int32),
+         ((z.slots * ROWS, LANES), F32)],
         [],
-        (),
+        (pos, cell_count, cell_scale, support_cell, support_atom, support_count),
         conn,
     )
-    (u,) = call(
-        functools.partial(first_window_kernel, z), [(cells, F32)], [], (*ranges, *first_list), p, index,
-    )
-    p, diag, sums, uw, pj = call(
+    (u,) = call(functools.partial(first_window_kernel, z), [(cells, F32)], [], (table,), p, index)
+    p, sums, uw, pj = call(
         functools.partial(first_kernel, z),
-        [(reach, F32), ((2, z.window), F32), (message, F32), (cells, F32), (entries, F32)],
+        [(reach, F32), (message, F32), (cells, F32), (entries, F32)],
         [(cells, F32)],
-        (pos, cell_count, cell_scale, *supports, *ranges, *first_list),
-        p, u, precond_row, potential_row, *halo, index, corner, flat_projector, atom_matrix,
+        (table,),
+        p, u, *halo, index, corner, weight, flat_projector, atom_matrix,
     )
     coupled = lax.all_to_all(sums, "dom", 0, 0)
     image, k_high, k_low = call(
         functools.partial(cells_kernel, z, True),
         [(window, F32), (square, BF16), (square, BF16)],
         [(cells, F32), (square, F32), (acc, F32)],
-        ranges,
+        (table,),
         index, corner, uw, stiffness,
     )
     image, send_a, send_b = call(
         functools.partial(support_kernel, z, False),
         [(window, F32), (more_rim, F32), (more_rim, F32)],
         [(entries, F32), (acc, F32)],
-        (pos, *supports, *ranges),
+        (table,),
         coupled, coupled, index, corner, pj, diag, image,
     )
     halo = exchange(send_a, send_b)
@@ -569,34 +603,34 @@
         functools.partial(second_window_kernel, z),
         [(window, F32), (reach, F32), (cells, F32)],
         [],
-        (*ranges, *second_list),
-        p, diag, shift_column, image, index,
+        (table,),
+        p, diag, shift_tile, image, index,
     )
     y, q, sums, e = call(
         functools.partial(second_kernel, z),
         [(window, F32), (reach, F32), (message, F32), (cells, F32)],
         [((2, z.window), F32), (cells, F32), (cells, F32)],
-        (pos, cell_count, cell_scale, *supports, *ranges, *second_list),
-        y, q, u, p, diag, shift_column, gamma, *halo, index, corner, k_high, k_low, pj,
+        (table,),
+        y, q, u, p, diag, shift_tile, gamma, *halo, index, corner, weight, k_high, k_low, pj,
     )
     totals = lax.all_to_all(sums, "dom", 0, 0)
-    (image,) = call(functools.partial(cells_kernel, z, False), [(window, F32)], [(acc, F32)], ranges, index, corner, e)
+    (image,) = call(functools.partial(cells_kernel, z, False), [(window, F32)], [(acc, F32)], (table,), index, corner, e)
     image, send_a, send_b, dots = call(
         functools.partial(support_kernel, z, True),
         [(window, F32), (rim, F32), (rim, F32), ((1, LANES), F32)],
         [(entries, F32), (acc, F32)],
-        (pos, *supports, *ranges),
+        (table,),
         totals, coupled, index, corner, pj, diag, image,
     )
     halo = exchange(send_a, send_b)
     answer, residual, factor = call(
         functools.partial(last_kernel, z),
-        [(own, F32), (own, F32), ((ROWS, LANES), F32)],
+        [(own, F32), (own, F32), (tile, F32)],
         [],
         (),
-        rhs, p, diag, shift_column, y, q, image, dots, in_hbm=(0,),
-    )
-    (residual,) = call(functools.partial(rim_kernel, z), [(own, F32)], [], (pos,), residual, *halo, factor, in_hbm=(0,))
+        rhs, p, diag, shift_tile, y, q, image, dots, in_hbm=(0,),
+    )
+    (residual,) = call(functools.partial(rim_kernel, z), [(own, F32)], [], (table,), residual, *halo, factor, in_hbm=(0,))
     return answer, residual
 
 

time: 63.7 us -> 59.2 us (0.929)
  between operations: 6.19 us -> 0.92 us
  other arithmetic: 2.6 us -> 0 us
  Pallas kernels: 24.9 us -> 27.2 us
  waiting for transfers between devices: 7.92 us -> 10 us
  local copies, waits for them, and re-layouts: 3.12 us -> 2.43 us
    pallas_call x12, Pallas kernels: 24.9 us -> 27.2 us  [call(): pl.pallas_call(kernel, out_shape=[jax.ShapeDtypeStruct(s, d) if i in in_h...]
    ppermute x6, waiting for transfers between devices: 2.22 us -> 3.83 us  [exchange(): return (lax.ppermute(a, 'dom', near), lax.ppermute(b, 'dom', far))]
    select_n x2 -> x0, other arithmetic: 1.31 us -> none  [listed(): place = jnp.where(good, before, total + number - before)]
    reduce_sum x5 -> x0, other arithmetic: 1.09 us -> none  [the longest x1 0.64 us: listed(): total = jnp.sum(one)]
  transfers between devices with their start and end apart: 8 -> 8, of which waited for: 3 -> 4; matrix products, arithmetic and copies ran while one was open for 4% -> 0% of each run, Pallas kernels for 20% -> 25%
where the time goes in v8:
time: 59.2 us; the launch traced here: 58.9 us
  Pallas kernels  27.2 us (46%)
  starting transfers between devices  18.3 us (31%)
  waiting for transfers between devices  10 us (17%)
  local copies, waits for them, and re-layouts  2.43 us (4%)
  between operations  0.92 us (2%)
    pallas_call x12, Pallas kernels, call(): pl.pallas_call(kernel, out_shape=[jax.ShapeDtypeStruct(s, d) if i in in_h...  27.2 us
    ppermute x6, starting transfers between devices, exchange(): return (lax.ppermute(a, 'dom', near), lax.ppermute(b, 'dom', far))  9.6 us
    all_to_all x1, starting transfers between devices, on_device(): coupled = lax.all_to_all(sums, 'dom', 0, 0)  5.12 us
    ppermute x6, waiting for transfers between devices, exchange(): return (lax.ppermute(a, 'dom', near), lax.ppermute(b, 'dom', far))  3.83 us
    all_to_all x1, starting transfers between devices, on_device(): totals = lax.all_to_all(sums, 'dom', 0, 0)  3.54 us
    all_to_all x1, waiting for transfers between devices, on_device(): totals = lax.all_to_all(sums, 'dom', 0, 0)  3.43 us
    all_to_all x1, waiting for transfers between devices, on_device(): coupled = lax.all_to_all(sums, 'dom', 0, 0)  2.79 us
    unnamed x26, local copies, waits for them, and re-layouts  1.64 us
  transfers between devices with their start and end apart: 8, of which 4 were waited for; matrix products, arithmetic and copies ran while one was open for 0% of the time, Pallas kernels for 25%

profile of v8, /device:TPU:1, one launch (start us, length us, event | category | flops | bytes accessed | tf_op | source)
XLA Modules:
  0.0 58.9 jit_solution(15685745170211619709)
XLA Ops:
  0.6 0.8 %broadcast_in_dim.7.potential_ref = f32[1,6656]{1,0:T(1,128)S(1)} reshape(f32[6656]{0:T(1024)} %param.14) | data formatting | bytes 53248 | tf_op jit(solution)/shard_map/broadcast_in_dim | solution.py:567
  1.5 0.6 %copy-done.6 = f32[8]{0:T(128)S(1)} copy-done((f32[8]{0:T(128)S(1)}, f32[8]{0:T(128)}, u32[]{:S(2)}) %copy-start.6) | copy-done | bytes 56
  2.1 0.9 %copy-done = f32[8,6656]{1,0:T(8,128)S(1)} copy-done((f32[8,6656]{1,0:T(8,128)S(1)}, f32[8,6656]{1,0:T(8,128)}, u32[]{:S(2)}) %copy-start) | copy-done | bytes 213016
  3.1 0.7 %shard_map.141 = (f32[8,9472]{1,0:T(8,128)S(1)}, f32[8,512]{1,0:T(8,128)S(1)}, f32[8,512]{1,0:T(8,128)S(1)}, f32[1,128]{1,0:T(1,128)S(1)}, f32[2,7680]{1,0:T(2,128)S(1)}, /*index=5*/f32[8,128]{1,0:T(8,128)S(1)}) custom-call(s32[1]{0:T(128)} %bitcast.pos_ref, f32[8]{0:T(128)S(1)} %copy-done.6, f32[8,6656]{1,0:T(8,128)S(1)} %copy-done, ...), custom_call_target="tpu_custom_call" | custom-call | tf_op jit(solution)/shard_map/pallas_call | solution.py:541
  3.9 4.5 %collective-permute-start.1 = (f32[8,512]{1,0:T(8,128)S(1)}, f32[8,512]{1,0:T(8,128)S(1)}, u32[]{:S(2)}, u32[]{:S(2)}) collective-permute-start(f32[8,512]{1,0:T(8,128)S(1)} %get-tuple-element.40), channel_id=1, source_target_pairs={{1,2},{2,1},{3,4},{4,3},{5,6},{6,5},{7,8},{8,7},{9,10},{10,9},{11,... | collective-permute-start | bytes 49160 | tf_op jit(solution)/shard_map/ppermute | solution.py:536
  8.4 0.9 %shard_map.140 = (s32[32,1,384]{2,1,0:T(1,128)S(1)}, s32[1,128]{1,0:T(1,128)S(1)}, s32[8,128]{1,0:T(8,128)S(1)}, f32[256,128]{1,0:T(8,128)S(1)}) custom-call(s32[1]{0:T(128)} %bitcast.pos_ref, s32[32]{0:T(128)S(1)} %copy-done.7, f32[32]{0:T(128)S(1)} %copy-done.8, s32[8]{0:T(128)S(1)} %copy-done.9, s32[8]{0:T(128)S(1)} %copy-done.10, s32[32]{0:T(128)S(1)} %copy-done.11, ...), custom_call_target="tpu_custom_call" | custom-call | tf_op jit(solution)/shard_map/pallas_call | solution.py:541
  9.3 2.4 %shard_map.142.u_in_ref = f32[256,384]{1,0:T(8,128)S(1)} custom-call(s32[8,128]{1,0:T(8,128)S(1)} %get-tuple-element.36.table_ref, f32[8,9472]{1,0:T(8,128)S(1)} %get-tuple-element.37.p_ref.p_in_ref, s32[32,1,384]{2,1,0:T(1,128)S(1)} %get-tuple-element.38.index_ref), custom_call_target="tpu_custom_call" | custom-call | tf_op jit(solution)/shard_map/pallas_call | solution.py:541
  11.8 2.6 %shard_map.143 = (f32[8,9472]{1,0:T(8,128)S(1)}, f32[32,4,128]{2,1,0:T(4,128)}, f32[256,384]{1,0:T(8,128)S(1)}, f32[64,384]{1,0:T(8,128)S(1)}) custom-call(s32[8,128]{1,0:T(8,128)S(1)} %get-tuple-element.36.table_ref, f32[8,9472]{1,0:T(8,128)S(1)} %get-tuple-element.37.p_ref.p_in_ref, f32[256,384]{1,0:T(8,128)S(1)} %shard_map.142.u_in_ref, ...), custom_call_target="tpu_custom_call" | custom-call | tf_op jit(solution)/shard_map/pallas_call | solution.py:541
  14.4 5.1 %all-to-all-start = ((f32[32,4,128]{2,1,0:T(4,128)}), f32[32,4,128]{2,1,0:T(4,128)S(1)}, u32[]{:S(2)}, u32[]{:S(2)}) async-start(f32[32,4,128]{2,1,0:T(4,128)} %get-tuple-element.46), calls=%async_computation | async-start | bytes 131072 | tf_op jit(solution)/shard_map/all_to_all | solution.py:586
  19.5 4.5 %shard_map.144 = (f32[8,7680]{1,0:T(8,128)S(1)}, bf16[384,384]{1,0:T(8,128)(2,1)S(1)}, bf16[384,384]{1,0:T(8,128)(2,1)S(1)}) custom-call(s32[8,128]{1,0:T(8,128)S(1)} %get-tuple-element.36.table_ref, s32[32,1,384]{2,1,0:T(1,128)S(1)} %get-tuple-element.38.index_ref, s32[1,128]{1,0:T(1,128)S(1)} %get-tuple-element.41.corner_ref, ...), custom_call_target="tpu_custom_call" | custom-call | tf_op jit(solution)/shard_map/pallas_call | solution.py:541
  24.0 2.8 %all-to-all-done.sums_ref.coupling_ref = f32[32,4,128]{2,1,0:T(4,128)S(1)} async-done(((f32[32,4,128]{2,1,0:T(4,128)}), f32[32,4,128]{2,1,0:T(4,128)S(1)}, u32[]{:S(2)}, u32[]{:S(2)}) %all-to-all-start) | async-done | bytes 65568 | tf_op jit(solution)/shard_map/all_to_all | solution.py:586
  26.8 2.1 %shard_map.145 = (f32[8,7680]{1,0:T(8,128)S(1)}, f32[10,1024]{1,0:T(8,128)S(1)}, f32[10,1024]{1,0:T(8,128)S(1)}) custom-call(s32[8,128]{1,0:T(8,128)S(1)} %get-tuple-element.36.table_ref, f32[32,4,128]{2,1,0:T(4,128)S(1)} %all-to-all-done.sums_ref.coupling_ref, f32[32,4,128]{2,1,0:T(4,128)S(1)} %all-to-all-done.sums_ref.coupling_ref, ...), custom_call_target="tpu_custom_call" | custom-call | tf_op jit(solution)/shard_map/pallas_call | solution.py:541
  29.4 2.0 %collective-permute-start.3 = (f32[10,1024]{1,0:T(8,128)S(1)}, f32[10,1024]{1,0:T(8,128)S(1)}, u32[]{:S(2)}, u32[]{:S(2)}) collective-permute-start(f32[10,1024]{1,0:T(8,128)S(1)} %get-tuple-element.56), channel_id=1, source_target_pairs={{1,2},{2,1},{3,4},{4,3},{5,6},{6,5},{7,8},{8,7},{9,10},{10,9},{11,... | collective-permute-start | bytes 122888 | tf_op jit(solution)/shard_map/ppermute | solution.py:536
  31.5 2.0 %shard_map.146 = (f32[8,7680]{1,0:T(8,128)S(1)}, f32[8,9472]{1,0:T(8,128)S(1)}, f32[256,384]{1,0:T(8,128)S(1)}) custom-call(s32[8,128]{1,0:T(8,128)S(1)} %get-tuple-element.36.table_ref, f32[8,9472]{1,0:T(8,128)S(1)} %get-tuple-element.43.p_ref, f32[2,7680]{1,0:T(2,128)S(1)} %get-tuple-element.44.diag_ref.diag_in_ref, ...), custom_call_target="tpu_custom_call" | custom-call | tf_op jit(solution)/shard_map/pallas_call | solution.py:541
  33.5 1.6 %collective-permute-done.3.halo_b_ref = f32[10,1024]{1,0:T(8,128)S(1)} collective-permute-done((f32[10,1024]{1,0:T(8,128)S(1)}, f32[10,1024]{1,0:T(8,128)S(1)}, u32[]{:S(2)}, u32[]{:S(2)}) %collective-permute-start.3) | collective-permute-done | bytes 40992 | tf_op jit(solution)/shard_map/ppermute | solution.py:536
  35.1 3.8 %shard_map.147 = (f32[8,7680]{1,0:T(8,128)S(1)}, f32[8,9472]{1,0:T(8,128)S(1)}, f32[32,4,128]{2,1,0:T(4,128)}, f32[256,384]{1,0:T(8,128)S(1)}) custom-call(s32[8,128]{1,0:T(8,128)S(1)} %get-tuple-element.36.table_ref, f32[8,7680]{1,0:T(8,128)S(1)} %get-tuple-element.51.y_in_ref, f32[8,9472]{1,0:T(8,128)S(1)} %get-tuple-element.52.q_in_ref, ...), custom_call_target="tpu_custom_call" | custom-call | tf_op jit(solution)/shard_map/pallas_call | solution.py:541
  38.8 3.5 %all-to-all-start.1 = ((f32[32,4,128]{2,1,0:T(4,128)}), f32[32,4,128]{2,1,0:T(4,128)S(1)}, u32[]{:S(2)}, u32[]{:S(2)}) async-start(f32[32,4,128]{2,1,0:T(4,128)} %get-tuple-element.61), calls=%async_computation.1 | async-start | bytes 131072 | tf_op jit(solution)/shard_map/all_to_all | solution.py:616
  42.4 3.8 %shard_map.148.cells_ref = f32[8,7680]{1,0:T(8,128)S(1)} custom-call(s32[8,128]{1,0:T(8,128)S(1)} %get-tuple-element.36.table_ref, s32[32,1,384]{2,1,0:T(1,128)S(1)} %get-tuple-element.38.index_ref, s32[1,128]{1,0:T(1,128)S(1)} %get-tuple-element.41.corner_ref, f32[256,384]{1,0:T(8,128)S(1)} %get-tuple-element.62.refs_0_), custom_call_target="tpu_custom_call" | custom-call | tf_op jit(solution)/shard_map/pallas_call | solution.py:541
  46.2 3.4 %all-to-all-done.1.sums_ref = f32[32,4,128]{2,1,0:T(4,128)S(1)} async-done(((f32[32,4,128]{2,1,0:T(4,128)}), f32[32,4,128]{2,1,0:T(4,128)S(1)}, u32[]{:S(2)}, u32[]{:S(2)}) %all-to-all-start.1) | async-done | bytes 65568 | tf_op jit(solution)/shard_map/all_to_all | solution.py:616
  49.7 2.1 %shard_map.149 = (f32[8,7680]{1,0:T(8,128)S(1)}, f32[8,1024]{1,0:T(8,128)S(1)}, f32[8,1024]{1,0:T(8,128)S(1)}, f32[1,128]{1,0:T(1,128)S(1)}) custom-call(s32[8,128]{1,0:T(8,128)S(1)} %get-tuple-element.36.table_ref, f32[32,4,128]{2,1,0:T(4,128)S(1)} %all-to-all-done.1.sums_ref, f32[32,4,128]{2,1,0:T(4,128)S(1)} %all-to-all-done.sums_ref.coupling_ref, ...), custom_call_target="tpu_custom_call" | custom-call | tf_op jit(solution)/shard_map/pallas_call | solution.py:541
  52.3 2.0 %collective-permute-start.5 = (f32[8,1024]{1,0:T(8,128)S(1)}, f32[8,1024]{1,0:T(8,128)S(1)}, u32[]{:S(2)}, u32[]{:S(2)}) collective-permute-start(f32[8,1024]{1,0:T(8,128)S(1)} %get-tuple-element.68), channel_id=1, source_target_pairs={{1,2},{2,1},{3,4},{4,3},{5,6},{6,5},{7,8},{8,7},{9,10},{10,9},{11,... | collective-permute-start | bytes 98312 | tf_op jit(solution)/shard_map/ppermute | solution.py:536
  54.3 0.9 %shard_map.150 = (f32[8,6656]{1,0:T(8,128)}, f32[8,6656]{1,0:T(8,128)S(1)}, f32[8,128]{1,0:T(8,128)S(1)}) custom-call(f32[8,6656]{1,0:T(8,128)S(1)} %copy-done.1, f32[8,9472]{1,0:T(8,128)S(1)} %get-tuple-element.43.p_ref, f32[2,7680]{1,0:T(2,128)S(1)} %get-tuple-element.44.diag_ref.diag_in_ref, f32[8,128]{1,0:T(8,128)S(1)} %get-tuple-element.45.shift_ref, ...), custom_call_target="tpu_custom_call" | custom-call | tf_op jit(solution)/shard_map/pallas_call | solution.py:541
  55.3 2.2 %collective-permute-done.5.halo_b_ref = f32[8,1024]{1,0:T(8,128)S(1)} collective-permute-done((f32[8,1024]{1,0:T(8,128)S(1)}, f32[8,1024]{1,0:T(8,128)S(1)}, u32[]{:S(2)}, u32[]{:S(2)}) %collective-permute-start.5) | collective-permute-done | bytes 32800 | tf_op jit(solution)/shard_map/ppermute | solution.py:536
  57.5 1.4 %shard_map.151 = f32[8,6656]{1,0:T(8,128)} custom-call(s32[8,128]{1,0:T(8,128)S(1)} %get-tuple-element.36.table_ref, f32[8,6656]{1,0:T(8,128)S(1)} %get-tuple-element.66.residual_in_ref, f32[8,1024]{1,0:T(8,128)S(1)} %collective-permute-done.4.halo_a_ref, f32[8,1024]{1,0:T(8,128)S(1)} %collective-permute-done.5.halo_b_ref, ...), custom_call_target="tpu_custom_call" | custom-call | tf_op jit(solution)/shard_map/pallas_call | solution.py:541
  (32 shorter events, 1.1 us)
Async XLA Ops:
  0.6 0.8 %copy-start.12 = (f32[6656]{0:T(1024)S(1)}, f32[6656]{0:T(1024)}, u32[]{:S(2)}) copy-start(f32[6656]{0:T(1024)} %param.15) | copy-start | bytes 79876
  1.5 0.7 %copy-start.6 = (f32[8]{0:T(128)S(1)}, f32[8]{0:T(128)}, u32[]{:S(2)}) copy-start(f32[8]{0:T(128)} %shift_ref.1) | copy-start | bytes 100
  2.1 0.9 %copy-start = (f32[8,6656]{1,0:T(8,128)S(1)}, f32[8,6656]{1,0:T(8,128)}, u32[]{:S(2)}) copy-start(f32[8,6656]{1,0:T(8,128)} %rhs_ref.3) | copy-start | bytes 638980
  3.0 5.3 %copy-start.4 = (s32[32,343]{1,0:T(8,128)S(1)}, s32[32,343]{1,0:T(8,128)}, u32[]{:S(2)}) copy-start(s32[32,343]{1,0:T(8,128)} %conn_ref.1) | copy-start | bytes 131716
  3.8 4.6 %copy-start.10 = (s32[8]{0:T(128)S(1)}, s32[8]{0:T(128)}, u32[]{:S(2)}) copy-start(s32[8]{0:T(128)} %atom_ref.1) | copy-start | bytes 100
  3.8 4.6 %copy-start.11 = (s32[32]{0:T(128)S(1)}, s32[32]{0:T(128)}, u32[]{:S(2)}) copy-start(s32[32]{0:T(128)} %scount_ref.1) | copy-start | bytes 388
  3.8 4.6 %copy-start.7 = (s32[32]{0:T(128)S(1)}, s32[32]{0:T(128)}, u32[]{:S(2)}) copy-start(s32[32]{0:T(128)} %count_ref.1) | copy-start | bytes 388
  3.8 4.7 %copy-start.8 = (f32[32]{0:T(128)S(1)}, f32[32]{0:T(128)}, u32[]{:S(2)}) copy-start(f32[32]{0:T(128)} %scale_ref.1) | copy-start | bytes 388
  3.8 4.6 %copy-start.9 = (s32[8]{0:T(128)S(1)}, s32[8]{0:T(128)}, u32[]{:S(2)}) copy-start(s32[8]{0:T(128)} %cell_ref.1) | copy-start | bytes 100
  3.8 8.0 %collective-permute-start = (f32[8,512]{1,0:T(8,128)S(1)}, f32[8,512]{1,0:T(8,128)S(1)}, u32[]{:S(2)}, u32[]{:S(2)}) collective-permute-start(f32[8,512]{1,0:T(8,128)S(1)} %get-tuple-element.39), channel_id=1, source_target_pairs={{0,1},{1,0},{2,3},{3,2},{4,5},{5,4},{6,7},{7,6},{8,9},{9,8},{10,11... | collective-permute-start | bytes 49160 | tf_op jit(solution)/shard_map/ppermute | solution.py:536
  3.9 7.9 %collective-permute-start.1 = (f32[8,512]{1,0:T(8,128)S(1)}, f32[8,512]{1,0:T(8,128)S(1)}, u32[]{:S(2)}, u32[]{:S(2)}) collective-permute-start(f32[8,512]{1,0:T(8,128)S(1)} %get-tuple-element.40), channel_id=1, source_target_pairs={{1,2},{2,1},{3,4},{4,3},{5,6},{6,5},{7,8},{8,7},{9,10},{10,9},{11,... | collective-permute-start | bytes 49160 | tf_op jit(solution)/shard_map/ppermute | solution.py:536
  9.3 2.5 %copy-start.3 = (f32[8,8,343]{2,1,0:T(8,128)S(1)}, f32[8,8,343]{2,1,0:T(8,128)}, u32[]{:S(2)}) copy-start(f32[8,8,343]{2,1,0:T(8,128)} %param.21) | copy-start | bytes 263428
  9.3 2.5 %copy-start.5 = (f32[2,8,8]{2,1,0:T(8,128)S(1)}, f32[2,8,8]{2,1,0:T(8,128)}, u32[]{:S(2)}) copy-start(f32[2,8,8]{2,1,0:T(8,128)} %coupling_ref.1) | copy-start | bytes 1540
  11.8 7.7 %copy-start.2 = (f32[343,343]{1,0:T(8,128)S(1)}, f32[343,343]{1,0:T(8,128)}, u32[]{:S(2)}) copy-start(f32[343,343]{1,0:T(8,128)} %refs_1_.1) | copy-start | bytes 1411792
  14.4 12.4 %all-to-all-start = ((f32[32,4,128]{2,1,0:T(4,128)}), f32[32,4,128]{2,1,0:T(4,128)S(1)}, u32[]{:S(2)}, u32[]{:S(2)}) async-start(f32[32,4,128]{2,1,0:T(4,128)} %get-tuple-element.46), calls=%async_computation | async-start | bytes 131072 | tf_op jit(solution)/shard_map/all_to_all | solution.py:586
  28.9 4.5 %collective-permute-start.2 = (f32[10,1024]{1,0:T(8,128)S(1)}, f32[10,1024]{1,0:T(8,128)S(1)}, u32[]{:S(2)}, u32[]{:S(2)}) collective-permute-start(f32[10,1024]{1,0:T(8,128)S(1)} %get-tuple-element.55), channel_id=1, source_target_pairs={{0,1},{1,0},{2,3},{3,2},{4,5},{5,4},{6,7},{7,6},{8,9},{9,8},{10,11... | collective-permute-start | bytes 122888 | tf_op jit(solution)/shard_map/ppermute | solution.py:536
  29.4 5.6 %collective-permute-start.3 = (f32[10,1024]{1,0:T(8,128)S(1)}, f32[10,1024]{1,0:T(8,128)S(1)}, u32[]{:S(2)}, u32[]{:S(2)}) collective-permute-start(f32[10,1024]{1,0:T(8,128)S(1)} %get-tuple-element.56), channel_id=1, source_target_pairs={{1,2},{2,1},{3,4},{4,3},{5,6},{6,5},{7,8},{8,7},{9,10},{10,9},{11,... | collective-permute-start | bytes 122888 | tf_op jit(solution)/shard_map/ppermute | solution.py:536
  38.8 10.8 %all-to-all-start.1 = ((f32[32,4,128]{2,1,0:T(4,128)}), f32[32,4,128]{2,1,0:T(4,128)S(1)}, u32[]{:S(2)}, u32[]{:S(2)}) async-start(f32[32,4,128]{2,1,0:T(4,128)} %get-tuple-element.61), calls=%async_computation.1 | async-start | bytes 131072 | tf_op jit(solution)/shard_map/all_to_all | solution.py:616
  46.2 8.1 %copy-start.1 = (f32[8,6656]{1,0:T(8,128)S(1)}, f32[8,6656]{1,0:T(8,128)}, u32[]{:S(2)}) copy-start(f32[8,6656]{1,0:T(8,128)} %rhs_ref.3) | copy-start | bytes 638980
  51.8 3.5 %collective-permute-start.4 = (f32[8,1024]{1,0:T(8,128)S(1)}, f32[8,1024]{1,0:T(8,128)S(1)}, u32[]{:S(2)}, u32[]{:S(2)}) collective-permute-start(f32[8,1024]{1,0:T(8,128)S(1)} %get-tuple-element.67), channel_id=1, source_target_pairs={{0,1},{1,0},{2,3},{3,2},{4,5},{5,4},{6,7},{7,6},{8,9},{9,8},{10,11... | collective-permute-start | bytes 98312 | tf_op jit(solution)/shard_map/ppermute | solution.py:536
  52.3 5.2 %collective-permute-start.5 = (f32[8,1024]{1,0:T(8,128)S(1)}, f32[8,1024]{1,0:T(8,128)S(1)}, u32[]{:S(2)}, u32[]{:S(2)}) collective-permute-start(f32[8,1024]{1,0:T(8,128)S(1)} %get-tuple-element.68), channel_id=1, source_target_pairs={{1,2},{2,1},{3,4},{4,3},{5,6},{6,5},{7,8},{8,7},{9,10},{10,9},{11,... | collective-permute-start | bytes 98312 | tf_op jit(solution)/shard_map/ppermute | solution.py:536

commit v9 on v8

--- a/solution.py
+++ b/solution.py
@@ -41,6 +41,11 @@
         self.tiles = self.width // LANES
         self.pairs = self.channels * self.vectors
         self.reach = self.window + SPAN * LANES
+        self.index_row = self.entries * self.channels
+        self.rim_row = self.index_row + round_up(self.entries, ROWS)
+        self.rim_pieces = -(-self.rim // self.width)
+        self.message = self.rim_row + self.rim_pieces * ROWS
+        assert self.elem + 3 <= self.width
         self.together = TOGETHER if self.slots % TOGETHER == 0 else 1
         assert self.vectors == ROWS and self.channels == ROWS and 2 * self.slots <= LANES
         assert self.nodes % WIDE == 0 and self.owned * self.pairs == LANES
@@ -65,7 +70,7 @@
     return jnp.sum(jnp.where(iota((ROWS, LANES), 1) == iota((ROWS, LANES), 0), spread, 0.0), axis=0, keepdims=True)
 
 
-LOW, HIGH, FIRST_LIST, SECOND_LIST, CELL, OWNER, LOCAL, OTHER = range(8)
+LOW, HIGH, LIST, NOTHING, CELL, OWNER, LOCAL, OTHER = range(8)
 
 
 def prepare_kernel(
@@ -96,15 +101,13 @@
         return jnp.sum(jnp.where(lane == cell, column, 0.0), axis=0, keepdims=True)
 
     rows = [as_row(low), as_row(high)]
-    for margin in (z.rim, 2 * z.rim):
-        good = jnp.where((low >= margin) & (high < z.window - margin), 1.0, 0.0)
-        good = jnp.broadcast_to(good, (z.slots, LANES))
-        number = cell.astype(F32)
-        before = jnp.sum(jnp.where(lane < cell, as_row(good), 0.0), axis=1, keepdims=True)
-        at = jnp.where(good > 0.5, before, z.slots - 1.0 - (number - before))
-        rows.append(
-            jnp.sum(jnp.where(lane.astype(F32) == at, number + z.slots * good, 0.0), axis=0, keepdims=True)
-        )
+    good = jnp.where((low >= z.rim) & (high < z.window - z.rim), 1.0, 0.0)
+    good = jnp.broadcast_to(good, (z.slots, LANES))
+    number = cell.astype(F32)
+    before = jnp.sum(jnp.where(lane < cell, as_row(good), 0.0), axis=1, keepdims=True)
+    at = jnp.where(good > 0.5, before, z.slots - 1.0 - (number - before))
+    rows.append(jnp.sum(jnp.where(lane.astype(F32) == at, number + z.slots * good, 0.0), axis=0, keepdims=True))
+    rows.append(jnp.zeros((1, LANES), F32))
     table = [row.astype(jnp.int32) for row in rows]
     facts = [jnp.zeros((1, LANES), jnp.int32)] * 3
     for s in range(z.entries):
@@ -117,15 +120,52 @@
 
 
 def start_kernel(
-    z, pos_ref, shift_ref, rhs_ref, precond_ref, potential_ref,
-    p_ref, send_a_ref, send_b_ref, gamma_ref, diag_ref, shift_tile_ref,
+    z, pos_ref, cell_ref, atom_ref, scount_ref, rhs_ref, precond_ref, conn_ref, projector_ref,
+    send_a_ref, send_b_ref, rhs_rim, precond_rim, conn_all, projector_all, sems,
+):
+    copies = [
+        pltpu.make_async_copy(conn_ref, conn_all, sems.at[0]),
+        pltpu.make_async_copy(projector_ref, projector_all, sems.at[1]),
+    ]
+    for k, first in enumerate((0, z.nodes - z.rim)):
+        at, to = pl.ds(first, z.rim), pl.ds(k * z.rim, z.rim)
+        copies.append(pltpu.make_async_copy(rhs_ref.at[:, at], rhs_rim.at[:, to], sems.at[2 + k]))
+        copies.append(pltpu.make_async_copy(precond_ref.at[:, at], precond_rim.at[:, to], sems.at[4 + k]))
+    for copy in copies:
+        copy.start()
+    for copy in copies:
+        copy.wait()
+    rims = rhs_rim[...] * precond_rim[...]
+    head, tail = rims[:, : z.rim], rims[:, z.rim :]
+    even = pos_ref[0] % 2 == 0
+    sides = jnp.where(even, tail, head), jnp.where(even, head, tail)
+    nodes = (conn_all[...] + z.shift).astype(F32)
+    cell = iota(nodes.shape, 0)
+    entry = iota((z.rim_row - z.index_row, z.width), 0)
+    place = iota((z.rim_row - z.index_row, z.width), 1)
+    rows = jnp.zeros((z.rim_row - z.index_row, z.width), F32)
+    for s in range(z.entries):
+        row = jnp.sum(jnp.where(cell == cell_ref[s], nodes, 0.0), axis=0, keepdims=True)
+        row = jnp.concatenate([row, jnp.zeros((1, z.width - z.elem), F32)], axis=1)
+        owner = atom_ref[s] // z.owned
+        facts = owner, atom_ref[s] - owner * z.owned, (s < scount_ref[pos_ref[0]]).astype(jnp.int32)
+        rows = jnp.where(entry == s, row, rows)
+        for k, fact in enumerate(facts):
+            rows = jnp.where((entry == s) & (place == z.elem + k), fact.astype(F32), rows)
+    for ref, side in zip((send_a_ref, send_b_ref), sides):
+        ref[...] = jnp.zeros_like(ref)
+        ref[: z.index_row, : z.elem] = projector_all[...]
+        ref[z.index_row : z.rim_row, :] = rows
+        for k in range(z.rim_pieces):
+            piece = side[:, k * z.width : min((k + 1) * z.width, z.rim)]
+            ref[z.rim_row + k * ROWS : z.rim_row + (k + 1) * ROWS, : piece.shape[1]] = piece
+
+
+def own_kernel(
+    z, shift_ref, rhs_ref, precond_ref, potential_ref, p_ref, gamma_ref, diag_ref, shift_tile_ref,
 ):
     product = rhs_ref[...] * precond_ref[...]
     own = slice(z.rim, z.rim + z.nodes)
-    head, tail = product[:, : z.rim], product[:, z.nodes - z.rim :]
-    even = pos_ref[0] % 2 == 0
-    send_a_ref[...] = jnp.where(even, tail, head)
-    send_b_ref[...] = jnp.where(even, head, tail)
     p_ref[:, own] = product
     p_ref[:, z.window :] = jnp.zeros((ROWS, z.reach - z.window), F32)
     gamma_ref[...] = lanes_by_vector(z, product * rhs_ref[...])
@@ -139,18 +179,20 @@
     shift_tile_ref[...] = tile
 
 
-def full_groups(z, table_ref, which):
-    ends = [table_ref[which, g * z.together + z.together - 1] for g in range(z.slots // z.together)]
+def full_groups(z, table_ref):
+    ends = [table_ref[LIST, g * z.together + z.together - 1] for g in range(z.slots // z.together)]
     return functools.reduce(jnp.add, [(end >= z.slots).astype(jnp.int32) for end in ends])
 
 
-def gather_middle(z, groups, which, table_ref, index_ref, window_ref, u_ref):
+def gather_middle(z, groups, listed, table_ref, index_ref, window_ref, u_ref):
     total = z.window // LANES
     tile = (ROWS, LANES)
 
     def some_cells(g, _):
-        cells = [table_ref[which, g * z.together + i] for i in range(z.together)]
-        cells = [jnp.where(c >= z.slots, c - z.slots, c) for c in cells]
+        cells = [g * z.together + i for i in range(z.together)]
+        if listed:
+            cells = [table_ref[LIST, c] for c in cells]
+            cells = [jnp.where(c >= z.slots, c - z.slots, c) for c in cells]
         starts = [table_ref[LOW, c] >> 7 for c in cells]
         ends = [table_ref[HIGH, c] >> 7 for c in cells]
         passes = functools.reduce(jnp.maximum, [(e - s) // SPAN + 1 for s, e in zip(starts, ends)])
@@ -239,8 +281,8 @@
 
 
 def first_window_kernel(z, table_ref, p_ref, index_ref, u_ref):
-    groups = 0, full_groups(z, table_ref, FIRST_LIST)
-    gather_middle(z, groups, FIRST_LIST, table_ref, index_ref, p_ref, u_ref)
+    groups = 0, full_groups(z, table_ref)
+    gather_middle(z, groups, True, table_ref, index_ref, p_ref, u_ref)
 
 
 def first_kernel(
@@ -248,15 +290,19 @@
     coupling_ref, p_ref, out_ref, uw_ref, pj_ref, u_ref,
 ):
     own = slice(z.rim, z.rim + z.nodes)
-    halo = sides(table_ref[OTHER, 0], halo_a_ref[...], halo_b_ref[...])
-    p_ref[:, : z.rim], p_ref[:, z.rim + z.nodes : z.window] = halo
+    for k in range(z.rim_pieces):
+        rows = slice(z.rim_row + k * ROWS, z.rim_row + (k + 1) * ROWS)
+        at, to = k * z.width, min((k + 1) * z.width, z.rim)
+        left, right = sides(table_ref[OTHER, 0], halo_a_ref[rows, : to - at], halo_b_ref[rows, : to - at])
+        p_ref[:, at:to] = left
+        p_ref[:, z.rim + z.nodes + at : z.rim + z.nodes + to] = right
     p_ref[:, own] = p_in_ref[:, own]
     p_ref[:, z.window :] = p_in_ref[:, z.window :]
     u_ref[...] = u_in_ref[...]
     pj_ref[...] = jnp.zeros_like(pj_ref)
     pj_ref[:, : z.elem] = projector_ref[...]
-    groups = full_groups(z, table_ref, FIRST_LIST), z.slots // z.together
-    gather_middle(z, groups, FIRST_LIST, table_ref, index_ref, p_ref, u_ref)
+    groups = full_groups(z, table_ref), z.slots // z.together
+    gather_middle(z, groups, True, table_ref, index_ref, p_ref, u_ref)
     gather_corners(z, corner_ref, p_ref, weight_ref, u_ref, uw_ref)
     parts = contributions(z, table_ref, pj_ref, u_ref)
     small_lane, small_row = iota((ROWS, LANES), 1), iota((ROWS, LANES), 0)
@@ -270,35 +316,20 @@
         out_ref[d] = message
 
 
-def second_window_kernel(
-    z, table_ref, p_ref, diag_ref, shift_ref, image_ref, index_ref, y_ref, q_ref, u_ref,
-):
-    y_ref[...] = image_ref[...] + (diag_ref[1:2, :] + shift_ref[:, :1]) * p_ref[:, : z.window]
-    q_ref[:, : z.window] = y_ref[...] * diag_ref[0:1, :]
-    q_ref[:, z.window :] = jnp.zeros((ROWS, z.reach - z.window), F32)
-    groups = 0, full_groups(z, table_ref, SECOND_LIST)
-    gather_middle(z, groups, SECOND_LIST, table_ref, index_ref, q_ref, u_ref)
-
-
 def second_kernel(
-    z, table_ref, y_in_ref, q_in_ref, u_in_ref, p_ref, diag_in_ref, shift_ref, gamma_ref, halo_a_ref, halo_b_ref,
+    z, table_ref, image_ref, p_ref, diag_in_ref, shift_ref, gamma_ref, halo_a_ref, halo_b_ref,
     index_ref, corner_ref, weight_ref, k_high_ref, k_low_ref, pj_ref, y_ref, q_ref, out_ref, e_ref, diag_ref, u_ref, uw_ref,
 ):
     left, right = sides(table_ref[OTHER, 0], halo_a_ref[...], halo_b_ref[...])
     own = slice(z.rim, z.rim + z.nodes)
-    ghosts = slice(0, z.rim), slice(z.rim + z.nodes, z.window)
     diag_ref[:, own] = diag_in_ref[:, own]
-    diag_ref[:, ghosts[0]] = left[ROWS : ROWS + 2, : z.rim]
-    diag_ref[:, ghosts[1]] = right[ROWS : ROWS + 2, z.rim :]
-    y_ref[...] = y_in_ref[...]
-    for ghost in ghosts:
-        y_ref[:, ghost] += (diag_ref[1:2, ghost] - diag_in_ref[1:2, ghost]) * p_ref[:, ghost]
+    diag_ref[:, : z.rim] = left[ROWS : ROWS + 2, : z.rim]
+    diag_ref[:, z.rim + z.nodes :] = right[ROWS : ROWS + 2, z.rim :]
+    y_ref[...] = image_ref[...] + (diag_ref[1:2, :] + shift_ref[:, :1]) * p_ref[:, : z.window]
     y_ref[:, : 2 * z.rim] += left[:ROWS]
     y_ref[:, z.window - 2 * z.rim :] += right[:ROWS]
-    q_ref[...] = q_in_ref[...]
-    for rims in (slice(0, 2 * z.rim), slice(z.window - 2 * z.rim, z.window)):
-        q_ref[:, rims] = y_ref[:, rims] * diag_ref[0:1, rims]
-    u_ref[...] = u_in_ref[...]
+    q_ref[:, : z.window] = y_ref[...] * diag_ref[0:1, :]
+    q_ref[:, z.window :] = jnp.zeros((ROWS, z.reach - z.window), F32)
     y, q = y_ref[:, own], q_ref[:, own]
     dots = [
         gamma_ref[...],
@@ -306,8 +337,8 @@
         lanes_by_vector(z, y * q),
     ]
     energy = jnp.sum(q * q * (diag_ref[1:2, own] + shift_ref[:, :1]), axis=1, keepdims=True)
-    groups = full_groups(z, table_ref, SECOND_LIST), z.slots // z.together
-    gather_middle(z, groups, SECOND_LIST, table_ref, index_ref, q_ref, u_ref)
+    groups = 0, z.slots // z.together
+    gather_middle(z, groups, False, table_ref, index_ref, q_ref, u_ref)
     gather_corners(z, corner_ref, q_ref, weight_ref, u_ref, uw_ref)
     parts = contributions(z, table_ref, pj_ref, u_ref)
     stiffness_product(k_high_ref, k_low_ref, uw_ref, e_ref)
@@ -391,6 +422,16 @@
 
         lax.fori_loop(0, passes, one_pass, 0)
 
+    def add_rows(self, index, values, first, rows):
+        lhs, hot = [], []
+        for t in range(values.shape[1] // LANES):
+            lanes = slice(t * LANES, (t + 1) * LANES)
+            at = jnp.broadcast_to(index[:, lanes], self.pair)
+            lhs.append(self.masked(at >> 8, self.two_parts(values[:, lanes]), rows))
+            hot.append(self.hot_rows(at))
+        to = slice(first * 2 * ROWS, (first + rows) * 2 * ROWS)
+        self.acc_ref[to, :] += self.product(jnp.concatenate(lhs, axis=1), jnp.concatenate(hot, axis=1))
+
     def result(self, h):
         at = h * 2 * ROWS
         return self.acc_ref[at : at + ROWS] + self.acc_ref[at + ROWS : at + 2 * ROWS]
@@ -398,13 +439,14 @@
 
 def cells_kernel(z, multiply, table_ref, index_ref, corner_ref, *refs):
     if multiply:
-        uw_ref, stiffness_ref, image_ref, k_high_ref, k_low_ref, e_ref, k_ref, acc_ref = refs
+        uw_ref, stiffness_ref, diag_ref, image_ref, send_a_ref, send_b_ref, k_high_ref, k_low_ref, *refs = refs
+        e_ref, k_ref, acc_ref = refs
         k_ref[...] = jnp.zeros_like(k_ref)
         k_ref[: z.elem, : z.elem] = stiffness_ref[...]
         k_high_ref[...], k_low_ref[...] = split(k_ref[...])
         stiffness_product(k_high_ref, k_low_ref, uw_ref, e_ref)
     else:
-        e_ref, image_ref, acc_ref = refs
+        e_ref, image_ref, send_a_ref, send_b_ref, acc_ref = refs
     scatter = Scatter(z, table_ref, index_ref, corner_ref, acc_ref)
     scatter.start([(c, e_ref[c * ROWS : (c + 1) * ROWS, :]) for c in range(z.slots)])
 
@@ -421,15 +463,22 @@
     lax.fori_loop(0, z.slots // z.together, some_cells, 0)
     for h in range(scatter.groups):
         image_ref[:, h * WIDE : (h + 1) * WIDE] = scatter.result(h)
+    even = table_ref[OTHER, 0] % 2 == 0
+    ends = [slice(0, 2 * z.rim), slice(z.window - 2 * z.rim, z.window)]
+    for source_ref, rows in ((image_ref, slice(0, ROWS)),) + (((diag_ref, slice(ROWS, ROWS + 2)),) if multiply else ()):
+        low_rim, high_rim = (source_ref[:, end] for end in ends)
+        send_a_ref[rows, :] = jnp.where(even, high_rim, low_rim)
+        send_b_ref[rows, :] = jnp.where(even, low_rim, high_rim)
 
 
 def support_kernel(
-    z, last, table_ref, sums_ref, coupling_ref, index_ref, corner_ref, pj_ref, diag_ref, cells_ref, *refs,
+    z, last, table_ref, sums_ref, coupling_ref, index_ref, corner_ref, pj_ref, ext_a_ref, ext_b_ref,
+    cells_ref, *refs,
 ):
     if last:
-        image_ref, send_a_ref, send_b_ref, dots_ref, support_ref, acc_ref = refs
+        image_ref, dots_ref, support_ref, acc_ref = refs
     else:
-        image_ref, send_a_ref, send_b_ref, support_ref, acc_ref = refs
+        image_ref, support_ref, acc_ref = refs
     position = table_ref[OTHER, 0]
     wanted = (
         pltpu.roll(sums_ref[:, 0, :], z.devices - 1, 0) + sums_ref[:, 1, :] + pltpu.roll(sums_ref[:, 2, :], 1, 0)
@@ -455,17 +504,20 @@
         )
     block = iota(shape, 0)
     small_lane, small_row = iota((ROWS, LANES), 1), iota((ROWS, LANES), 0)
-    spread = []
-    for s in range(z.entries):
-        owner, local, alive = entry_facts(table_ref, s)
-        mine = jnp.sum(jnp.where(block == owner, term, 0.0), axis=0, keepdims=True)
-        got = lane_gather(
-            jnp.broadcast_to(mine, (ROWS, LANES)), local * z.pairs + small_lane % ROWS * ROWS + small_row
+
+    def values(facts, projectors):
+        spread = []
+        for s, (owner, local, alive) in enumerate(facts):
+            mine = jnp.sum(jnp.where(block == owner, term, 0.0), axis=0, keepdims=True)
+            got = lane_gather(
+                jnp.broadcast_to(mine, (ROWS, LANES)), local * z.pairs + small_lane % ROWS * ROWS + small_row
+            )
+            spread.append(jnp.where((small_lane // ROWS == s) & alive, got, 0.0)[:, : z.entries * ROWS])
+        return jnp.dot(
+            jnp.concatenate(spread, axis=0), projectors, precision=HIGHEST, preferred_element_type=F32
         )
-        spread.append(jnp.where((small_lane // ROWS == s) & alive, got, 0.0)[:, : z.entries * ROWS])
-    support_ref[...] = jnp.dot(
-        jnp.concatenate(spread, axis=0), pj_ref[...], precision=HIGHEST, preferred_element_type=F32
-    )
+
+    support_ref[...] = values([entry_facts(table_ref, s) for s in range(z.entries)], pj_ref[...])
     scatter = Scatter(z, table_ref, index_ref, corner_ref, acc_ref)
     cells = [table_ref[CELL, s] for s in range(z.entries)]
     scatter.start([(cell, support_ref[s * ROWS : (s + 1) * ROWS, :]) for s, cell in enumerate(cells)])
@@ -477,19 +529,28 @@
             return support_ref[s * ROWS : (s + 1) * ROWS, t * LANES : (t + 1) * LANES]
 
         scatter.add(some, value_of)
+    used = slice(0, z.rim_row)
+    shared = 2 * z.rim // WIDE
+    neighbours = sides(position, ext_a_ref[used, :], ext_b_ref[used, :])
+    for ext, first, offset in zip(neighbours, (0, scatter.groups - shared), (z.window - 2 * z.rim, 0)):
+        nodes = ext[z.index_row :].astype(jnp.int32)
+        facts = []
+        for s in range(z.entries):
+            fact = [jnp.broadcast_to(nodes[s : s + 1, z.elem + k : z.elem + k + 1], (1, LANES)) for k in range(3)]
+            facts.append((fact[0], fact[1], fact[2] > 0))
+        rows = values(facts, jnp.where(iota((z.index_row, z.width), 1) < z.elem, ext[: z.index_row], 0.0))
+        for s in range(0, z.entries, 2):
+            index = jnp.concatenate([nodes[s : s + 1], nodes[s + 1 : s + 2]], axis=1) - offset
+            pair = jnp.concatenate([rows[s * ROWS : (s + 1) * ROWS], rows[(s + 1) * ROWS : (s + 2) * ROWS]], axis=1)
+            scatter.add_rows(index, pair, first, shared)
     for h in range(scatter.groups):
         at = slice(h * WIDE, (h + 1) * WIDE)
         image_ref[:, at] = cells_ref[:, at] + scatter.result(h)
-    even = position % 2 == 0
-    ends = [slice(0, 2 * z.rim), slice(z.window - 2 * z.rim, z.window)]
-    for source_ref, rows in ((image_ref, slice(0, ROWS)),) + (() if last else ((diag_ref, slice(ROWS, ROWS + 2)),)):
-        low_rim, high_rim = (source_ref[:, end] for end in ends)
-        send_a_ref[rows, :] = jnp.where(even, high_rim, low_rim)
-        send_b_ref[rows, :] = jnp.where(even, low_rim, high_rim)
 
 
 def last_kernel(
-    z, rhs_ref, p_ref, diag_ref, shift_ref, y_ref, q_ref, image_ref, dots_ref, solution_ref, residual_ref, factor_ref,
+    z, table_ref, rhs_ref, p_ref, diag_ref, shift_ref, y_ref, q_ref, image_ref, dots_ref, halo_a_ref, halo_b_ref,
+    solution_ref, residual_ref,
 ):
     own = slice(z.rim, z.rim + z.nodes)
     lane, row = iota((ROWS, LANES), 1), iota((ROWS, LANES), 0)
@@ -509,16 +570,9 @@
     search = (p - alpha * q) + beta * p
     solution_ref[...] = alpha * p + step * search
     residual_ref[...] = (rhs_ref[...] - alpha * y) - step * (more * y - alpha * second)
-    factor_ref[...] = jnp.broadcast_to(step * alpha, (ROWS, LANES))
-
-
-def rim_kernel(z, table_ref, residual_in_ref, halo_a_ref, halo_b_ref, factor_ref, residual_ref):
     left, right = sides(table_ref[OTHER, 0], halo_a_ref[...], halo_b_ref[...])
-    factor = factor_ref[:, :1]
-    first, last = slice(0, z.rim), slice(z.nodes - z.rim, z.nodes)
-    residual_ref[:, z.rim : z.nodes - z.rim] = residual_in_ref[:, z.rim : z.nodes - z.rim]
-    residual_ref[:, first] = residual_in_ref[:, first] + factor * left[:, z.rim :]
-    residual_ref[:, last] = residual_in_ref[:, last] + factor * right[:, : z.rim]
+    residual_ref[:, : z.rim] += step * alpha * left[:, z.rim :]
+    residual_ref[:, z.nodes - z.rim :] += step * alpha * right[:, : z.rim]
 
 
 def on_device(
@@ -535,17 +589,17 @@
     def exchange(a, b):
         return lax.ppermute(a, "dom", near), lax.ppermute(b, "dom", far)
 
-    def call(kernel, outs, scratch, scalars, *args, in_hbm=(), copied=False):
-        if not copied:
-            args = [pltpu.with_memory_space_constraint(x, pltpu.VMEM) for x in args]
+    def call(kernel, outs, scratch, scalars, *args, in_hbm=(), by_hand=False):
+        space = pltpu.HBM if by_hand else pltpu.VMEM
+        args = [pltpu.with_memory_space_constraint(x, space) for x in args]
         return pl.pallas_call(
             kernel,
             out_shape=[
                 jax.ShapeDtypeStruct(s, d) if i in in_hbm else pltpu.VMEM(s, d) for i, (s, d) in enumerate(outs)
             ],
-            in_specs=[SMEM] * len(scalars) + [VMEM] * len(args),
+            in_specs=[SMEM] * len(scalars) + [pl.BlockSpec(memory_space=space)] * len(args),
             out_specs=[VMEM] * len(outs),
-            scratch_shapes=[pltpu.VMEM(s, d) for s, d in scratch],
+            scratch_shapes=[pltpu.VMEM(*s) if isinstance(s, tuple) else s for s in scratch],
             compiler_params=pltpu.CompilerParams(vmem_limit_bytes=16 * 1024 * 1024),
         )(*scalars, *args)
 
@@ -558,15 +612,17 @@
     acc = ((z.window // WIDE + BAND) * 2 * ROWS, WIDE)
 
     tile = (ROWS, LANES)
-    p, send_a, send_b, gamma, diag, shift_tile = call(
-        functools.partial(start_kernel, z),
-        [(reach, F32), ((z.vectors, z.rim), F32), ((z.vectors, z.rim), F32), ((1, LANES), F32), ((2, z.window), F32),
-         (tile, F32)],
-        [],
-        (pos, shift),
-        rhs, precond[None, :], potential[None, :], copied=True,
-    )
-    halo = exchange(send_a, send_b)
+    first_message = (z.message, z.width)
+    ext = exchange(
+        *call(
+            functools.partial(start_kernel, z),
+            [(first_message, F32)] * 2,
+            [((z.vectors, 2 * z.rim), F32), ((1, 2 * z.rim), F32), (conn.shape, jnp.int32), (flat_projector.shape, F32),
+             pltpu.SemaphoreType.DMA((6,))],
+            (pos, support_cell, support_atom, support_count),
+            rhs, precond[None, :], conn, flat_projector, by_hand=True,
+        )
+    )
     index, corner, table, weight = call(
         functools.partial(prepare_kernel, z),
         [((z.slots, 1, z.width), jnp.int32), ((1, LANES), jnp.int32), ((ROWS, LANES), jnp.int32),
@@ -575,63 +631,66 @@
         (pos, cell_count, cell_scale, support_cell, support_atom, support_count),
         conn,
     )
+    p, gamma, diag, shift_tile = call(
+        functools.partial(own_kernel, z),
+        [(reach, F32), ((1, LANES), F32), ((2, z.window), F32), (tile, F32)],
+        [],
+        (shift,),
+        rhs, precond[None, :], potential[None, :],
+    )
     (u,) = call(functools.partial(first_window_kernel, z), [(cells, F32)], [], (table,), p, index)
     p, sums, uw, pj = call(
         functools.partial(first_kernel, z),
         [(reach, F32), (message, F32), (cells, F32), (entries, F32)],
         [(cells, F32)],
         (table,),
-        p, u, *halo, index, corner, weight, flat_projector, atom_matrix,
+        p, u, *ext, index, corner, weight, flat_projector, atom_matrix,
     )
     coupled = lax.all_to_all(sums, "dom", 0, 0)
-    image, k_high, k_low = call(
+    image, send_a, send_b, k_high, k_low = call(
         functools.partial(cells_kernel, z, True),
-        [(window, F32), (square, BF16), (square, BF16)],
+        [(window, F32), (more_rim, F32), (more_rim, F32), (square, BF16), (square, BF16)],
         [(cells, F32), (square, F32), (acc, F32)],
         (table,),
-        index, corner, uw, stiffness,
-    )
-    image, send_a, send_b = call(
+        index, corner, uw, stiffness, diag,
+    )
+    halo = exchange(send_a, send_b)
+    (image,) = call(
         functools.partial(support_kernel, z, False),
-        [(window, F32), (more_rim, F32), (more_rim, F32)],
+        [(window, F32)],
         [(entries, F32), (acc, F32)],
         (table,),
-        coupled, coupled, index, corner, pj, diag, image,
-    )
-    halo = exchange(send_a, send_b)
-    y, q, u = call(
-        functools.partial(second_window_kernel, z),
-        [(window, F32), (reach, F32), (cells, F32)],
-        [],
-        (table,),
-        p, diag, shift_tile, image, index,
+        coupled, coupled, index, corner, pj, *ext, image,
     )
     y, q, sums, e = call(
         functools.partial(second_kernel, z),
         [(window, F32), (reach, F32), (message, F32), (cells, F32)],
         [((2, z.window), F32), (cells, F32), (cells, F32)],
         (table,),
-        y, q, u, p, diag, shift_tile, gamma, *halo, index, corner, weight, k_high, k_low, pj,
+        image, p, diag, shift_tile, gamma, *halo, index, corner, weight, k_high, k_low, pj,
     )
     totals = lax.all_to_all(sums, "dom", 0, 0)
-    (image,) = call(functools.partial(cells_kernel, z, False), [(window, F32)], [(acc, F32)], (table,), index, corner, e)
-    image, send_a, send_b, dots = call(
+    image, send_a, send_b = call(
+        functools.partial(cells_kernel, z, False), [(window, F32), (rim, F32), (rim, F32)], [(acc, F32)], (table,),
+        index, corner, e,
+    )
+    halo = exchange(send_a, send_b)
+    image, dots = call(
         functools.partial(support_kernel, z, True),
-        [(window, F32), (rim, F32), (rim, F32), ((1, LANES), F32)],
+        [(window, F32), ((1, LANES), F32)],
         [(entries, F32), (acc, F32)],
         (table,),
-        totals, coupled, index, corner, pj, diag, image,
-    )
-    halo = exchange(send_a, send_b)
-    answer, residual, factor = call(
-        functools.partial(last_kernel, z),
-        [(own, F32), (own, F32), (tile, F32)],
-        [],
-        (),
-        rhs, p, diag, shift_tile, y, q, image, dots, in_hbm=(0,),
-    )
-    (residual,) = call(functools.partial(rim_kernel, z), [(own, F32)], [], (table,), residual, *halo, factor, in_hbm=(0,))
-    return answer, residual
+        totals, coupled, index, corner, pj, *ext, image,
+    )
+    return tuple(
+        call(
+            functools.partial(last_kernel, z),
+            [(own, F32), (own, F32)],
+            [],
+            (table,),
+            rhs, p, diag, shift_tile, y, q, image, dots, *halo, in_hbm=(0, 1),
+        )
+    )
 
 
 def solution(mesh):

time: 59.2 us -> 56.8 us (0.959)
  waiting for transfers between devices: 10 us -> 0.02 us
  starting transfers between devices: 18.3 us -> 23.1 us
  Pallas kernels: 27.2 us -> 30.2 us
    ppermute x6, waiting for transfers between devices: 3.83 us -> 0.02 us  [exchange(): return (lax.ppermute(a, 'dom', near), lax.ppermute(b, 'dom', far))]
    all_to_all x1, waiting for transfers between devices: 3.43 us -> 0.01 us  [on_device(): totals = lax.all_to_all(sums, 'dom', 0, 0)]
    pallas_call x12 -> x11, Pallas kernels: 27.2 us -> 30.2 us  [call(): pl.pallas_call(kernel, out_shape=[jax.ShapeDtypeStruct(s, d) if i in in_h...]
    all_to_all x1, waiting for transfers between devices: 2.79 us -> 0.01 us  [on_device(): coupled = lax.all_to_all(sums, 'dom', 0, 0)]
    ppermute x6, starting transfers between devices: 9.6 us -> 12 us  [exchange(): return (lax.ppermute(a, 'dom', near), lax.ppermute(b, 'dom', far))]
    all_to_all x1, starting transfers between devices: 3.54 us -> 5.16 us  [on_device(): totals = lax.all_to_all(sums, 'dom', 0, 0)]
    broadcast_in_dim x1, local copies, waits for them, and re-layouts: 0.02 us -> 1.37 us  [on_device(): precond[None, :]]
    unnamed x26, local copies, waits for them, and re-layouts: 1.64 us -> 0.73 us
  transfers between devices with their start and end apart: 8 -> 8, of which waited for: 4 -> 0; matrix products, arithmetic and copies ran while one was open for 0% -> 0% of each run, Pallas kernels for 25% -> 34%
where the time goes in v9:
time: 56.8 us; the launch traced here: 56.4 us
  Pallas kernels  30.2 us (53%)
  starting transfers between devices  23.1 us (41%)
  local copies, waits for them, and re-layouts  2.13 us (4%)
  between operations  0.93 us (2%)
    pallas_call x11, Pallas kernels, call(): pl.pallas_call(kernel, out_shape=[jax.ShapeDtypeStruct(s, d) if i in in_h...  30.2 us
    ppermute x6, starting transfers between devices, exchange(): return (lax.ppermute(a, 'dom', near), lax.ppermute(b, 'dom', far))  12 us
    all_to_all x1, starting transfers between devices, on_device(): coupled = lax.all_to_all(sums, 'dom', 0, 0)  5.96 us
    all_to_all x1, starting transfers between devices, on_device(): totals = lax.all_to_all(sums, 'dom', 0, 0)  5.16 us
    broadcast_in_dim x1, local copies, waits for them, and re-layouts, on_device(): precond[None, :]  1.37 us
  transfers between devices with their start and end apart: 8, of which 0 were waited for; matrix products, arithmetic and copies ran while one was open for 0% of the time, Pallas kernels for 34%

profile of v9, /device:TPU:1, one launch (start us, length us, event | category | flops | bytes accessed | tf_op | source)
XLA Modules:
  0.0 56.4 jit_solution(5577045935448300770)
XLA Ops:
  0.6 1.4 %broadcast_in_dim.7.precond_ref = f32[1,6656]{1,0:T(1,128)} reshape(f32[6656]{0:T(1024)} %param.15) | data formatting | bytes 53248 | tf_op jit(solution)/shard_map/broadcast_in_dim | solution.py:639
  2.0 0.6 %copy-done.6 = s32[8]{0:T(128)S(1)} copy-done((s32[8]{0:T(128)S(1)}, s32[8]{0:T(128)}, u32[]{:S(2)}) %copy-start.6) | copy-done | bytes 56
  2.7 0.0 copy-done.7
  2.7 0.0 copy-done.8
  2.7 1.6 %shard_map.143 = (f32[88,384]{1,0:T(8,128)S(1)}, f32[88,384]{1,0:T(8,128)S(1)}) custom-call(s32[1]{0:T(128)} %bitcast.pos_ref, s32[8]{0:T(128)S(1)} %copy-done.6, s32[8]{0:T(128)S(1)} %copy-done.7, s32[32]{0:T(128)S(1)} %copy-done.8, f32[8,6656]{1,0:T(8,128)} %rhs_ref.5, f32[1,6656]{1,0:T(1,128)} %broadcast_in_dim.7.precond_ref, s32[32,343]{1,0:T(8,128)} %conn_ref.3, ...), custom_call_target="tpu_custom_call" | custom-call | tf_op jit(solution)/shard_map/pallas_call | solution.py:595
  4.3 0.0 copy-start.4
  4.3 0.1 collective-permute-start
  4.5 4.5 %collective-permute-start.1 = (f32[88,384]{1,0:T(8,128)S(1)}, f32[88,384]{1,0:T(8,128)S(1)}, u32[]{:S(2)}, u32[]{:S(2)}) collective-permute-start(f32[88,384]{1,0:T(8,128)S(1)} %get-tuple-element.34), channel_id=1, source_target_pairs={{1,2},{2,1},{3,4},{4,3},{5,6},{6,5},{7,8},{8,7},{9,10},{10,9},{11,... | collective-permute-start | bytes 405512 | tf_op jit(solution)/shard_map/ppermute | solution.py:590
  9.0 0.8 %shard_map.140 = (s32[32,1,384]{2,1,0:T(1,128)S(1)}, s32[1,128]{1,0:T(1,128)S(1)}, s32[8,128]{1,0:T(8,128)S(1)}, f32[256,128]{1,0:T(8,128)S(1)}) custom-call(s32[1]{0:T(128)} %bitcast.pos_ref, s32[32]{0:T(128)S(1)} %copy-done.9, f32[32]{0:T(128)S(1)} %copy-done.10, s32[8]{0:T(128)S(1)} %copy-done.6, s32[8]{0:T(128)S(1)} %copy-done.7, s32[32]{0:T(128)S(1)} %copy-done.8, ...), custom_call_target="tpu_custom_call" | custom-call | tf_op jit(solution)/shard_map/pallas_call | solution.py:595
  9.9 0.7 %shard_map.141 = (f32[8,9472]{1,0:T(8,128)S(1)}, f32[1,128]{1,0:T(1,128)S(1)}, f32[2,7680]{1,0:T(2,128)S(1)}, f32[8,128]{1,0:T(8,128)S(1)}) custom-call(f32[8]{0:T(128)S(1)} %copy-done.11, f32[8,6656]{1,0:T(8,128)S(1)} %copy-done, f32[1,6656]{1,0:T(1,128)S(1)} %copy-done.3, f32[1,6656]{1,0:T(1,128)S(1)} %broadcast_in_dim.8.potential_ref), custom_call_target="tpu_custom_call" | custom-call | tf_op jit(solution)/shard_map/pallas_call | solution.py:595
  10.6 2.4 %shard_map.142.u_in_ref = f32[256,384]{1,0:T(8,128)S(1)} custom-call(s32[8,128]{1,0:T(8,128)S(1)} %get-tuple-element.30.table_ref, f32[8,9472]{1,0:T(8,128)S(1)} %get-tuple-element.31.p_ref.p_in_ref, s32[32,1,384]{2,1,0:T(1,128)S(1)} %get-tuple-element.32.index_ref), custom_call_target="tpu_custom_call" | custom-call | tf_op jit(solution)/shard_map/pallas_call | solution.py:595
  13.2 2.6 %shard_map.144 = (f32[8,9472]{1,0:T(8,128)S(1)}, f32[32,4,128]{2,1,0:T(4,128)}, f32[256,384]{1,0:T(8,128)S(1)}, f32[64,384]{1,0:T(8,128)S(1)}) custom-call(s32[8,128]{1,0:T(8,128)S(1)} %get-tuple-element.30.table_ref, f32[8,9472]{1,0:T(8,128)S(1)} %get-tuple-element.31.p_ref.p_in_ref, f32[256,384]{1,0:T(8,128)S(1)} %shard_map.142.u_in_ref, ...), custom_call_target="tpu_custom_call" | custom-call | tf_op jit(solution)/shard_map/pallas_call | solution.py:595
  15.7 6.0 %all-to-all-start = ((f32[32,4,128]{2,1,0:T(4,128)}), f32[32,4,128]{2,1,0:T(4,128)S(1)}, u32[]{:S(2)}, u32[]{:S(2)}) async-start(f32[32,4,128]{2,1,0:T(4,128)} %get-tuple-element.40), calls=%async_computation | async-start | bytes 131072 | tf_op jit(solution)/shard_map/all_to_all | solution.py:649
  21.7 4.5 %shard_map.145 = (f32[8,7680]{1,0:T(8,128)S(1)}, f32[10,1024]{1,0:T(8,128)S(1)}, f32[10,1024]{1,0:T(8,128)S(1)}, bf16[384,384]{1,0:T(8,128)(2,1)S(1)}, bf16[384,384]{1,0:T(8,128)(2,1)S(1)}) custom-call(s32[8,128]{1,0:T(8,128)S(1)} %get-tuple-element.30.table_ref, s32[32,1,384]{2,1,0:T(1,128)S(1)} %get-tuple-element.32.index_ref, ...), custom_call_target="tpu_custom_call" | custom-call | tf_op jit(solution)/shard_map/pallas_call | solution.py:595
  26.2 0.3 collective-permute-start.2
  26.5 3.4 %collective-permute-start.3 = (f32[10,1024]{1,0:T(8,128)S(1)}, f32[10,1024]{1,0:T(8,128)S(1)}, u32[]{:S(2)}, u32[]{:S(2)}) collective-permute-start(f32[10,1024]{1,0:T(8,128)S(1)} %get-tuple-element.46), channel_id=1, source_target_pairs={{1,2},{2,1},{3,4},{4,3},{5,6},{6,5},{7,8},{8,7},{9,10},{10,9},{11,... | collective-permute-start | bytes 122888 | tf_op jit(solution)/shard_map/ppermute | solution.py:590
  29.9 3.5 %shard_map.146.image_ref = f32[8,7680]{1,0:T(8,128)S(1)} custom-call(s32[8,128]{1,0:T(8,128)S(1)} %get-tuple-element.30.table_ref, f32[32,4,128]{2,1,0:T(4,128)S(1)} %all-to-all-done.sums_ref.coupling_ref, f32[32,4,128]{2,1,0:T(4,128)S(1)} %all-to-all-done.sums_ref.coupling_ref, s32[32,1,384]{2,1,0:T(1,128)S(1)} %get-tuple-element.32.index_ref, ...), custom_call_target="tpu_custom_call" | custom-call | tf_op jit(solution)/shard_map/pallas_call | solution.py:595
  33.4 5.0 %shard_map.147 = (f32[8,7680]{1,0:T(8,128)S(1)}, f32[8,9472]{1,0:T(8,128)S(1)}, f32[32,4,128]{2,1,0:T(4,128)}, f32[256,384]{1,0:T(8,128)S(1)}) custom-call(s32[8,128]{1,0:T(8,128)S(1)} %get-tuple-element.30.table_ref, f32[8,7680]{1,0:T(8,128)S(1)} %shard_map.146.image_ref, f32[8,9472]{1,0:T(8,128)S(1)} %get-tuple-element.37.p_ref, ...), custom_call_target="tpu_custom_call" | custom-call | tf_op jit(solution)/shard_map/pallas_call | solution.py:595
  38.4 5.2 %all-to-all-start.1 = ((f32[32,4,128]{2,1,0:T(4,128)}), f32[32,4,128]{2,1,0:T(4,128)S(1)}, u32[]{:S(2)}, u32[]{:S(2)}) async-start(f32[32,4,128]{2,1,0:T(4,128)} %get-tuple-element.51), calls=%async_computation.1 | async-start | bytes 131072 | tf_op jit(solution)/shard_map/all_to_all | solution.py:672
  43.6 3.8 %shard_map.148 = (f32[8,7680]{1,0:T(8,128)S(1)}, f32[8,1024]{1,0:T(8,128)S(1)}, f32[8,1024]{1,0:T(8,128)S(1)}) custom-call(s32[8,128]{1,0:T(8,128)S(1)} %get-tuple-element.30.table_ref, s32[32,1,384]{2,1,0:T(1,128)S(1)} %get-tuple-element.32.index_ref, s32[1,128]{1,0:T(1,128)S(1)} %get-tuple-element.35.corner_ref, f32[256,384]{1,0:T(8,128)S(1)} %get-tuple-element.52.refs_0_), custom_call_target="tpu_custom_call" | custom-call | tf_op jit(solution)/shard_map/pallas_call | solution.py:595
  47.5 0.3 collective-permute-start.4
  47.8 3.4 %collective-permute-start.5 = (f32[8,1024]{1,0:T(8,128)S(1)}, f32[8,1024]{1,0:T(8,128)S(1)}, u32[]{:S(2)}, u32[]{:S(2)}) collective-permute-start(f32[8,1024]{1,0:T(8,128)S(1)} %get-tuple-element.57), channel_id=1, source_target_pairs={{1,2},{2,1},{3,4},{4,3},{5,6},{6,5},{7,8},{8,7},{9,10},{10,9},{11,... | collective-permute-start | bytes 98312 | tf_op jit(solution)/shard_map/ppermute | solution.py:590
  51.2 3.5 %shard_map.149 = (f32[8,7680]{1,0:T(8,128)S(1)}, f32[1,128]{1,0:T(1,128)S(1)}) custom-call(s32[8,128]{1,0:T(8,128)S(1)} %get-tuple-element.30.table_ref, f32[32,4,128]{2,1,0:T(4,128)S(1)} %all-to-all-done.1.sums_ref, f32[32,4,128]{2,1,0:T(4,128)S(1)} %all-to-all-done.sums_ref.coupling_ref, s32[32,1,384]{2,1,0:T(1,128)S(1)} %get-tuple-element.32.index_ref, ...), custom_call_target="tpu_custom_call" | custom-call | tf_op jit(solution)/shard_map/pallas_call | solution.py:595
  54.7 1.6 %shard_map.150 = (f32[8,6656]{1,0:T(8,128)}, f32[8,6656]{1,0:T(8,128)}) custom-call(s32[8,128]{1,0:T(8,128)S(1)} %get-tuple-element.30.table_ref, f32[8,6656]{1,0:T(8,128)S(1)} %copy-done, f32[8,9472]{1,0:T(8,128)S(1)} %get-tuple-element.37.p_ref, f32[2,7680]{1,0:T(2,128)S(1)} %get-tuple-element.38.refs_2_.diag_in_ref.diag_ref, ...), custom_call_target="tpu_custom_call" | custom-call | tf_op jit(solution)/shard_map/pallas_call | solution.py:595
  (31 shorter events, 0.1 us)
Async XLA Ops:
  2.0 0.7 %copy-start.6 = (s32[8]{0:T(128)S(1)}, s32[8]{0:T(128)}, u32[]{:S(2)}) copy-start(s32[8]{0:T(128)} %cell_ref.3) | copy-start | bytes 100
  2.0 0.7 %copy-start.7 = (s32[8]{0:T(128)S(1)}, s32[8]{0:T(128)}, u32[]{:S(2)}) copy-start(s32[8]{0:T(128)} %atom_ref.3) | copy-start | bytes 100
  2.0 0.7 %copy-start.8 = (s32[32]{0:T(128)S(1)}, s32[32]{0:T(128)}, u32[]{:S(2)}) copy-start(s32[32]{0:T(128)} %scount_ref.3) | copy-start | bytes 388
  2.7 6.3 %copy-start.12 = (f32[6656]{0:T(1024)S(1)}, f32[6656]{0:T(1024)}, u32[]{:S(2)}) copy-start(f32[6656]{0:T(1024)} %param.14) | copy-start | bytes 79876
  2.7 7.2 %copy-start = (f32[8,6656]{1,0:T(8,128)S(1)}, f32[8,6656]{1,0:T(8,128)}, u32[]{:S(2)}) copy-start(f32[8,6656]{1,0:T(8,128)} %rhs_ref.5) | copy-start | bytes 638980
  4.3 4.7 %copy-start.4 = (s32[32,343]{1,0:T(8,128)S(1)}, s32[32,343]{1,0:T(8,128)}, u32[]{:S(2)}) copy-start(s32[32,343]{1,0:T(8,128)} %conn_ref.3) | copy-start | bytes 131716
  4.3 8.8 %collective-permute-start = (f32[88,384]{1,0:T(8,128)S(1)}, f32[88,384]{1,0:T(8,128)S(1)}, u32[]{:S(2)}, u32[]{:S(2)}) collective-permute-start(f32[88,384]{1,0:T(8,128)S(1)} %get-tuple-element.33), channel_id=1, source_target_pairs={{0,1},{1,0},{2,3},{3,2},{4,5},{5,4},{6,7},{7,6},{8,9},{9,8},{10,11... | collective-permute-start | bytes 405512 | tf_op jit(solution)/shard_map/ppermute | solution.py:590
  4.4 4.6 %copy-start.9 = (s32[32]{0:T(128)S(1)}, s32[32]{0:T(128)}, u32[]{:S(2)}) copy-start(s32[32]{0:T(128)} %count_ref.1) | copy-start | bytes 388
  4.4 4.6 %copy-start.10 = (f32[32]{0:T(128)S(1)}, f32[32]{0:T(128)}, u32[]{:S(2)}) copy-start(f32[32]{0:T(128)} %scale_ref.1) | copy-start | bytes 388
  4.5 8.7 %collective-permute-start.1 = (f32[88,384]{1,0:T(8,128)S(1)}, f32[88,384]{1,0:T(8,128)S(1)}, u32[]{:S(2)}, u32[]{:S(2)}) collective-permute-start(f32[88,384]{1,0:T(8,128)S(1)} %get-tuple-element.34), channel_id=1, source_target_pairs={{1,2},{2,1},{3,4},{4,3},{5,6},{6,5},{7,8},{8,7},{9,10},{10,9},{11,... | collective-permute-start | bytes 405512 | tf_op jit(solution)/shard_map/ppermute | solution.py:590
  9.0 0.9 %copy-start.3 = (f32[1,6656]{1,0:T(1,128)S(1)}, f32[1,6656]{1,0:T(1,128)}, u32[]{:S(2)}) copy-start(f32[1,6656]{1,0:T(1,128)} %broadcast_in_dim.7.precond_ref) | copy-start | bytes 79876
  9.0 0.9 %copy-start.11 = (f32[8]{0:T(128)S(1)}, f32[8]{0:T(128)}, u32[]{:S(2)}) copy-start(f32[8]{0:T(128)} %shift_ref.1) | copy-start | bytes 100
  10.6 2.5 %copy-start.2 = (f32[8,8,343]{2,1,0:T(8,128)S(1)}, f32[8,8,343]{2,1,0:T(8,128)}, u32[]{:S(2)}) copy-start(f32[8,8,343]{2,1,0:T(8,128)} %param.21) | copy-start | bytes 263428
  10.6 2.5 %copy-start.5 = (f32[2,8,8]{2,1,0:T(8,128)S(1)}, f32[2,8,8]{2,1,0:T(8,128)}, u32[]{:S(2)}) copy-start(f32[2,8,8]{2,1,0:T(8,128)} %coupling_ref.1) | copy-start | bytes 1540
  13.1 8.5 %copy-start.1 = (f32[343,343]{1,0:T(8,128)S(1)}, f32[343,343]{1,0:T(8,128)}, u32[]{:S(2)}) copy-start(f32[343,343]{1,0:T(8,128)} %refs_1_.1) | copy-start | bytes 1411792
  15.7 14.2 %all-to-all-start = ((f32[32,4,128]{2,1,0:T(4,128)}), f32[32,4,128]{2,1,0:T(4,128)S(1)}, u32[]{:S(2)}, u32[]{:S(2)}) async-start(f32[32,4,128]{2,1,0:T(4,128)} %get-tuple-element.40), calls=%async_computation | async-start | bytes 131072 | tf_op jit(solution)/shard_map/all_to_all | solution.py:649
  26.2 7.2 %collective-permute-start.2 = (f32[10,1024]{1,0:T(8,128)S(1)}, f32[10,1024]{1,0:T(8,128)S(1)}, u32[]{:S(2)}, u32[]{:S(2)}) collective-permute-start(f32[10,1024]{1,0:T(8,128)S(1)} %get-tuple-element.45), channel_id=1, source_target_pairs={{0,1},{1,0},{2,3},{3,2},{4,5},{5,4},{6,7},{7,6},{8,9},{9,8},{10,11... | collective-permute-start | bytes 122888 | tf_op jit(solution)/shard_map/ppermute | solution.py:590
  26.5 6.9 %collective-permute-start.3 = (f32[10,1024]{1,0:T(8,128)S(1)}, f32[10,1024]{1,0:T(8,128)S(1)}, u32[]{:S(2)}, u32[]{:S(2)}) collective-permute-start(f32[10,1024]{1,0:T(8,128)S(1)} %get-tuple-element.46), channel_id=1, source_target_pairs={{1,2},{2,1},{3,4},{4,3},{5,6},{6,5},{7,8},{8,7},{9,10},{10,9},{11,... | collective-permute-start | bytes 122888 | tf_op jit(solution)/shard_map/ppermute | solution.py:590
  38.4 12.7 %all-to-all-start.1 = ((f32[32,4,128]{2,1,0:T(4,128)}), f32[32,4,128]{2,1,0:T(4,128)S(1)}, u32[]{:S(2)}, u32[]{:S(2)}) async-start(f32[32,4,128]{2,1,0:T(4,128)} %get-tuple-element.51), calls=%async_computation.1 | async-start | bytes 131072 | tf_op jit(solution)/shard_map/all_to_all | solution.py:672
  47.5 7.2 %collective-permute-start.4 = (f32[8,1024]{1,0:T(8,128)S(1)}, f32[8,1024]{1,0:T(8,128)S(1)}, u32[]{:S(2)}, u32[]{:S(2)}) collective-permute-start(f32[8,1024]{1,0:T(8,128)S(1)} %get-tuple-element.56), channel_id=1, source_target_pairs={{0,1},{1,0},{2,3},{3,2},{4,5},{5,4},{6,7},{7,6},{8,9},{9,8},{10,11... | collective-permute-start | bytes 98312 | tf_op jit(solution)/shard_map/ppermute | solution.py:590
  47.8 7.0 %collective-permute-start.5 = (f32[8,1024]{1,0:T(8,128)S(1)}, f32[8,1024]{1,0:T(8,128)S(1)}, u32[]{:S(2)}, u32[]{:S(2)}) collective-permute-start(f32[8,1024]{1,0:T(8,128)S(1)} %get-tuple-element.57), channel_id=1, source_target_pairs={{1,2},{2,1},{3,4},{4,3},{5,6},{6,5},{7,8},{8,7},{9,10},{10,9},{11,... | collective-permute-start | bytes 98312 | tf_op jit(solution)/shard_map/ppermute | solution.py:590

commit v10 on v9

--- a/solution.py
+++ b/solution.py
@@ -40,6 +40,11 @@
         self.width = round_up(self.elem, LANES)
         self.tiles = self.width // LANES
         self.pairs = self.channels * self.vectors
+        self.low, self.high, self.list = 0, self.slots, 2 * self.slots
+        self.cell = 3 * self.slots
+        self.owner, self.local = self.cell + self.entries, self.cell + 2 * self.entries
+        self.position = self.cell + 3 * self.entries
+        assert self.position + 1 < LANES
         self.reach = self.window + SPAN * LANES
         self.index_row = self.entries * self.channels
         self.rim_row = self.index_row + round_up(self.entries, ROWS)
@@ -68,9 +73,6 @@
     total = jnp.sum(values, axis=1, keepdims=True)
     spread = jnp.broadcast_to(total, (ROWS, LANES))
     return jnp.sum(jnp.where(iota((ROWS, LANES), 1) == iota((ROWS, LANES), 0), spread, 0.0), axis=0, keepdims=True)
-
-
-LOW, HIGH, LIST, NOTHING, CELL, OWNER, LOCAL, OTHER = range(8)
 
 
 def prepare_kernel(
@@ -97,46 +99,53 @@
     high = jnp.max(jnp.where(middle, nodes, 0.0), axis=1, keepdims=True)
     lane, cell = iota((z.slots, LANES), 1), iota((z.slots, LANES), 0)
 
-    def as_row(column):
-        return jnp.sum(jnp.where(lane == cell, column, 0.0), axis=0, keepdims=True)
-
-    rows = [as_row(low), as_row(high)]
+    def as_row(column, first=0):
+        return jnp.sum(jnp.where(lane == cell + first, column, 0.0), axis=0, keepdims=True)
+
     good = jnp.where((low >= z.rim) & (high < z.window - z.rim), 1.0, 0.0)
     good = jnp.broadcast_to(good, (z.slots, LANES))
     number = cell.astype(F32)
     before = jnp.sum(jnp.where(lane < cell, as_row(good), 0.0), axis=1, keepdims=True)
     at = jnp.where(good > 0.5, before, z.slots - 1.0 - (number - before))
-    rows.append(jnp.sum(jnp.where(lane.astype(F32) == at, number + z.slots * good, 0.0), axis=0, keepdims=True))
-    rows.append(jnp.zeros((1, LANES), F32))
-    table = [row.astype(jnp.int32) for row in rows]
-    facts = [jnp.zeros((1, LANES), jnp.int32)] * 3
+    listed = jnp.where(lane.astype(F32) == at + z.list, number + z.slots * good, 0.0)
+    table = as_row(low, z.low) + as_row(high, z.high) + jnp.sum(listed, axis=0, keepdims=True)
+    table = table.astype(jnp.int32)
     for s in range(z.entries):
         atom = atom_ref[s]
         owner = atom // z.owned
-        for k, fact in enumerate((cell_ref[s], owner, atom - owner * z.owned)):
-            facts[k] = jnp.where(line == s, fact, facts[k])
-    other = jnp.where(line == 0, position, jnp.where(line == 1, scount_ref[position], 0))
-    table_ref[...] = jnp.concatenate(table + facts + [other], axis=0)
+        for first, fact in ((z.cell, cell_ref[s]), (z.owner, owner), (z.local, atom - owner * z.owned)):
+            table = jnp.where(line == first + s, fact, table)
+    table = jnp.where(line == z.position, position, table)
+    table_ref[...] = jnp.where(line == z.position + 1, scount_ref[position], table)
 
 
 def start_kernel(
-    z, pos_ref, cell_ref, atom_ref, scount_ref, rhs_ref, precond_ref, conn_ref, projector_ref,
-    send_a_ref, send_b_ref, rhs_rim, precond_rim, conn_all, projector_all, sems,
+    z, pos_ref, cell_hbm, atom_hbm, scount_hbm, rhs_ref, precond_ref, conn_ref, projector_ref,
+    send_a_ref, send_b_ref, rhs_rim, precond_rim, conn_all, projector_all, cell_ref, atom_ref, scount_ref, sems,
 ):
-    copies = [
-        pltpu.make_async_copy(conn_ref, conn_all, sems.at[0]),
-        pltpu.make_async_copy(projector_ref, projector_all, sems.at[1]),
+    lines = z.rim // LANES
+    moves = [
+        (cell_hbm, cell_ref), (atom_hbm, atom_ref), (scount_hbm, scount_ref), (conn_ref, conn_all),
+        (projector_ref, projector_all),
     ]
     for k, first in enumerate((0, z.nodes - z.rim)):
-        at, to = pl.ds(first, z.rim), pl.ds(k * z.rim, z.rim)
-        copies.append(pltpu.make_async_copy(rhs_ref.at[:, at], rhs_rim.at[:, to], sems.at[2 + k]))
-        copies.append(pltpu.make_async_copy(precond_ref.at[:, at], precond_rim.at[:, to], sems.at[4 + k]))
+        moves.append((rhs_ref.at[:, pl.ds(first, z.rim)], rhs_rim.at[k]))
+        moves.append((precond_ref.at[pl.ds(first // LANES, lines), :], precond_rim.at[k]))
+    copies = [pltpu.make_async_copy(source, to, sems.at[k]) for k, (source, to) in enumerate(moves)]
     for copy in copies:
         copy.start()
     for copy in copies:
         copy.wait()
-    rims = rhs_rim[...] * precond_rim[...]
-    head, tail = rims[:, : z.rim], rims[:, z.rim :]
+    head, tail = (
+        jnp.concatenate(
+            [
+                rhs_rim[k, :, i * LANES : (i + 1) * LANES] * precond_rim[k, i : i + 1, :]
+                for i in range(lines)
+            ],
+            axis=1,
+        )
+        for k in range(2)
+    )
     even = pos_ref[0] % 2 == 0
     sides = jnp.where(even, tail, head), jnp.where(even, head, tail)
     nodes = (conn_all[...] + z.shift).astype(F32)
@@ -164,14 +173,20 @@
 def own_kernel(
     z, shift_ref, rhs_ref, precond_ref, potential_ref, p_ref, gamma_ref, diag_ref, shift_tile_ref,
 ):
-    product = rhs_ref[...] * precond_ref[...]
-    own = slice(z.rim, z.rim + z.nodes)
-    p_ref[:, own] = product
+    diag_ref[...] = jnp.zeros_like(diag_ref)
+    gamma = jnp.zeros((ROWS, LANES), F32)
+    for i in range(z.nodes // LANES):
+        at = slice(i * LANES, (i + 1) * LANES)
+        to = slice(z.rim + i * LANES, z.rim + (i + 1) * LANES)
+        value = rhs_ref[:, at]
+        scale = precond_ref[i : i + 1, :]
+        product = value * scale
+        p_ref[:, to] = product
+        gamma = gamma + product * value
+        diag_ref[0:1, to] = scale
+        diag_ref[1:2, to] = potential_ref[i : i + 1, :]
     p_ref[:, z.window :] = jnp.zeros((ROWS, z.reach - z.window), F32)
-    gamma_ref[...] = lanes_by_vector(z, product * rhs_ref[...])
-    diag_ref[...] = jnp.zeros_like(diag_ref)
-    diag_ref[0:1, own] = precond_ref[...]
-    diag_ref[1:2, own] = potential_ref[...]
+    gamma_ref[...] = lanes_by_vector(z, gamma)
     row = iota((ROWS, LANES), 0)
     tile = jnp.zeros((ROWS, LANES), F32)
     for v in range(z.vectors):
@@ -180,7 +195,7 @@
 
 
 def full_groups(z, table_ref):
-    ends = [table_ref[LIST, g * z.together + z.together - 1] for g in range(z.slots // z.together)]
+    ends = [table_ref[0, z.list + g * z.together + z.together - 1] for g in range(z.slots // z.together)]
     return functools.reduce(jnp.add, [(end >= z.slots).astype(jnp.int32) for end in ends])
 
 
@@ -191,10 +206,10 @@
     def some_cells(g, _):
         cells = [g * z.together + i for i in range(z.together)]
         if listed:
-            cells = [table_ref[LIST, c] for c in cells]
+            cells = [table_ref[0, z.list + c] for c in cells]
             cells = [jnp.where(c >= z.slots, c - z.slots, c) for c in cells]
-        starts = [table_ref[LOW, c] >> 7 for c in cells]
-        ends = [table_ref[HIGH, c] >> 7 for c in cells]
+        starts = [table_ref[0, z.low + c] >> 7 for c in cells]
+        ends = [table_ref[0, z.high + c] >> 7 for c in cells]
         passes = functools.reduce(jnp.maximum, [(e - s) // SPAN + 1 for s, e in zip(starts, ends)])
 
         def one_pass(k, values):
@@ -253,21 +268,21 @@
     e_ref[...] = dot(u_high, k_high) + (dot(u_high, k_low) + dot(u_low, k_high))
 
 
-def entry_facts(table_ref, s):
-    return table_ref[OWNER, s], table_ref[LOCAL, s], s < table_ref[OTHER, 1]
+def entry_facts(z, table_ref, s):
+    return table_ref[0, z.owner + s], table_ref[0, z.local + s], s < table_ref[0, z.position + 1]
 
 
 def contributions(z, table_ref, pj_ref, u_ref):
-    values = [u_ref[pl.ds(pl.multiple_of(table_ref[CELL, s] * ROWS, ROWS), ROWS), :] for s in range(z.entries)]
+    values = [u_ref[pl.ds(pl.multiple_of(table_ref[0, z.cell + s] * ROWS, ROWS), ROWS), :] for s in range(z.entries)]
     sums = lax.dot_general(
         pj_ref[...], jnp.concatenate(values, axis=0), NT, precision=HIGHEST, preferred_element_type=F32
     )
     sums = jnp.concatenate([sums, jnp.zeros((sums.shape[0], LANES - sums.shape[1]), F32)], axis=1)
     lane, row = iota((ROWS, LANES), 1), iota((ROWS, LANES), 0)
-    position = table_ref[OTHER, 0]
+    position = table_ref[0, z.position]
     parts = [jnp.zeros((ROWS, LANES), F32)] * 3
     for s in range(z.entries):
-        owner, local, alive = entry_facts(table_ref, s)
+        owner, local, alive = entry_facts(z, table_ref, s)
         got = lane_gather(sums[s * ROWS : (s + 1) * ROWS], s * ROWS + lane % ROWS)
         here = (lane // ROWS % ROWS == row) & (lane // z.pairs == local) & alive
         for k in range(3):
@@ -293,7 +308,7 @@
     for k in range(z.rim_pieces):
         rows = slice(z.rim_row + k * ROWS, z.rim_row + (k + 1) * ROWS)
         at, to = k * z.width, min((k + 1) * z.width, z.rim)
-        left, right = sides(table_ref[OTHER, 0], halo_a_ref[rows, : to - at], halo_b_ref[rows, : to - at])
+        left, right = sides(table_ref[0, z.position], halo_a_ref[rows, : to - at], halo_b_ref[rows, : to - at])
         p_ref[:, at:to] = left
         p_ref[:, z.rim + z.nodes + at : z.rim + z.nodes + to] = right
     p_ref[:, own] = p_in_ref[:, own]
@@ -320,7 +335,7 @@
     z, table_ref, image_ref, p_ref, diag_in_ref, shift_ref, gamma_ref, halo_a_ref, halo_b_ref,
     index_ref, corner_ref, weight_ref, k_high_ref, k_low_ref, pj_ref, y_ref, q_ref, out_ref, e_ref, diag_ref, u_ref, uw_ref,
 ):
-    left, right = sides(table_ref[OTHER, 0], halo_a_ref[...], halo_b_ref[...])
+    left, right = sides(table_ref[0, z.position], halo_a_ref[...], halo_b_ref[...])
     own = slice(z.rim, z.rim + z.nodes)
     diag_ref[:, own] = diag_in_ref[:, own]
     diag_ref[:, : z.rim] = left[ROWS : ROWS + 2, : z.rim]
@@ -399,8 +414,8 @@
 
     def add(self, cells, value_of):
         z = self.z
-        starts = [self.table_ref[LOW, c] >> 8 for c in cells]
-        ends = [self.table_ref[HIGH, c] >> 8 for c in cells]
+        starts = [self.table_ref[0, z.low + c] >> 8 for c in cells]
+        ends = [self.table_ref[0, z.high + c] >> 8 for c in cells]
         passes = functools.reduce(jnp.maximum, [(e - s) // BAND + 1 for s, e in zip(starts, ends)])
 
         def one_pass(k, _):
@@ -463,7 +478,7 @@
     lax.fori_loop(0, z.slots // z.together, some_cells, 0)
     for h in range(scatter.groups):
         image_ref[:, h * WIDE : (h + 1) * WIDE] = scatter.result(h)
-    even = table_ref[OTHER, 0] % 2 == 0
+    even = table_ref[0, z.position] % 2 == 0
     ends = [slice(0, 2 * z.rim), slice(z.window - 2 * z.rim, z.window)]
     for source_ref, rows in ((image_ref, slice(0, ROWS)),) + (((diag_ref, slice(ROWS, ROWS + 2)),) if multiply else ()):
         low_rim, high_rim = (source_ref[:, end] for end in ends)
@@ -479,7 +494,7 @@
         image_ref, dots_ref, support_ref, acc_ref = refs
     else:
         image_ref, support_ref, acc_ref = refs
-    position = table_ref[OTHER, 0]
+    position = table_ref[0, z.position]
     wanted = (
         pltpu.roll(sums_ref[:, 0, :], z.devices - 1, 0) + sums_ref[:, 1, :] + pltpu.roll(sums_ref[:, 2, :], 1, 0)
     )
@@ -517,9 +532,9 @@
             jnp.concatenate(spread, axis=0), projectors, precision=HIGHEST, preferred_element_type=F32
         )
 
-    support_ref[...] = values([entry_facts(table_ref, s) for s in range(z.entries)], pj_ref[...])
+    support_ref[...] = values([entry_facts(z, table_ref, s) for s in range(z.entries)], pj_ref[...])
     scatter = Scatter(z, table_ref, index_ref, corner_ref, acc_ref)
-    cells = [table_ref[CELL, s] for s in range(z.entries)]
+    cells = [table_ref[0, z.cell + s] for s in range(z.entries)]
     scatter.start([(cell, support_ref[s * ROWS : (s + 1) * ROWS, :]) for s, cell in enumerate(cells)])
     for first in range(0, z.entries, z.together):
         some = cells[first : first + z.together]
@@ -570,7 +585,7 @@
     search = (p - alpha * q) + beta * p
     solution_ref[...] = alpha * p + step * search
     residual_ref[...] = (rhs_ref[...] - alpha * y) - step * (more * y - alpha * second)
-    left, right = sides(table_ref[OTHER, 0], halo_a_ref[...], halo_b_ref[...])
+    left, right = sides(table_ref[0, z.position], halo_a_ref[...], halo_b_ref[...])
     residual_ref[:, : z.rim] += step * alpha * left[:, z.rim :]
     residual_ref[:, z.nodes - z.rim :] += step * alpha * right[:, : z.rim]
 
@@ -611,21 +626,24 @@
     rim, more_rim = (z.vectors, 2 * z.rim), (z.vectors + 2, 2 * z.rim)
     acc = ((z.window // WIDE + BAND) * 2 * ROWS, WIDE)
 
+    precond_lines = precond.reshape(-1, LANES)
     tile = (ROWS, LANES)
     first_message = (z.message, z.width)
     ext = exchange(
         *call(
             functools.partial(start_kernel, z),
             [(first_message, F32)] * 2,
-            [((z.vectors, 2 * z.rim), F32), ((1, 2 * z.rim), F32), (conn.shape, jnp.int32), (flat_projector.shape, F32),
-             pltpu.SemaphoreType.DMA((6,))],
-            (pos, support_cell, support_atom, support_count),
-            rhs, precond[None, :], conn, flat_projector, by_hand=True,
+            [((2, z.vectors, z.rim), F32), ((2, z.rim // LANES, LANES), F32), (conn.shape, jnp.int32),
+             (flat_projector.shape, F32), pltpu.SMEM(support_cell.shape, jnp.int32),
+             pltpu.SMEM(support_atom.shape, jnp.int32), pltpu.SMEM(support_count.shape, jnp.int32),
+             pltpu.SemaphoreType.DMA((9,))],
+            (pos,),
+            support_cell, support_atom, support_count, rhs, precond_lines, conn, flat_projector, by_hand=True,
         )
     )
     index, corner, table, weight = call(
         functools.partial(prepare_kernel, z),
-        [((z.slots, 1, z.width), jnp.int32), ((1, LANES), jnp.int32), ((ROWS, LANES), jnp.int32),
+        [((z.slots, 1, z.width), jnp.int32), ((1, LANES), jnp.int32), ((1, LANES), jnp.int32),
          ((z.slots * ROWS, LANES), F32)],
         [],
         (pos, cell_count, cell_scale, support_cell, support_atom, support_count),
@@ -636,7 +654,7 @@
         [(reach, F32), ((1, LANES), F32), ((2, z.window), F32), (tile, F32)],
         [],
         (shift,),
-        rhs, precond[None, :], potential[None, :],
+        rhs, precond_lines, potential.reshape(-1, LANES),
     )
     (u,) = call(functools.partial(first_window_kernel, z), [(cells, F32)], [], (table,), p, index)
     p, sums, uw, pj = call(

time: 56.8 us -> 53.7 us (0.945)
  local copies, waits for them, and re-layouts: 2.13 us -> 0.68 us
  Pallas kernels: 30.2 us -> 29 us
    broadcast_in_dim x2 -> x0, local copies, waits for them, and re-layouts: 1.39 us -> none  [the longest x1 1.37 us: on_device(): precond[None, :]]
    pallas_call x11, Pallas kernels: 30.2 us -> 29 us  [call(): pl.pallas_call(kernel, out_shape=[jax.ShapeDtypeStruct(s, d) if i in in_h...]
    all_to_all x1, starting transfers between devices: 5.96 us -> 5.38 us  [on_device(): coupled = lax.all_to_all(sums, 'dom', 0, 0)]
  transfers between devices with their start and end apart: 8 -> 8, of which waited for: 0 -> 0; matrix products, arithmetic and copies ran while one was open for 0% -> 0% of each run, Pallas kernels for 34% -> 35%
where the time goes in v10:
time: 53.7 us; the launch traced here: 53.2 us
  Pallas kernels  29 us (54%)
  starting transfers between devices  22.6 us (42%)
  between operations  0.98 us (2%)
  local copies, waits for them, and re-layouts  0.68 us (1%)
    pallas_call x11, Pallas kernels, call(): pl.pallas_call(kernel, out_shape=[jax.ShapeDtypeStruct(s, d) if i in in_h...  29 us
    ppermute x6, starting transfers between devices, exchange(): return (lax.ppermute(a, 'dom', near), lax.ppermute(b, 'dom', far))  12 us
    all_to_all x1, starting transfers between devices, on_device(): coupled = lax.all_to_all(sums, 'dom', 0, 0)  5.38 us
    all_to_all x1, starting transfers between devices, on_device(): totals = lax.all_to_all(sums, 'dom', 0, 0)  5.2 us
  transfers between devices with their start and end apart: 8, of which 0 were waited for; matrix products, arithmetic and copies ran while one was open for 0% of the time, Pallas kernels for 35%

profile of v10, /device:TPU:1, one launch (start us, length us, event | category | flops | bytes accessed | tf_op | source)
XLA Modules:
  0.0 53.2 jit_solution(12863125802280572065)
XLA Ops:
  0.7 1.2 %shard_map.143 = (f32[88,384]{1,0:T(8,128)S(1)}, f32[88,384]{1,0:T(8,128)S(1)}) custom-call(s32[1]{0:T(128)} %bitcast.pos_ref, s32[8]{0:T(128)} %cell_hbm.1, s32[8]{0:T(128)} %atom_hbm.1, s32[32]{0:T(128)} %scount_hbm.1, f32[8,6656]{1,0:T(8,128)} %rhs_ref.5, f32[52,128]{1,0:T(8,128)} %bitcast.6, s32[32,343]{1,0:T(8,128)} %conn_ref.3, f32[64,343]{1,0:T(8,128)} %bitcast.4), custom_call_target="tpu_custom_call" | custom-call | tf_op jit(solution)/shard_map/pallas_call | solution.py:610
  1.9 0.0 copy-start.4
  1.9 0.0 copy-start.5
  1.9 0.1 collective-permute-start
  2.0 4.5 %collective-permute-start.1 = (f32[88,384]{1,0:T(8,128)S(1)}, f32[88,384]{1,0:T(8,128)S(1)}, u32[]{:S(2)}, u32[]{:S(2)}) collective-permute-start(f32[88,384]{1,0:T(8,128)S(1)} %get-tuple-element.34), channel_id=1, source_target_pairs={{1,2},{2,1},{3,4},{4,3},{5,6},{6,5},{7,8},{8,7},{9,10},{10,9},{11,... | collective-permute-start | bytes 405512 | tf_op jit(solution)/shard_map/ppermute | solution.py:605
  6.6 0.8 %shard_map.140 = (s32[32,1,384]{2,1,0:T(1,128)S(1)}, s32[1,128]{1,0:T(1,128)S(1)}, s32[1,128]{1,0:T(1,128)S(1)}, f32[256,128]{1,0:T(8,128)S(1)}) custom-call(s32[1]{0:T(128)} %bitcast.pos_ref, s32[32]{0:T(128)S(1)} %copy-done.10, f32[32]{0:T(128)S(1)} %copy-done.11, s32[8]{0:T(128)S(1)} %copy-done.7, s32[8]{0:T(128)S(1)} %copy-done.8, s32[32]{0:T(128)S(1)} %copy-done.9, ...), custom_call_target="tpu_custom_call" | custom-call | tf_op jit(solution)/shard_map/pallas_call | solution.py:610
  7.4 0.0 copy-start.12
  7.4 0.6 %copy-done.12 = f32[8]{0:T(128)S(1)} copy-done((f32[8]{0:T(128)S(1)}, f32[8]{0:T(128)}, u32[]{:S(2)}) %copy-start.12) | copy-done | bytes 56
  8.1 0.7 %shard_map.141 = (f32[8,9472]{1,0:T(8,128)S(1)}, f32[1,128]{1,0:T(1,128)S(1)}, f32[2,7680]{1,0:T(2,128)S(1)}, f32[8,128]{1,0:T(8,128)S(1)}) custom-call(f32[8]{0:T(128)S(1)} %copy-done.12, f32[8,6656]{1,0:T(8,128)S(1)} %copy-done, f32[52,128]{1,0:T(8,128)S(1)} %bitcast.7, f32[52,128]{1,0:T(8,128)S(1)} %bitcast.8), custom_call_target="tpu_custom_call" | custom-call | tf_op jit(solution)/shard_map/pallas_call | solution.py:610
  8.8 2.3 %shard_map.142.u_in_ref = f32[256,384]{1,0:T(8,128)S(1)} custom-call(s32[1,128]{1,0:T(1,128)S(1)} %get-tuple-element.30.table_ref, f32[8,9472]{1,0:T(8,128)S(1)} %get-tuple-element.31.p_ref.p_in_ref, s32[32,1,384]{2,1,0:T(1,128)S(1)} %get-tuple-element.32.index_ref), custom_call_target="tpu_custom_call" | custom-call | tf_op jit(solution)/shard_map/pallas_call | solution.py:610
  11.1 0.0 copy-start.1
  11.2 2.5 %shard_map.144 = (f32[8,9472]{1,0:T(8,128)S(1)}, f32[32,4,128]{2,1,0:T(4,128)}, f32[256,384]{1,0:T(8,128)S(1)}, f32[64,384]{1,0:T(8,128)S(1)}) custom-call(s32[1,128]{1,0:T(1,128)S(1)} %get-tuple-element.30.table_ref, f32[8,9472]{1,0:T(8,128)S(1)} %get-tuple-element.31.p_ref.p_in_ref, f32[256,384]{1,0:T(8,128)S(1)} %shard_map.142.u_in_ref, ...), custom_call_target="tpu_custom_call" | custom-call | tf_op jit(solution)/shard_map/pallas_call | solution.py:610
  13.6 5.4 %all-to-all-start = ((f32[32,4,128]{2,1,0:T(4,128)}), f32[32,4,128]{2,1,0:T(4,128)S(1)}, u32[]{:S(2)}, u32[]{:S(2)}) async-start(f32[32,4,128]{2,1,0:T(4,128)} %get-tuple-element.40), calls=%async_computation | async-start | bytes 131072 | tf_op jit(solution)/shard_map/all_to_all | solution.py:667
  19.0 4.4 %shard_map.145 = (f32[8,7680]{1,0:T(8,128)S(1)}, f32[10,1024]{1,0:T(8,128)S(1)}, f32[10,1024]{1,0:T(8,128)S(1)}, bf16[384,384]{1,0:T(8,128)(2,1)S(1)}, bf16[384,384]{1,0:T(8,128)(2,1)S(1)}) custom-call(s32[1,128]{1,0:T(1,128)S(1)} %get-tuple-element.30.table_ref, s32[32,1,384]{2,1,0:T(1,128)S(1)} %get-tuple-element.32.index_ref, ...), custom_call_target="tpu_custom_call" | custom-call | tf_op jit(solution)/shard_map/pallas_call | solution.py:610
  23.4 0.3 collective-permute-start.2
  23.7 3.4 %collective-permute-start.3 = (f32[10,1024]{1,0:T(8,128)S(1)}, f32[10,1024]{1,0:T(8,128)S(1)}, u32[]{:S(2)}, u32[]{:S(2)}) collective-permute-start(f32[10,1024]{1,0:T(8,128)S(1)} %get-tuple-element.46), channel_id=1, source_target_pairs={{1,2},{2,1},{3,4},{4,3},{5,6},{6,5},{7,8},{8,7},{9,10},{10,9},{11,... | collective-permute-start | bytes 122888 | tf_op jit(solution)/shard_map/ppermute | solution.py:605
  27.1 3.4 %shard_map.146.image_ref = f32[8,7680]{1,0:T(8,128)S(1)} custom-call(s32[1,128]{1,0:T(1,128)S(1)} %get-tuple-element.30.table_ref, f32[32,4,128]{2,1,0:T(4,128)S(1)} %all-to-all-done.sums_ref.coupling_ref, f32[32,4,128]{2,1,0:T(4,128)S(1)} %all-to-all-done.sums_ref.coupling_ref, s32[32,1,384]{2,1,0:T(1,128)S(1)} %get-tuple-element.32.index_ref, ...), custom_call_target="tpu_custom_call" | custom-call | tf_op jit(solution)/shard_map/pallas_call | solution.py:610
  30.6 4.9 %shard_map.147 = (f32[8,7680]{1,0:T(8,128)S(1)}, f32[8,9472]{1,0:T(8,128)S(1)}, f32[32,4,128]{2,1,0:T(4,128)}, f32[256,384]{1,0:T(8,128)S(1)}) custom-call(s32[1,128]{1,0:T(1,128)S(1)} %get-tuple-element.30.table_ref, f32[8,7680]{1,0:T(8,128)S(1)} %shard_map.146.image_ref, f32[8,9472]{1,0:T(8,128)S(1)} %get-tuple-element.37.p_ref, ...), custom_call_target="tpu_custom_call" | custom-call | tf_op jit(solution)/shard_map/pallas_call | solution.py:610
  35.5 5.2 %all-to-all-start.1 = ((f32[32,4,128]{2,1,0:T(4,128)}), f32[32,4,128]{2,1,0:T(4,128)S(1)}, u32[]{:S(2)}, u32[]{:S(2)}) async-start(f32[32,4,128]{2,1,0:T(4,128)} %get-tuple-element.51), calls=%async_computation.1 | async-start | bytes 131072 | tf_op jit(solution)/shard_map/all_to_all | solution.py:690
  40.7 3.7 %shard_map.148 = (f32[8,7680]{1,0:T(8,128)S(1)}, f32[8,1024]{1,0:T(8,128)S(1)}, f32[8,1024]{1,0:T(8,128)S(1)}) custom-call(s32[1,128]{1,0:T(1,128)S(1)} %get-tuple-element.30.table_ref, s32[32,1,384]{2,1,0:T(1,128)S(1)} %get-tuple-element.32.index_ref, s32[1,128]{1,0:T(1,128)S(1)} %get-tuple-element.35.corner_ref, f32[256,384]{1,0:T(8,128)S(1)} %get-tuple-element.52.refs_0_), custom_call_target="tpu_custom_call" | custom-call | tf_op jit(solution)/shard_map/pallas_call | solution.py:610
  44.4 0.3 collective-permute-start.4
  44.8 3.4 %collective-permute-start.5 = (f32[8,1024]{1,0:T(8,128)S(1)}, f32[8,1024]{1,0:T(8,128)S(1)}, u32[]{:S(2)}, u32[]{:S(2)}) collective-permute-start(f32[8,1024]{1,0:T(8,128)S(1)} %get-tuple-element.57), channel_id=1, source_target_pairs={{1,2},{2,1},{3,4},{4,3},{5,6},{6,5},{7,8},{8,7},{9,10},{10,9},{11,... | collective-permute-start | bytes 98312 | tf_op jit(solution)/shard_map/ppermute | solution.py:605
  48.2 3.4 %shard_map.149 = (f32[8,7680]{1,0:T(8,128)S(1)}, f32[1,128]{1,0:T(1,128)S(1)}) custom-call(s32[1,128]{1,0:T(1,128)S(1)} %get-tuple-element.30.table_ref, f32[32,4,128]{2,1,0:T(4,128)S(1)} %all-to-all-done.1.sums_ref, f32[32,4,128]{2,1,0:T(4,128)S(1)} %all-to-all-done.sums_ref.coupling_ref, s32[32,1,384]{2,1,0:T(1,128)S(1)} %get-tuple-element.32.index_ref, ...), custom_call_target="tpu_custom_call" | custom-call | tf_op jit(solution)/shard_map/pallas_call | solution.py:610
  51.6 1.6 %shard_map.150 = (f32[8,6656]{1,0:T(8,128)}, f32[8,6656]{1,0:T(8,128)}) custom-call(s32[1,128]{1,0:T(1,128)S(1)} %get-tuple-element.30.table_ref, f32[8,6656]{1,0:T(8,128)S(1)} %copy-done, f32[8,9472]{1,0:T(8,128)S(1)} %get-tuple-element.37.p_ref, f32[2,7680]{1,0:T(2,128)S(1)} %get-tuple-element.38.refs_2_.diag_in_ref.diag_ref, ...), custom_call_target="tpu_custom_call" | custom-call | tf_op jit(solution)/shard_map/pallas_call | solution.py:610
  (29 shorter events, 0.1 us)
Async XLA Ops:
  0.6 5.9 %copy-start.3 = (s32[32,343]{1,0:T(8,128)S(1)}, s32[32,343]{1,0:T(8,128)}, u32[]{:S(2)}) copy-start(s32[32,343]{1,0:T(8,128)} %conn_ref.3) | copy-start | bytes 131716
  0.6 5.9 %copy-start.7 = (s32[8]{0:T(128)S(1)}, s32[8]{0:T(128)}, u32[]{:S(2)}) copy-start(s32[8]{0:T(128)} %cell_hbm.1) | copy-start | bytes 100
  0.7 5.9 %copy-start.8 = (s32[8]{0:T(128)S(1)}, s32[8]{0:T(128)}, u32[]{:S(2)}) copy-start(s32[8]{0:T(128)} %atom_hbm.1) | copy-start | bytes 100
  0.7 5.9 %copy-start.9 = (s32[32]{0:T(128)S(1)}, s32[32]{0:T(128)}, u32[]{:S(2)}) copy-start(s32[32]{0:T(128)} %scount_hbm.1) | copy-start | bytes 388
  0.7 5.9 %copy-start.10 = (s32[32]{0:T(128)S(1)}, s32[32]{0:T(128)}, u32[]{:S(2)}) copy-start(s32[32]{0:T(128)} %count_ref.1) | copy-start | bytes 388
  0.7 5.9 %copy-start.11 = (f32[32]{0:T(128)S(1)}, f32[32]{0:T(128)}, u32[]{:S(2)}) copy-start(f32[32]{0:T(128)} %scale_ref.1) | copy-start | bytes 388
  0.7 6.7 %copy-start = (f32[8,6656]{1,0:T(8,128)S(1)}, f32[8,6656]{1,0:T(8,128)}, u32[]{:S(2)}) copy-start(f32[8,6656]{1,0:T(8,128)} %rhs_ref.5) | copy-start | bytes 638980
  1.9 5.5 %copy-start.4 = (f32[6656]{0:T(1024)S(1)}, f32[6656]{0:T(1024)}, u32[]{:S(2)}) copy-start(f32[6656]{0:T(1024)} %param.15) | copy-start | bytes 79876
  1.9 5.5 %copy-start.5 = (f32[6656]{0:T(1024)S(1)}, f32[6656]{0:T(1024)}, u32[]{:S(2)}) copy-start(f32[6656]{0:T(1024)} %param.14) | copy-start | bytes 79876
  1.9 9.2 %collective-permute-start = (f32[88,384]{1,0:T(8,128)S(1)}, f32[88,384]{1,0:T(8,128)S(1)}, u32[]{:S(2)}, u32[]{:S(2)}) collective-permute-start(f32[88,384]{1,0:T(8,128)S(1)} %get-tuple-element.33), channel_id=1, source_target_pairs={{0,1},{1,0},{2,3},{3,2},{4,5},{5,4},{6,7},{7,6},{8,9},{9,8},{10,11... | collective-permute-start | bytes 405512 | tf_op jit(solution)/shard_map/ppermute | solution.py:605
  2.0 9.1 %collective-permute-start.1 = (f32[88,384]{1,0:T(8,128)S(1)}, f32[88,384]{1,0:T(8,128)S(1)}, u32[]{:S(2)}, u32[]{:S(2)}) collective-permute-start(f32[88,384]{1,0:T(8,128)S(1)} %get-tuple-element.34), channel_id=1, source_target_pairs={{1,2},{2,1},{3,4},{4,3},{5,6},{6,5},{7,8},{8,7},{9,10},{10,9},{11,... | collective-permute-start | bytes 405512 | tf_op jit(solution)/shard_map/ppermute | solution.py:605
  7.4 0.7 %copy-start.12 = (f32[8]{0:T(128)S(1)}, f32[8]{0:T(128)}, u32[]{:S(2)}) copy-start(f32[8]{0:T(128)} %shift_ref.1) | copy-start | bytes 100
  8.8 2.4 %copy-start.2 = (f32[8,8,343]{2,1,0:T(8,128)S(1)}, f32[8,8,343]{2,1,0:T(8,128)}, u32[]{:S(2)}) copy-start(f32[8,8,343]{2,1,0:T(8,128)} %param.21) | copy-start | bytes 263428
  8.8 2.4 %copy-start.6 = (f32[2,8,8]{2,1,0:T(8,128)S(1)}, f32[2,8,8]{2,1,0:T(8,128)}, u32[]{:S(2)}) copy-start(f32[2,8,8]{2,1,0:T(8,128)} %coupling_ref.1) | copy-start | bytes 1540
  11.1 7.9 %copy-start.1 = (f32[343,343]{1,0:T(8,128)S(1)}, f32[343,343]{1,0:T(8,128)}, u32[]{:S(2)}) copy-start(f32[343,343]{1,0:T(8,128)} %refs_1_.1) | copy-start | bytes 1411792
  13.6 13.5 %all-to-all-start = ((f32[32,4,128]{2,1,0:T(4,128)}), f32[32,4,128]{2,1,0:T(4,128)S(1)}, u32[]{:S(2)}, u32[]{:S(2)}) async-start(f32[32,4,128]{2,1,0:T(4,128)} %get-tuple-element.40), calls=%async_computation | async-start | bytes 131072 | tf_op jit(solution)/shard_map/all_to_all | solution.py:667
  23.4 7.2 %collective-permute-start.2 = (f32[10,1024]{1,0:T(8,128)S(1)}, f32[10,1024]{1,0:T(8,128)S(1)}, u32[]{:S(2)}, u32[]{:S(2)}) collective-permute-start(f32[10,1024]{1,0:T(8,128)S(1)} %get-tuple-element.45), channel_id=1, source_target_pairs={{0,1},{1,0},{2,3},{3,2},{4,5},{5,4},{6,7},{7,6},{8,9},{9,8},{10,11... | collective-permute-start | bytes 122888 | tf_op jit(solution)/shard_map/ppermute | solution.py:605
  23.7 6.9 %collective-permute-start.3 = (f32[10,1024]{1,0:T(8,128)S(1)}, f32[10,1024]{1,0:T(8,128)S(1)}, u32[]{:S(2)}, u32[]{:S(2)}) collective-permute-start(f32[10,1024]{1,0:T(8,128)S(1)} %get-tuple-element.46), channel_id=1, source_target_pairs={{1,2},{2,1},{3,4},{4,3},{5,6},{6,5},{7,8},{8,7},{9,10},{10,9},{11,... | collective-permute-start | bytes 122888 | tf_op jit(solution)/shard_map/ppermute | solution.py:605
  35.5 12.7 %all-to-all-start.1 = ((f32[32,4,128]{2,1,0:T(4,128)}), f32[32,4,128]{2,1,0:T(4,128)S(1)}, u32[]{:S(2)}, u32[]{:S(2)}) async-start(f32[32,4,128]{2,1,0:T(4,128)} %get-tuple-element.51), calls=%async_computation.1 | async-start | bytes 131072 | tf_op jit(solution)/shard_map/all_to_all | solution.py:690
  44.4 7.2 %collective-permute-start.4 = (f32[8,1024]{1,0:T(8,128)S(1)}, f32[8,1024]{1,0:T(8,128)S(1)}, u32[]{:S(2)}, u32[]{:S(2)}) collective-permute-start(f32[8,1024]{1,0:T(8,128)S(1)} %get-tuple-element.56), channel_id=1, source_target_pairs={{0,1},{1,0},{2,3},{3,2},{4,5},{5,4},{6,7},{7,6},{8,9},{9,8},{10,11... | collective-permute-start | bytes 98312 | tf_op jit(solution)/shard_map/ppermute | solution.py:605
  44.8 6.9 %collective-permute-start.5 = (f32[8,1024]{1,0:T(8,128)S(1)}, f32[8,1024]{1,0:T(8,128)S(1)}, u32[]{:S(2)}, u32[]{:S(2)}) collective-permute-start(f32[8,1024]{1,0:T(8,128)S(1)} %get-tuple-element.57), channel_id=1, source_target_pairs={{1,2},{2,1},{3,4},{4,3},{5,6},{6,5},{7,8},{8,7},{9,10},{10,9},{11,... | collective-permute-start | bytes 98312 | tf_op jit(solution)/shard_map/ppermute | solution.py:605

commit v11 on v10

--- a/solution.py
+++ b/solution.py
@@ -44,13 +44,14 @@
         self.cell = 3 * self.slots
         self.owner, self.local = self.cell + self.entries, self.cell + 2 * self.entries
         self.position = self.cell + 3 * self.entries
-        assert self.position + 1 < LANES
+        self.beside = 2 * self.slots
+        assert self.position + 1 < LANES and self.beside + 4 * self.entries <= LANES
         self.reach = self.window + SPAN * LANES
         self.index_row = self.entries * self.channels
         self.rim_row = self.index_row + round_up(self.entries, ROWS)
         self.rim_pieces = -(-self.rim // self.width)
         self.message = self.rim_row + self.rim_pieces * ROWS
-        assert self.elem + 3 <= self.width
+        assert self.elem + 5 <= self.width and 2 * self.entries <= self.slots
         self.together = TOGETHER if self.slots % TOGETHER == 0 else 1
         assert self.vectors == ROWS and self.channels == ROWS and 2 * self.slots <= LANES
         assert self.nodes % WIDE == 0 and self.owned * self.pairs == LANES
@@ -120,13 +121,14 @@
 
 
 def start_kernel(
-    z, pos_ref, cell_hbm, atom_hbm, scount_hbm, rhs_ref, precond_ref, conn_ref, projector_ref,
-    send_a_ref, send_b_ref, rhs_rim, precond_rim, conn_all, projector_all, cell_ref, atom_ref, scount_ref, sems,
+    z, pos_ref, cell_hbm, atom_hbm, scount_hbm, shift_hbm, rhs_ref, precond_ref, conn_ref, projector_ref,
+    send_a_ref, send_b_ref, shift_tile_ref, rhs_rim, precond_rim, conn_all, projector_all, cell_ref, atom_ref,
+    scount_ref, shift_ref, sems,
 ):
     lines = z.rim // LANES
     moves = [
-        (cell_hbm, cell_ref), (atom_hbm, atom_ref), (scount_hbm, scount_ref), (conn_ref, conn_all),
-        (projector_ref, projector_all),
+        (cell_hbm, cell_ref), (atom_hbm, atom_ref), (scount_hbm, scount_ref), (shift_hbm, shift_ref),
+        (conn_ref, conn_all), (projector_ref, projector_all),
     ]
     for k, first in enumerate((0, z.nodes - z.rim)):
         moves.append((rhs_ref.at[:, pl.ds(first, z.rim)], rhs_rim.at[k]))
@@ -136,6 +138,11 @@
         copy.start()
     for copy in copies:
         copy.wait()
+    row = iota((ROWS, LANES), 0)
+    tile = jnp.zeros((ROWS, LANES), F32)
+    for v in range(z.vectors):
+        tile = jnp.where(row == v, shift_ref[v], tile)
+    shift_tile_ref[...] = tile
     head, tail = (
         jnp.concatenate(
             [
@@ -161,6 +168,10 @@
         rows = jnp.where(entry == s, row, rows)
         for k, fact in enumerate(facts):
             rows = jnp.where((entry == s) & (place == z.elem + k), fact.astype(F32), rows)
+    middle = (place > 0) & (place < z.elem - 1)
+    low = jnp.min(jnp.where(middle, rows, 1.0 * z.window), axis=1, keepdims=True)
+    high = jnp.max(jnp.where(middle, rows, 0.0), axis=1, keepdims=True)
+    rows = jnp.where(place == z.elem + 3, low, jnp.where(place == z.elem + 4, high, rows))
     for ref, side in zip((send_a_ref, send_b_ref), sides):
         ref[...] = jnp.zeros_like(ref)
         ref[: z.index_row, : z.elem] = projector_all[...]
@@ -171,7 +182,7 @@
 
 
 def own_kernel(
-    z, shift_ref, rhs_ref, precond_ref, potential_ref, p_ref, gamma_ref, diag_ref, shift_tile_ref,
+    z, rhs_ref, precond_ref, potential_ref, p_ref, gamma_ref, diag_ref,
 ):
     diag_ref[...] = jnp.zeros_like(diag_ref)
     gamma = jnp.zeros((ROWS, LANES), F32)
@@ -187,11 +198,6 @@
         diag_ref[1:2, to] = potential_ref[i : i + 1, :]
     p_ref[:, z.window :] = jnp.zeros((ROWS, z.reach - z.window), F32)
     gamma_ref[...] = lanes_by_vector(z, gamma)
-    row = iota((ROWS, LANES), 0)
-    tile = jnp.zeros((ROWS, LANES), F32)
-    for v in range(z.vectors):
-        tile = jnp.where(row == v, shift_ref[v], tile)
-    shift_tile_ref[...] = tile
 
 
 def full_groups(z, table_ref):
@@ -301,9 +307,27 @@
 
 
 def first_kernel(
-    z, table_ref, p_in_ref, u_in_ref, halo_a_ref, halo_b_ref, index_ref, corner_ref, weight_ref, projector_ref,
-    coupling_ref, p_ref, out_ref, uw_ref, pj_ref, u_ref,
+    z, table_ref, table_row_ref, p_in_ref, u_in_ref, halo_a_ref, halo_b_ref, index_ref, corner_ref, weight_ref,
+    projector_ref, coupling_ref, p_ref, out_ref, uw_ref, pj_ref, marked_ref, beside_ref, u_ref,
 ):
+    rows = slice(z.index_row, z.index_row + z.entries)
+    marked = table_row_ref[...]
+    line = iota((1, LANES), 1)
+    left, right = sides(table_ref[0, z.position], halo_a_ref[rows, :], halo_b_ref[rows, :])
+    for s in range(z.entries):
+        high = left[s : s + 1, z.elem + 4 : z.elem + 5]
+        marked = jnp.where(line == z.list + s, (high >= z.window - 2 * z.rim).astype(jnp.int32), marked)
+        low = right[s : s + 1, z.elem + 3 : z.elem + 4]
+        marked = jnp.where(line == z.list + z.entries + s, (low < 2 * z.rim).astype(jnp.int32), marked)
+    marked_ref[...] = marked
+    beside = corner_ref[...]
+    for k, (side, move) in enumerate(((left, -z.nodes), (right, z.nodes))):
+        side = side.astype(jnp.int32) + move
+        for s in range(z.entries):
+            lane = z.beside + 2 * z.entries * k + s
+            beside = jnp.where(line == lane, side[s : s + 1, :1], beside)
+            beside = jnp.where(line == lane + z.entries, side[s : s + 1, z.elem - 1 : z.elem], beside)
+    beside_ref[...] = beside
     own = slice(z.rim, z.rim + z.nodes)
     for k in range(z.rim_pieces):
         rows = slice(z.rim_row + k * ROWS, z.rim_row + (k + 1) * ROWS)
@@ -398,13 +422,17 @@
     def product(self, lhs, hot):
         return lax.dot_general(lhs, hot, NT, preferred_element_type=F32)
 
-    def start(self, sources):
+    def start(self, sources, beside=()):
         z = self.z
         corners = jnp.zeros((ROWS, LANES), F32)
         at = (z.tiles - 1) * LANES + self.end
         for cell, values in sources:
             corners = corners + jnp.where(self.lane == cell, values[:, 0:1], 0.0)
             corners = corners + jnp.where(self.lane == z.slots + cell, values[:, at : at + 1], 0.0)
+        for s, values in enumerate(beside):
+            lane = z.beside + s + s // z.entries * z.entries
+            corners = jnp.where(self.lane == lane, values[:, 0:1], corners)
+            corners = jnp.where(self.lane == lane + z.entries, values[:, at : at + 1], corners)
         index = jnp.broadcast_to(self.corner_ref[...], self.pair)
         rows = self.groups * 2 * ROWS
         self.acc_ref[:rows, :] = self.product(
@@ -491,9 +519,9 @@
     cells_ref, *refs,
 ):
     if last:
-        image_ref, dots_ref, support_ref, acc_ref = refs
+        image_ref, dots_ref, support_ref, nodes_ref, acc_ref = refs
     else:
-        image_ref, support_ref, acc_ref = refs
+        image_ref, support_ref, nodes_ref, acc_ref = refs
     position = table_ref[0, z.position]
     wanted = (
         pltpu.roll(sums_ref[:, 0, :], z.devices - 1, 0) + sums_ref[:, 1, :] + pltpu.roll(sums_ref[:, 2, :], 1, 0)
@@ -532,32 +560,42 @@
             jnp.concatenate(spread, axis=0), projectors, precision=HIGHEST, preferred_element_type=F32
         )
 
-    support_ref[...] = values([entry_facts(z, table_ref, s) for s in range(z.entries)], pj_ref[...])
-    scatter = Scatter(z, table_ref, index_ref, corner_ref, acc_ref)
-    cells = [table_ref[0, z.cell + s] for s in range(z.entries)]
-    scatter.start([(cell, support_ref[s * ROWS : (s + 1) * ROWS, :]) for s, cell in enumerate(cells)])
-    for first in range(0, z.entries, z.together):
-        some = cells[first : first + z.together]
-
-        def value_of(i, t):
-            s = first + i
-            return support_ref[s * ROWS : (s + 1) * ROWS, t * LANES : (t + 1) * LANES]
-
-        scatter.add(some, value_of)
+    count = z.entries * ROWS
+    support_ref[:count, :] = values([entry_facts(z, table_ref, s) for s in range(z.entries)], pj_ref[...])
     used = slice(0, z.rim_row)
-    shared = 2 * z.rim // WIDE
-    neighbours = sides(position, ext_a_ref[used, :], ext_b_ref[used, :])
-    for ext, first, offset in zip(neighbours, (0, scatter.groups - shared), (z.window - 2 * z.rim, 0)):
+    for side, ext in enumerate(sides(position, ext_a_ref[used, :], ext_b_ref[used, :])):
         nodes = ext[z.index_row :].astype(jnp.int32)
         facts = []
         for s in range(z.entries):
             fact = [jnp.broadcast_to(nodes[s : s + 1, z.elem + k : z.elem + k + 1], (1, LANES)) for k in range(3)]
             facts.append((fact[0], fact[1], fact[2] > 0))
-        rows = values(facts, jnp.where(iota((z.index_row, z.width), 1) < z.elem, ext[: z.index_row], 0.0))
-        for s in range(0, z.entries, 2):
-            index = jnp.concatenate([nodes[s : s + 1], nodes[s + 1 : s + 2]], axis=1) - offset
-            pair = jnp.concatenate([rows[s * ROWS : (s + 1) * ROWS], rows[(s + 1) * ROWS : (s + 2) * ROWS]], axis=1)
-            scatter.add_rows(index, pair, first, shared)
+        projectors = jnp.where(iota((z.index_row, z.width), 1) < z.elem, ext[: z.index_row], 0.0)
+        support_ref[(side + 1) * count : (side + 2) * count, :] = values(facts, projectors)
+        nodes_ref[side] = nodes
+    scatter = Scatter(z, table_ref, index_ref, corner_ref, acc_ref)
+    cells = [table_ref[0, z.cell + s] for s in range(z.entries)]
+    blocks = [support_ref[s * ROWS : (s + 1) * ROWS, :] for s in range(3 * z.entries)]
+    scatter.start(list(zip(cells, blocks)), blocks[z.entries :])
+    for first in range(0, z.entries, z.together):
+        some = cells[first : first + z.together]
+
+        def value_of(i, t):
+            s = first + i
+            return support_ref[s * ROWS : (s + 1) * ROWS, t * LANES : (t + 1) * LANES]
+
+        scatter.add(some, value_of)
+    shared = 2 * z.rim // WIDE
+    place = iota((ROWS, z.width), 1)
+    middle = (place > 0) & (place < z.elem - 1)
+    for side, (first, offset) in enumerate(((0, z.window - 2 * z.rim), (scatter.groups - shared, 0))):
+        for s in range(z.entries):
+
+            @pl.when(table_ref[0, z.list + side * z.entries + s] > 0)
+            def _():
+                at = ((side + 1) * z.entries + s) * ROWS
+                value = jnp.where(middle, support_ref[at : at + ROWS, :], 0.0)
+                scatter.add_rows(nodes_ref[side, s : s + 1, :] - offset, value, first, shared)
+
     for h in range(scatter.groups):
         at = slice(h * WIDE, (h + 1) * WIDE)
         image_ref[:, at] = cells_ref[:, at] + scatter.result(h)
@@ -625,22 +663,24 @@
     square, entries = (z.width, z.width), (z.entries * ROWS, z.width)
     rim, more_rim = (z.vectors, 2 * z.rim), (z.vectors + 2, 2 * z.rim)
     acc = ((z.window // WIDE + BAND) * 2 * ROWS, WIDE)
+    support_scratch = [
+        ((3 * z.entries * ROWS, z.width), F32), ((2, z.rim_row - z.index_row, z.width), jnp.int32), (acc, F32),
+    ]
 
     precond_lines = precond.reshape(-1, LANES)
     tile = (ROWS, LANES)
     first_message = (z.message, z.width)
-    ext = exchange(
-        *call(
+    send_a, send_b, shift_tile = call(
             functools.partial(start_kernel, z),
-            [(first_message, F32)] * 2,
+            [(first_message, F32), (first_message, F32), (tile, F32)],
             [((2, z.vectors, z.rim), F32), ((2, z.rim // LANES, LANES), F32), (conn.shape, jnp.int32),
              (flat_projector.shape, F32), pltpu.SMEM(support_cell.shape, jnp.int32),
              pltpu.SMEM(support_atom.shape, jnp.int32), pltpu.SMEM(support_count.shape, jnp.int32),
-             pltpu.SemaphoreType.DMA((9,))],
+             pltpu.SMEM(shift.shape, F32), pltpu.SemaphoreType.DMA((10,))],
             (pos,),
-            support_cell, support_atom, support_count, rhs, precond_lines, conn, flat_projector, by_hand=True,
-        )
-    )
+            support_cell, support_atom, support_count, shift, rhs, precond_lines, conn, flat_projector, by_hand=True,
+    )
+    ext = exchange(send_a, send_b)
     index, corner, table, weight = call(
         functools.partial(prepare_kernel, z),
         [((z.slots, 1, z.width), jnp.int32), ((1, LANES), jnp.int32), ((1, LANES), jnp.int32),
@@ -649,20 +689,21 @@
         (pos, cell_count, cell_scale, support_cell, support_atom, support_count),
         conn,
     )
-    p, gamma, diag, shift_tile = call(
+    p, gamma, diag = call(
         functools.partial(own_kernel, z),
-        [(reach, F32), ((1, LANES), F32), ((2, z.window), F32), (tile, F32)],
+        [(reach, F32), ((1, LANES), F32), ((2, z.window), F32)],
         [],
-        (shift,),
+        (),
         rhs, precond_lines, potential.reshape(-1, LANES),
     )
     (u,) = call(functools.partial(first_window_kernel, z), [(cells, F32)], [], (table,), p, index)
-    p, sums, uw, pj = call(
+    p, sums, uw, pj, marked, beside = call(
         functools.partial(first_kernel, z),
-        [(reach, F32), (message, F32), (cells, F32), (entries, F32)],
+        [(reach, F32), (message, F32), (cells, F32), (entries, F32), ((1, LANES), jnp.int32),
+         ((1, LANES), jnp.int32)],
         [(cells, F32)],
         (table,),
-        p, u, *ext, index, corner, weight, flat_projector, atom_matrix,
+        table, p, u, *ext, index, corner, weight, flat_projector, atom_matrix,
     )
     coupled = lax.all_to_all(sums, "dom", 0, 0)
     image, send_a, send_b, k_high, k_low = call(
@@ -676,9 +717,9 @@
     (image,) = call(
         functools.partial(support_kernel, z, False),
         [(window, F32)],
-        [(entries, F32), (acc, F32)],
-        (table,),
-        coupled, coupled, index, corner, pj, *ext, image,
+        support_scratch,
+        (marked,),
+        coupled, coupled, index, beside, pj, *ext, image,
     )
     y, q, sums, e = call(
         functools.partial(second_kernel, z),
@@ -696,9 +737,9 @@
     image, dots = call(
         functools.partial(support_kernel, z, True),
         [(window, F32), ((1, LANES), F32)],
-        [(entries, F32), (acc, F32)],
-        (table,),
-        totals, coupled, index, corner, pj, *ext, image,
+        support_scratch,
+        (marked,),
+        totals, coupled, index, beside, pj, *ext, image,
     )
     return tuple(
         call(

time: 53.7 us -> 53.4 us (level)
  Pallas kernels: 29 us -> 27 us
  starting transfers between devices: 22.6 us -> 23.9 us
    pallas_call x11, Pallas kernels: 29 us -> 27 us  [call(): pl.pallas_call(kernel, out_shape=[jax.ShapeDtypeStruct(s, d) if i in in_h...]
    all_to_all x1, starting transfers between devices: 5.2 us -> 6.03 us  [on_device(): totals = lax.all_to_all(sums, 'dom', 0, 0)]
    all_to_all x1, starting transfers between devices: 5.38 us -> 5.92 us  [on_device(): coupled = lax.all_to_all(sums, 'dom', 0, 0)]
  transfers between devices with their start and end apart: 8 -> 8, of which waited for: 0 -> 0; matrix products, arithmetic and copies ran while one was open for 0% -> 0% of each run, Pallas kernels for 35% -> 32%
where the time goes in v11:
time: 53.4 us; the launch traced here: 52.5 us
  Pallas kernels  27 us (51%)
  starting transfers between devices  23.9 us (45%)
  between operations  0.94 us (2%)
  local copies, waits for them, and re-layouts  0.63 us (1%)
    pallas_call x11, Pallas kernels, call(): pl.pallas_call(kernel, out_shape=[jax.ShapeDtypeStruct(s, d) if i in in_h...  27 us
    ppermute x6, starting transfers between devices, exchange(): return (lax.ppermute(a, 'dom', near), lax.ppermute(b, 'dom', far))  12 us
    all_to_all x1, starting transfers between devices, on_device(): totals = lax.all_to_all(sums, 'dom', 0, 0)  6.03 us
    all_to_all x1, starting transfers between devices, on_device(): coupled = lax.all_to_all(sums, 'dom', 0, 0)  5.92 us
  transfers between devices with their start and end apart: 8, of which 0 were waited for; matrix products, arithmetic and copies ran while one was open for 0% of the time, Pallas kernels for 32%

profile of v11, /device:TPU:1, one launch (start us, length us, event | category | flops | bytes accessed | tf_op | source)
XLA Modules:
  0.0 52.5 jit_solution(770890676770845055)
XLA Ops:
  0.7 1.2 %shard_map.143 = (f32[88,384]{1,0:T(8,128)S(1)}, f32[88,384]{1,0:T(8,128)S(1)}, f32[8,128]{1,0:T(8,128)S(1)}) custom-call(s32[1]{0:T(128)} %bitcast.pos_ref, s32[8]{0:T(128)} %cell_hbm.1, s32[8]{0:T(128)} %atom_hbm.1, s32[32]{0:T(128)} %scount_hbm.1, f32[8]{0:T(128)} %shift_hbm.1, f32[8,6656]{1,0:T(8,128)} %rhs_ref.5, f32[52,128]{1,0:T(8,128)} %bitcast.6, ...), custom_call_target="tpu_custom_call" | custom-call | tf_op jit(solution)/shard_map/pallas_call | solution.py:648
  1.9 0.1 collective-permute-start
  2.0 4.5 %collective-permute-start.1 = (f32[88,384]{1,0:T(8,128)S(1)}, f32[88,384]{1,0:T(8,128)S(1)}, u32[]{:S(2)}, u32[]{:S(2)}) collective-permute-start(f32[88,384]{1,0:T(8,128)S(1)} %get-tuple-element.36), channel_id=1, source_target_pairs={{1,2},{2,1},{3,4},{4,3},{5,6},{6,5},{7,8},{8,7},{9,10},{10,9},{11,... | collective-permute-start | bytes 405512 | tf_op jit(solution)/shard_map/ppermute | solution.py:643
  6.5 0.0 copy-start.3
  6.5 0.0 copy-start.7
  6.6 0.0 copy-start.10
  6.6 0.0 copy-start.11
  6.6 0.2 shard_map.141
  6.8 0.6 %copy-done.3 = s32[32,343]{1,0:T(8,128)S(1)} copy-done((s32[32,343]{1,0:T(8,128)S(1)}, s32[32,343]{1,0:T(8,128)}, u32[]{:S(2)}) %copy-start.3) | copy-done | bytes 43928
  7.4 0.8 %shard_map.140 = (s32[32,1,384]{2,1,0:T(1,128)S(1)}, s32[1,128]{1,0:T(1,128)S(1)}, s32[1,128]{1,0:T(1,128)S(1)}, f32[256,128]{1,0:T(8,128)S(1)}) custom-call(s32[1]{0:T(128)} %bitcast.pos_ref, s32[32]{0:T(128)S(1)} %copy-done.10, f32[32]{0:T(128)S(1)} %copy-done.11, s32[8]{0:T(128)S(1)} %copy-done.7, s32[8]{0:T(128)S(1)} %copy-done.8, s32[32]{0:T(128)S(1)} %copy-done.9, ...), custom_call_target="tpu_custom_call" | custom-call | tf_op jit(solution)/shard_map/pallas_call | solution.py:648
  8.2 2.3 %shard_map.142.u_in_ref = f32[256,384]{1,0:T(8,128)S(1)} custom-call(s32[1,128]{1,0:T(1,128)S(1)} %get-tuple-element.32.table_ref.table_row_ref, f32[8,9472]{1,0:T(8,128)S(1)} %get-tuple-element.33.p_ref.p_in_ref, s32[32,1,384]{2,1,0:T(1,128)S(1)} %get-tuple-element.34.index_ref), custom_call_target="tpu_custom_call" | custom-call | tf_op jit(solution)/shard_map/pallas_call | solution.py:648
  10.6 2.5 %shard_map.144 = (f32[8,9472]{1,0:T(8,128)S(1)}, f32[32,4,128]{2,1,0:T(4,128)}, f32[256,384]{1,0:T(8,128)S(1)}, f32[64,384]{1,0:T(8,128)S(1)}, s32[1,128]{1,0:T(1,128)S(1)}, /*index=5*/s32[1,128]{1,0:T(1,128)S(1)}) custom-call(s32[1,128]{1,0:T(1,128)S(1)} %get-tuple-element.32.table_ref.table_row_ref, ...), custom_call_target="tpu_custom_call" | custom-call | tf_op jit(solution)/shard_map/pallas_call | solution.py:648
  13.2 5.9 %all-to-all-start = ((f32[32,4,128]{2,1,0:T(4,128)}), f32[32,4,128]{2,1,0:T(4,128)S(1)}, u32[]{:S(2)}, u32[]{:S(2)}) async-start(f32[32,4,128]{2,1,0:T(4,128)} %get-tuple-element.43), calls=%async_computation | async-start | bytes 131072 | tf_op jit(solution)/shard_map/all_to_all | solution.py:708
  19.1 4.4 %shard_map.145 = (f32[8,7680]{1,0:T(8,128)S(1)}, f32[10,1024]{1,0:T(8,128)S(1)}, f32[10,1024]{1,0:T(8,128)S(1)}, bf16[384,384]{1,0:T(8,128)(2,1)S(1)}, bf16[384,384]{1,0:T(8,128)(2,1)S(1)}) custom-call(s32[1,128]{1,0:T(1,128)S(1)} %get-tuple-element.32.table_ref.table_row_ref, s32[32,1,384]{2,1,0:T(1,128)S(1)} %get-tuple-element.34.index_ref, ...), custom_call_target="tpu_custom_call" | custom-call | tf_op jit(solution)/shard_map/pallas_call | solution.py:648
  23.5 0.3 collective-permute-start.2
  23.8 3.4 %collective-permute-start.3 = (f32[10,1024]{1,0:T(8,128)S(1)}, f32[10,1024]{1,0:T(8,128)S(1)}, u32[]{:S(2)}, u32[]{:S(2)}) collective-permute-start(f32[10,1024]{1,0:T(8,128)S(1)} %get-tuple-element.50), channel_id=1, source_target_pairs={{1,2},{2,1},{3,4},{4,3},{5,6},{6,5},{7,8},{8,7},{9,10},{10,9},{11,... | collective-permute-start | bytes 122888 | tf_op jit(solution)/shard_map/ppermute | solution.py:643
  27.2 2.6 %shard_map.146.image_ref = f32[8,7680]{1,0:T(8,128)S(1)} custom-call(s32[1,128]{1,0:T(1,128)S(1)} %get-tuple-element.42.table_ref, f32[32,4,128]{2,1,0:T(4,128)S(1)} %all-to-all-done.sums_ref.coupling_ref, f32[32,4,128]{2,1,0:T(4,128)S(1)} %all-to-all-done.sums_ref.coupling_ref, s32[32,1,384]{2,1,0:T(1,128)S(1)} %get-tuple-element.34.index_ref, ...), custom_call_target="tpu_custom_call" | custom-call | tf_op jit(solution)/shard_map/pallas_call | solution.py:648
  29.8 4.9 %shard_map.147 = (f32[8,7680]{1,0:T(8,128)S(1)}, f32[8,9472]{1,0:T(8,128)S(1)}, f32[32,4,128]{2,1,0:T(4,128)}, f32[256,384]{1,0:T(8,128)S(1)}) custom-call(s32[1,128]{1,0:T(1,128)S(1)} %get-tuple-element.32.table_ref.table_row_ref, f32[8,7680]{1,0:T(8,128)S(1)} %shard_map.146.image_ref, f32[8,9472]{1,0:T(8,128)S(1)} %get-tuple-element.39.p_ref, ...), custom_call_target="tpu_custom_call" | custom-call | tf_op jit(solution)/shard_map/pallas_call | solution.py:648
  34.8 6.0 %all-to-all-start.1 = ((f32[32,4,128]{2,1,0:T(4,128)}), f32[32,4,128]{2,1,0:T(4,128)S(1)}, u32[]{:S(2)}, u32[]{:S(2)}) async-start(f32[32,4,128]{2,1,0:T(4,128)} %get-tuple-element.55), calls=%async_computation.1 | async-start | bytes 131072 | tf_op jit(solution)/shard_map/all_to_all | solution.py:731
  40.8 3.7 %shard_map.148 = (f32[8,7680]{1,0:T(8,128)S(1)}, f32[8,1024]{1,0:T(8,128)S(1)}, f32[8,1024]{1,0:T(8,128)S(1)}) custom-call(s32[1,128]{1,0:T(1,128)S(1)} %get-tuple-element.32.table_ref.table_row_ref, s32[32,1,384]{2,1,0:T(1,128)S(1)} %get-tuple-element.34.index_ref, s32[1,128]{1,0:T(1,128)S(1)} %get-tuple-element.37.corner_ref, ...), custom_call_target="tpu_custom_call" | custom-call | tf_op jit(solution)/shard_map/pallas_call | solution.py:648
  44.5 0.3 collective-permute-start.4
  44.8 3.4 %collective-permute-start.5 = (f32[8,1024]{1,0:T(8,128)S(1)}, f32[8,1024]{1,0:T(8,128)S(1)}, u32[]{:S(2)}, u32[]{:S(2)}) collective-permute-start(f32[8,1024]{1,0:T(8,128)S(1)} %get-tuple-element.61), channel_id=1, source_target_pairs={{1,2},{2,1},{3,4},{4,3},{5,6},{6,5},{7,8},{8,7},{9,10},{10,9},{11,... | collective-permute-start | bytes 98312 | tf_op jit(solution)/shard_map/ppermute | solution.py:643
  48.2 2.7 %shard_map.149 = (f32[8,7680]{1,0:T(8,128)S(1)}, f32[1,128]{1,0:T(1,128)S(1)}) custom-call(s32[1,128]{1,0:T(1,128)S(1)} %get-tuple-element.42.table_ref, f32[32,4,128]{2,1,0:T(4,128)S(1)} %all-to-all-done.1.sums_ref, f32[32,4,128]{2,1,0:T(4,128)S(1)} %all-to-all-done.sums_ref.coupling_ref, s32[32,1,384]{2,1,0:T(1,128)S(1)} %get-tuple-element.34.index_ref, ...), custom_call_target="tpu_custom_call" | custom-call | tf_op jit(solution)/shard_map/pallas_call | solution.py:648
  50.9 1.6 %shard_map.150 = (f32[8,6656]{1,0:T(8,128)}, f32[8,6656]{1,0:T(8,128)}) custom-call(s32[1,128]{1,0:T(1,128)S(1)} %get-tuple-element.32.table_ref.table_row_ref, f32[8,6656]{1,0:T(8,128)S(1)} %copy-done, f32[8,9472]{1,0:T(8,128)S(1)} %get-tuple-element.39.p_ref, f32[2,7680]{1,0:T(2,128)S(1)} %get-tuple-element.40.refs_2_.diag_in_ref.diag_ref, ...), custom_call_target="tpu_custom_call" | custom-call | tf_op jit(solution)/shard_map/pallas_call | solution.py:648
  (27 shorter events, 0.1 us)
Async XLA Ops:
  0.6 5.9 %copy-start = (f32[8,6656]{1,0:T(8,128)S(1)}, f32[8,6656]{1,0:T(8,128)}, u32[]{:S(2)}) copy-start(f32[8,6656]{1,0:T(8,128)} %rhs_ref.5) | copy-start | bytes 638980
  0.6 5.9 %copy-start.4 = (f32[6656]{0:T(1024)S(1)}, f32[6656]{0:T(1024)}, u32[]{:S(2)}) copy-start(f32[6656]{0:T(1024)} %param.15) | copy-start | bytes 79876
  0.7 5.9 %copy-start.5 = (f32[6656]{0:T(1024)S(1)}, f32[6656]{0:T(1024)}, u32[]{:S(2)}) copy-start(f32[6656]{0:T(1024)} %param.14) | copy-start | bytes 79876
  1.9 8.7 %collective-permute-start = (f32[88,384]{1,0:T(8,128)S(1)}, f32[88,384]{1,0:T(8,128)S(1)}, u32[]{:S(2)}, u32[]{:S(2)}) collective-permute-start(f32[88,384]{1,0:T(8,128)S(1)} %get-tuple-element.35), channel_id=1, source_target_pairs={{0,1},{1,0},{2,3},{3,2},{4,5},{5,4},{6,7},{7,6},{8,9},{9,8},{10,11... | collective-permute-start | bytes 405512 | tf_op jit(solution)/shard_map/ppermute | solution.py:643
  2.0 8.6 %collective-permute-start.1 = (f32[88,384]{1,0:T(8,128)S(1)}, f32[88,384]{1,0:T(8,128)S(1)}, u32[]{:S(2)}, u32[]{:S(2)}) collective-permute-start(f32[88,384]{1,0:T(8,128)S(1)} %get-tuple-element.36), channel_id=1, source_target_pairs={{1,2},{2,1},{3,4},{4,3},{5,6},{6,5},{7,8},{8,7},{9,10},{10,9},{11,... | collective-permute-start | bytes 405512 | tf_op jit(solution)/shard_map/ppermute | solution.py:643
  6.5 0.8 %copy-start.3 = (s32[32,343]{1,0:T(8,128)S(1)}, s32[32,343]{1,0:T(8,128)}, u32[]{:S(2)}) copy-start(s32[32,343]{1,0:T(8,128)} %conn_ref.3) | copy-start | bytes 131716
  6.5 0.8 %copy-start.7 = (s32[8]{0:T(128)S(1)}, s32[8]{0:T(128)}, u32[]{:S(2)}) copy-start(s32[8]{0:T(128)} %cell_hbm.1) | copy-start | bytes 100
  6.6 0.8 %copy-start.8 = (s32[8]{0:T(128)S(1)}, s32[8]{0:T(128)}, u32[]{:S(2)}) copy-start(s32[8]{0:T(128)} %atom_hbm.1) | copy-start | bytes 100
  6.6 0.8 %copy-start.9 = (s32[32]{0:T(128)S(1)}, s32[32]{0:T(128)}, u32[]{:S(2)}) copy-start(s32[32]{0:T(128)} %scount_hbm.1) | copy-start | bytes 388
  6.6 0.8 %copy-start.10 = (s32[32]{0:T(128)S(1)}, s32[32]{0:T(128)}, u32[]{:S(2)}) copy-start(s32[32]{0:T(128)} %count_ref.1) | copy-start | bytes 388
  6.6 0.8 %copy-start.11 = (f32[32]{0:T(128)S(1)}, f32[32]{0:T(128)}, u32[]{:S(2)}) copy-start(f32[32]{0:T(128)} %scale_ref.1) | copy-start | bytes 388
  8.2 2.4 %copy-start.2 = (f32[8,8,343]{2,1,0:T(8,128)S(1)}, f32[8,8,343]{2,1,0:T(8,128)}, u32[]{:S(2)}) copy-start(f32[8,8,343]{2,1,0:T(8,128)} %param.21) | copy-start | bytes 263428
  8.2 2.4 %copy-start.6 = (f32[2,8,8]{2,1,0:T(8,128)S(1)}, f32[2,8,8]{2,1,0:T(8,128)}, u32[]{:S(2)}) copy-start(f32[2,8,8]{2,1,0:T(8,128)} %coupling_ref.1) | copy-start | bytes 1540
  10.6 8.5 %copy-start.1 = (f32[343,343]{1,0:T(8,128)S(1)}, f32[343,343]{1,0:T(8,128)}, u32[]{:S(2)}) copy-start(f32[343,343]{1,0:T(8,128)} %refs_1_.1) | copy-start | bytes 1411792
  13.2 14.0 %all-to-all-start = ((f32[32,4,128]{2,1,0:T(4,128)}), f32[32,4,128]{2,1,0:T(4,128)S(1)}, u32[]{:S(2)}, u32[]{:S(2)}) async-start(f32[32,4,128]{2,1,0:T(4,128)} %get-tuple-element.43), calls=%async_computation | async-start | bytes 131072 | tf_op jit(solution)/shard_map/all_to_all | solution.py:708
  23.5 6.4 %collective-permute-start.2 = (f32[10,1024]{1,0:T(8,128)S(1)}, f32[10,1024]{1,0:T(8,128)S(1)}, u32[]{:S(2)}, u32[]{:S(2)}) collective-permute-start(f32[10,1024]{1,0:T(8,128)S(1)} %get-tuple-element.49), channel_id=1, source_target_pairs={{0,1},{1,0},{2,3},{3,2},{4,5},{5,4},{6,7},{7,6},{8,9},{9,8},{10,11... | collective-permute-start | bytes 122888 | tf_op jit(solution)/shard_map/ppermute | solution.py:643
  23.8 6.0 %collective-permute-start.3 = (f32[10,1024]{1,0:T(8,128)S(1)}, f32[10,1024]{1,0:T(8,128)S(1)}, u32[]{:S(2)}, u32[]{:S(2)}) collective-permute-start(f32[10,1024]{1,0:T(8,128)S(1)} %get-tuple-element.50), channel_id=1, source_target_pairs={{1,2},{2,1},{3,4},{4,3},{5,6},{6,5},{7,8},{8,7},{9,10},{10,9},{11,... | collective-permute-start | bytes 122888 | tf_op jit(solution)/shard_map/ppermute | solution.py:643
  34.8 13.5 %all-to-all-start.1 = ((f32[32,4,128]{2,1,0:T(4,128)}), f32[32,4,128]{2,1,0:T(4,128)S(1)}, u32[]{:S(2)}, u32[]{:S(2)}) async-start(f32[32,4,128]{2,1,0:T(4,128)} %get-tuple-element.55), calls=%async_computation.1 | async-start | bytes 131072 | tf_op jit(solution)/shard_map/all_to_all | solution.py:731
  44.5 6.4 %collective-permute-start.4 = (f32[8,1024]{1,0:T(8,128)S(1)}, f32[8,1024]{1,0:T(8,128)S(1)}, u32[]{:S(2)}, u32[]{:S(2)}) collective-permute-start(f32[8,1024]{1,0:T(8,128)S(1)} %get-tuple-element.60), channel_id=1, source_target_pairs={{0,1},{1,0},{2,3},{3,2},{4,5},{5,4},{6,7},{7,6},{8,9},{9,8},{10,11... | collective-permute-start | bytes 98312 | tf_op jit(solution)/shard_map/ppermute | solution.py:643
  44.8 6.1 %collective-permute-start.5 = (f32[8,1024]{1,0:T(8,128)S(1)}, f32[8,1024]{1,0:T(8,128)S(1)}, u32[]{:S(2)}, u32[]{:S(2)}) collective-permute-start(f32[8,1024]{1,0:T(8,128)S(1)} %get-tuple-element.61), channel_id=1, source_target_pairs={{1,2},{2,1},{3,4},{4,3},{5,6},{6,5},{7,8},{8,7},{9,10},{10,9},{11,... | collective-permute-start | bytes 98312 | tf_op jit(solution)/shard_map/ppermute | solution.py:643

commit v12 on v11

--- a/solution.py
+++ b/solution.py
@@ -9,10 +9,13 @@
 
 LANES = 128
 ROWS = 8
-WIDE = 256
+BITS = 8
+WIDE = 1 << BITS
+NARROW = 7
 CHAINS = 4
 SPAN = 14
 BAND = 8
+BESIDE = 4
 TOGETHER = 8
 F32 = jnp.float32
 BF16 = jnp.bfloat16
@@ -34,7 +37,7 @@
         self.entries, self.channels = projector.shape[:2]
         self.owned = atom_matrix.shape[0]
         self.ghost = self.nodes // 16
-        self.rim = round_up(self.ghost, WIDE)
+        self.rim = round_up(self.ghost, 2 * LANES)
         self.shift = self.rim - self.ghost
         self.window = self.nodes + 2 * self.rim
         self.width = round_up(self.elem, LANES)
@@ -51,7 +54,7 @@
         self.rim_row = self.index_row + round_up(self.entries, ROWS)
         self.rim_pieces = -(-self.rim // self.width)
         self.message = self.rim_row + self.rim_pieces * ROWS
-        assert self.elem + 5 <= self.width and 2 * self.entries <= self.slots
+        assert self.elem + 3 <= self.width and self.entries % BESIDE == 0
         self.together = TOGETHER if self.slots % TOGETHER == 0 else 1
         assert self.vectors == ROWS and self.channels == ROWS and 2 * self.slots <= LANES
         assert self.nodes % WIDE == 0 and self.owned * self.pairs == LANES
@@ -168,10 +171,6 @@
         rows = jnp.where(entry == s, row, rows)
         for k, fact in enumerate(facts):
             rows = jnp.where((entry == s) & (place == z.elem + k), fact.astype(F32), rows)
-    middle = (place > 0) & (place < z.elem - 1)
-    low = jnp.min(jnp.where(middle, rows, 1.0 * z.window), axis=1, keepdims=True)
-    high = jnp.max(jnp.where(middle, rows, 0.0), axis=1, keepdims=True)
-    rows = jnp.where(place == z.elem + 3, low, jnp.where(place == z.elem + 4, high, rows))
     for ref, side in zip((send_a_ref, send_b_ref), sides):
         ref[...] = jnp.zeros_like(ref)
         ref[: z.index_row, : z.elem] = projector_all[...]
@@ -205,9 +204,37 @@
     return functools.reduce(jnp.add, [(end >= z.slots).astype(jnp.int32) for end in ends])
 
 
-def gather_middle(z, groups, listed, table_ref, index_ref, window_ref, u_ref):
+def split_window(z, window_ref, parts_ref):
+    count = z.window // WIDE
+    for h in range(count):
+        value = window_ref[:, h * WIDE : (h + 1) * WIDE]
+        rounded = value.astype(BF16).astype(F32)
+        both = jnp.concatenate([rounded, value - rounded], axis=0).astype(BF16)
+        parts_ref[h * 2 * ROWS : (h + 1) * 2 * ROWS, :] = both
+    parts_ref[count * 2 * ROWS :, :] = jnp.zeros((BAND * 2 * ROWS, WIDE), BF16)
+
+
+def gather_middle(z, groups, listed, table_ref, index_ref, window_ref, u_ref, parts_ref=None):
     total = z.window // LANES
     tile = (ROWS, LANES)
+    pair = (2 * ROWS, LANES)
+    sub = iota(pair, 0)
+    lows = [(sub + n * 2 * ROWS).astype(jnp.int16) for n in range(WIDE // (2 * ROWS))]
+    one, none = jnp.ones(pair, BF16), jnp.zeros(pair, BF16)
+
+    def product_tile(c, k):
+        start = jnp.minimum((table_ref[0, z.low + c] >> BITS) + k * BAND, z.window // WIDE)
+        index = index_ref[c, :, (z.tiles - 1) * LANES : z.tiles * LANES]
+        low = (jnp.broadcast_to(index, pair) & (WIDE - 1)).astype(jnp.int16)
+        hot = jnp.concatenate([jnp.where(low == n, one, none) for n in lows], axis=0)
+        rows = pl.ds(pl.multiple_of(start * 2 * ROWS, 2 * ROWS), BAND * 2 * ROWS)
+        got = jnp.dot(parts_ref[rows, :], hot, preferred_element_type=F32)
+        high = (jnp.broadcast_to(index, tile) >> BITS) - start
+        value = jnp.zeros(tile, F32)
+        for h in range(BAND):
+            at = h * 2 * ROWS
+            value = jnp.where(high == h, got[at : at + ROWS] + got[at + ROWS : at + 2 * ROWS], value)
+        return value
 
     def some_cells(g, _):
         cells = [g * z.together + i for i in range(z.together)]
@@ -223,6 +250,9 @@
             for i, c in enumerate(cells):
                 start = jnp.minimum(starts[i] + k * SPAN, total)
                 for t in range(z.tiles):
+                    if parts_ref is not None and t == z.tiles - 1:
+                        values[i * z.tiles + t] += product_tile(c, k)
+                        continue
                     index = jnp.broadcast_to(index_ref[c, :, t * LANES : (t + 1) * LANES], tile)
                     low, high = index & (LANES - 1), (index >> 7) - start
                     value = values[i * z.tiles + t]
@@ -307,19 +337,12 @@
 
 
 def first_kernel(
-    z, table_ref, table_row_ref, p_in_ref, u_in_ref, halo_a_ref, halo_b_ref, index_ref, corner_ref, weight_ref,
-    projector_ref, coupling_ref, p_ref, out_ref, uw_ref, pj_ref, marked_ref, beside_ref, u_ref,
+    z, table_ref, p_in_ref, u_in_ref, halo_a_ref, halo_b_ref, index_ref, corner_ref, weight_ref,
+    projector_ref, coupling_ref, p_ref, out_ref, uw_ref, pj_ref, beside_ref, u_ref,
 ):
     rows = slice(z.index_row, z.index_row + z.entries)
-    marked = table_row_ref[...]
     line = iota((1, LANES), 1)
     left, right = sides(table_ref[0, z.position], halo_a_ref[rows, :], halo_b_ref[rows, :])
-    for s in range(z.entries):
-        high = left[s : s + 1, z.elem + 4 : z.elem + 5]
-        marked = jnp.where(line == z.list + s, (high >= z.window - 2 * z.rim).astype(jnp.int32), marked)
-        low = right[s : s + 1, z.elem + 3 : z.elem + 4]
-        marked = jnp.where(line == z.list + z.entries + s, (low < 2 * z.rim).astype(jnp.int32), marked)
-    marked_ref[...] = marked
     beside = corner_ref[...]
     for k, (side, move) in enumerate(((left, -z.nodes), (right, z.nodes))):
         side = side.astype(jnp.int32) + move
@@ -358,6 +381,7 @@
 def second_kernel(
     z, table_ref, image_ref, p_ref, diag_in_ref, shift_ref, gamma_ref, halo_a_ref, halo_b_ref,
     index_ref, corner_ref, weight_ref, k_high_ref, k_low_ref, pj_ref, y_ref, q_ref, out_ref, e_ref, diag_ref, u_ref, uw_ref,
+    parts_ref,
 ):
     left, right = sides(table_ref[0, z.position], halo_a_ref[...], halo_b_ref[...])
     own = slice(z.rim, z.rim + z.nodes)
@@ -377,7 +401,8 @@
     ]
     energy = jnp.sum(q * q * (diag_ref[1:2, own] + shift_ref[:, :1]), axis=1, keepdims=True)
     groups = 0, z.slots // z.together
-    gather_middle(z, groups, False, table_ref, index_ref, q_ref, u_ref)
+    split_window(z, q_ref, parts_ref)
+    gather_middle(z, groups, False, table_ref, index_ref, q_ref, u_ref, parts_ref)
     gather_corners(z, corner_ref, q_ref, weight_ref, u_ref, uw_ref)
     parts = contributions(z, table_ref, pj_ref, u_ref)
     stiffness_product(k_high_ref, k_low_ref, uw_ref, e_ref)
@@ -395,14 +420,23 @@
         out_ref[d] = message
 
 
+def band_of(bits):
+    return BAND if bits == BITS else SPAN
+
+
+def acc_shape(z, bits):
+    return ((z.window >> bits) + band_of(bits)) * 2 * ROWS, 1 << bits
+
+
 class Scatter:
-    def __init__(self, z, table_ref, index_ref, corner_ref, acc_ref):
+    def __init__(self, z, bits, table_ref, index_ref, corner_ref, acc_ref):
+        self.bits, self.wide, self.band = bits, 1 << bits, band_of(bits)
         self.z, self.index_ref, self.corner_ref, self.acc_ref = z, index_ref, corner_ref, acc_ref
         self.table_ref = table_ref
-        self.groups = z.window // WIDE
+        self.groups = z.window // self.wide
         self.pair = (2 * ROWS, LANES)
         sub = iota(self.pair, 0)
-        self.lows = [(sub + k * 2 * ROWS).astype(jnp.int16) for k in range(WIDE // (2 * ROWS))]
+        self.lows = [(sub + k * 2 * ROWS).astype(jnp.int16) for k in range(self.wide // (2 * ROWS))]
         self.one, self.none = jnp.ones(self.pair, BF16), jnp.zeros(self.pair, BF16)
         self.lane = iota((ROWS, LANES), 1)
         self.end = (z.elem - 1) % LANES
@@ -412,7 +446,7 @@
         return jnp.concatenate([rounded, value - rounded], axis=0).astype(BF16)
 
     def hot_rows(self, index):
-        low = (index & (WIDE - 1)).astype(jnp.int16)
+        low = (index & (self.wide - 1)).astype(jnp.int16)
         return jnp.concatenate([jnp.where(low == k, self.one, self.none) for k in self.lows], axis=0)
 
     def masked(self, high, both, rows):
@@ -436,19 +470,19 @@
         index = jnp.broadcast_to(self.corner_ref[...], self.pair)
         rows = self.groups * 2 * ROWS
         self.acc_ref[:rows, :] = self.product(
-            self.masked(index >> 8, self.two_parts(corners), self.groups), self.hot_rows(index)
+            self.masked(index >> self.bits, self.two_parts(corners), self.groups), self.hot_rows(index)
         )
-        self.acc_ref[rows:, :] = jnp.zeros((BAND * 2 * ROWS, WIDE), F32)
+        self.acc_ref[rows:, :] = jnp.zeros((self.band * 2 * ROWS, self.wide), F32)
 
     def add(self, cells, value_of):
         z = self.z
-        starts = [self.table_ref[0, z.low + c] >> 8 for c in cells]
-        ends = [self.table_ref[0, z.high + c] >> 8 for c in cells]
-        passes = functools.reduce(jnp.maximum, [(e - s) // BAND + 1 for s, e in zip(starts, ends)])
+        starts = [self.table_ref[0, z.low + c] >> self.bits for c in cells]
+        ends = [self.table_ref[0, z.high + c] >> self.bits for c in cells]
+        passes = functools.reduce(jnp.maximum, [(e - s) // self.band + 1 for s, e in zip(starts, ends)])
 
         def one_pass(k, _):
             for i, c in enumerate(cells):
-                start = jnp.minimum(starts[i] + k * BAND, self.groups)
+                start = jnp.minimum(starts[i] + k * self.band, self.groups)
                 lhs, hot = [], []
                 for t in range(z.tiles):
                     index = jnp.broadcast_to(self.index_ref[c, :, t * LANES : (t + 1) * LANES], self.pair)
@@ -457,9 +491,9 @@
                         value = jnp.where(self.lane == 0, 0.0, value)
                     if t == z.tiles - 1:
                         value = jnp.where(self.lane == self.end, 0.0, value)
-                    lhs.append(self.masked((index >> 8) - start, self.two_parts(value), BAND))
+                    lhs.append(self.masked((index >> self.bits) - start, self.two_parts(value), self.band))
                     hot.append(self.hot_rows(index))
-                to = pl.ds(pl.multiple_of(start * 2 * ROWS, 2 * ROWS), BAND * 2 * ROWS)
+                to = pl.ds(pl.multiple_of(start * 2 * ROWS, 2 * ROWS), self.band * 2 * ROWS)
                 self.acc_ref[to, :] += self.product(jnp.concatenate(lhs, axis=1), jnp.concatenate(hot, axis=1))
             return 0
 
@@ -470,7 +504,7 @@
         for t in range(values.shape[1] // LANES):
             lanes = slice(t * LANES, (t + 1) * LANES)
             at = jnp.broadcast_to(index[:, lanes], self.pair)
-            lhs.append(self.masked(at >> 8, self.two_parts(values[:, lanes]), rows))
+            lhs.append(self.masked(at >> self.bits, self.two_parts(values[:, lanes]), rows))
             hot.append(self.hot_rows(at))
         to = slice(first * 2 * ROWS, (first + rows) * 2 * ROWS)
         self.acc_ref[to, :] += self.product(jnp.concatenate(lhs, axis=1), jnp.concatenate(hot, axis=1))
@@ -490,7 +524,7 @@
         stiffness_product(k_high_ref, k_low_ref, uw_ref, e_ref)
     else:
         e_ref, image_ref, send_a_ref, send_b_ref, acc_ref = refs
-    scatter = Scatter(z, table_ref, index_ref, corner_ref, acc_ref)
+    scatter = Scatter(z, BITS, table_ref, index_ref, corner_ref, acc_ref)
     scatter.start([(c, e_ref[c * ROWS : (c + 1) * ROWS, :]) for c in range(z.slots)])
 
     def some_cells(g, _):
@@ -572,7 +606,7 @@
         projectors = jnp.where(iota((z.index_row, z.width), 1) < z.elem, ext[: z.index_row], 0.0)
         support_ref[(side + 1) * count : (side + 2) * count, :] = values(facts, projectors)
         nodes_ref[side] = nodes
-    scatter = Scatter(z, table_ref, index_ref, corner_ref, acc_ref)
+    scatter = Scatter(z, NARROW, table_ref, index_ref, corner_ref, acc_ref)
     cells = [table_ref[0, z.cell + s] for s in range(z.entries)]
     blocks = [support_ref[s * ROWS : (s + 1) * ROWS, :] for s in range(3 * z.entries)]
     scatter.start(list(zip(cells, blocks)), blocks[z.entries :])
@@ -584,20 +618,18 @@
             return support_ref[s * ROWS : (s + 1) * ROWS, t * LANES : (t + 1) * LANES]
 
         scatter.add(some, value_of)
-    shared = 2 * z.rim // WIDE
+    shared = 2 * z.rim // scatter.wide
     place = iota((ROWS, z.width), 1)
     middle = (place > 0) & (place < z.elem - 1)
     for side, (first, offset) in enumerate(((0, z.window - 2 * z.rim), (scatter.groups - shared, 0))):
-        for s in range(z.entries):
-
-            @pl.when(table_ref[0, z.list + side * z.entries + s] > 0)
-            def _():
-                at = ((side + 1) * z.entries + s) * ROWS
-                value = jnp.where(middle, support_ref[at : at + ROWS, :], 0.0)
-                scatter.add_rows(nodes_ref[side, s : s + 1, :] - offset, value, first, shared)
-
+        for s in range(0, z.entries, BESIDE):
+            some = range(s, s + BESIDE)
+            base = (side + 1) * z.entries
+            value = [jnp.where(middle, support_ref[(base + i) * ROWS : (base + i + 1) * ROWS, :], 0.0) for i in some]
+            index = [nodes_ref[side, i : i + 1, :] - offset for i in some]
+            scatter.add_rows(jnp.concatenate(index, axis=1), jnp.concatenate(value, axis=1), first, shared)
     for h in range(scatter.groups):
-        at = slice(h * WIDE, (h + 1) * WIDE)
+        at = slice(h * scatter.wide, (h + 1) * scatter.wide)
         image_ref[:, at] = cells_ref[:, at] + scatter.result(h)
 
 
@@ -662,9 +694,10 @@
     message = (z.devices, 4, LANES)
     square, entries = (z.width, z.width), (z.entries * ROWS, z.width)
     rim, more_rim = (z.vectors, 2 * z.rim), (z.vectors + 2, 2 * z.rim)
-    acc = ((z.window // WIDE + BAND) * 2 * ROWS, WIDE)
+    acc = acc_shape(z, BITS)
     support_scratch = [
-        ((3 * z.entries * ROWS, z.width), F32), ((2, z.rim_row - z.index_row, z.width), jnp.int32), (acc, F32),
+        ((3 * z.entries * ROWS, z.width), F32), ((2, z.rim_row - z.index_row, z.width), jnp.int32),
+        (acc_shape(z, NARROW), F32),
     ]
 
     precond_lines = precond.reshape(-1, LANES)
@@ -697,13 +730,12 @@
         rhs, precond_lines, potential.reshape(-1, LANES),
     )
     (u,) = call(functools.partial(first_window_kernel, z), [(cells, F32)], [], (table,), p, index)
-    p, sums, uw, pj, marked, beside = call(
+    p, sums, uw, pj, beside = call(
         functools.partial(first_kernel, z),
-        [(reach, F32), (message, F32), (cells, F32), (entries, F32), ((1, LANES), jnp.int32),
-         ((1, LANES), jnp.int32)],
+        [(reach, F32), (message, F32), (cells, F32), (entries, F32), ((1, LANES), jnp.int32)],
         [(cells, F32)],
         (table,),
-        table, p, u, *ext, index, corner, weight, flat_projector, atom_matrix,
+        p, u, *ext, index, corner, weight, flat_projector, atom_matrix,
     )
     coupled = lax.all_to_all(sums, "dom", 0, 0)
     image, send_a, send_b, k_high, k_low = call(
@@ -718,13 +750,13 @@
         functools.partial(support_kernel, z, False),
         [(window, F32)],
         support_scratch,
-        (marked,),
+        (table,),
         coupled, coupled, index, beside, pj, *ext, image,
     )
     y, q, sums, e = call(
         functools.partial(second_kernel, z),
         [(window, F32), (reach, F32), (message, F32), (cells, F32)],
-        [((2, z.window), F32), (cells, F32), (cells, F32)],
+        [((2, z.window), F32), (cells, F32), (cells, F32), (acc, BF16)],
         (table,),
         image, p, diag, shift_tile, gamma, *halo, index, corner, weight, k_high, k_low, pj,
     )
@@ -738,7 +770,7 @@
         functools.partial(support_kernel, z, True),
         [(window, F32), ((1, LANES), F32)],
         support_scratch,
-        (marked,),
+        (table,),
         totals, coupled, index, beside, pj, *ext, image,
     )
     return tuple(

time: 53.4 us -> 52.7 us (0.987)
  no operation moved by 1% of the time
where the time goes in v12:
time: 52.7 us; the launch traced here: 52.1 us
  Pallas kernels  26.7 us (51%)
  starting transfers between devices  23.8 us (45%)
  between operations  0.94 us (2%)
  local copies, waits for them, and re-layouts  0.63 us (1%)
    pallas_call x11, Pallas kernels, call(): pl.pallas_call(kernel, out_shape=[jax.ShapeDtypeStruct(s, d) if i in in_h...  26.7 us
    ppermute x6, starting transfers between devices, exchange(): return (lax.ppermute(a, 'dom', near), lax.ppermute(b, 'dom', far))  12 us
    all_to_all x1, starting transfers between devices, on_device(): coupled = lax.all_to_all(sums, 'dom', 0, 0)  5.93 us
    all_to_all x1, starting transfers between devices, on_device(): totals = lax.all_to_all(sums, 'dom', 0, 0)  5.92 us
  transfers between devices with their start and end apart: 8, of which 0 were waited for; matrix products, arithmetic and copies ran while one was open for 0% of the time, Pallas kernels for 32%

profile of v12, /device:TPU:1, one launch (start us, length us, event | category | flops | bytes accessed | tf_op | source)
XLA Modules:
  0.0 52.1 jit_solution(3983281593831851557)
XLA Ops:
  0.7 1.2 %shard_map.143 = (f32[88,384]{1,0:T(8,128)S(1)}, f32[88,384]{1,0:T(8,128)S(1)}, f32[8,128]{1,0:T(8,128)S(1)}) custom-call(s32[1]{0:T(128)} %bitcast.pos_ref, s32[8]{0:T(128)} %cell_hbm.1, s32[8]{0:T(128)} %atom_hbm.1, s32[32]{0:T(128)} %scount_hbm.1, f32[8]{0:T(128)} %shift_hbm.1, f32[8,6656]{1,0:T(8,128)} %rhs_ref.5, f32[52,128]{1,0:T(8,128)} %bitcast.6, ...), custom_call_target="tpu_custom_call" | custom-call | tf_op jit(solution)/shard_map/pallas_call | solution.py:680
  1.9 0.1 collective-permute-start
  1.9 4.5 %collective-permute-start.1 = (f32[88,384]{1,0:T(8,128)S(1)}, f32[88,384]{1,0:T(8,128)S(1)}, u32[]{:S(2)}, u32[]{:S(2)}) collective-permute-start(f32[88,384]{1,0:T(8,128)S(1)} %get-tuple-element.35), channel_id=1, source_target_pairs={{1,2},{2,1},{3,4},{4,3},{5,6},{6,5},{7,8},{8,7},{9,10},{10,9},{11,... | collective-permute-start | bytes 405512 | tf_op jit(solution)/shard_map/ppermute | solution.py:675
  6.5 0.0 copy-start.3
  6.5 0.0 copy-start.8
  6.5 0.0 copy-start.9
  6.5 0.2 shard_map.141
  6.7 0.6 %copy-done.3 = s32[32,343]{1,0:T(8,128)S(1)} copy-done((s32[32,343]{1,0:T(8,128)S(1)}, s32[32,343]{1,0:T(8,128)}, u32[]{:S(2)}) %copy-start.3) | copy-done | bytes 43928
  7.3 0.8 %shard_map.140 = (s32[32,1,384]{2,1,0:T(1,128)S(1)}, s32[1,128]{1,0:T(1,128)S(1)}, s32[1,128]{1,0:T(1,128)S(1)}, f32[256,128]{1,0:T(8,128)S(1)}) custom-call(s32[1]{0:T(128)} %bitcast.pos_ref, s32[32]{0:T(128)S(1)} %copy-done.10, f32[32]{0:T(128)S(1)} %copy-done.11, s32[8]{0:T(128)S(1)} %copy-done.7, s32[8]{0:T(128)S(1)} %copy-done.8, s32[32]{0:T(128)S(1)} %copy-done.9, ...), custom_call_target="tpu_custom_call" | custom-call | tf_op jit(solution)/shard_map/pallas_call | solution.py:680
  8.1 0.0 copy-start.2
  8.2 2.3 %shard_map.142.u_in_ref = f32[256,384]{1,0:T(8,128)S(1)} custom-call(s32[1,128]{1,0:T(1,128)S(1)} %get-tuple-element.31.table_ref, f32[8,9472]{1,0:T(8,128)S(1)} %get-tuple-element.32.p_ref.p_in_ref, s32[32,1,384]{2,1,0:T(1,128)S(1)} %get-tuple-element.33.index_ref), custom_call_target="tpu_custom_call" | custom-call | tf_op jit(solution)/shard_map/pallas_call | solution.py:680
  10.6 2.5 %shard_map.144 = (f32[8,9472]{1,0:T(8,128)S(1)}, f32[32,4,128]{2,1,0:T(4,128)}, f32[256,384]{1,0:T(8,128)S(1)}, f32[64,384]{1,0:T(8,128)S(1)}, s32[1,128]{1,0:T(1,128)S(1)}) custom-call(s32[1,128]{1,0:T(1,128)S(1)} %get-tuple-element.31.table_ref, f32[8,9472]{1,0:T(8,128)S(1)} %get-tuple-element.32.p_ref.p_in_ref, f32[256,384]{1,0:T(8,128)S(1)} %shard_map.142.u_in_ref, ...), custom_call_target="tpu_custom_call" | custom-call | tf_op jit(solution)/shard_map/pallas_call | solution.py:680
  13.1 5.9 %all-to-all-start = ((f32[32,4,128]{2,1,0:T(4,128)}), f32[32,4,128]{2,1,0:T(4,128)S(1)}, u32[]{:S(2)}, u32[]{:S(2)}) async-start(f32[32,4,128]{2,1,0:T(4,128)} %get-tuple-element.41), calls=%async_computation | async-start | bytes 131072 | tf_op jit(solution)/shard_map/all_to_all | solution.py:740
  19.0 4.4 %shard_map.145 = (f32[8,7680]{1,0:T(8,128)S(1)}, f32[10,1024]{1,0:T(8,128)S(1)}, f32[10,1024]{1,0:T(8,128)S(1)}, bf16[384,384]{1,0:T(8,128)(2,1)S(1)}, bf16[384,384]{1,0:T(8,128)(2,1)S(1)}) custom-call(s32[1,128]{1,0:T(1,128)S(1)} %get-tuple-element.31.table_ref, s32[32,1,384]{2,1,0:T(1,128)S(1)} %get-tuple-element.33.index_ref, ...), custom_call_target="tpu_custom_call" | custom-call | tf_op jit(solution)/shard_map/pallas_call | solution.py:680
  23.4 0.3 collective-permute-start.2
  23.7 3.4 %collective-permute-start.3 = (f32[10,1024]{1,0:T(8,128)S(1)}, f32[10,1024]{1,0:T(8,128)S(1)}, u32[]{:S(2)}, u32[]{:S(2)}) collective-permute-start(f32[10,1024]{1,0:T(8,128)S(1)} %get-tuple-element.48), channel_id=1, source_target_pairs={{1,2},{2,1},{3,4},{4,3},{5,6},{6,5},{7,8},{8,7},{9,10},{10,9},{11,... | collective-permute-start | bytes 122888 | tf_op jit(solution)/shard_map/ppermute | solution.py:675
  27.1 2.7 %shard_map.146.image_ref = f32[8,7680]{1,0:T(8,128)S(1)} custom-call(s32[1,128]{1,0:T(1,128)S(1)} %get-tuple-element.31.table_ref, f32[32,4,128]{2,1,0:T(4,128)S(1)} %all-to-all-done.sums_ref.coupling_ref, f32[32,4,128]{2,1,0:T(4,128)S(1)} %all-to-all-done.sums_ref.coupling_ref, s32[32,1,384]{2,1,0:T(1,128)S(1)} %get-tuple-element.33.index_ref, ...), custom_call_target="tpu_custom_call" | custom-call | tf_op jit(solution)/shard_map/pallas_call | solution.py:680
  29.9 4.5 %shard_map.147 = (f32[8,7680]{1,0:T(8,128)S(1)}, f32[8,9472]{1,0:T(8,128)S(1)}, f32[32,4,128]{2,1,0:T(4,128)}, f32[256,384]{1,0:T(8,128)S(1)}) custom-call(s32[1,128]{1,0:T(1,128)S(1)} %get-tuple-element.31.table_ref, f32[8,7680]{1,0:T(8,128)S(1)} %shard_map.146.image_ref, f32[8,9472]{1,0:T(8,128)S(1)} %get-tuple-element.38.p_ref, ...), custom_call_target="tpu_custom_call" | custom-call | tf_op jit(solution)/shard_map/pallas_call | solution.py:680
  34.4 5.9 %all-to-all-start.1 = ((f32[32,4,128]{2,1,0:T(4,128)}), f32[32,4,128]{2,1,0:T(4,128)S(1)}, u32[]{:S(2)}, u32[]{:S(2)}) async-start(f32[32,4,128]{2,1,0:T(4,128)} %get-tuple-element.53), calls=%async_computation.1 | async-start | bytes 131072 | tf_op jit(solution)/shard_map/all_to_all | solution.py:763
  40.3 3.7 %shard_map.148 = (f32[8,7680]{1,0:T(8,128)S(1)}, f32[8,1024]{1,0:T(8,128)S(1)}, f32[8,1024]{1,0:T(8,128)S(1)}) custom-call(s32[1,128]{1,0:T(1,128)S(1)} %get-tuple-element.31.table_ref, s32[32,1,384]{2,1,0:T(1,128)S(1)} %get-tuple-element.33.index_ref, s32[1,128]{1,0:T(1,128)S(1)} %get-tuple-element.36.corner_ref, f32[256,384]{1,0:T(8,128)S(1)} %get-tuple-element.54.refs_0_), custom_call_target="tpu_custom_call" | custom-call | tf_op jit(solution)/shard_map/pallas_call | solution.py:680
  44.0 0.3 collective-permute-start.4
  44.4 3.4 %collective-permute-start.5 = (f32[8,1024]{1,0:T(8,128)S(1)}, f32[8,1024]{1,0:T(8,128)S(1)}, u32[]{:S(2)}, u32[]{:S(2)}) collective-permute-start(f32[8,1024]{1,0:T(8,128)S(1)} %get-tuple-element.59), channel_id=1, source_target_pairs={{1,2},{2,1},{3,4},{4,3},{5,6},{6,5},{7,8},{8,7},{9,10},{10,9},{11,... | collective-permute-start | bytes 98312 | tf_op jit(solution)/shard_map/ppermute | solution.py:675
  47.8 2.8 %shard_map.149 = (f32[8,7680]{1,0:T(8,128)S(1)}, f32[1,128]{1,0:T(1,128)S(1)}) custom-call(s32[1,128]{1,0:T(1,128)S(1)} %get-tuple-element.31.table_ref, f32[32,4,128]{2,1,0:T(4,128)S(1)} %all-to-all-done.1.sums_ref, f32[32,4,128]{2,1,0:T(4,128)S(1)} %all-to-all-done.sums_ref.coupling_ref, s32[32,1,384]{2,1,0:T(1,128)S(1)} %get-tuple-element.33.index_ref, ...), custom_call_target="tpu_custom_call" | custom-call | tf_op jit(solution)/shard_map/pallas_call | solution.py:680
  50.5 1.6 %shard_map.150 = (f32[8,6656]{1,0:T(8,128)}, f32[8,6656]{1,0:T(8,128)}) custom-call(s32[1,128]{1,0:T(1,128)S(1)} %get-tuple-element.31.table_ref, f32[8,6656]{1,0:T(8,128)S(1)} %copy-done, f32[8,9472]{1,0:T(8,128)S(1)} %get-tuple-element.38.p_ref, f32[2,7680]{1,0:T(2,128)S(1)} %get-tuple-element.39.refs_2_.diag_in_ref.diag_ref, ...), custom_call_target="tpu_custom_call" | custom-call | tf_op jit(solution)/shard_map/pallas_call | solution.py:680
  (27 shorter events, 0.1 us)
Async XLA Ops:
  0.6 5.8 %copy-start = (f32[8,6656]{1,0:T(8,128)S(1)}, f32[8,6656]{1,0:T(8,128)}, u32[]{:S(2)}) copy-start(f32[8,6656]{1,0:T(8,128)} %rhs_ref.5) | copy-start | bytes 638980
  0.6 5.8 %copy-start.4 = (f32[6656]{0:T(1024)S(1)}, f32[6656]{0:T(1024)}, u32[]{:S(2)}) copy-start(f32[6656]{0:T(1024)} %param.15) | copy-start | bytes 79876
  0.7 5.8 %copy-start.5 = (f32[6656]{0:T(1024)S(1)}, f32[6656]{0:T(1024)}, u32[]{:S(2)}) copy-start(f32[6656]{0:T(1024)} %param.14) | copy-start | bytes 79876
  1.9 8.7 %collective-permute-start = (f32[88,384]{1,0:T(8,128)S(1)}, f32[88,384]{1,0:T(8,128)S(1)}, u32[]{:S(2)}, u32[]{:S(2)}) collective-permute-start(f32[88,384]{1,0:T(8,128)S(1)} %get-tuple-element.34), channel_id=1, source_target_pairs={{0,1},{1,0},{2,3},{3,2},{4,5},{5,4},{6,7},{7,6},{8,9},{9,8},{10,11... | collective-permute-start | bytes 405512 | tf_op jit(solution)/shard_map/ppermute | solution.py:675
  1.9 8.6 %collective-permute-start.1 = (f32[88,384]{1,0:T(8,128)S(1)}, f32[88,384]{1,0:T(8,128)S(1)}, u32[]{:S(2)}, u32[]{:S(2)}) collective-permute-start(f32[88,384]{1,0:T(8,128)S(1)} %get-tuple-element.35), channel_id=1, source_target_pairs={{1,2},{2,1},{3,4},{4,3},{5,6},{6,5},{7,8},{8,7},{9,10},{10,9},{11,... | collective-permute-start | bytes 405512 | tf_op jit(solution)/shard_map/ppermute | solution.py:675
  6.5 0.8 %copy-start.3 = (s32[32,343]{1,0:T(8,128)S(1)}, s32[32,343]{1,0:T(8,128)}, u32[]{:S(2)}) copy-start(s32[32,343]{1,0:T(8,128)} %conn_ref.3) | copy-start | bytes 131716
  6.5 0.8 %copy-start.7 = (s32[8]{0:T(128)S(1)}, s32[8]{0:T(128)}, u32[]{:S(2)}) copy-start(s32[8]{0:T(128)} %cell_hbm.1) | copy-start | bytes 100
  6.5 0.8 %copy-start.8 = (s32[8]{0:T(128)S(1)}, s32[8]{0:T(128)}, u32[]{:S(2)}) copy-start(s32[8]{0:T(128)} %atom_hbm.1) | copy-start | bytes 100
  6.5 0.8 %copy-start.9 = (s32[32]{0:T(128)S(1)}, s32[32]{0:T(128)}, u32[]{:S(2)}) copy-start(s32[32]{0:T(128)} %scount_hbm.1) | copy-start | bytes 388
  6.5 0.8 %copy-start.10 = (s32[32]{0:T(128)S(1)}, s32[32]{0:T(128)}, u32[]{:S(2)}) copy-start(s32[32]{0:T(128)} %count_ref.1) | copy-start | bytes 388
  6.5 0.8 %copy-start.11 = (f32[32]{0:T(128)S(1)}, f32[32]{0:T(128)}, u32[]{:S(2)}) copy-start(f32[32]{0:T(128)} %scale_ref.1) | copy-start | bytes 388
  8.1 2.4 %copy-start.2 = (f32[8,8,343]{2,1,0:T(8,128)S(1)}, f32[8,8,343]{2,1,0:T(8,128)}, u32[]{:S(2)}) copy-start(f32[8,8,343]{2,1,0:T(8,128)} %param.21) | copy-start | bytes 263428
  8.1 2.4 %copy-start.6 = (f32[2,8,8]{2,1,0:T(8,128)S(1)}, f32[2,8,8]{2,1,0:T(8,128)}, u32[]{:S(2)}) copy-start(f32[2,8,8]{2,1,0:T(8,128)} %coupling_ref.1) | copy-start | bytes 1540
  10.5 8.5 %copy-start.1 = (f32[343,343]{1,0:T(8,128)S(1)}, f32[343,343]{1,0:T(8,128)}, u32[]{:S(2)}) copy-start(f32[343,343]{1,0:T(8,128)} %refs_1_.1) | copy-start | bytes 1411792
  13.1 14.0 %all-to-all-start = ((f32[32,4,128]{2,1,0:T(4,128)}), f32[32,4,128]{2,1,0:T(4,128)S(1)}, u32[]{:S(2)}, u32[]{:S(2)}) async-start(f32[32,4,128]{2,1,0:T(4,128)} %get-tuple-element.41), calls=%async_computation | async-start | bytes 131072 | tf_op jit(solution)/shard_map/all_to_all | solution.py:740
  23.4 6.5 %collective-permute-start.2 = (f32[10,1024]{1,0:T(8,128)S(1)}, f32[10,1024]{1,0:T(8,128)S(1)}, u32[]{:S(2)}, u32[]{:S(2)}) collective-permute-start(f32[10,1024]{1,0:T(8,128)S(1)} %get-tuple-element.47), channel_id=1, source_target_pairs={{0,1},{1,0},{2,3},{3,2},{4,5},{5,4},{6,7},{7,6},{8,9},{9,8},{10,11... | collective-permute-start | bytes 122888 | tf_op jit(solution)/shard_map/ppermute | solution.py:675
  23.7 6.2 %collective-permute-start.3 = (f32[10,1024]{1,0:T(8,128)S(1)}, f32[10,1024]{1,0:T(8,128)S(1)}, u32[]{:S(2)}, u32[]{:S(2)}) collective-permute-start(f32[10,1024]{1,0:T(8,128)S(1)} %get-tuple-element.48), channel_id=1, source_target_pairs={{1,2},{2,1},{3,4},{4,3},{5,6},{6,5},{7,8},{8,7},{9,10},{10,9},{11,... | collective-permute-start | bytes 122888 | tf_op jit(solution)/shard_map/ppermute | solution.py:675
  34.4 13.4 %all-to-all-start.1 = ((f32[32,4,128]{2,1,0:T(4,128)}), f32[32,4,128]{2,1,0:T(4,128)S(1)}, u32[]{:S(2)}, u32[]{:S(2)}) async-start(f32[32,4,128]{2,1,0:T(4,128)} %get-tuple-element.53), calls=%async_computation.1 | async-start | bytes 131072 | tf_op jit(solution)/shard_map/all_to_all | solution.py:763
  44.0 6.5 %collective-permute-start.4 = (f32[8,1024]{1,0:T(8,128)S(1)}, f32[8,1024]{1,0:T(8,128)S(1)}, u32[]{:S(2)}, u32[]{:S(2)}) collective-permute-start(f32[8,1024]{1,0:T(8,128)S(1)} %get-tuple-element.58), channel_id=1, source_target_pairs={{0,1},{1,0},{2,3},{3,2},{4,5},{5,4},{6,7},{7,6},{8,9},{9,8},{10,11... | collective-permute-start | bytes 98312 | tf_op jit(solution)/shard_map/ppermute | solution.py:675
  44.4 6.2 %collective-permute-start.5 = (f32[8,1024]{1,0:T(8,128)S(1)}, f32[8,1024]{1,0:T(8,128)S(1)}, u32[]{:S(2)}, u32[]{:S(2)}) collective-permute-start(f32[8,1024]{1,0:T(8,128)S(1)} %get-tuple-element.59), channel_id=1, source_target_pairs={{1,2},{2,1},{3,4},{4,3},{5,6},{6,5},{7,8},{8,7},{9,10},{10,9},{11,... | collective-permute-start | bytes 98312 | tf_op jit(solution)/shard_map/ppermute | solution.py:675

commit v13 on v12

--- a/solution.py
+++ b/solution.py
@@ -9,14 +9,15 @@
 
 LANES = 128
 ROWS = 8
-BITS = 8
+BITS = 7
 WIDE = 1 << BITS
 NARROW = 7
 CHAINS = 4
 SPAN = 14
-BAND = 8
+BAND = 14
 BESIDE = 4
 TOGETHER = 8
+MANY = 32
 F32 = jnp.float32
 BF16 = jnp.bfloat16
 HIGHEST = lax.Precision.HIGHEST
@@ -56,6 +57,7 @@
         self.message = self.rim_row + self.rim_pieces * ROWS
         assert self.elem + 3 <= self.width and self.entries % BESIDE == 0
         self.together = TOGETHER if self.slots % TOGETHER == 0 else 1
+        self.many = MANY if self.slots % MANY == 0 else 1
         assert self.vectors == ROWS and self.channels == ROWS and 2 * self.slots <= LANES
         assert self.nodes % WIDE == 0 and self.owned * self.pairs == LANES
 
@@ -236,8 +238,10 @@
             value = jnp.where(high == h, got[at : at + ROWS] + got[at + ROWS : at + 2 * ROWS], value)
         return value
 
+    size = z.together if listed else z.many
+
     def some_cells(g, _):
-        cells = [g * z.together + i for i in range(z.together)]
+        cells = [g * size + i for i in range(size)]
         if listed:
             cells = [table_ref[0, z.list + c] for c in cells]
             cells = [jnp.where(c >= z.slots, c - z.slots, c) for c in cells]
@@ -262,7 +266,7 @@
                     values[i * z.tiles + t] = value
             return tuple(values)
 
-        values = lax.fori_loop(0, passes, one_pass, (jnp.zeros(tile, F32),) * (z.together * z.tiles))
+        values = lax.fori_loop(0, passes, one_pass, (jnp.zeros(tile, F32),) * (size * z.tiles))
         for i, c in enumerate(cells):
             rows = pl.ds(pl.multiple_of(c * ROWS, ROWS), ROWS)
             for t in range(z.tiles):
@@ -400,7 +404,7 @@
         lanes_by_vector(z, y * q),
     ]
     energy = jnp.sum(q * q * (diag_ref[1:2, own] + shift_ref[:, :1]), axis=1, keepdims=True)
-    groups = 0, z.slots // z.together
+    groups = 0, z.slots // z.many
     split_window(z, q_ref, parts_ref)
     gather_middle(z, groups, False, table_ref, index_ref, q_ref, u_ref, parts_ref)
     gather_corners(z, corner_ref, q_ref, weight_ref, u_ref, uw_ref)
@@ -528,7 +532,7 @@
     scatter.start([(c, e_ref[c * ROWS : (c + 1) * ROWS, :]) for c in range(z.slots)])
 
     def some_cells(g, _):
-        cells = [g * z.together + i for i in range(z.together)]
+        cells = [g * z.many + i for i in range(z.many)]
 
         def value_of(i, t):
             rows = pl.ds(pl.multiple_of(cells[i] * ROWS, ROWS), ROWS)
@@ -537,7 +541,7 @@
         scatter.add(cells, value_of)
         return 0
 
-    lax.fori_loop(0, z.slots // z.together, some_cells, 0)
+    lax.fori_loop(0, z.slots // z.many, some_cells, 0)
     for h in range(scatter.groups):
         image_ref[:, h * WIDE : (h + 1) * WIDE] = scatter.result(h)
     even = table_ref[0, z.position] % 2 == 0

time: 52.7 us -> 51.1 us (0.970)
  Pallas kernels: 26.7 us -> 24 us
  waiting for transfers between devices: 0.02 us -> 1.31 us
    pallas_call x11, Pallas kernels: 26.7 us -> 24 us  [call(): pl.pallas_call(kernel, out_shape=[jax.ShapeDtypeStruct(s, d) if i in in_h...]
    all_to_all x1, waiting for transfers between devices: 0.01 us -> 0.98 us  [on_device(): totals = lax.all_to_all(sums, 'dom', 0, 0)]
  transfers between devices with their start and end apart: 8 -> 8, of which waited for: 0 -> 2; matrix products, arithmetic and copies ran while one was open for 0% -> 0% of each run, Pallas kernels for 32% -> 29%
where the time goes in v13:
time: 51.1 us; the launch traced here: 50.4 us
  Pallas kernels  24 us (47%)
  starting transfers between devices  23.5 us (46%)
  waiting for transfers between devices  1.31 us (3%)
  between operations  0.93 us (2%)
  local copies, waits for them, and re-layouts  0.63 us (1%)
    pallas_call x11, Pallas kernels, call(): pl.pallas_call(kernel, out_shape=[jax.ShapeDtypeStruct(s, d) if i in in_h...  24 us
    ppermute x6, starting transfers between devices, exchange(): return (lax.ppermute(a, 'dom', near), lax.ppermute(b, 'dom', far))  12 us
    all_to_all x1, starting transfers between devices, on_device(): coupled = lax.all_to_all(sums, 'dom', 0, 0)  5.92 us
    all_to_all x1, starting transfers between devices, on_device(): totals = lax.all_to_all(sums, 'dom', 0, 0)  5.61 us
  transfers between devices with their start and end apart: 8, of which 2 were waited for; matrix products, arithmetic and copies ran while one was open for 0% of the time, Pallas kernels for 29%

profile of v13, /device:TPU:1, one launch (start us, length us, event | category | flops | bytes accessed | tf_op | source)
XLA Modules:
  0.0 50.4 jit_solution(487014569437900028)
XLA Ops:
  0.7 1.2 %shard_map.143 = (f32[88,384]{1,0:T(8,128)S(1)}, f32[88,384]{1,0:T(8,128)S(1)}, f32[8,128]{1,0:T(8,128)S(1)}) custom-call(s32[1]{0:T(128)} %bitcast.pos_ref, s32[8]{0:T(128)} %cell_hbm.1, s32[8]{0:T(128)} %atom_hbm.1, s32[32]{0:T(128)} %scount_hbm.1, f32[8]{0:T(128)} %shift_hbm.1, f32[8,6656]{1,0:T(8,128)} %rhs_ref.5, f32[52,128]{1,0:T(8,128)} %bitcast.6, ...), custom_call_target="tpu_custom_call" | custom-call | tf_op jit(solution)/shard_map/pallas_call | solution.py:684
  1.9 0.1 collective-permute-start
  1.9 4.5 %collective-permute-start.1 = (f32[88,384]{1,0:T(8,128)S(1)}, f32[88,384]{1,0:T(8,128)S(1)}, u32[]{:S(2)}, u32[]{:S(2)}) collective-permute-start(f32[88,384]{1,0:T(8,128)S(1)} %get-tuple-element.35), channel_id=1, source_target_pairs={{1,2},{2,1},{3,4},{4,3},{5,6},{6,5},{7,8},{8,7},{9,10},{10,9},{11,... | collective-permute-start | bytes 405512 | tf_op jit(solution)/shard_map/ppermute | solution.py:679
  6.5 0.0 copy-start.8
  6.5 0.0 copy-start.9
  6.5 0.2 shard_map.141
  6.7 0.6 %copy-done.3 = s32[32,343]{1,0:T(8,128)S(1)} copy-done((s32[32,343]{1,0:T(8,128)S(1)}, s32[32,343]{1,0:T(8,128)}, u32[]{:S(2)}) %copy-start.3) | copy-done | bytes 43928
  7.3 0.8 %shard_map.140 = (s32[32,1,384]{2,1,0:T(1,128)S(1)}, s32[1,128]{1,0:T(1,128)S(1)}, s32[1,128]{1,0:T(1,128)S(1)}, f32[256,128]{1,0:T(8,128)S(1)}) custom-call(s32[1]{0:T(128)} %bitcast.pos_ref, s32[32]{0:T(128)S(1)} %copy-done.10, f32[32]{0:T(128)S(1)} %copy-done.11, s32[8]{0:T(128)S(1)} %copy-done.7, s32[8]{0:T(128)S(1)} %copy-done.8, s32[32]{0:T(128)S(1)} %copy-done.9, ...), custom_call_target="tpu_custom_call" | custom-call | tf_op jit(solution)/shard_map/pallas_call | solution.py:684
  8.2 2.3 %shard_map.142.u_in_ref = f32[256,384]{1,0:T(8,128)S(1)} custom-call(s32[1,128]{1,0:T(1,128)S(1)} %get-tuple-element.31.table_ref, f32[8,9472]{1,0:T(8,128)S(1)} %get-tuple-element.32.p_ref.p_in_ref, s32[32,1,384]{2,1,0:T(1,128)S(1)} %get-tuple-element.33.index_ref), custom_call_target="tpu_custom_call" | custom-call | tf_op jit(solution)/shard_map/pallas_call | solution.py:684
  10.6 2.5 %shard_map.144 = (f32[8,9472]{1,0:T(8,128)S(1)}, f32[32,4,128]{2,1,0:T(4,128)}, f32[256,384]{1,0:T(8,128)S(1)}, f32[64,384]{1,0:T(8,128)S(1)}, s32[1,128]{1,0:T(1,128)S(1)}) custom-call(s32[1,128]{1,0:T(1,128)S(1)} %get-tuple-element.31.table_ref, f32[8,9472]{1,0:T(8,128)S(1)} %get-tuple-element.32.p_ref.p_in_ref, f32[256,384]{1,0:T(8,128)S(1)} %shard_map.142.u_in_ref, ...), custom_call_target="tpu_custom_call" | custom-call | tf_op jit(solution)/shard_map/pallas_call | solution.py:684
  13.1 5.9 %all-to-all-start = ((f32[32,4,128]{2,1,0:T(4,128)}), f32[32,4,128]{2,1,0:T(4,128)S(1)}, u32[]{:S(2)}, u32[]{:S(2)}) async-start(f32[32,4,128]{2,1,0:T(4,128)} %get-tuple-element.41), calls=%async_computation | async-start | bytes 131072 | tf_op jit(solution)/shard_map/all_to_all | solution.py:744
  19.0 3.2 %shard_map.145 = (f32[8,7680]{1,0:T(8,128)S(1)}, f32[10,1024]{1,0:T(8,128)S(1)}, f32[10,1024]{1,0:T(8,128)S(1)}, bf16[384,384]{1,0:T(8,128)(2,1)S(1)}, bf16[384,384]{1,0:T(8,128)(2,1)S(1)}) custom-call(s32[1,128]{1,0:T(1,128)S(1)} %get-tuple-element.31.table_ref, s32[32,1,384]{2,1,0:T(1,128)S(1)} %get-tuple-element.33.index_ref, ...), custom_call_target="tpu_custom_call" | custom-call | tf_op jit(solution)/shard_map/pallas_call | solution.py:684
  22.3 0.3 collective-permute-start.2
  22.6 3.4 %collective-permute-start.3 = (f32[10,1024]{1,0:T(8,128)S(1)}, f32[10,1024]{1,0:T(8,128)S(1)}, u32[]{:S(2)}, u32[]{:S(2)}) collective-permute-start(f32[10,1024]{1,0:T(8,128)S(1)} %get-tuple-element.48), channel_id=1, source_target_pairs={{1,2},{2,1},{3,4},{4,3},{5,6},{6,5},{7,8},{8,7},{9,10},{10,9},{11,... | collective-permute-start | bytes 122888 | tf_op jit(solution)/shard_map/ppermute | solution.py:679
  26.0 0.3 all-to-all-done.sums_ref.coupling_ref
  26.3 2.7 %shard_map.146.image_ref = f32[8,7680]{1,0:T(8,128)S(1)} custom-call(s32[1,128]{1,0:T(1,128)S(1)} %get-tuple-element.31.table_ref, f32[32,4,128]{2,1,0:T(4,128)S(1)} %all-to-all-done.sums_ref.coupling_ref, f32[32,4,128]{2,1,0:T(4,128)S(1)} %all-to-all-done.sums_ref.coupling_ref, s32[32,1,384]{2,1,0:T(1,128)S(1)} %get-tuple-element.33.index_ref, ...), custom_call_target="tpu_custom_call" | custom-call | tf_op jit(solution)/shard_map/pallas_call | solution.py:684
  29.1 4.1 %shard_map.147 = (f32[8,7680]{1,0:T(8,128)S(1)}, f32[8,9472]{1,0:T(8,128)S(1)}, f32[32,4,128]{2,1,0:T(4,128)}, f32[256,384]{1,0:T(8,128)S(1)}) custom-call(s32[1,128]{1,0:T(1,128)S(1)} %get-tuple-element.31.table_ref, f32[8,7680]{1,0:T(8,128)S(1)} %shard_map.146.image_ref, f32[8,9472]{1,0:T(8,128)S(1)} %get-tuple-element.38.p_ref, ...), custom_call_target="tpu_custom_call" | custom-call | tf_op jit(solution)/shard_map/pallas_call | solution.py:684
  33.2 5.6 %all-to-all-start.1 = ((f32[32,4,128]{2,1,0:T(4,128)}), f32[32,4,128]{2,1,0:T(4,128)S(1)}, u32[]{:S(2)}, u32[]{:S(2)}) async-start(f32[32,4,128]{2,1,0:T(4,128)} %get-tuple-element.53), calls=%async_computation.1 | async-start | bytes 131072 | tf_op jit(solution)/shard_map/all_to_all | solution.py:767
  38.8 2.6 %shard_map.148 = (f32[8,7680]{1,0:T(8,128)S(1)}, f32[8,1024]{1,0:T(8,128)S(1)}, f32[8,1024]{1,0:T(8,128)S(1)}) custom-call(s32[1,128]{1,0:T(1,128)S(1)} %get-tuple-element.31.table_ref, s32[32,1,384]{2,1,0:T(1,128)S(1)} %get-tuple-element.33.index_ref, s32[1,128]{1,0:T(1,128)S(1)} %get-tuple-element.36.corner_ref, f32[256,384]{1,0:T(8,128)S(1)} %get-tuple-element.54.refs_0_), custom_call_target="tpu_custom_call" | custom-call | tf_op jit(solution)/shard_map/pallas_call | solution.py:684
  41.4 0.3 collective-permute-start.4
  41.7 3.4 %collective-permute-start.5 = (f32[8,1024]{1,0:T(8,128)S(1)}, f32[8,1024]{1,0:T(8,128)S(1)}, u32[]{:S(2)}, u32[]{:S(2)}) collective-permute-start(f32[8,1024]{1,0:T(8,128)S(1)} %get-tuple-element.59), channel_id=1, source_target_pairs={{1,2},{2,1},{3,4},{4,3},{5,6},{6,5},{7,8},{8,7},{9,10},{10,9},{11,... | collective-permute-start | bytes 98312 | tf_op jit(solution)/shard_map/ppermute | solution.py:679
  45.1 1.0 %all-to-all-done.1.sums_ref = f32[32,4,128]{2,1,0:T(4,128)S(1)} async-done(((f32[32,4,128]{2,1,0:T(4,128)}), f32[32,4,128]{2,1,0:T(4,128)S(1)}, u32[]{:S(2)}, u32[]{:S(2)}) %all-to-all-start.1) | async-done | bytes 65568 | tf_op jit(solution)/shard_map/all_to_all | solution.py:767
  46.1 2.8 %shard_map.149 = (f32[8,7680]{1,0:T(8,128)S(1)}, f32[1,128]{1,0:T(1,128)S(1)}) custom-call(s32[1,128]{1,0:T(1,128)S(1)} %get-tuple-element.31.table_ref, f32[32,4,128]{2,1,0:T(4,128)S(1)} %all-to-all-done.1.sums_ref, f32[32,4,128]{2,1,0:T(4,128)S(1)} %all-to-all-done.sums_ref.coupling_ref, s32[32,1,384]{2,1,0:T(1,128)S(1)} %get-tuple-element.33.index_ref, ...), custom_call_target="tpu_custom_call" | custom-call | tf_op jit(solution)/shard_map/pallas_call | solution.py:684
  48.8 1.6 %shard_map.150 = (f32[8,6656]{1,0:T(8,128)}, f32[8,6656]{1,0:T(8,128)}) custom-call(s32[1,128]{1,0:T(1,128)S(1)} %get-tuple-element.31.table_ref, f32[8,6656]{1,0:T(8,128)S(1)} %copy-done, f32[8,9472]{1,0:T(8,128)S(1)} %get-tuple-element.38.p_ref, f32[2,7680]{1,0:T(2,128)S(1)} %get-tuple-element.39.refs_2_.diag_in_ref.diag_ref, ...), custom_call_target="tpu_custom_call" | custom-call | tf_op jit(solution)/shard_map/pallas_call | solution.py:684
  (27 shorter events, 0.1 us)
Async XLA Ops:
  0.6 5.8 %copy-start = (f32[8,6656]{1,0:T(8,128)S(1)}, f32[8,6656]{1,0:T(8,128)}, u32[]{:S(2)}) copy-start(f32[8,6656]{1,0:T(8,128)} %rhs_ref.5) | copy-start | bytes 638980
  0.6 5.8 %copy-start.4 = (f32[6656]{0:T(1024)S(1)}, f32[6656]{0:T(1024)}, u32[]{:S(2)}) copy-start(f32[6656]{0:T(1024)} %param.15) | copy-start | bytes 79876
  0.7 5.8 %copy-start.5 = (f32[6656]{0:T(1024)S(1)}, f32[6656]{0:T(1024)}, u32[]{:S(2)}) copy-start(f32[6656]{0:T(1024)} %param.14) | copy-start | bytes 79876
  1.9 8.7 %collective-permute-start = (f32[88,384]{1,0:T(8,128)S(1)}, f32[88,384]{1,0:T(8,128)S(1)}, u32[]{:S(2)}, u32[]{:S(2)}) collective-permute-start(f32[88,384]{1,0:T(8,128)S(1)} %get-tuple-element.34), channel_id=1, source_target_pairs={{0,1},{1,0},{2,3},{3,2},{4,5},{5,4},{6,7},{7,6},{8,9},{9,8},{10,11... | collective-permute-start | bytes 405512 | tf_op jit(solution)/shard_map/ppermute | solution.py:679
  1.9 8.6 %collective-permute-start.1 = (f32[88,384]{1,0:T(8,128)S(1)}, f32[88,384]{1,0:T(8,128)S(1)}, u32[]{:S(2)}, u32[]{:S(2)}) collective-permute-start(f32[88,384]{1,0:T(8,128)S(1)} %get-tuple-element.35), channel_id=1, source_target_pairs={{1,2},{2,1},{3,4},{4,3},{5,6},{6,5},{7,8},{8,7},{9,10},{10,9},{11,... | collective-permute-start | bytes 405512 | tf_op jit(solution)/shard_map/ppermute | solution.py:679
  6.5 0.8 %copy-start.3 = (s32[32,343]{1,0:T(8,128)S(1)}, s32[32,343]{1,0:T(8,128)}, u32[]{:S(2)}) copy-start(s32[32,343]{1,0:T(8,128)} %conn_ref.3) | copy-start | bytes 131716
  6.5 0.8 %copy-start.7 = (s32[8]{0:T(128)S(1)}, s32[8]{0:T(128)}, u32[]{:S(2)}) copy-start(s32[8]{0:T(128)} %cell_hbm.1) | copy-start | bytes 100
  6.5 0.8 %copy-start.8 = (s32[8]{0:T(128)S(1)}, s32[8]{0:T(128)}, u32[]{:S(2)}) copy-start(s32[8]{0:T(128)} %atom_hbm.1) | copy-start | bytes 100
  6.5 0.8 %copy-start.9 = (s32[32]{0:T(128)S(1)}, s32[32]{0:T(128)}, u32[]{:S(2)}) copy-start(s32[32]{0:T(128)} %scount_hbm.1) | copy-start | bytes 388
  6.5 0.8 %copy-start.10 = (s32[32]{0:T(128)S(1)}, s32[32]{0:T(128)}, u32[]{:S(2)}) copy-start(s32[32]{0:T(128)} %count_ref.1) | copy-start | bytes 388
  6.5 0.8 %copy-start.11 = (f32[32]{0:T(128)S(1)}, f32[32]{0:T(128)}, u32[]{:S(2)}) copy-start(f32[32]{0:T(128)} %scale_ref.1) | copy-start | bytes 388
  8.1 2.4 %copy-start.2 = (f32[8,8,343]{2,1,0:T(8,128)S(1)}, f32[8,8,343]{2,1,0:T(8,128)}, u32[]{:S(2)}) copy-start(f32[8,8,343]{2,1,0:T(8,128)} %param.21) | copy-start | bytes 263428
  8.1 2.4 %copy-start.6 = (f32[2,8,8]{2,1,0:T(8,128)S(1)}, f32[2,8,8]{2,1,0:T(8,128)}, u32[]{:S(2)}) copy-start(f32[2,8,8]{2,1,0:T(8,128)} %coupling_ref.1) | copy-start | bytes 1540
  10.5 8.5 %copy-start.1 = (f32[343,343]{1,0:T(8,128)S(1)}, f32[343,343]{1,0:T(8,128)}, u32[]{:S(2)}) copy-start(f32[343,343]{1,0:T(8,128)} %refs_1_.1) | copy-start | bytes 1411792
  13.1 13.2 %all-to-all-start = ((f32[32,4,128]{2,1,0:T(4,128)}), f32[32,4,128]{2,1,0:T(4,128)S(1)}, u32[]{:S(2)}, u32[]{:S(2)}) async-start(f32[32,4,128]{2,1,0:T(4,128)} %get-tuple-element.41), calls=%async_computation | async-start | bytes 131072 | tf_op jit(solution)/shard_map/all_to_all | solution.py:744
  22.3 6.8 %collective-permute-start.2 = (f32[10,1024]{1,0:T(8,128)S(1)}, f32[10,1024]{1,0:T(8,128)S(1)}, u32[]{:S(2)}, u32[]{:S(2)}) collective-permute-start(f32[10,1024]{1,0:T(8,128)S(1)} %get-tuple-element.47), channel_id=1, source_target_pairs={{0,1},{1,0},{2,3},{3,2},{4,5},{5,4},{6,7},{7,6},{8,9},{9,8},{10,11... | collective-permute-start | bytes 122888 | tf_op jit(solution)/shard_map/ppermute | solution.py:679
  22.6 6.5 %collective-permute-start.3 = (f32[10,1024]{1,0:T(8,128)S(1)}, f32[10,1024]{1,0:T(8,128)S(1)}, u32[]{:S(2)}, u32[]{:S(2)}) collective-permute-start(f32[10,1024]{1,0:T(8,128)S(1)} %get-tuple-element.48), channel_id=1, source_target_pairs={{1,2},{2,1},{3,4},{4,3},{5,6},{6,5},{7,8},{8,7},{9,10},{10,9},{11,... | collective-permute-start | bytes 122888 | tf_op jit(solution)/shard_map/ppermute | solution.py:679
  33.2 12.9 %all-to-all-start.1 = ((f32[32,4,128]{2,1,0:T(4,128)}), f32[32,4,128]{2,1,0:T(4,128)S(1)}, u32[]{:S(2)}, u32[]{:S(2)}) async-start(f32[32,4,128]{2,1,0:T(4,128)} %get-tuple-element.53), calls=%async_computation.1 | async-start | bytes 131072 | tf_op jit(solution)/shard_map/all_to_all | solution.py:767
  41.4 7.5 %collective-permute-start.4 = (f32[8,1024]{1,0:T(8,128)S(1)}, f32[8,1024]{1,0:T(8,128)S(1)}, u32[]{:S(2)}, u32[]{:S(2)}) collective-permute-start(f32[8,1024]{1,0:T(8,128)S(1)} %get-tuple-element.58), channel_id=1, source_target_pairs={{0,1},{1,0},{2,3},{3,2},{4,5},{5,4},{6,7},{7,6},{8,9},{9,8},{10,11... | collective-permute-start | bytes 98312 | tf_op jit(solution)/shard_map/ppermute | solution.py:679
  41.7 7.1 %collective-permute-start.5 = (f32[8,1024]{1,0:T(8,128)S(1)}, f32[8,1024]{1,0:T(8,128)S(1)}, u32[]{:S(2)}, u32[]{:S(2)}) collective-permute-start(f32[8,1024]{1,0:T(8,128)S(1)} %get-tuple-element.59), channel_id=1, source_target_pairs={{1,2},{2,1},{3,4},{4,3},{5,6},{6,5},{7,8},{8,7},{9,10},{10,9},{11,... | collective-permute-start | bytes 98312 | tf_op jit(solution)/shard_map/ppermute | solution.py:679

commit v14 on v13

--- a/solution.py
+++ b/solution.py
@@ -44,6 +44,7 @@
         self.width = round_up(self.elem, LANES)
         self.tiles = self.width // LANES
         self.pairs = self.channels * self.vectors
+        self.pieces = 4 if self.nodes % (4 * LANES) == 0 and self.nodes // 4 >= self.rim else 1
         self.low, self.high, self.list = 0, self.slots, 2 * self.slots
         self.cell = 3 * self.slots
         self.owner, self.local = self.cell + self.entries, self.cell + 2 * self.entries
@@ -147,7 +148,8 @@
     tile = jnp.zeros((ROWS, LANES), F32)
     for v in range(z.vectors):
         tile = jnp.where(row == v, shift_ref[v], tile)
-    shift_tile_ref[...] = tile
+    shift_tile_ref[:ROWS, :] = tile
+    shift_tile_ref[ROWS:, :] = jnp.zeros((ROWS, LANES), F32) + jnp.where(pos_ref[0] % 2 == 0, 1.0, 0.0)
     head, tail = (
         jnp.concatenate(
             [
@@ -224,9 +226,9 @@
     lows = [(sub + n * 2 * ROWS).astype(jnp.int16) for n in range(WIDE // (2 * ROWS))]
     one, none = jnp.ones(pair, BF16), jnp.zeros(pair, BF16)
 
-    def product_tile(c, k):
+    def product_tile(c, k, t):
         start = jnp.minimum((table_ref[0, z.low + c] >> BITS) + k * BAND, z.window // WIDE)
-        index = index_ref[c, :, (z.tiles - 1) * LANES : z.tiles * LANES]
+        index = index_ref[c, :, t * LANES : (t + 1) * LANES]
         low = (jnp.broadcast_to(index, pair) & (WIDE - 1)).astype(jnp.int16)
         hot = jnp.concatenate([jnp.where(low == n, one, none) for n in lows], axis=0)
         rows = pl.ds(pl.multiple_of(start * 2 * ROWS, 2 * ROWS), BAND * 2 * ROWS)
@@ -254,8 +256,8 @@
             for i, c in enumerate(cells):
                 start = jnp.minimum(starts[i] + k * SPAN, total)
                 for t in range(z.tiles):
-                    if parts_ref is not None and t == z.tiles - 1:
-                        values[i * z.tiles + t] += product_tile(c, k)
+                    if parts_ref is not None and t >= z.tiles - 2:
+                        values[i * z.tiles + t] += product_tile(c, k, t)
                         continue
                     index = jnp.broadcast_to(index_ref[c, :, t * LANES : (t + 1) * LANES], tile)
                     low, high = index & (LANES - 1), (index >> 7) - start
@@ -392,7 +394,7 @@
     diag_ref[:, own] = diag_in_ref[:, own]
     diag_ref[:, : z.rim] = left[ROWS : ROWS + 2, : z.rim]
     diag_ref[:, z.rim + z.nodes :] = right[ROWS : ROWS + 2, z.rim :]
-    y_ref[...] = image_ref[...] + (diag_ref[1:2, :] + shift_ref[:, :1]) * p_ref[:, : z.window]
+    y_ref[...] = image_ref[...] + (diag_ref[1:2, :] + shift_ref[:ROWS, :1]) * p_ref[:, : z.window]
     y_ref[:, : 2 * z.rim] += left[:ROWS]
     y_ref[:, z.window - 2 * z.rim :] += right[:ROWS]
     q_ref[:, : z.window] = y_ref[...] * diag_ref[0:1, :]
@@ -403,7 +405,7 @@
         lanes_by_vector(z, y * p_ref[:, own]),
         lanes_by_vector(z, y * q),
     ]
-    energy = jnp.sum(q * q * (diag_ref[1:2, own] + shift_ref[:, :1]), axis=1, keepdims=True)
+    energy = jnp.sum(q * q * (diag_ref[1:2, own] + shift_ref[:ROWS, :1]), axis=1, keepdims=True)
     groups = 0, z.slots // z.many
     split_window(z, q_ref, parts_ref)
     gather_middle(z, groups, False, table_ref, index_ref, q_ref, u_ref, parts_ref)
@@ -561,11 +563,22 @@
     else:
         image_ref, support_ref, nodes_ref, acc_ref = refs
     position = table_ref[0, z.position]
-    wanted = (
-        pltpu.roll(sums_ref[:, 0, :], z.devices - 1, 0) + sums_ref[:, 1, :] + pltpu.roll(sums_ref[:, 2, :], 1, 0)
-    )
+    parts = [sums_ref[:, k, :] for k in range(3)]
     coupling = coupling_ref[:, 3, :]
-    shape = (z.devices, LANES)
+    wanted = pltpu.roll(parts[0], z.devices - 1, 0) + parts[1] + pltpu.roll(parts[2], 1, 0)
+    block = iota((z.devices, LANES), 0)
+    if not last:
+        near = iota((ROWS, LANES), 0)
+
+        def nearby(values):
+            rows = [jnp.sum(jnp.where(block == position - 2 + k, values, 0.0), axis=0, keepdims=True) for k in range(5)]
+            return functools.reduce(
+                jnp.add, [jnp.where(near == k, jnp.broadcast_to(row, near.shape), 0.0) for k, row in enumerate(rows)]
+            )
+
+        wanted, coupling = nearby(wanted), nearby(coupling)
+        block = near + (position - 2)
+    shape = wanted.shape
     lane = iota(shape, 1)
     term = jnp.zeros(shape, F32)
     for j in range(z.channels):
@@ -583,7 +596,6 @@
         dots_ref[...] = jnp.sum(sums_ref[:, 3, :], axis=0, keepdims=True) + jnp.where(
             line // ROWS == 3, energy[0:1], 0.0
         )
-    block = iota(shape, 0)
     small_lane, small_row = iota((ROWS, LANES), 1), iota((ROWS, LANES), 0)
 
     def values(facts, projectors):
@@ -638,10 +650,9 @@
 
 
 def last_kernel(
-    z, table_ref, rhs_ref, p_ref, diag_ref, shift_ref, y_ref, q_ref, image_ref, dots_ref, halo_a_ref, halo_b_ref,
-    solution_ref, residual_ref,
+    z, rhs_ref, p_ref, diag_ref, shift_ref, y_ref, q_ref, image_ref, dots_ref, halo_a_ref, halo_b_ref,
+    solution_hbm, residual_hbm, solution_ref, residual_ref, sems,
 ):
-    own = slice(z.rim, z.rim + z.nodes)
     lane, row = iota((ROWS, LANES), 1), iota((ROWS, LANES), 0)
     line = jnp.broadcast_to(dots_ref[...], (ROWS, LANES))
 
@@ -654,14 +665,28 @@
     beta = fresh / gamma
     more = 1.0 + beta
     step = fresh / (more * more * py - 2.0 * more * alpha * qy + alpha * alpha * qq)
-    p, q, y = p_ref[:, own], q_ref[:, own], y_ref[:, own]
-    second = image_ref[:, own] + (diag_ref[1:2, own] + shift_ref[:, :1]) * q
-    search = (p - alpha * q) + beta * p
-    solution_ref[...] = alpha * p + step * search
-    residual_ref[...] = (rhs_ref[...] - alpha * y) - step * (more * y - alpha * second)
-    left, right = sides(table_ref[0, z.position], halo_a_ref[...], halo_b_ref[...])
-    residual_ref[:, : z.rim] += step * alpha * left[:, z.rim :]
-    residual_ref[:, z.nodes - z.rim :] += step * alpha * right[:, : z.rim]
+    even = shift_ref[ROWS:, :1] > 0.5
+    a, b = halo_a_ref[...], halo_b_ref[...]
+    left, right = jnp.where(even, b, a)[:, z.rim :], jnp.where(even, a, b)[:, : z.rim]
+    size = z.nodes // z.pieces
+    copies = []
+    for k in range(z.pieces):
+        at, own = slice(k * size, (k + 1) * size), slice(z.rim + k * size, z.rim + (k + 1) * size)
+        p, q, y = p_ref[:, own], q_ref[:, own], y_ref[:, own]
+        second = image_ref[:, own] + (diag_ref[1:2, own] + shift_ref[:ROWS, :1]) * q
+        search = (p - alpha * q) + beta * p
+        solution_ref[:, at] = alpha * p + step * search
+        residual_ref[:, at] = (rhs_ref[:, at] - alpha * y) - step * (more * y - alpha * second)
+        if k == 0:
+            residual_ref[:, : z.rim] += step * alpha * left
+        if k == z.pieces - 1:
+            residual_ref[:, z.nodes - z.rim :] += step * alpha * right
+        for n, (source, to) in enumerate(((solution_ref, solution_hbm), (residual_ref, residual_hbm))):
+            part = pl.ds(k * size, size)
+            copies.append(pltpu.make_async_copy(source.at[:, part], to.at[:, part], sems.at[2 * k + n]))
+            copies[-1].start()
+    for copy in copies:
+        copy.wait()
 
 
 def on_device(
@@ -709,7 +734,7 @@
     first_message = (z.message, z.width)
     send_a, send_b, shift_tile = call(
             functools.partial(start_kernel, z),
-            [(first_message, F32), (first_message, F32), (tile, F32)],
+            [(first_message, F32), (first_message, F32), ((2 * ROWS, LANES), F32)],
             [((2, z.vectors, z.rim), F32), ((2, z.rim // LANES, LANES), F32), (conn.shape, jnp.int32),
              (flat_projector.shape, F32), pltpu.SMEM(support_cell.shape, jnp.int32),
              pltpu.SMEM(support_atom.shape, jnp.int32), pltpu.SMEM(support_count.shape, jnp.int32),
@@ -777,14 +802,16 @@
         (table,),
         totals, coupled, index, beside, pj, *ext, image,
     )
+    values = rhs, p, diag, shift_tile, y, q, image, dots, *halo
     return tuple(
-        call(
+        pl.pallas_call(
             functools.partial(last_kernel, z),
-            [(own, F32), (own, F32)],
-            [],
-            (table,),
-            rhs, p, diag, shift_tile, y, q, image, dots, *halo, in_hbm=(0, 1),
-        )
+            out_shape=[jax.ShapeDtypeStruct(own, F32)] * 2,
+            in_specs=[VMEM] * len(values),
+            out_specs=[pl.BlockSpec(memory_space=pl.ANY)] * 2,
+            scratch_shapes=[pltpu.VMEM(own, F32)] * 2 + [pltpu.SemaphoreType.DMA((2 * z.pieces,))],
+            compiler_params=pltpu.CompilerParams(vmem_limit_bytes=16 * 1024 * 1024),
+        )(*[pltpu.with_memory_space_constraint(x, pltpu.VMEM) for x in values])
     )
 
 

time: 51.1 us -> 50.6 us (level)
  Pallas kernels: 24 us -> 23.3 us
    pallas_call x11 -> x10, Pallas kernels: 24 us -> 22.2 us  [call(): pl.pallas_call(kernel, out_shape=[jax.ShapeDtypeStruct(s, d) if i in in_h...]
    pallas_call x0 -> x1, Pallas kernels: none -> 1.05 us  [on_device(): pl.pallas_call(functools.partial(last_kernel, z), out_shape=[jax.ShapeDty...]
where the time goes in v14:
time: 50.6 us; the launch traced here: 50.1 us
  starting transfers between devices  24 us (47%)
  Pallas kernels  23.3 us (46%)
  waiting for transfers between devices  1.31 us (3%)
  between operations  0.93 us (2%)
  local copies, waits for them, and re-layouts  0.64 us (1%)
    pallas_call x10, Pallas kernels, call(): pl.pallas_call(kernel, out_shape=[jax.ShapeDtypeStruct(s, d) if i in in_h...  22.2 us
    ppermute x6, starting transfers between devices, exchange(): return (lax.ppermute(a, 'dom', near), lax.ppermute(b, 'dom', far))  12 us
    all_to_all x1, starting transfers between devices, on_device(): coupled = lax.all_to_all(sums, 'dom', 0, 0)  6.26 us
    all_to_all x1, starting transfers between devices, on_device(): totals = lax.all_to_all(sums, 'dom', 0, 0)  5.7 us
    pallas_call x1, Pallas kernels, on_device(): pl.pallas_call(functools.partial(last_kernel, z), out_shape=[jax.ShapeDty...  1.05 us
  transfers between devices with their start and end apart: 8, of which 2 were waited for; matrix products, arithmetic and copies ran while one was open for 0% of the time, Pallas kernels for 29%

profile of v14, /device:TPU:1, one launch (start us, length us, event | category | flops | bytes accessed | tf_op | source)
XLA Modules:
  0.0 50.1 jit_solution(17625212695572540592)
XLA Ops:
  0.7 1.2 %shard_map.143 = (f32[88,384]{1,0:T(8,128)S(1)}, f32[88,384]{1,0:T(8,128)S(1)}, f32[16,128]{1,0:T(8,128)S(1)}) custom-call(s32[1]{0:T(128)} %bitcast.pos_ref, s32[8]{0:T(128)} %cell_hbm.1, s32[8]{0:T(128)} %atom_hbm.1, s32[32]{0:T(128)} %scount_hbm.1, f32[8]{0:T(128)} %shift_hbm.1, f32[8,6656]{1,0:T(8,128)} %rhs_ref.5, f32[52,128]{1,0:T(8,128)} %bitcast.6, ...), custom_call_target="tpu_custom_call" | custom-call | tf_op jit(solution)/shard_map/pallas_call | solution.py:709
  1.9 0.1 collective-permute-start
  1.9 4.5 %collective-permute-start.1 = (f32[88,384]{1,0:T(8,128)S(1)}, f32[88,384]{1,0:T(8,128)S(1)}, u32[]{:S(2)}, u32[]{:S(2)}) collective-permute-start(f32[88,384]{1,0:T(8,128)S(1)} %get-tuple-element.35), channel_id=1, source_target_pairs={{1,2},{2,1},{3,4},{4,3},{5,6},{6,5},{7,8},{8,7},{9,10},{10,9},{11,... | collective-permute-start | bytes 405512 | tf_op jit(solution)/shard_map/ppermute | solution.py:704
  6.5 0.0 copy-start.3
  6.5 0.0 copy-start.9
  6.5 0.2 shard_map.141
  6.7 0.6 %copy-done.3 = s32[32,343]{1,0:T(8,128)S(1)} copy-done((s32[32,343]{1,0:T(8,128)S(1)}, s32[32,343]{1,0:T(8,128)}, u32[]{:S(2)}) %copy-start.3) | copy-done | bytes 43928
  7.3 0.8 %shard_map.140 = (s32[32,1,384]{2,1,0:T(1,128)S(1)}, s32[1,128]{1,0:T(1,128)S(1)}, s32[1,128]{1,0:T(1,128)S(1)}, f32[256,128]{1,0:T(8,128)S(1)}) custom-call(s32[1]{0:T(128)} %bitcast.pos_ref, s32[32]{0:T(128)S(1)} %copy-done.10, f32[32]{0:T(128)S(1)} %copy-done.11, s32[8]{0:T(128)S(1)} %copy-done.7, s32[8]{0:T(128)S(1)} %copy-done.8, s32[32]{0:T(128)S(1)} %copy-done.9, ...), custom_call_target="tpu_custom_call" | custom-call | tf_op jit(solution)/shard_map/pallas_call | solution.py:709
  8.2 2.3 %shard_map.142.u_in_ref = f32[256,384]{1,0:T(8,128)S(1)} custom-call(s32[1,128]{1,0:T(1,128)S(1)} %get-tuple-element.31.table_ref, f32[8,9472]{1,0:T(8,128)S(1)} %get-tuple-element.32.p_ref.p_in_ref, s32[32,1,384]{2,1,0:T(1,128)S(1)} %get-tuple-element.33.index_ref), custom_call_target="tpu_custom_call" | custom-call | tf_op jit(solution)/shard_map/pallas_call | solution.py:709
  10.6 2.5 %shard_map.144 = (f32[8,9472]{1,0:T(8,128)S(1)}, f32[32,4,128]{2,1,0:T(4,128)}, f32[256,384]{1,0:T(8,128)S(1)}, f32[64,384]{1,0:T(8,128)S(1)}, s32[1,128]{1,0:T(1,128)S(1)}) custom-call(s32[1,128]{1,0:T(1,128)S(1)} %get-tuple-element.31.table_ref, f32[8,9472]{1,0:T(8,128)S(1)} %get-tuple-element.32.p_ref.p_in_ref, f32[256,384]{1,0:T(8,128)S(1)} %shard_map.142.u_in_ref, ...), custom_call_target="tpu_custom_call" | custom-call | tf_op jit(solution)/shard_map/pallas_call | solution.py:709
  13.1 6.3 %all-to-all-start = ((f32[32,4,128]{2,1,0:T(4,128)}), f32[32,4,128]{2,1,0:T(4,128)S(1)}, u32[]{:S(2)}, u32[]{:S(2)}) async-start(f32[32,4,128]{2,1,0:T(4,128)} %get-tuple-element.41), calls=%async_computation | async-start | bytes 131072 | tf_op jit(solution)/shard_map/all_to_all | solution.py:769
  19.4 3.2 %shard_map.145 = (f32[8,7680]{1,0:T(8,128)S(1)}, f32[10,1024]{1,0:T(8,128)S(1)}, f32[10,1024]{1,0:T(8,128)S(1)}, bf16[384,384]{1,0:T(8,128)(2,1)S(1)}, bf16[384,384]{1,0:T(8,128)(2,1)S(1)}) custom-call(s32[1,128]{1,0:T(1,128)S(1)} %get-tuple-element.31.table_ref, s32[32,1,384]{2,1,0:T(1,128)S(1)} %get-tuple-element.33.index_ref, ...), custom_call_target="tpu_custom_call" | custom-call | tf_op jit(solution)/shard_map/pallas_call | solution.py:709
  22.6 0.3 collective-permute-start.2
  22.9 3.4 %collective-permute-start.3 = (f32[10,1024]{1,0:T(8,128)S(1)}, f32[10,1024]{1,0:T(8,128)S(1)}, u32[]{:S(2)}, u32[]{:S(2)}) collective-permute-start(f32[10,1024]{1,0:T(8,128)S(1)} %get-tuple-element.48), channel_id=1, source_target_pairs={{1,2},{2,1},{3,4},{4,3},{5,6},{6,5},{7,8},{8,7},{9,10},{10,9},{11,... | collective-permute-start | bytes 122888 | tf_op jit(solution)/shard_map/ppermute | solution.py:704
  26.3 0.3 all-to-all-done.sums_ref.coupling_ref
  26.6 2.6 %shard_map.146.image_ref = f32[8,7680]{1,0:T(8,128)S(1)} custom-call(s32[1,128]{1,0:T(1,128)S(1)} %get-tuple-element.31.table_ref, f32[32,4,128]{2,1,0:T(4,128)S(1)} %all-to-all-done.sums_ref.coupling_ref, f32[32,4,128]{2,1,0:T(4,128)S(1)} %all-to-all-done.sums_ref.coupling_ref, s32[32,1,384]{2,1,0:T(1,128)S(1)} %get-tuple-element.33.index_ref, ...), custom_call_target="tpu_custom_call" | custom-call | tf_op jit(solution)/shard_map/pallas_call | solution.py:709
  29.3 4.0 %shard_map.147 = (f32[8,7680]{1,0:T(8,128)S(1)}, f32[8,9472]{1,0:T(8,128)S(1)}, f32[32,4,128]{2,1,0:T(4,128)}, f32[256,384]{1,0:T(8,128)S(1)}) custom-call(s32[1,128]{1,0:T(1,128)S(1)} %get-tuple-element.31.table_ref, f32[8,7680]{1,0:T(8,128)S(1)} %shard_map.146.image_ref, f32[8,9472]{1,0:T(8,128)S(1)} %get-tuple-element.38.p_ref, ...), custom_call_target="tpu_custom_call" | custom-call | tf_op jit(solution)/shard_map/pallas_call | solution.py:709
  33.3 5.7 %all-to-all-start.1 = ((f32[32,4,128]{2,1,0:T(4,128)}), f32[32,4,128]{2,1,0:T(4,128)S(1)}, u32[]{:S(2)}, u32[]{:S(2)}) async-start(f32[32,4,128]{2,1,0:T(4,128)} %get-tuple-element.53), calls=%async_computation.1 | async-start | bytes 131072 | tf_op jit(solution)/shard_map/all_to_all | solution.py:792
  39.0 2.6 %shard_map.148 = (f32[8,7680]{1,0:T(8,128)S(1)}, f32[8,1024]{1,0:T(8,128)S(1)}, f32[8,1024]{1,0:T(8,128)S(1)}) custom-call(s32[1,128]{1,0:T(1,128)S(1)} %get-tuple-element.31.table_ref, s32[32,1,384]{2,1,0:T(1,128)S(1)} %get-tuple-element.33.index_ref, s32[1,128]{1,0:T(1,128)S(1)} %get-tuple-element.36.corner_ref, f32[256,384]{1,0:T(8,128)S(1)} %get-tuple-element.54.refs_0_), custom_call_target="tpu_custom_call" | custom-call | tf_op jit(solution)/shard_map/pallas_call | solution.py:709
  41.6 0.3 collective-permute-start.4
  41.9 3.4 %collective-permute-start.5 = (f32[8,1024]{1,0:T(8,128)S(1)}, f32[8,1024]{1,0:T(8,128)S(1)}, u32[]{:S(2)}, u32[]{:S(2)}) collective-permute-start(f32[8,1024]{1,0:T(8,128)S(1)} %get-tuple-element.59), channel_id=1, source_target_pairs={{1,2},{2,1},{3,4},{4,3},{5,6},{6,5},{7,8},{8,7},{9,10},{10,9},{11,... | collective-permute-start | bytes 98312 | tf_op jit(solution)/shard_map/ppermute | solution.py:704
  45.3 1.0 %all-to-all-done.1.sums_ref = f32[32,4,128]{2,1,0:T(4,128)S(1)} async-done(((f32[32,4,128]{2,1,0:T(4,128)}), f32[32,4,128]{2,1,0:T(4,128)S(1)}, u32[]{:S(2)}, u32[]{:S(2)}) %all-to-all-start.1) | async-done | bytes 65568 | tf_op jit(solution)/shard_map/all_to_all | solution.py:792
  46.3 2.8 %shard_map.149 = (f32[8,7680]{1,0:T(8,128)S(1)}, f32[1,128]{1,0:T(1,128)S(1)}) custom-call(s32[1,128]{1,0:T(1,128)S(1)} %get-tuple-element.31.table_ref, f32[32,4,128]{2,1,0:T(4,128)S(1)} %all-to-all-done.1.sums_ref, f32[32,4,128]{2,1,0:T(4,128)S(1)} %all-to-all-done.sums_ref.coupling_ref, s32[32,1,384]{2,1,0:T(1,128)S(1)} %get-tuple-element.33.index_ref, ...), custom_call_target="tpu_custom_call" | custom-call | tf_op jit(solution)/shard_map/pallas_call | solution.py:709
  49.0 1.1 %shard_map.150 = (f32[8,6656]{1,0:T(8,128)}, f32[8,6656]{1,0:T(8,128)}) custom-call(f32[8,6656]{1,0:T(8,128)S(1)} %copy-done, f32[8,9472]{1,0:T(8,128)S(1)} %get-tuple-element.38.p_ref, f32[2,7680]{1,0:T(2,128)S(1)} %get-tuple-element.39.refs_2_.diag_in_ref.diag_ref, f32[16,128]{1,0:T(8,128)S(1)} %get-tuple-element.40.shift_ref, ...), custom_call_target="tpu_custom_call" | custom-call | tf_op jit(solution)/shard_map/pallas_call | solution.py:807
  (27 shorter events, 0.1 us)
Async XLA Ops:
  0.6 5.8 %copy-start = (f32[8,6656]{1,0:T(8,128)S(1)}, f32[8,6656]{1,0:T(8,128)}, u32[]{:S(2)}) copy-start(f32[8,6656]{1,0:T(8,128)} %rhs_ref.5) | copy-start | bytes 638980
  0.6 5.8 %copy-start.4 = (f32[6656]{0:T(1024)S(1)}, f32[6656]{0:T(1024)}, u32[]{:S(2)}) copy-start(f32[6656]{0:T(1024)} %param.15) | copy-start | bytes 79876
  0.7 5.8 %copy-start.5 = (f32[6656]{0:T(1024)S(1)}, f32[6656]{0:T(1024)}, u32[]{:S(2)}) copy-start(f32[6656]{0:T(1024)} %param.14) | copy-start | bytes 79876
  1.9 8.7 %collective-permute-start = (f32[88,384]{1,0:T(8,128)S(1)}, f32[88,384]{1,0:T(8,128)S(1)}, u32[]{:S(2)}, u32[]{:S(2)}) collective-permute-start(f32[88,384]{1,0:T(8,128)S(1)} %get-tuple-element.34), channel_id=1, source_target_pairs={{0,1},{1,0},{2,3},{3,2},{4,5},{5,4},{6,7},{7,6},{8,9},{9,8},{10,11... | collective-permute-start | bytes 405512 | tf_op jit(solution)/shard_map/ppermute | solution.py:704
  1.9 8.6 %collective-permute-start.1 = (f32[88,384]{1,0:T(8,128)S(1)}, f32[88,384]{1,0:T(8,128)S(1)}, u32[]{:S(2)}, u32[]{:S(2)}) collective-permute-start(f32[88,384]{1,0:T(8,128)S(1)} %get-tuple-element.35), channel_id=1, source_target_pairs={{1,2},{2,1},{3,4},{4,3},{5,6},{6,5},{7,8},{8,7},{9,10},{10,9},{11,... | collective-permute-start | bytes 405512 | tf_op jit(solution)/shard_map/ppermute | solution.py:704
  6.5 0.8 %copy-start.3 = (s32[32,343]{1,0:T(8,128)S(1)}, s32[32,343]{1,0:T(8,128)}, u32[]{:S(2)}) copy-start(s32[32,343]{1,0:T(8,128)} %conn_ref.3) | copy-start | bytes 131716
  6.5 0.8 %copy-start.7 = (s32[8]{0:T(128)S(1)}, s32[8]{0:T(128)}, u32[]{:S(2)}) copy-start(s32[8]{0:T(128)} %cell_hbm.1) | copy-start | bytes 100
  6.5 0.8 %copy-start.8 = (s32[8]{0:T(128)S(1)}, s32[8]{0:T(128)}, u32[]{:S(2)}) copy-start(s32[8]{0:T(128)} %atom_hbm.1) | copy-start | bytes 100
  6.5 0.8 %copy-start.9 = (s32[32]{0:T(128)S(1)}, s32[32]{0:T(128)}, u32[]{:S(2)}) copy-start(s32[32]{0:T(128)} %scount_hbm.1) | copy-start | bytes 388
  6.5 0.8 %copy-start.10 = (s32[32]{0:T(128)S(1)}, s32[32]{0:T(128)}, u32[]{:S(2)}) copy-start(s32[32]{0:T(128)} %count_ref.1) | copy-start | bytes 388
  6.5 0.8 %copy-start.11 = (f32[32]{0:T(128)S(1)}, f32[32]{0:T(128)}, u32[]{:S(2)}) copy-start(f32[32]{0:T(128)} %scale_ref.1) | copy-start | bytes 388
  8.1 2.4 %copy-start.2 = (f32[8,8,343]{2,1,0:T(8,128)S(1)}, f32[8,8,343]{2,1,0:T(8,128)}, u32[]{:S(2)}) copy-start(f32[8,8,343]{2,1,0:T(8,128)} %param.21) | copy-start | bytes 263428
  8.1 2.4 %copy-start.6 = (f32[2,8,8]{2,1,0:T(8,128)S(1)}, f32[2,8,8]{2,1,0:T(8,128)}, u32[]{:S(2)}) copy-start(f32[2,8,8]{2,1,0:T(8,128)} %coupling_ref.1) | copy-start | bytes 1540
  10.5 8.8 %copy-start.1 = (f32[343,343]{1,0:T(8,128)S(1)}, f32[343,343]{1,0:T(8,128)}, u32[]{:S(2)}) copy-start(f32[343,343]{1,0:T(8,128)} %refs_1_.1) | copy-start | bytes 1411792
  13.1 13.5 %all-to-all-start = ((f32[32,4,128]{2,1,0:T(4,128)}), f32[32,4,128]{2,1,0:T(4,128)S(1)}, u32[]{:S(2)}, u32[]{:S(2)}) async-start(f32[32,4,128]{2,1,0:T(4,128)} %get-tuple-element.41), calls=%async_computation | async-start | bytes 131072 | tf_op jit(solution)/shard_map/all_to_all | solution.py:769
  22.6 6.7 %collective-permute-start.2 = (f32[10,1024]{1,0:T(8,128)S(1)}, f32[10,1024]{1,0:T(8,128)S(1)}, u32[]{:S(2)}, u32[]{:S(2)}) collective-permute-start(f32[10,1024]{1,0:T(8,128)S(1)} %get-tuple-element.47), channel_id=1, source_target_pairs={{0,1},{1,0},{2,3},{3,2},{4,5},{5,4},{6,7},{7,6},{8,9},{9,8},{10,11... | collective-permute-start | bytes 122888 | tf_op jit(solution)/shard_map/ppermute | solution.py:704
  22.9 6.4 %collective-permute-start.3 = (f32[10,1024]{1,0:T(8,128)S(1)}, f32[10,1024]{1,0:T(8,128)S(1)}, u32[]{:S(2)}, u32[]{:S(2)}) collective-permute-start(f32[10,1024]{1,0:T(8,128)S(1)} %get-tuple-element.48), channel_id=1, source_target_pairs={{1,2},{2,1},{3,4},{4,3},{5,6},{6,5},{7,8},{8,7},{9,10},{10,9},{11,... | collective-permute-start | bytes 122888 | tf_op jit(solution)/shard_map/ppermute | solution.py:704
  33.3 13.0 %all-to-all-start.1 = ((f32[32,4,128]{2,1,0:T(4,128)}), f32[32,4,128]{2,1,0:T(4,128)S(1)}, u32[]{:S(2)}, u32[]{:S(2)}) async-start(f32[32,4,128]{2,1,0:T(4,128)} %get-tuple-element.53), calls=%async_computation.1 | async-start | bytes 131072 | tf_op jit(solution)/shard_map/all_to_all | solution.py:792
  41.6 7.5 %collective-permute-start.4 = (f32[8,1024]{1,0:T(8,128)S(1)}, f32[8,1024]{1,0:T(8,128)S(1)}, u32[]{:S(2)}, u32[]{:S(2)}) collective-permute-start(f32[8,1024]{1,0:T(8,128)S(1)} %get-tuple-element.58), channel_id=1, source_target_pairs={{0,1},{1,0},{2,3},{3,2},{4,5},{5,4},{6,7},{7,6},{8,9},{9,8},{10,11... | collective-permute-start | bytes 98312 | tf_op jit(solution)/shard_map/ppermute | solution.py:704
  41.9 7.1 %collective-permute-start.5 = (f32[8,1024]{1,0:T(8,128)S(1)}, f32[8,1024]{1,0:T(8,128)S(1)}, u32[]{:S(2)}, u32[]{:S(2)}) collective-permute-start(f32[8,1024]{1,0:T(8,128)S(1)} %get-tuple-element.59), channel_id=1, source_target_pairs={{1,2},{2,1},{3,4},{4,3},{5,6},{6,5},{7,8},{8,7},{9,10},{10,9},{11,... | collective-permute-start | bytes 98312 | tf_op jit(solution)/shard_map/ppermute | solution.py:704

commit v15 on v14

--- a/solution.py
+++ b/solution.py
@@ -344,7 +344,7 @@
 
 def first_kernel(
     z, table_ref, p_in_ref, u_in_ref, halo_a_ref, halo_b_ref, index_ref, corner_ref, weight_ref,
-    projector_ref, coupling_ref, p_ref, out_ref, uw_ref, pj_ref, beside_ref, u_ref,
+    projector_ref, coupling_ref, p_ref, out_ref, uw_ref, pj_ref, beside_ref, u_ref, parts_ref,
 ):
     rows = slice(z.index_row, z.index_row + z.entries)
     line = iota((1, LANES), 1)
@@ -370,7 +370,8 @@
     pj_ref[...] = jnp.zeros_like(pj_ref)
     pj_ref[:, : z.elem] = projector_ref[...]
     groups = full_groups(z, table_ref), z.slots // z.together
-    gather_middle(z, groups, True, table_ref, index_ref, p_ref, u_ref)
+    split_window(z, p_ref, parts_ref)
+    gather_middle(z, groups, True, table_ref, index_ref, p_ref, u_ref, parts_ref)
     gather_corners(z, corner_ref, p_ref, weight_ref, u_ref, uw_ref)
     parts = contributions(z, table_ref, pj_ref, u_ref)
     small_lane, small_row = iota((ROWS, LANES), 1), iota((ROWS, LANES), 0)
@@ -762,7 +763,7 @@
     p, sums, uw, pj, beside = call(
         functools.partial(first_kernel, z),
         [(reach, F32), (message, F32), (cells, F32), (entries, F32), ((1, LANES), jnp.int32)],
-        [(cells, F32)],
+        [(cells, F32), (acc, BF16)],
         (table,),
         p, u, *ext, index, corner, weight, flat_projector, atom_matrix,
     )

time: 50.6 us -> 50.4 us (level)
  no operation moved by 1% of the time
where the time goes in v15:
time: 50.4 us; the launch traced here: 49.7 us
  starting transfers between devices  23.6 us (47%)
  Pallas kernels  23.2 us (46%)
  waiting for transfers between devices  1.31 us (3%)
  between operations  0.93 us (2%)
  local copies, waits for them, and re-layouts  0.64 us (1%)
    pallas_call x10, Pallas kernels, call(): pl.pallas_call(kernel, out_shape=[jax.ShapeDtypeStruct(s, d) if i in in_h...  22.1 us
    ppermute x6, starting transfers between devices, exchange(): return (lax.ppermute(a, 'dom', near), lax.ppermute(b, 'dom', far))  12 us
    all_to_all x1, starting transfers between devices, on_device(): coupled = lax.all_to_all(sums, 'dom', 0, 0)  5.92 us
    all_to_all x1, starting transfers between devices, on_device(): totals = lax.all_to_all(sums, 'dom', 0, 0)  5.7 us
    pallas_call x1, Pallas kernels, on_device(): pl.pallas_call(functools.partial(last_kernel, z), out_shape=[jax.ShapeDty...  1.05 us
  transfers between devices with their start and end apart: 8, of which 2 were waited for; matrix products, arithmetic and copies ran while one was open for 0% of the time, Pallas kernels for 29%

profile of v15, /device:TPU:1, one launch (start us, length us, event | category | flops | bytes accessed | tf_op | source)
XLA Modules:
  0.0 49.7 jit_solution(4659543629679446819)
XLA Ops:
  0.7 1.2 %shard_map.143 = (f32[88,384]{1,0:T(8,128)S(1)}, f32[88,384]{1,0:T(8,128)S(1)}, f32[16,128]{1,0:T(8,128)S(1)}) custom-call(s32[1]{0:T(128)} %bitcast.pos_ref, s32[8]{0:T(128)} %cell_hbm.1, s32[8]{0:T(128)} %atom_hbm.1, s32[32]{0:T(128)} %scount_hbm.1, f32[8]{0:T(128)} %shift_hbm.1, f32[8,6656]{1,0:T(8,128)} %rhs_ref.5, f32[52,128]{1,0:T(8,128)} %bitcast.6, ...), custom_call_target="tpu_custom_call" | custom-call | tf_op jit(solution)/shard_map/pallas_call | solution.py:710
  1.9 0.1 collective-permute-start
  1.9 4.5 %collective-permute-start.1 = (f32[88,384]{1,0:T(8,128)S(1)}, f32[88,384]{1,0:T(8,128)S(1)}, u32[]{:S(2)}, u32[]{:S(2)}) collective-permute-start(f32[88,384]{1,0:T(8,128)S(1)} %get-tuple-element.35), channel_id=1, source_target_pairs={{1,2},{2,1},{3,4},{4,3},{5,6},{6,5},{7,8},{8,7},{9,10},{10,9},{11,... | collective-permute-start | bytes 405512 | tf_op jit(solution)/shard_map/ppermute | solution.py:705
  6.5 0.0 copy-start.3
  6.5 0.0 copy-start.8
  6.5 0.2 shard_map.141
  6.7 0.6 %copy-done.3 = s32[32,343]{1,0:T(8,128)S(1)} copy-done((s32[32,343]{1,0:T(8,128)S(1)}, s32[32,343]{1,0:T(8,128)}, u32[]{:S(2)}) %copy-start.3) | copy-done | bytes 43928
  7.3 0.8 %shard_map.140 = (s32[32,1,384]{2,1,0:T(1,128)S(1)}, s32[1,128]{1,0:T(1,128)S(1)}, s32[1,128]{1,0:T(1,128)S(1)}, f32[256,128]{1,0:T(8,128)S(1)}) custom-call(s32[1]{0:T(128)} %bitcast.pos_ref, s32[32]{0:T(128)S(1)} %copy-done.10, f32[32]{0:T(128)S(1)} %copy-done.11, s32[8]{0:T(128)S(1)} %copy-done.7, s32[8]{0:T(128)S(1)} %copy-done.8, s32[32]{0:T(128)S(1)} %copy-done.9, ...), custom_call_target="tpu_custom_call" | custom-call | tf_op jit(solution)/shard_map/pallas_call | solution.py:710
  8.2 2.3 %shard_map.142.u_in_ref = f32[256,384]{1,0:T(8,128)S(1)} custom-call(s32[1,128]{1,0:T(1,128)S(1)} %get-tuple-element.31.table_ref, f32[8,9472]{1,0:T(8,128)S(1)} %get-tuple-element.32.p_ref.p_in_ref, s32[32,1,384]{2,1,0:T(1,128)S(1)} %get-tuple-element.33.index_ref), custom_call_target="tpu_custom_call" | custom-call | tf_op jit(solution)/shard_map/pallas_call | solution.py:710
  10.6 2.5 %shard_map.144 = (f32[8,9472]{1,0:T(8,128)S(1)}, f32[32,4,128]{2,1,0:T(4,128)}, f32[256,384]{1,0:T(8,128)S(1)}, f32[64,384]{1,0:T(8,128)S(1)}, s32[1,128]{1,0:T(1,128)S(1)}) custom-call(s32[1,128]{1,0:T(1,128)S(1)} %get-tuple-element.31.table_ref, f32[8,9472]{1,0:T(8,128)S(1)} %get-tuple-element.32.p_ref.p_in_ref, f32[256,384]{1,0:T(8,128)S(1)} %shard_map.142.u_in_ref, ...), custom_call_target="tpu_custom_call" | custom-call | tf_op jit(solution)/shard_map/pallas_call | solution.py:710
  13.0 5.9 %all-to-all-start = ((f32[32,4,128]{2,1,0:T(4,128)}), f32[32,4,128]{2,1,0:T(4,128)S(1)}, u32[]{:S(2)}, u32[]{:S(2)}) async-start(f32[32,4,128]{2,1,0:T(4,128)} %get-tuple-element.41), calls=%async_computation | async-start | bytes 131072 | tf_op jit(solution)/shard_map/all_to_all | solution.py:770
  18.9 3.2 %shard_map.145 = (f32[8,7680]{1,0:T(8,128)S(1)}, f32[10,1024]{1,0:T(8,128)S(1)}, f32[10,1024]{1,0:T(8,128)S(1)}, bf16[384,384]{1,0:T(8,128)(2,1)S(1)}, bf16[384,384]{1,0:T(8,128)(2,1)S(1)}) custom-call(s32[1,128]{1,0:T(1,128)S(1)} %get-tuple-element.31.table_ref, s32[32,1,384]{2,1,0:T(1,128)S(1)} %get-tuple-element.33.index_ref, ...), custom_call_target="tpu_custom_call" | custom-call | tf_op jit(solution)/shard_map/pallas_call | solution.py:710
  22.2 0.3 collective-permute-start.2
  22.5 3.4 %collective-permute-start.3 = (f32[10,1024]{1,0:T(8,128)S(1)}, f32[10,1024]{1,0:T(8,128)S(1)}, u32[]{:S(2)}, u32[]{:S(2)}) collective-permute-start(f32[10,1024]{1,0:T(8,128)S(1)} %get-tuple-element.48), channel_id=1, source_target_pairs={{1,2},{2,1},{3,4},{4,3},{5,6},{6,5},{7,8},{8,7},{9,10},{10,9},{11,... | collective-permute-start | bytes 122888 | tf_op jit(solution)/shard_map/ppermute | solution.py:705
  25.9 0.3 all-to-all-done.sums_ref.coupling_ref
  26.2 2.6 %shard_map.146.image_ref = f32[8,7680]{1,0:T(8,128)S(1)} custom-call(s32[1,128]{1,0:T(1,128)S(1)} %get-tuple-element.31.table_ref, f32[32,4,128]{2,1,0:T(4,128)S(1)} %all-to-all-done.sums_ref.coupling_ref, f32[32,4,128]{2,1,0:T(4,128)S(1)} %all-to-all-done.sums_ref.coupling_ref, s32[32,1,384]{2,1,0:T(1,128)S(1)} %get-tuple-element.33.index_ref, ...), custom_call_target="tpu_custom_call" | custom-call | tf_op jit(solution)/shard_map/pallas_call | solution.py:710
  28.9 4.0 %shard_map.147 = (f32[8,7680]{1,0:T(8,128)S(1)}, f32[8,9472]{1,0:T(8,128)S(1)}, f32[32,4,128]{2,1,0:T(4,128)}, f32[256,384]{1,0:T(8,128)S(1)}) custom-call(s32[1,128]{1,0:T(1,128)S(1)} %get-tuple-element.31.table_ref, f32[8,7680]{1,0:T(8,128)S(1)} %shard_map.146.image_ref, f32[8,9472]{1,0:T(8,128)S(1)} %get-tuple-element.38.p_ref, ...), custom_call_target="tpu_custom_call" | custom-call | tf_op jit(solution)/shard_map/pallas_call | solution.py:710
  32.9 5.7 %all-to-all-start.1 = ((f32[32,4,128]{2,1,0:T(4,128)}), f32[32,4,128]{2,1,0:T(4,128)S(1)}, u32[]{:S(2)}, u32[]{:S(2)}) async-start(f32[32,4,128]{2,1,0:T(4,128)} %get-tuple-element.53), calls=%async_computation.1 | async-start | bytes 131072 | tf_op jit(solution)/shard_map/all_to_all | solution.py:793
  38.6 2.6 %shard_map.148 = (f32[8,7680]{1,0:T(8,128)S(1)}, f32[8,1024]{1,0:T(8,128)S(1)}, f32[8,1024]{1,0:T(8,128)S(1)}) custom-call(s32[1,128]{1,0:T(1,128)S(1)} %get-tuple-element.31.table_ref, s32[32,1,384]{2,1,0:T(1,128)S(1)} %get-tuple-element.33.index_ref, s32[1,128]{1,0:T(1,128)S(1)} %get-tuple-element.36.corner_ref, f32[256,384]{1,0:T(8,128)S(1)} %get-tuple-element.54.refs_0_), custom_call_target="tpu_custom_call" | custom-call | tf_op jit(solution)/shard_map/pallas_call | solution.py:710
  41.1 0.3 collective-permute-start.4
  41.5 3.4 %collective-permute-start.5 = (f32[8,1024]{1,0:T(8,128)S(1)}, f32[8,1024]{1,0:T(8,128)S(1)}, u32[]{:S(2)}, u32[]{:S(2)}) collective-permute-start(f32[8,1024]{1,0:T(8,128)S(1)} %get-tuple-element.59), channel_id=1, source_target_pairs={{1,2},{2,1},{3,4},{4,3},{5,6},{6,5},{7,8},{8,7},{9,10},{10,9},{11,... | collective-permute-start | bytes 98312 | tf_op jit(solution)/shard_map/ppermute | solution.py:705
  44.9 1.0 %all-to-all-done.1.sums_ref = f32[32,4,128]{2,1,0:T(4,128)S(1)} async-done(((f32[32,4,128]{2,1,0:T(4,128)}), f32[32,4,128]{2,1,0:T(4,128)S(1)}, u32[]{:S(2)}, u32[]{:S(2)}) %all-to-all-start.1) | async-done | bytes 65568 | tf_op jit(solution)/shard_map/all_to_all | solution.py:793
  45.8 2.8 %shard_map.149 = (f32[8,7680]{1,0:T(8,128)S(1)}, f32[1,128]{1,0:T(1,128)S(1)}) custom-call(s32[1,128]{1,0:T(1,128)S(1)} %get-tuple-element.31.table_ref, f32[32,4,128]{2,1,0:T(4,128)S(1)} %all-to-all-done.1.sums_ref, f32[32,4,128]{2,1,0:T(4,128)S(1)} %all-to-all-done.sums_ref.coupling_ref, s32[32,1,384]{2,1,0:T(1,128)S(1)} %get-tuple-element.33.index_ref, ...), custom_call_target="tpu_custom_call" | custom-call | tf_op jit(solution)/shard_map/pallas_call | solution.py:710
  48.6 1.1 %shard_map.150 = (f32[8,6656]{1,0:T(8,128)}, f32[8,6656]{1,0:T(8,128)}) custom-call(f32[8,6656]{1,0:T(8,128)S(1)} %copy-done, f32[8,9472]{1,0:T(8,128)S(1)} %get-tuple-element.38.p_ref, f32[2,7680]{1,0:T(2,128)S(1)} %get-tuple-element.39.refs_2_.diag_in_ref.diag_ref, f32[16,128]{1,0:T(8,128)S(1)} %get-tuple-element.40.shift_ref, ...), custom_call_target="tpu_custom_call" | custom-call | tf_op jit(solution)/shard_map/pallas_call | solution.py:808
  (27 shorter events, 0.1 us)
Async XLA Ops:
  0.6 5.8 %copy-start = (f32[8,6656]{1,0:T(8,128)S(1)}, f32[8,6656]{1,0:T(8,128)}, u32[]{:S(2)}) copy-start(f32[8,6656]{1,0:T(8,128)} %rhs_ref.5) | copy-start | bytes 638980
  0.6 5.8 %copy-start.4 = (f32[6656]{0:T(1024)S(1)}, f32[6656]{0:T(1024)}, u32[]{:S(2)}) copy-start(f32[6656]{0:T(1024)} %param.15) | copy-start | bytes 79876
  0.7 5.8 %copy-start.5 = (f32[6656]{0:T(1024)S(1)}, f32[6656]{0:T(1024)}, u32[]{:S(2)}) copy-start(f32[6656]{0:T(1024)} %param.14) | copy-start | bytes 79876
  1.9 8.7 %collective-permute-start = (f32[88,384]{1,0:T(8,128)S(1)}, f32[88,384]{1,0:T(8,128)S(1)}, u32[]{:S(2)}, u32[]{:S(2)}) collective-permute-start(f32[88,384]{1,0:T(8,128)S(1)} %get-tuple-element.34), channel_id=1, source_target_pairs={{0,1},{1,0},{2,3},{3,2},{4,5},{5,4},{6,7},{7,6},{8,9},{9,8},{10,11... | collective-permute-start | bytes 405512 | tf_op jit(solution)/shard_map/ppermute | solution.py:705
  1.9 8.6 %collective-permute-start.1 = (f32[88,384]{1,0:T(8,128)S(1)}, f32[88,384]{1,0:T(8,128)S(1)}, u32[]{:S(2)}, u32[]{:S(2)}) collective-permute-start(f32[88,384]{1,0:T(8,128)S(1)} %get-tuple-element.35), channel_id=1, source_target_pairs={{1,2},{2,1},{3,4},{4,3},{5,6},{6,5},{7,8},{8,7},{9,10},{10,9},{11,... | collective-permute-start | bytes 405512 | tf_op jit(solution)/shard_map/ppermute | solution.py:705
  6.5 0.8 %copy-start.3 = (s32[32,343]{1,0:T(8,128)S(1)}, s32[32,343]{1,0:T(8,128)}, u32[]{:S(2)}) copy-start(s32[32,343]{1,0:T(8,128)} %conn_ref.3) | copy-start | bytes 131716
  6.5 0.8 %copy-start.7 = (s32[8]{0:T(128)S(1)}, s32[8]{0:T(128)}, u32[]{:S(2)}) copy-start(s32[8]{0:T(128)} %cell_hbm.1) | copy-start | bytes 100
  6.5 0.8 %copy-start.8 = (s32[8]{0:T(128)S(1)}, s32[8]{0:T(128)}, u32[]{:S(2)}) copy-start(s32[8]{0:T(128)} %atom_hbm.1) | copy-start | bytes 100
  6.5 0.8 %copy-start.9 = (s32[32]{0:T(128)S(1)}, s32[32]{0:T(128)}, u32[]{:S(2)}) copy-start(s32[32]{0:T(128)} %scount_hbm.1) | copy-start | bytes 388
  6.5 0.8 %copy-start.10 = (s32[32]{0:T(128)S(1)}, s32[32]{0:T(128)}, u32[]{:S(2)}) copy-start(s32[32]{0:T(128)} %count_ref.1) | copy-start | bytes 388
  6.5 0.8 %copy-start.11 = (f32[32]{0:T(128)S(1)}, f32[32]{0:T(128)}, u32[]{:S(2)}) copy-start(f32[32]{0:T(128)} %scale_ref.1) | copy-start | bytes 388
  8.1 2.4 %copy-start.2 = (f32[8,8,343]{2,1,0:T(8,128)S(1)}, f32[8,8,343]{2,1,0:T(8,128)}, u32[]{:S(2)}) copy-start(f32[8,8,343]{2,1,0:T(8,128)} %param.21) | copy-start | bytes 263428
  8.1 2.4 %copy-start.6 = (f32[2,8,8]{2,1,0:T(8,128)S(1)}, f32[2,8,8]{2,1,0:T(8,128)}, u32[]{:S(2)}) copy-start(f32[2,8,8]{2,1,0:T(8,128)} %coupling_ref.1) | copy-start | bytes 1540
  10.5 8.4 %copy-start.1 = (f32[343,343]{1,0:T(8,128)S(1)}, f32[343,343]{1,0:T(8,128)}, u32[]{:S(2)}) copy-start(f32[343,343]{1,0:T(8,128)} %refs_1_.1) | copy-start | bytes 1411792
  13.0 13.2 %all-to-all-start = ((f32[32,4,128]{2,1,0:T(4,128)}), f32[32,4,128]{2,1,0:T(4,128)S(1)}, u32[]{:S(2)}, u32[]{:S(2)}) async-start(f32[32,4,128]{2,1,0:T(4,128)} %get-tuple-element.41), calls=%async_computation | async-start | bytes 131072 | tf_op jit(solution)/shard_map/all_to_all | solution.py:770
  22.2 6.7 %collective-permute-start.2 = (f32[10,1024]{1,0:T(8,128)S(1)}, f32[10,1024]{1,0:T(8,128)S(1)}, u32[]{:S(2)}, u32[]{:S(2)}) collective-permute-start(f32[10,1024]{1,0:T(8,128)S(1)} %get-tuple-element.47), channel_id=1, source_target_pairs={{0,1},{1,0},{2,3},{3,2},{4,5},{5,4},{6,7},{7,6},{8,9},{9,8},{10,11... | collective-permute-start | bytes 122888 | tf_op jit(solution)/shard_map/ppermute | solution.py:705
  22.5 6.4 %collective-permute-start.3 = (f32[10,1024]{1,0:T(8,128)S(1)}, f32[10,1024]{1,0:T(8,128)S(1)}, u32[]{:S(2)}, u32[]{:S(2)}) collective-permute-start(f32[10,1024]{1,0:T(8,128)S(1)} %get-tuple-element.48), channel_id=1, source_target_pairs={{1,2},{2,1},{3,4},{4,3},{5,6},{6,5},{7,8},{8,7},{9,10},{10,9},{11,... | collective-permute-start | bytes 122888 | tf_op jit(solution)/shard_map/ppermute | solution.py:705
  32.9 13.0 %all-to-all-start.1 = ((f32[32,4,128]{2,1,0:T(4,128)}), f32[32,4,128]{2,1,0:T(4,128)S(1)}, u32[]{:S(2)}, u32[]{:S(2)}) async-start(f32[32,4,128]{2,1,0:T(4,128)} %get-tuple-element.53), calls=%async_computation.1 | async-start | bytes 131072 | tf_op jit(solution)/shard_map/all_to_all | solution.py:793
  41.1 7.5 %collective-permute-start.4 = (f32[8,1024]{1,0:T(8,128)S(1)}, f32[8,1024]{1,0:T(8,128)S(1)}, u32[]{:S(2)}, u32[]{:S(2)}) collective-permute-start(f32[8,1024]{1,0:T(8,128)S(1)} %get-tuple-element.58), channel_id=1, source_target_pairs={{0,1},{1,0},{2,3},{3,2},{4,5},{5,4},{6,7},{7,6},{8,9},{9,8},{10,11... | collective-permute-start | bytes 98312 | tf_op jit(solution)/shard_map/ppermute | solution.py:705
  41.5 7.1 %collective-permute-start.5 = (f32[8,1024]{1,0:T(8,128)S(1)}, f32[8,1024]{1,0:T(8,128)S(1)}, u32[]{:S(2)}, u32[]{:S(2)}) collective-permute-start(f32[8,1024]{1,0:T(8,128)S(1)} %get-tuple-element.59), channel_id=1, source_target_pairs={{1,2},{2,1},{3,4},{4,3},{5,6},{6,5},{7,8},{8,7},{9,10},{10,9},{11,... | collective-permute-start | bytes 98312 | tf_op jit(solution)/shard_map/ppermute | solution.py:705
